TPU v7x, 32 devices: a whole 2x2x4 slice. The times are simulated.
32 devices in a mesh: orb: 8 (over y, x, core), grid: 4 (over z).
Axes of the slice: x: 2, y: 2, z: 4, core: 2. Of those that a mesh axis runs over, the one named last changes fastest.
Arguments:
- orbitals: float32 [128, 32, 4096], P('orb', 'grid'), may hold values from -6 to 6
- rotation: float32 [128, 128], replicated, may hold values from -0.5 to 0.5
- tile_list: int32 [4, 2], replicated, may hold values from 0 to 31, as said below
- pair_mask: int32 [128, 128], replicated, may hold values from 0 to 1, as said below
Outputs:
- exchange_term: float32 [128, 32, 4096], P('orb', 'grid')
Inputs may be any that keep to these rules, and one draw needn't show every extreme that they name: `tile_list`: row t names one tile: its target block and its source block of 4 orbitals each; no tile is named twice. `pair_mask`: among the 64 orbital pairs that lie in listed tiles, exactly 32 are 1.
All inputs are finite; a program needn't handle non-finite values.
Results may differ from a plain program's by a relative error of at most 0.0003.
Values sent between devices are 32-bit elements; how exact they have to be, the bound alone decides.
No kernel may reach another device: no remote copies, remote signals or barrier semaphores. Data moves between devices by JAX's collectives and lax.ppermute only.
A program may use at most 64 MiB of HBM per device.

v0:
```python
import functools
import itertools

import jax
import jax.numpy as jnp
import numpy as np
from jax import lax
from jax.experimental import pallas as pl
from jax.experimental.pallas import tpu as pltpu
from jax.sharding import PartitionSpec as P


BLK = 4
NY = 64
NZ = 64
LANES = 128
SUB = 8
CHUNKS = 2
COUPLING = 0.25
SCREENING = 0.1

precise = lax.Precision.HIGHEST
f32 = jnp.float32
bf16 = jnp.bfloat16

VM = pl.BlockSpec(memory_space=pltpu.VMEM)
SM = pl.BlockSpec(memory_space=pltpu.SMEM)
ANY = pl.BlockSpec(memory_space=pl.ANY)
HBM = pl.BlockSpec(memory_space=pltpu.HBM)
DMA = pltpu.SemaphoreType.DMA


def grant(mib):
    return pltpu.CompilerParams(vmem_limit_bytes=mib << 20)


def sine_np(n):
    k = np.arange(1, n + 1, dtype=np.float64)
    return np.sqrt(2.0 / (n + 1)) * np.sin(np.pi * k[:, None] * k[None, :] / (n + 1))


def eigen_np(n):
    k = np.arange(1, n + 1, dtype=np.float64)
    return 2.0 - 2.0 * np.cos(np.pi * k / (n + 1))


def halves_np(table):
    high = np.asarray(table, np.float32).astype(jnp.bfloat16)
    low = (np.asarray(table, np.float64) - high.astype(np.float64)).astype(jnp.bfloat16)
    return jnp.asarray(high), jnp.asarray(low)


def y_order():
    rows = LANES // NZ
    return np.arange(NY).reshape(NY // rows, rows).T.reshape(-1)


def y_tables():
    sine, planes = sine_np(NY), sine_np(SUB)
    even, odd = np.kron(sine[0::2, 0::2], planes), np.kron(sine[1::2, 0::2], planes)
    return np.stack([even, odd]), np.stack([even, odd.T])


def turned(x):
    count = x.shape[0] // SUB
    return jnp.concatenate([x[(count - 1 - t) * SUB:(count - t) * SUB] for t in range(count)])


def z_table():
    half = LANES // NZ
    sine = sine_np(NZ)
    table = np.zeros((2, half, NZ, half, 2, NZ))
    for pair in range(2):
        for h in range(half):
            table[pair, h, :, h, pair, :] = sine
    return table.reshape(2 * half * NZ, half * 2 * NZ)


def line_np():
    c = eigen_np(NY)[y_order()][:, None] + eigen_np(NZ)[None, :] + SCREENING
    c = np.concatenate([c, c], axis=1)
    return c, 2.0 / (2.0 + c + np.sqrt(c * (c + 4.0)))


def host_np(chips):
    table = np.zeros((chips**chips, chips), np.int32)
    for owners in itertools.product(range(chips), repeat=chips):
        best = None
        for tiles in itertools.permutations(range(chips)):
            hops = [bin(chip ^ owners[tile]).count("1") for chip, tile in enumerate(tiles)]
            cost = (max(hops), sum(hops))
            if best is None or cost < best[0]:
                best = (cost, tiles)
        table[sum(own * chips**t for t, own in enumerate(owners))] = best[1]
    return table


def dot(a, b):
    return jnp.dot(a, b, preferred_element_type=f32)


def split(x):
    high = x.astype(bf16)
    return high, (x - high.astype(f32)).astype(bf16)


def dot3(a, b):
    return dot(a[0], b[0]) + dot(a[0], b[1]) + dot(a[1], b[0])


def my_core():
    return lax.rem(lax.axis_index("orb"), 2)


def my_place():
    o = lax.axis_index("orb")
    return o, lax.rem(o, 2), lax.div(o, 2)


def fetch(source, out, sem, side, start, number):
    at = pl.multiple_of(side * (source.shape[2] // 2) + start, LANES)
    step = out.shape[0] // number
    return [
        pltpu.make_async_copy(
            source.at[pl.ds(n * step, step), :, pl.ds(at, out.shape[2])], out.at[pl.ds(n * step, step)], sem.at[n]
        )
        for n in range(number)
    ]


def take_kernel(start, source, *rest):
    out, sem = rest[-2:]
    copies = fetch(source, out, sem, 1 - my_core(), start, sem.shape[0])
    for copy in copies:
        copy.start()
    for copy in copies:
        copy.wait()


class Place:
    def __init__(self, per_device, tiles, host):
        self.o, self.core, self.chip = my_place()
        self.tiles, self.host = tiles, host
        self.chips = tiles.shape[0]
        owners = [lax.div(tiles[t, 0] * BLK, 2 * per_device) for t in range(self.chips)]
        key, same = 0, True
        for t in range(self.chips):
            key = key + owners[t] * self.chips**t
            same = same & (owners[t] == owners[0])
        self.key, self.same = key, same
        self.bit_1 = jnp.where(self.core == 0, 1, 2)
        self.bit_2 = 3 - self.bit_1

    def tile(self, chip):
        return self.host[self.key * self.chips + chip]

    def heads(self, chip):
        tile = self.tile(chip)
        return BLK * self.tiles[tile, 0], BLK * self.tiles[tile, 1]


def setup_kernel(per_device, tiles, host, rotation, source, after, *rest):
    fetched, (high, low, sem) = rest[:-3], rest[-3:]
    core = my_core()
    copies = []
    for n, out in enumerate(fetched):
        side, chunk = (1 - core, n + 1) if n < CHUNKS - 1 else (core, n - CHUNKS + 1)
        copies += fetch(source, out, sem.at[n], side, chunk * out.shape[2], sem.shape[1])
    for copy in copies:
        copy.start()
    at = Place(per_device, tiles, host)
    pair = BLK // 2
    heads = [at.heads(chip) for chip in (at.chip ^ 3, at.chip ^ at.bit_1, at.chip ^ at.bit_2, at.chip)]
    wanted = []
    for a, b in heads:
        wanted += [a + (1 - core) * pair] + [b + w for w in range(BLK)] + [a + core * pair]
    for u in range(1, pair):
        for a, b in heads:
            wanted += [a + (1 - core) * pair + u, a + core * pair + u]
    lane = lax.broadcasted_iota(jnp.int32, (SUB, LANES), 1)
    chosen = jnp.concatenate([jnp.where(lane == n, 1.0, 0.0) for n in wanted]).astype(bf16)
    rows = chosen.shape[0]
    row = lax.broadcasted_iota(jnp.int32, (LANES, LANES), 0)
    column = lax.broadcasted_iota(jnp.int32, (LANES, LANES), 1)
    columns = [
        jnp.where(row - (at.o ^ e) * per_device == jnp.right_shift(column, 3), 1.0, 0.0).astype(bf16)
        for e in range(2)
    ]
    keep = (lax.broadcasted_iota(jnp.int32, (rows, LANES), 0) & (SUB - 1)) == (
        lax.broadcasted_iota(jnp.int32, (rows, LANES), 1) & (SUB - 1)
    )
    for out, values in zip((high, low), split(rotation[...])):
        picked = lax.dot_general(chosen, values, (((1,), (1,)), ((), ())), preferred_element_type=f32).astype(bf16)
        for e in range(2):
            out[:, e * LANES:(e + 1) * LANES] = jnp.where(keep, dot(picked, columns[e]), 0.0).astype(bf16)
    for copy in copies:
        copy.wait()


def ready_kernel(per_device, n_grid, tiles, host, mask, log_r, *rest):
    out, powers, flags, match, alone, zeros, sem = rest[-7:]
    zeros[...] = jnp.zeros(zeros.shape, f32)
    step = zeros.shape[0]
    copies = [
        pltpu.make_async_copy(zeros, out.at[pl.ds(n * step, step)], sem.at[n]) for n in range(out.shape[0] // step)
    ]
    for copy in copies:
        copy.start()
    begin, size_x = SUB * lax.axis_index("grid"), SUB * n_grid
    exponents = (
        2 * begin + SUB + 1,
        2 * size_x + 1 - SUB - 2 * begin,
        2 * size_x + 2 - 2 * begin,
        2 * begin,
        2 * begin + 2 * SUB + 2,
        2 * size_x - 2 * SUB - 2 * begin,
    )
    for n, exponent in enumerate(exponents):
        power = jnp.exp(exponent.astype(f32) * log_r[...])
        powers[n] = power if n < 2 else 1.0 - power
    at = Place(per_device, tiles, host)
    alone[0] = at.same.astype(jnp.int32)
    a, b = at.heads(at.chip)
    pair = BLK // 2
    live = mask[...].astype(f32)
    row = lax.broadcasted_iota(jnp.int32, live.shape, 0)
    column = lax.broadcasted_iota(jnp.int32, (1, live.shape[1]), 1)
    for u in range(pair):
        line = jnp.sum(jnp.where(row == a + at.core * pair + u, live, 0.0), axis=0, keepdims=True)
        for w in range(BLK):
            flags[u * BLK + w] = jnp.sum(jnp.where(column == b + w, line, 0.0))
    blocks = per_device // BLK
    parts = [0, at.bit_1, at.bit_2, 3, 0, at.bit_2, at.bit_1, 3]
    for n, flip in enumerate(parts):
        home = tiles[at.tile(at.chip ^ flip), 0]
        for block in range(blocks):
            hit = home == at.o * blocks + block
            if n % 4 == 3:
                hit = hit & at.same
            match[block * len(parts) + n] = hit.astype(jnp.int32)
    for copy in copies:
        copy.wait()


def join_kernel(x, y, out):
    out[0] = x[...]
    out[1] = y[...]


def rotate_kernel(first, high, low, *rest):
    send, keep = rest[-2:]
    rows = send.shape[0] * SUB
    part = pl.ds(first, 2 * rows)
    table = (high[part, :], low[part, :])
    at = 0
    step = 2 * LANES
    while at < send.shape[2]:
        width = rest[0].shape[2]
        n, inner = at // width, at % width
        lanes = slice(inner, inner + step)
        mine, theirs = rest[2 * n], rest[2 * n + 1]
        depth = mine.shape[0] * SUB
        cells = jnp.concatenate([mine[:, :, lanes].reshape(depth, step), theirs[:, :, lanes].reshape(depth, step)])
        total = dot3(table, split(cells))
        lanes = slice(at, at + step)
        send[:, :, lanes] = total[:rows].reshape(send.shape[0], SUB, step)
        keep[:, :, lanes] = total[rows:].reshape(keep.shape[0], SUB, step)
        at += step


def pass_kernel(keep, got, *rest):
    out = rest[-1]
    count = out.shape[0]
    out[...] = keep[:count] + got[:count]


def finish_kernel(keep, got, passed, *rest):
    out = rest[-1]
    count = out.shape[0]
    out[...] = keep[count:] + got[count:] + passed[...]


def sub_sums(values):
    row = lax.broadcasted_iota(jnp.int32, values[0].shape, 0)
    for s in (4, 2):
        low = (row & s) == 0
        paired = []
        for n in range(s):
            a, b = values[n], values[n + s]
            paired.append(jnp.where(low, a, pltpu.roll(b, s, 0)) + jnp.where(low, pltpu.roll(a, SUB - s, 0), b))
        values = paired
    even = (row & 1) == 0
    a, b = values
    return jnp.where(even, a, pltpu.roll(b, 1, 0)), jnp.where(even, pltpu.roll(a, SUB - 1, 0), b)


def fields(u, own, other, first_own, first_other):
    table = []
    for side, sources, targets in ((0, first_own, own), (1, first_other, other)):
        for n, ref in enumerate(sources):
            if u == 0:
                table.append((side, n, ref, targets[n], BLK + 1 if side == 0 else 0, 0))
            else:
                table.append((side, n, ref, targets[0], 1 if side == 0 else 0, n * ref.shape[2]))
    return table


def forward_kernel(u, counts, *refs):
    groups = []
    for count in counts[:-1]:
        groups.append(refs[:count])
        refs = refs[count:]
    first_own, first_other, own, other = groups[:4]
    y_hi, y_lo, z_hi, z_lo, ends, powers = refs[:6]
    messages, (spectrum, a_out, b_out, dens) = refs[-4 - counts[-1]:-4], refs[-4:]
    if u == 0:
        own, other = first_own, first_other
    core, g = my_core(), lax.axis_index("grid")
    tiles = first_own[0].shape[2] // LANES
    for side, n, source, target, slot, offset in fields(u, own, other, first_own, first_other):
        half = (core if side == 0 else 1 - core) * (len(first_own) * tiles * SUB)
        for t in range(tiles):
            lanes = pl.ds(t * LANES, LANES)
            value = target[slot, :, pl.ds(offset + t * LANES, LANES)]
            rows = pl.ds(pl.multiple_of(half + (n * tiles + t) * SUB, SUB), SUB)
            for w in range(BLK):
                dens[rows, w * LANES:(w + 1) * LANES] = value * source[1 + w, :, lanes]
    z = (z_hi[...], z_lo[...])
    half = dens.shape[0]
    for q in range(BLK // 2):
        out = dot3(split(dens[:, q * 2 * LANES:(q + 1) * 2 * LANES]), z)
        mirror = turned(out[:, LANES:])
        spectrum[:half, q * LANES:(q + 1) * LANES] = out[:, :LANES] + mirror
        spectrum[half:, q * LANES:(q + 1) * LANES] = out[:, :LANES] - mirror
    for parity in range(2):
        part = pl.ds(parity * half, half)
        spectrum[part, :] = dot3((y_hi[parity], y_lo[parity]), split(spectrum[part, :]))

    def reduce(group, carry):
        lines = pl.ds(pl.multiple_of(group * SUB, SUB), SUB)
        near, far = powers[0, lines, :], powers[1, lines, :]
        for q in range(BLK // 2):
            lanes = slice(q * LANES, (q + 1) * LANES)
            values = []
            for k in range(SUB):
                rows = pl.ds(pl.multiple_of((group * SUB + k) * SUB, SUB), SUB)
                values.append(ends[rows, :] * spectrum[rows, lanes])
            even, odd = sub_sums(values)
            rightward = (even + odd) - near * (even - odd)
            leftward = (even - odd) - far * (even + odd)
            a_out[lines, lanes] = rightward
            b_out[lines, lanes] = leftward
            for k, out in enumerate(messages, 1):
                out[lines, lanes] = jnp.where((g ^ k) > g, rightward, leftward)
        return carry

    lax.fori_loop(0, NY // SUB, reduce, 0)


def backward_kernel(u, counts, flags, *refs):
    groups = []
    for count in counts:
        groups.append(refs[:count])
        refs = refs[count:]
    own, other, received = groups
    (y_hi, y_lo, z_hi, z_lo, inverse, basis, powers, steady, spectrum, a_in, b_in) = refs[:11]
    out, work, pot = refs[-3:]
    core, g = my_core(), lax.axis_index("grid")
    tiles = own[0].shape[2] // LANES
    first, last = basis[0], basis[1]

    def ends(group, carry):
        lines = pl.ds(pl.multiple_of(group * SUB, SUB), SUB)
        scale, r, slab = steady[0, lines, :], steady[1, lines, :], steady[2, lines, :]
        decays = [None, jnp.ones((SUB, LANES), f32), slab]
        while len(decays) <= len(received):
            decays.append(decays[-1] * slab)
        for q in range(BLK // 2):
            lanes = slice(q * LANES, (q + 1) * LANES)
            from_left = from_right = jnp.zeros((SUB, LANES), f32)
            for n, ref in enumerate(received, 1):
                distance = jnp.abs((g ^ n) - g)
                factor = decays[n]
                for d in range(1, n):
                    factor = jnp.where(distance == d, decays[d], factor)
                value = factor * ref[lines, lanes]
                is_left = (g ^ n) < g
                from_left = from_left + jnp.where(is_left, value, 0.0)
                from_right = from_right + jnp.where(is_left, 0.0, value)
            before = scale * (powers[2, lines, :] * from_left
                              + r * powers[3, lines, :] * (b_in[lines, lanes] + slab * from_right))
            after = scale * (powers[4, lines, :] * from_right
                             + r * powers[5, lines, :] * (a_in[lines, lanes] + slab * from_left))
            for k in range(SUB):
                rows = pl.ds(pl.multiple_of((group * SUB + k) * SUB, SUB), SUB)
                edge = first * before[k:k + 1] + last * after[k:k + 1]
                work[rows, lanes] = inverse[rows, :] * (spectrum[rows, lanes] + edge)
        return carry

    lax.fori_loop(0, NY // SUB, ends, 0)
    z = (z_hi[...], z_lo[...])
    half = pot.shape[0]
    for parity in range(2):
        part = pl.ds(parity * half, half)
        work[part, :] = dot3((y_hi[parity], y_lo[parity]), split(work[part, :]))
    for q in range(BLK // 2):
        lanes = slice(q * LANES, (q + 1) * LANES)
        even, odd = work[:half, lanes], work[half:, lanes]
        rows = jnp.concatenate([even + odd, turned(even - odd)], axis=1)
        pot[:, q * 2 * LANES:(q + 1) * 2 * LANES] = dot3(split(rows), z)
    for side, group in ((0, own), (1, other)):
        half = (core if side == 0 else 1 - core) * (len(own) * tiles)
        for n, ref in enumerate(group):
            for t in range(tiles):
                lanes = pl.ds(t * LANES, LANES)
                at = half + n * tiles + t
                rows = pl.ds(pl.multiple_of(at * SUB, SUB), SUB)
                total = None
                for w in range(BLK):
                    term = flags[u * BLK + w] * (pot[rows, w * LANES:(w + 1) * LANES] * ref[1 + w, :, lanes])
                    total = term if total is None else total + term
                out[:, pl.ds(pl.multiple_of(at * LANES, LANES), LANES)] = -total


def place_kernel(stride, match, *refs):
    parts, (out, rows, sem) = refs[:-4], refs[-3:]
    pair = BLK // 2
    blocks = out.shape[0] // BLK
    core = my_core()
    values = []
    for part in parts:
        values += [part] if len(part.shape) == 2 else [part.at[n] for n in range(part.shape[0])]
    parts, count = values, len(values) // pair

    def hits(b, side):
        return [(match[b * stride + side * stride // 2 + n], side * count // 2 + n) for n in range(count // 2)]

    def found(b, side):
        return sum(hit for hit, n in hits(b, side)) > 0

    def move(b, side):
        which = core if side == 0 else 1 - core
        at = b * BLK + which * pair
        return pltpu.make_async_copy(rows.at[b, side], out.at[pl.ds(at, pair)], sem.at[b, side])

    for b in range(blocks):
        for side in range(2):

            @pl.when(found(b, side))
            def _():
                rows[b, side] = jnp.zeros(rows.shape[2:], f32)
                for hit, n in hits(b, side):

                    @pl.when(hit > 0)
                    def _():
                        for u in range(pair):
                            rows[b, side, u] += parts[u * count + n][...]

                move(b, side).start()

    for b in range(blocks):
        for side in range(2):

            @pl.when(found(b, side))
            def _():
                move(b, side).wait()


def tile_device(orbitals, rotation, tile_list, pair_mask):
    shape = per_device, planes, width = orbitals.shape
    n_orb, n_grid = lax.axis_size("orb"), lax.axis_size("grid")
    size_x = planes * n_grid
    half = width // 2
    chips = n_orb // 2
    axes = ("orb", "grid")

    def swap(x, even, odd):
        moves = []
        for a in range(n_orb):
            flip = even if a % 2 == 0 else odd
            moves += [(a * n_grid + b, (a ^ flip) * n_grid + b) for b in range(n_grid)]
        return lax.ppermute(x, axes, moves)

    def cross(x, k):
        moves = [(a * n_grid + b, a * n_grid + (b ^ k)) for a in range(n_orb) for b in range(n_grid)]
        return lax.ppermute(x, axes, moves)

    chunk = half // CHUNKS
    orbitals = pltpu.with_memory_space_constraint(orbitals, pltpu.HBM)

    part = jax.ShapeDtypeStruct((per_device, planes, chunk), f32)
    copies = per_device // 2
    taken = pl.pallas_call(
        functools.partial(take_kernel, 0), out_shape=part, in_specs=[HBM], out_specs=VM,
        scratch_shapes=[DMA((copies,))], name="take", compiler_params=grant(4),
    )(orbitals)
    theirs = [swap(taken, 1, 1)]

    pair = BLK // 2
    firsts = (BLK + 2) * chips
    rows = (firsts + 2 * (pair - 1) * chips) * SUB
    wide_table = jax.ShapeDtypeStruct((rows, 2 * LANES), bf16)
    blocks = per_device // BLK
    c, r = line_np()
    c, r = line_np()
    host = jnp.asarray(host_np(chips).reshape(-1))
    *fetched, high, low = pl.pallas_call(
        functools.partial(setup_kernel, per_device),
        out_shape=[part] * (2 * CHUNKS - 1) + [wide_table] * 2,
        in_specs=[SM, SM, VM, HBM, ANY], out_specs=[VM] * (2 * CHUNKS + 1),
        scratch_shapes=[DMA((2 * CHUNKS - 1, copies))], name="setup", compiler_params=grant(8),
    )(tile_list, host, rotation, orbitals, taken)
    mine = fetched[CHUNKS - 1:]
    for n, taken in enumerate(fetched[:CHUNKS - 1], 1):
        theirs.append(swap(taken, 1, 1))

    def rotate(first, count, fields, *after):
        part = jax.ShapeDtypeStruct((count, planes, chunk * (len(fields) // 2)), f32)
        send, keep = pl.pallas_call(
            functools.partial(rotate_kernel, first * SUB), out_shape=(part, part),
            in_specs=[VM] * (2 + len(fields)) + [ANY] * len(after),
            out_specs=(VM, VM), compiler_params=grant(8),
        )(high, low, *fields, *after)
        return send, keep, swap(send, 2, 4)

    sums, last = [], ()
    for n in range(CHUNKS):
        sums.append(rotate(0, firsts // 2, [mine[n], theirs[n]], *last))
        last = (sums[-1][0],)
    both = [x for n in range(CHUNKS) for x in (mine[n], theirs[n])]
    sums.append(rotate(firsts, (pair - 1) * chips, both, *last))
    empty, powers, flags, match, alone = pl.pallas_call(
        functools.partial(ready_kernel, per_device, n_grid),
        out_shape=(pltpu.HBM(shape, f32), jax.ShapeDtypeStruct((6, NY, LANES), f32),
                   jax.ShapeDtypeStruct((pair * BLK,), f32), jax.ShapeDtypeStruct((blocks * 8,), jnp.int32),
                   jax.ShapeDtypeStruct((1,), jnp.int32)),
        in_specs=[SM, SM, VM, VM, ANY], out_specs=(HBM, VM, SM, SM, SM),
        scratch_shapes=[pltpu.VMEM((pair, planes, width), f32), DMA((per_device // pair,))], name="ready",
        compiler_params=grant(4),
    )(tile_list, host, pair_mask, jnp.asarray(np.log(r), f32), sums[-1][0])
    passing, own, other = [], [], []

    def pass_on(n, *after, spec=ANY):
        _, keep, got = sums[n]
        count = keep.shape[0] // 2
        value = pl.pallas_call(
            pass_kernel, out_shape=jax.ShapeDtypeStruct((count,) + keep.shape[1:], f32),
            in_specs=[VM] * 2 + [spec] * len(after), out_specs=VM, compiler_params=grant(4),
        )(keep, got, *after)
        passing.append((keep, got, swap(value, 4, 2)))
        return value

    def finish(n, *after):
        keep, got, passed = passing[n]
        own.append(pl.pallas_call(
            finish_kernel, out_shape=jax.ShapeDtypeStruct(passed.shape, f32), in_specs=[VM] * 3 + [ANY] * len(after),
            out_specs=VM, compiler_params=grant(4),
        )(keep, got, passed, *after))
        other.append(swap(own[-1], 1, 1))
        return own[-1]

    step = pass_on(0, empty, spec=HBM)
    for n in range(1, CHUNKS):
        step = pass_on(n, step)
    for n in range(CHUNKS):
        step = finish(n, step)
    last = (step,)

    sine_x, eigen_x = sine_np(planes), eigen_np(planes)
    ends = jnp.asarray(np.einsum("jp,pkl->kjl", sine_x, r[None] ** np.arange(planes - 1, -1, -1)[:, None, None])
                       .reshape(-1, LANES), f32)
    inverse = jnp.asarray((COUPLING / (eigen_x[None, :, None] + c[:, None, :])).reshape(-1, LANES), f32)
    basis = jnp.asarray(np.broadcast_to(sine_x[:, [0, -1]].T[:, :, None], (2, planes, LANES)), f32)
    steady = jnp.asarray(np.stack([r / ((1 - r**2) * (1 - r ** (2 * size_x + 2))), r, r**planes]), f32)

    y_there, y_back = y_tables()
    y_hi, y_lo = halves_np(y_there)
    yt_hi, yt_lo = halves_np(y_back)
    z_hi, z_lo = halves_np(z_table())
    zt_hi, zt_lo = halves_np(z_table().T)
    solved = []
    lines = jax.ShapeDtypeStruct((NY, 2 * LANES), f32)
    cube = (NY * SUB, 2 * LANES)
    wide = pltpu.VMEM((width // LANES * SUB, BLK * LANES), f32)
    base_own, base_other = own[:CHUNKS], other[:CHUNKS]
    for u in range(pair):
        if u:
            pass_on(CHUNKS, *last)
            finish(CHUNKS, *last)
        more_own, more_other = own[CHUNKS:][:u], other[CHUNKS:][:u]
        counts = (CHUNKS, CHUNKS, len(more_own), len(more_other))
        inputs = [*base_own, *base_other, *more_own, *more_other, y_hi, y_lo, z_hi, z_lo, ends, powers]
        *messages, spectrum, a, b = pl.pallas_call(
            functools.partial(forward_kernel, u, counts + (n_grid - 1,)),
            out_shape=[lines] * (n_grid - 1) + [jax.ShapeDtypeStruct(cube, f32), lines, lines],
            in_specs=[VM] * len(inputs) + [ANY] * len(last),
            out_specs=[VM] * (n_grid + 2),
            scratch_shapes=[wide],
            compiler_params=grant(16),
        )(*inputs, *last)
        last = (spectrum,)
        received = []
        for k, message in enumerate(messages, 1):
            received.append(cross(message, k))
        solved.append((spectrum, a, b, received))

    terms, last = [], ()
    for u, (spectrum, a, b, received) in enumerate(solved):
        inputs = [*base_own, *base_other, *received, yt_hi, yt_lo, zt_hi, zt_lo, inverse, basis, powers, steady,
                  spectrum, a, b]
        terms.append(pl.pallas_call(
            functools.partial(backward_kernel, u, (CHUNKS, CHUNKS, len(received))),
            out_shape=jax.ShapeDtypeStruct((planes, width), f32),
            in_specs=[SM] + [VM] * len(inputs) + [ANY] * len(last),
            out_specs=VM,
            scratch_shapes=[pltpu.VMEM(cube, f32), wide],
            compiler_params=grant(16),
        )(flags, *inputs, *last))
        last = (terms[-1],)

    near_1 = [swap(term, 2, 4) for term in terms]
    near_2 = [swap(term, 4, 2) for term in terms]
    own_parts = [[term, x, y] for term, x, y in zip(terms, near_1, near_2)]
    sib_parts = []
    for term, x, y in own_parts:
        joined = pl.pallas_call(
            join_kernel, out_shape=jax.ShapeDtypeStruct((2,) + term.shape, f32), in_specs=[VM] * 2, out_specs=VM,
            compiler_params=grant(4),
        )(x, y)
        given = swap(term, 1, 1)
        sib_parts.append([given, swap(joined, 1, 1)])

    def place(target, groups):
        parts = [part for group in groups for part in group]
        return pl.pallas_call(
            functools.partial(place_kernel, 8),
            out_shape=pltpu.HBM(shape, f32),
            in_specs=[SM] + [VM] * len(parts) + [HBM],
            out_specs=HBM,
            input_output_aliases={len(parts) + 1: 0},
            scratch_shapes=[pltpu.VMEM((blocks, 2, pair, planes, width), f32), DMA((blocks, 2))],
            name="place",
            compiler_params=grant(8),
        )(match, *parts, target)

    def place_near(target, mine, sibs):
        return place(target, [a + b for a, b in zip(mine, sibs)])

    def place_far(target, mine, sibs):
        far = [swap(group[1], 4, 2) for group in mine]
        return place(target, [a + [x] + b + [swap(x, 1, 1)] for a, b, x in zip(mine, sibs, far)])

    return lax.cond(alone[0] != 0, place_far, place_near, empty, own_parts, sib_parts)


def sine_table(length):
    wave_index = jnp.arange(length, dtype=f32) + 1.0
    return jnp.sqrt(2.0 / (length + 1.0)) * jnp.sin(
        jnp.pi * wave_index[:, None] * wave_index[None, :] / (length + 1.0)
    )


def eigen_values(length):
    wave_index = jnp.arange(length, dtype=f32) + 1.0
    return 2.0 - 2.0 * jnp.cos(jnp.pi * wave_index / (length + 1.0))


def green_kernel(size_x, size_y, size_z):
    summed = (
        eigen_values(size_x)[:, None, None]
        + eigen_values(size_y)[None, :, None]
        + eigen_values(size_z)[None, None, :]
    )
    return COUPLING / (summed + SCREENING)


def pair_lists(tile_list, pair_mask):
    within = jnp.arange(BLK * BLK, dtype=jnp.int32)
    targets = (BLK * tile_list[:, 0:1] + within[None, :] // BLK).reshape(-1)
    sources = (BLK * tile_list[:, 1:2] + within[None, :] % BLK).reshape(-1)
    return (targets, sources, pair_mask[targets, sources])


def compact(targets, sources, live_flags, number):
    ranking = jnp.cumsum(live_flags) - 1
    places = jnp.where(live_flags == 1, ranking, number)
    picked = (
        jnp.zeros((number,), jnp.int32)
        .at[places]
        .set(jnp.arange(live_flags.shape[0], dtype=jnp.int32), mode="drop")
    )
    return (targets[picked], sources[picked])


def along_z(values, matrix):
    number, planes, width_yz = values.shape
    size_z = matrix.shape[0]
    shaped = values.reshape(number, planes, width_yz // size_z, size_z)
    return jnp.einsum("pxrz,zk->pxrk", shaped, matrix, precision=precise).reshape(number, planes, width_yz)


def along_y(values, matrix):
    number, planes, width_yz = values.shape
    size_y = matrix.shape[0]
    shaped = values.reshape(number, planes, size_y, width_yz // size_y)
    return jnp.einsum("pxyz,yk->pxkz", shaped, matrix, precision=precise).reshape(number, planes, width_yz)


def along_x(values, matrix):
    return jnp.einsum("pxc,xk->pkc", values, matrix, precision=precise)


def any_device(orbitals, rotation, tile_list, pair_mask):
    n_grid = lax.axis_size("grid")
    number_orbitals, size_x = rotation.shape[0], orbitals.shape[1] * n_grid
    rotated = jnp.einsum(
        "ij,ixc->jxc",
        rotation,
        lax.all_to_all(orbitals, "orb", split_axis=2, concat_axis=0, tiled=True),
        precision=precise,
    )
    planes, width_yz = rotated.shape[1:]
    targets, sources, live_flags = pair_lists(tile_list, pair_mask)
    matrix_x, matrix_y, matrix_z = sine_table(size_x), sine_table(NY), sine_table(NZ)
    kernel = green_kernel(size_x, NY, NZ).reshape(size_x, NY * NZ)
    orbital_ids = jnp.arange(number_orbitals, dtype=jnp.int32)
    targets, sources = compact(targets, sources, live_flags, targets.shape[0] // 2)
    density = rotated[targets] * rotated[sources]
    number = density.shape[0]
    spectrum = along_z(density, matrix_z)
    spectrum = lax.all_to_all(spectrum, "orb", split_axis=0, concat_axis=2, tiled=True)
    spectrum = along_y(spectrum, matrix_y)
    spectrum = lax.all_to_all(spectrum, "grid", split_axis=0, concat_axis=1, tiled=True)
    spectrum = along_x(along_x(spectrum, matrix_x) * kernel, matrix_x)
    spectrum = lax.all_to_all(spectrum, "grid", split_axis=1, concat_axis=0, tiled=True)
    spectrum = along_y(spectrum, matrix_y)
    spectrum = lax.all_to_all(spectrum, "orb", split_axis=2, concat_axis=0, tiled=True)
    potential = along_z(spectrum, matrix_z)
    products = potential * rotated[sources]
    selector = (targets[None, :] == orbital_ids[:, None]).astype(f32)
    partial_value = -jnp.dot(selector, products.reshape(number, planes * width_yz), precision=precise)
    partial_value = partial_value.reshape(number_orbitals, planes, width_yz)
    return lax.all_to_all(partial_value, "orb", split_axis=0, concat_axis=2, tiled=True)


def solution(mesh):
    n_orb, n_grid = mesh.shape["orb"], mesh.shape["grid"]

    def on_device(orbitals, rotation, tile_list, pair_mask):
        per_device, planes, width = orbitals.shape
        fits = n_orb == 8 and 2 * tile_list.shape[0] == n_orb and planes == SUB and per_device % BLK == 0
        fits = fits and width == NY * NZ and 2 * NZ == LANES and n_grid in (2, 4, 8)
        fits = fits and per_device * SUB == LANES and rotation.shape == (LANES, LANES)
        if not fits:
            return any_device(orbitals, rotation, tile_list, pair_mask)
        return tile_device(orbitals, rotation, tile_list, pair_mask)

    in_specs = (P("orb", "grid", None), P(), P(), P())
    out_specs = P("orb", "grid", None)
    return jax.shard_map(on_device, mesh=mesh, in_specs=in_specs, out_specs=out_specs, check_vma=False)
```

profile of v0, /device:TPU:0, one launch (start us, length us, event | category | flops | bytes accessed | tf_op | source)
XLA Modules:
  0.0 61.3 jit_solution(6417162946312580094)
XLA Ops:
  0.0 1.2 %take.1.after = f32[16,8,1024]{2,1,0:T(8,128)S(1)} custom-call(f32[16,8,4096]{2,1,0:T(8,128)} %source.3), custom_call_target="tpu_custom_call" | custom-call | tf_op jit(solution)/shard_map/take/pallas_call | solution.py:493
  1.2 0.6 collective-permute-start.4
  1.8 0.1 copy.24.tiles
  1.9 2.3 %setup.1 = (f32[16,8,1024]{2,1,0:T(8,128)S(1)}, f32[16,8,1024]{2,1,0:T(8,128)S(1)}, f32[16,8,1024]{2,1,0:T(8,128)S(1)}, bf16[256,256]{1,0:T(8,128)(2,1)S(1)}, bf16[256,256]{1,0:T(8,128)(2,1)S(1)}) custom-call(s32[4,2]{1,0:T(4,128)S(1)} %copy.24.tiles, s32[1024]{0:T(1024)S(1)} %copy-done.15, f32[128,128]{1,0:T(8,128)S(1)} %copy-done.11, ...), custom_call_target="tpu_custom_call" | custom-call | tf_op jit(solution)/shard_map/setup/pallas_call | solution.py:507
  4.2 0.1 collective-permute-start.5
  4.2 0.5 shard_map.174
  4.7 3.0 %collective-permute-start.6 = (f32[12,8,1024]{2,1,0:T(8,128)S(1)}, f32[12,8,1024]{2,1,0:T(8,128)S(1)}, u32[]{:S(2)}, u32[]{:S(2)}) collective-permute-start(f32[12,8,1024]{2,1,0:T(8,128)S(1)} %get-tuple-element.113.rest_2_), channel_id=1, source_target_pairs={{0,8},{1,9},{2,10},{3,11},{4,20},{5,21},{6,22},{7,23},{8,0},{9,1},... | collective-permute-start | bytes 1179656 | tf_op jit(solution)/shard_map/ppermute | solution.py:482
  7.8 0.5 shard_map.175
  8.3 1.0 %collective-permute-start.8 = (f32[12,8,1024]{2,1,0:T(8,128)S(1)}, f32[12,8,1024]{2,1,0:T(8,128)S(1)}, u32[]{:S(2)}, u32[]{:S(2)}) collective-permute-start(f32[12,8,1024]{2,1,0:T(8,128)S(1)} %get-tuple-element.114.rest_4_), channel_id=1, source_target_pairs={{0,8},{1,9},{2,10},{3,11},{4,20},{5,21},{6,22},{7,23},{8,0},{9,1},... | collective-permute-start | bytes 1179656 | tf_op jit(solution)/shard_map/ppermute | solution.py:482
  9.3 0.7 %shard_map.176 = (f32[4,8,2048]{2,1,0:T(8,128)S(1)}, f32[4,8,2048]{2,1,0:T(8,128)S(1)}) custom-call(bf16[256,256]{1,0:T(8,128)(2,1)S(1)} %get-tuple-element.108.high, bf16[256,256]{1,0:T(8,128)(2,1)S(1)} %get-tuple-element.109.low, f32[16,8,1024]{2,1,0:T(8,128)S(1)} %get-tuple-element.110.rest_0_, f32[16,8,1024]{2,1,0:T(8,128)S(1)} %collective-permute-done.4.rest_1_, ...), custom_call_target="tpu_custom_call" | custom-call | tf_op jit(solution)/shard_map/pallas_call | solution.py:519
  10.0 2.7 %ready.1 = (f32[16,8,4096]{2,1,0:T(8,128)}, f32[6,64,128]{2,1,0:T(8,128)S(1)}, f32[8]{0:T(128)S(1)}, s32[32]{0:T(128)S(1)}, s32[1]{0:T(128)}) custom-call(s32[4,2]{1,0:T(4,128)S(1)} %copy.24.tiles, s32[1024]{0:T(1024)S(1)} %copy-done.15, s32[128,128]{1,0:T(8,128)S(1)} %copy-done.12, f32[64,128]{1,0:T(8,128)S(1)} %copy-done.13, ...), custom_call_target="tpu_custom_call" | custom-call | tf_op jit(solution)/shard_map/ready/pallas_call | solution.py:532
  12.7 0.8 %collective-permute-done.6.got = f32[12,8,1024]{2,1,0:T(8,128)S(1)} collective-permute-done((f32[12,8,1024]{2,1,0:T(8,128)S(1)}, f32[12,8,1024]{2,1,0:T(8,128)S(1)}, u32[]{:S(2)}, u32[]{:S(2)}) %collective-permute-start.6) | collective-permute-done | bytes 393248 | tf_op jit(solution)/shard_map/ppermute | solution.py:482
  13.6 2.1 %collective-permute-start.7 = (f32[6,8,1024]{2,1,0:T(8,128)S(1)}, f32[6,8,1024]{2,1,0:T(8,128)S(1)}, u32[]{:S(2)}, u32[]{:S(2)}) collective-permute-start(f32[6,8,1024]{2,1,0:T(8,128)S(1)} %shard_map.177.rest_0_), channel_id=1, source_target_pairs={{0,16},{1,17},{2,18},{3,19},{4,12},{5,13},{6,14},{7,15},{8,24},{9,... | collective-permute-start | bytes 589832 | tf_op jit(solution)/shard_map/ppermute | solution.py:482
  15.7 4.0 %collective-permute-done.8.got = f32[12,8,1024]{2,1,0:T(8,128)S(1)} collective-permute-done((f32[12,8,1024]{2,1,0:T(8,128)S(1)}, f32[12,8,1024]{2,1,0:T(8,128)S(1)}, u32[]{:S(2)}, u32[]{:S(2)}) %collective-permute-start.8) | collective-permute-done | bytes 393248 | tf_op jit(solution)/shard_map/ppermute | solution.py:482
  19.8 2.4 %collective-permute-start.9 = (f32[6,8,1024]{2,1,0:T(8,128)S(1)}, f32[6,8,1024]{2,1,0:T(8,128)S(1)}, u32[]{:S(2)}, u32[]{:S(2)}) collective-permute-start(f32[6,8,1024]{2,1,0:T(8,128)S(1)} %shard_map.178.rest_0_), channel_id=1, source_target_pairs={{0,16},{1,17},{2,18},{3,19},{4,12},{5,13},{6,14},{7,15},{8,24},{9,... | collective-permute-start | bytes 589832 | tf_op jit(solution)/shard_map/ppermute | solution.py:482
  22.2 1.5 %collective-permute-start.19 = (f32[4,8,2048]{2,1,0:T(8,128)S(1)}, f32[4,8,2048]{2,1,0:T(8,128)S(1)}, u32[]{:S(2)}, u32[]{:S(2)}) collective-permute-start(f32[4,8,2048]{2,1,0:T(8,128)S(1)} %get-tuple-element.115.rest_0_), channel_id=1, source_target_pairs={{0,8},{1,9},{2,10},{3,11},{4,20},{5,21},{6,22},{7,23},{8,0},{9,1},... | collective-permute-start | bytes 786440 | tf_op jit(solution)/shard_map/ppermute | solution.py:482
  23.7 2.5 %collective-permute-done.9.passed = f32[6,8,1024]{2,1,0:T(8,128)S(1)} collective-permute-done((f32[6,8,1024]{2,1,0:T(8,128)S(1)}, f32[6,8,1024]{2,1,0:T(8,128)S(1)}, u32[]{:S(2)}, u32[]{:S(2)}) %collective-permute-start.9) | collective-permute-done | bytes 196640 | tf_op jit(solution)/shard_map/ppermute | solution.py:482
  26.3 0.1 collective-permute-start.11
  26.4 0.5 collective-permute-start.10
  26.9 0.9 %collective-permute-done.11.refs_3_ = f32[6,8,1024]{2,1,0:T(8,128)S(1)} collective-permute-done((f32[6,8,1024]{2,1,0:T(8,128)S(1)}, f32[6,8,1024]{2,1,0:T(8,128)S(1)}, u32[]{:S(2)}, u32[]{:S(2)}) %collective-permute-start.11) | collective-permute-done | bytes 196640 | tf_op jit(solution)/shard_map/ppermute | solution.py:482
  27.8 0.3 collective-permute-done.10.refs_2_
  28.1 1.0 %shard_map.181 = (f32[64,256]{1,0:T(8,128)S(1)}, f32[64,256]{1,0:T(8,128)S(1)}, f32[64,256]{1,0:T(8,128)S(1)}, f32[512,256]{1,0:T(8,128)S(1)}, f32[64,256]{1,0:T(8,128)S(1)}, /*index=5*/f32[64,256]{1,0:T(8,128)S(1)}) custom-call(f32[6,8,1024]{2,1,0:T(8,128)S(1)} %shard_map.179.rest_0_.refs_0_, f32[6,8,1024]{2,1,0:T(8,128)S(1)} %shard_map.180.refs_1_.refs_10_, ...), custom_call_target="tpu_custom_call" | custom-call | tf_op jit(solution)/shard_map/pallas_call | solution.py:593
  29.2 1.7 %collective-permute-start.20 = (f32[2,8,2048]{2,1,0:T(8,128)S(1)}, f32[2,8,2048]{2,1,0:T(8,128)S(1)}, u32[]{:S(2)}, u32[]{:S(2)}) collective-permute-start(f32[2,8,2048]{2,1,0:T(8,128)S(1)} %shard_map.184), channel_id=1, source_target_pairs={{0,16},{1,17},{2,18},{3,19},{4,12},{5,13},{6,14},{7,15},{8,24},{9,... | collective-permute-start | bytes 393224 | tf_op jit(solution)/shard_map/ppermute | solution.py:482
  30.9 3.4 %collective-permute-done.20.passed = f32[2,8,2048]{2,1,0:T(8,128)S(1)} collective-permute-done((f32[2,8,2048]{2,1,0:T(8,128)S(1)}, f32[2,8,2048]{2,1,0:T(8,128)S(1)}, u32[]{:S(2)}, u32[]{:S(2)}) %collective-permute-start.20) | collective-permute-done | bytes 131104 | tf_op jit(solution)/shard_map/ppermute | solution.py:482
  34.3 0.1 collective-permute-start.21
  34.4 1.7 %collective-permute-start.12 = (f32[64,256]{1,0:T(8,128)S(1)}, f32[64,256]{1,0:T(8,128)S(1)}, u32[]{:S(2)}, u32[]{:S(2)}) collective-permute-start(f32[64,256]{1,0:T(8,128)S(1)} %get-tuple-element.123), channel_id=1, source_target_pairs={{0,1},{1,0},{2,3},{3,2},{4,5},{5,4},{6,7},{7,6},{8,9},{9,8},{10,11... | collective-permute-start | bytes 196616 | tf_op jit(solution)/shard_map/ppermute | solution.py:486
  36.1 2.6 %collective-permute-start.13 = (f32[64,256]{1,0:T(8,128)S(1)}, f32[64,256]{1,0:T(8,128)S(1)}, u32[]{:S(2)}, u32[]{:S(2)}) collective-permute-start(f32[64,256]{1,0:T(8,128)S(1)} %get-tuple-element.124), channel_id=1, source_target_pairs={{0,2},{1,3},{2,0},{3,1},{4,6},{5,7},{6,4},{7,5},{8,10},{9,11},{10,... | collective-permute-start | bytes 196616 | tf_op jit(solution)/shard_map/ppermute | solution.py:486
  38.7 0.1 collective-permute-start.14
  38.8 1.0 %shard_map.186 = (f32[64,256]{1,0:T(8,128)S(1)}, f32[64,256]{1,0:T(8,128)S(1)}, f32[64,256]{1,0:T(8,128)S(1)}, f32[512,256]{1,0:T(8,128)S(1)}, f32[64,256]{1,0:T(8,128)S(1)}, /*index=5*/f32[64,256]{1,0:T(8,128)S(1)}) custom-call(f32[6,8,1024]{2,1,0:T(8,128)S(1)} %shard_map.179.rest_0_.refs_0_, f32[6,8,1024]{2,1,0:T(8,128)S(1)} %shard_map.180.refs_1_.refs_10_, ...), custom_call_target="tpu_custom_call" | custom-call | tf_op jit(solution)/shard_map/pallas_call | solution.py:593
  39.8 0.8 %collective-permute-start.22 = (f32[64,256]{1,0:T(8,128)S(1)}, f32[64,256]{1,0:T(8,128)S(1)}, u32[]{:S(2)}, u32[]{:S(2)}) collective-permute-start(f32[64,256]{1,0:T(8,128)S(1)} %get-tuple-element.130), channel_id=1, source_target_pairs={{0,1},{1,0},{2,3},{3,2},{4,5},{5,4},{6,7},{7,6},{8,9},{9,8},{10,11... | collective-permute-start | bytes 196616 | tf_op jit(solution)/shard_map/ppermute | solution.py:486
  40.7 3.5 %collective-permute-start.23 = (f32[64,256]{1,0:T(8,128)S(1)}, f32[64,256]{1,0:T(8,128)S(1)}, u32[]{:S(2)}, u32[]{:S(2)}) collective-permute-start(f32[64,256]{1,0:T(8,128)S(1)} %get-tuple-element.131), channel_id=1, source_target_pairs={{0,2},{1,3},{2,0},{3,1},{4,6},{5,7},{6,4},{7,5},{8,10},{9,11},{10,... | collective-permute-start | bytes 196616 | tf_op jit(solution)/shard_map/ppermute | solution.py:486
  44.1 0.1 collective-permute-start.24
  44.3 1.2 %collective-permute-done.14.refs_6_ = f32[64,256]{1,0:T(8,128)S(1)} collective-permute-done((f32[64,256]{1,0:T(8,128)S(1)}, f32[64,256]{1,0:T(8,128)S(1)}, u32[]{:S(2)}, u32[]{:S(2)}) %collective-permute-start.14) | collective-permute-done | bytes 65568 | tf_op jit(solution)/shard_map/ppermute | solution.py:486
  45.5 1.8 %shard_map.182.refs_18_ = f32[8,4096]{1,0:T(8,128)S(1)} custom-call(f32[8]{0:T(128)S(1)} %get-tuple-element.118.flags, f32[6,8,1024]{2,1,0:T(8,128)S(1)} %shard_map.179.rest_0_.refs_0_, f32[6,8,1024]{2,1,0:T(8,128)S(1)} %shard_map.180.refs_1_.refs_10_, f32[6,8,1024]{2,1,0:T(8,128)S(1)} %collective-permute-done.10.refs_2_, ...), custom_call_target="tpu_custom_call" | custom-call | tf_op jit(solution)/shard_map/pallas_call | solution.py:611
  47.3 1.6 %collective-permute-start.16 = (f32[8,4096]{1,0:T(8,128)S(1)}, f32[8,4096]{1,0:T(8,128)S(1)}, u32[]{:S(2)}, u32[]{:S(2)}) collective-permute-start(f32[8,4096]{1,0:T(8,128)S(1)} %shard_map.182.refs_18_), channel_id=1, source_target_pairs={{0,16},{1,17},{2,18},{3,19},{4,12},{5,13},{6,14},{7,15},{8,24},{9,... | collective-permute-start | bytes 393224 | tf_op jit(solution)/shard_map/ppermute | solution.py:482
  48.8 1.5 %collective-permute-start.15 = (f32[8,4096]{1,0:T(8,128)S(1)}, f32[8,4096]{1,0:T(8,128)S(1)}, u32[]{:S(2)}, u32[]{:S(2)}) collective-permute-start(f32[8,4096]{1,0:T(8,128)S(1)} %shard_map.182.refs_18_), channel_id=1, source_target_pairs={{0,8},{1,9},{2,10},{3,11},{4,20},{5,21},{6,22},{7,23},{8,0},{9,1},... | collective-permute-start | bytes 393224 | tf_op jit(solution)/shard_map/ppermute | solution.py:482
  50.3 1.8 %shard_map.187 = f32[8,4096]{1,0:T(8,128)S(1)} custom-call(f32[8]{0:T(128)S(1)} %get-tuple-element.118.flags, f32[6,8,1024]{2,1,0:T(8,128)S(1)} %shard_map.179.rest_0_.refs_0_, f32[6,8,1024]{2,1,0:T(8,128)S(1)} %shard_map.180.refs_1_.refs_10_, f32[6,8,1024]{2,1,0:T(8,128)S(1)} %collective-permute-done.10.refs_2_, ...), custom_call_target="tpu_custom_call" | custom-call | tf_op jit(solution)/shard_map/pallas_call | solution.py:611
  52.1 1.5 %collective-permute-start.26 = (f32[8,4096]{1,0:T(8,128)S(1)}, f32[8,4096]{1,0:T(8,128)S(1)}, u32[]{:S(2)}, u32[]{:S(2)}) collective-permute-start(f32[8,4096]{1,0:T(8,128)S(1)} %shard_map.187), channel_id=1, source_target_pairs={{0,16},{1,17},{2,18},{3,19},{4,12},{5,13},{6,14},{7,15},{8,24},{9,... | collective-permute-start | bytes 393224 | tf_op jit(solution)/shard_map/ppermute | solution.py:482
  53.6 1.5 %collective-permute-start.25 = (f32[8,4096]{1,0:T(8,128)S(1)}, f32[8,4096]{1,0:T(8,128)S(1)}, u32[]{:S(2)}, u32[]{:S(2)}) collective-permute-start(f32[8,4096]{1,0:T(8,128)S(1)} %shard_map.187), channel_id=1, source_target_pairs={{0,8},{1,9},{2,10},{3,11},{4,20},{5,21},{6,22},{7,23},{8,0},{9,1},... | collective-permute-start | bytes 393224 | tf_op jit(solution)/shard_map/ppermute | solution.py:482
  55.2 0.1 collective-permute-start.18
  55.2 1.9 %collective-permute-done.26.y = f32[8,4096]{1,0:T(8,128)S(1)} collective-permute-done((f32[8,4096]{1,0:T(8,128)S(1)}, f32[8,4096]{1,0:T(8,128)S(1)}, u32[]{:S(2)}, u32[]{:S(2)}) %collective-permute-start.26) | collective-permute-done | bytes 131104 | tf_op jit(solution)/shard_map/ppermute | solution.py:482
  57.1 1.5 %collective-permute-done.25.x = f32[8,4096]{1,0:T(8,128)S(1)} collective-permute-done((f32[8,4096]{1,0:T(8,128)S(1)}, f32[8,4096]{1,0:T(8,128)S(1)}, u32[]{:S(2)}, u32[]{:S(2)}) %collective-permute-start.25) | collective-permute-done | bytes 131104 | tf_op jit(solution)/shard_map/ppermute | solution.py:482
  58.7 0.5 collective-permute-start.17
  59.2 0.1 collective-permute-start.27
  59.9 0.5 collective-permute-done.17
  60.4 0.2 collective-permute-done.27
  60.6 0.7 %conditional.1 = (f32[16,8,4096]{2,1,0:T(8,128)}) conditional(s32[]{:T(128)} %bitcast, (s32[32]{0:T(128)S(1)}, f32[8,4096]{1,0:T(8,128)S(1)}, f32[8,4096]{1,0:T(8,128)S(1)}, f32[8,4096]{1,0:T(8,128)S(1)}, f32[8,4096]{1,0:T(8,128)S(1)}, /*index=5*/f32[2,8,4096]{2,1,0:T(8,128)S(1)}, f32[8,4096]{1,0:T(8,128)S(1)}, f32[8,4096]{1,0:T(8,128)S(1)}, ...), branch_computations={%region_0.0_spmd, %region_1.0_spmd} | conditional | bytes 2097320 | solution.py:653
  60.6 0.7 %place.2 = f32[16,8,4096]{2,1,0:T(8,128)} custom-call(s32[32]{0:T(128)S(1)} %get-tuple-element.56.match, f32[8,4096]{1,0:T(8,128)S(1)} %get-tuple-element.57.refs_0_, f32[8,4096]{1,0:T(8,128)S(1)} %get-tuple-element.58.refs_1_, f32[8,4096]{1,0:T(8,128)S(1)} %get-tuple-element.59.refs_2_, ...), custom_call_target="tpu_custom_call", output_to_operand_aliasing={{}: (11, {})} | custom-call | tf_op jit(solution)/shard_map/cond/branch_0_fun/place/pallas_call | solution.py:635
  (57 shorter events, 0.4 us)
Async XLA Ops:
  0.0 1.9 %copy-start.15 = (s32[1024]{0:T(1024)S(1)}, s32[1024]{0:T(1024)}, u32[]{:S(2)}) copy-start(s32[1024]{0:T(1024)} %constant.31.clone.host) | copy-start | bytes 12292
  0.0 1.8 %copy-start.16 = (s32[4,2]{0,1:T(2,128)S(1)}, s32[4,2]{0,1:T(2,128)}, u32[]{:S(2)}) copy-start(s32[4,2]{0,1:T(2,128)} %param.22) | copy-start | bytes 100
  0.0 1.8 %copy-start.11 = (f32[128,128]{1,0:T(8,128)S(1)}, f32[128,128]{1,0:T(8,128)}, u32[]{:S(2)}) copy-start(f32[128,128]{1,0:T(8,128)} %rotation.1) | copy-start | bytes 196612
  1.2 3.1 %collective-permute-start.4 = (f32[16,8,1024]{2,1,0:T(8,128)S(1)}, f32[16,8,1024]{2,1,0:T(8,128)S(1)}, u32[]{:S(2)}, u32[]{:S(2)}) collective-permute-start(f32[16,8,1024]{2,1,0:T(8,128)S(1)} %take.1.after), channel_id=1, source_target_pairs={{0,4},{1,5},{2,6},{3,7},{4,0},{5,1},{6,2},{7,3},{8,12},{9,13},{10,... | collective-permute-start | bytes 1572872 | tf_op jit(solution)/shard_map/ppermute | solution.py:482
  4.2 3.6 %collective-permute-start.5 = (f32[16,8,1024]{2,1,0:T(8,128)S(1)}, f32[16,8,1024]{2,1,0:T(8,128)S(1)}, u32[]{:S(2)}, u32[]{:S(2)}) collective-permute-start(f32[16,8,1024]{2,1,0:T(8,128)S(1)} %get-tuple-element.112), channel_id=1, source_target_pairs={{0,4},{1,5},{2,6},{3,7},{4,0},{5,1},{6,2},{7,3},{8,12},{9,13},{10,... | collective-permute-start | bytes 1572872 | tf_op jit(solution)/shard_map/ppermute | solution.py:482
  4.7 8.8 %collective-permute-start.6 = (f32[12,8,1024]{2,1,0:T(8,128)S(1)}, f32[12,8,1024]{2,1,0:T(8,128)S(1)}, u32[]{:S(2)}, u32[]{:S(2)}) collective-permute-start(f32[12,8,1024]{2,1,0:T(8,128)S(1)} %get-tuple-element.113.rest_2_), channel_id=1, source_target_pairs={{0,8},{1,9},{2,10},{3,11},{4,20},{5,21},{6,22},{7,23},{8,0},{9,1},... | collective-permute-start | bytes 1179656 | tf_op jit(solution)/shard_map/ppermute | solution.py:482
  7.8 2.2 %copy-start.12 = (s32[128,128]{1,0:T(8,128)S(1)}, s32[128,128]{1,0:T(8,128)}, u32[]{:S(2)}) copy-start(s32[128,128]{1,0:T(8,128)} %mask.1) | copy-start | bytes 196612
  7.8 2.2 %copy-start.13 = (f32[64,128]{1,0:T(8,128)S(1)}, f32[64,128]{1,0:T(8,128)}, u32[]{:S(2)}) copy-start(f32[64,128]{1,0:T(8,128)} %constant.32.clone.log_r) | copy-start | bytes 98308
  8.3 11.4 %collective-permute-start.8 = (f32[12,8,1024]{2,1,0:T(8,128)S(1)}, f32[12,8,1024]{2,1,0:T(8,128)S(1)}, u32[]{:S(2)}, u32[]{:S(2)}) collective-permute-start(f32[12,8,1024]{2,1,0:T(8,128)S(1)} %get-tuple-element.114.rest_4_), channel_id=1, source_target_pairs={{0,8},{1,9},{2,10},{3,11},{4,20},{5,21},{6,22},{7,23},{8,0},{9,1},... | collective-permute-start | bytes 1179656 | tf_op jit(solution)/shard_map/ppermute | solution.py:482
  13.6 14.5 %copy-start = (bf16[2,256,256]{2,1,0:T(8,128)(2,1)S(1)}, bf16[2,256,256]{2,1,0:T(8,128)(2,1)}, u32[]{:S(2)}) copy-start(bf16[2,256,256]{2,1,0:T(8,128)(2,1)} %constant.38.clone.refs_5_.refs_7_) | copy-start | bytes 786436
  13.6 14.5 %copy-start.1 = (bf16[2,256,256]{2,1,0:T(8,128)(2,1)S(1)}, bf16[2,256,256]{2,1,0:T(8,128)(2,1)}, u32[]{:S(2)}) copy-start(bf16[2,256,256]{2,1,0:T(8,128)(2,1)} %constant.37.clone.refs_4_.refs_6_) | copy-start | bytes 786436
  13.6 14.5 %copy-start.2 = (f32[512,128]{1,0:T(8,128)S(1)}, f32[512,128]{1,0:T(8,128)}, u32[]{:S(2)}) copy-start(f32[512,128]{1,0:T(8,128)} %constant.33.clone.refs_8_.refs_10_) | copy-start | bytes 786436
  13.6 14.5 %copy-start.6 = (bf16[256,256]{1,0:T(8,128)(2,1)S(1)}, bf16[256,256]{1,0:T(8,128)(2,1)}, u32[]{:S(2)}) copy-start(bf16[256,256]{1,0:T(8,128)(2,1)} %constant.42.clone.refs_7_.refs_9_) | copy-start | bytes 393220
  13.6 14.5 %copy-start.7 = (bf16[256,256]{1,0:T(8,128)(2,1)S(1)}, bf16[256,256]{1,0:T(8,128)(2,1)}, u32[]{:S(2)}) copy-start(bf16[256,256]{1,0:T(8,128)(2,1)} %constant.41.clone.refs_6_.refs_8_) | copy-start | bytes 393220
  13.6 10.1 %collective-permute-start.7 = (f32[6,8,1024]{2,1,0:T(8,128)S(1)}, f32[6,8,1024]{2,1,0:T(8,128)S(1)}, u32[]{:S(2)}, u32[]{:S(2)}) collective-permute-start(f32[6,8,1024]{2,1,0:T(8,128)S(1)} %shard_map.177.rest_0_), channel_id=1, source_target_pairs={{0,16},{1,17},{2,18},{3,19},{4,12},{5,13},{6,14},{7,15},{8,24},{9,... | collective-permute-start | bytes 589832 | tf_op jit(solution)/shard_map/ppermute | solution.py:482
  19.8 6.5 %collective-permute-start.9 = (f32[6,8,1024]{2,1,0:T(8,128)S(1)}, f32[6,8,1024]{2,1,0:T(8,128)S(1)}, u32[]{:S(2)}, u32[]{:S(2)}) collective-permute-start(f32[6,8,1024]{2,1,0:T(8,128)S(1)} %shard_map.178.rest_0_), channel_id=1, source_target_pairs={{0,16},{1,17},{2,18},{3,19},{4,12},{5,13},{6,14},{7,15},{8,24},{9,... | collective-permute-start | bytes 589832 | tf_op jit(solution)/shard_map/ppermute | solution.py:482
  22.2 6.9 %collective-permute-start.19 = (f32[4,8,2048]{2,1,0:T(8,128)S(1)}, f32[4,8,2048]{2,1,0:T(8,128)S(1)}, u32[]{:S(2)}, u32[]{:S(2)}) collective-permute-start(f32[4,8,2048]{2,1,0:T(8,128)S(1)} %get-tuple-element.115.rest_0_), channel_id=1, source_target_pairs={{0,8},{1,9},{2,10},{3,11},{4,20},{5,21},{6,22},{7,23},{8,0},{9,1},... | collective-permute-start | bytes 786440 | tf_op jit(solution)/shard_map/ppermute | solution.py:482
  26.3 1.5 %collective-permute-start.11 = (f32[6,8,1024]{2,1,0:T(8,128)S(1)}, f32[6,8,1024]{2,1,0:T(8,128)S(1)}, u32[]{:S(2)}, u32[]{:S(2)}) collective-permute-start(f32[6,8,1024]{2,1,0:T(8,128)S(1)} %shard_map.180.refs_1_.refs_10_), channel_id=1, source_target_pairs={{0,4},{1,5},{2,6},{3,7},{4,0},{5,1},{6,2},{7,3},{8,12},{9,13},{10,... | collective-permute-start | bytes 589832 | tf_op jit(solution)/shard_map/ppermute | solution.py:482
  26.4 1.7 %collective-permute-start.10 = (f32[6,8,1024]{2,1,0:T(8,128)S(1)}, f32[6,8,1024]{2,1,0:T(8,128)S(1)}, u32[]{:S(2)}, u32[]{:S(2)}) collective-permute-start(f32[6,8,1024]{2,1,0:T(8,128)S(1)} %shard_map.179.rest_0_.refs_0_), channel_id=1, source_target_pairs={{0,4},{1,5},{2,6},{3,7},{4,0},{5,1},{6,2},{7,3},{8,12},{9,13},{10,... | collective-permute-start | bytes 589832 | tf_op jit(solution)/shard_map/ppermute | solution.py:482
  29.1 16.3 %copy-start.3 = (bf16[2,256,256]{2,1,0:T(8,128)(2,1)S(1)}, bf16[2,256,256]{2,1,0:T(8,128)(2,1)}, u32[]{:S(2)}) copy-start(bf16[2,256,256]{2,1,0:T(8,128)(2,1)} %constant.40.clone.refs_8_) | copy-start | bytes 786436
  29.2 16.3 %copy-start.4 = (bf16[2,256,256]{2,1,0:T(8,128)(2,1)S(1)}, bf16[2,256,256]{2,1,0:T(8,128)(2,1)}, u32[]{:S(2)}) copy-start(bf16[2,256,256]{2,1,0:T(8,128)(2,1)} %constant.39.clone.refs_7_) | copy-start | bytes 786436
  29.2 16.3 %copy-start.5 = (f32[512,128]{1,0:T(8,128)S(1)}, f32[512,128]{1,0:T(8,128)}, u32[]{:S(2)}) copy-start(f32[512,128]{1,0:T(8,128)} %constant.34.clone.refs_11_) | copy-start | bytes 786436
  29.2 16.3 %copy-start.8 = (bf16[256,256]{1,0:T(8,128)(2,1)S(1)}, bf16[256,256]{1,0:T(8,128)(2,1)}, u32[]{:S(2)}) copy-start(bf16[256,256]{1,0:T(8,128)(2,1)} %constant.44.clone.refs_10_) | copy-start | bytes 393220
  29.2 16.3 %copy-start.9 = (bf16[256,256]{1,0:T(8,128)(2,1)S(1)}, bf16[256,256]{1,0:T(8,128)(2,1)}, u32[]{:S(2)}) copy-start(bf16[256,256]{1,0:T(8,128)(2,1)} %constant.43.clone.refs_9_) | copy-start | bytes 393220
  29.2 16.3 %copy-start.10 = (f32[3,64,128]{2,1,0:T(8,128)S(1)}, f32[3,64,128]{2,1,0:T(8,128)}, u32[]{:S(2)}) copy-start(f32[3,64,128]{2,1,0:T(8,128)} %constant.36.clone.refs_14_) | copy-start | bytes 294916
  29.2 16.3 %copy-start.14 = (f32[2,8,128]{2,1,0:T(8,128)S(1)}, f32[2,8,128]{2,1,0:T(8,128)}, u32[]{:S(2)}) copy-start(f32[2,8,128]{2,1,0:T(8,128)} %constant.35.clone.refs_12_) | copy-start | bytes 24580
  29.2 5.0 %collective-permute-start.20 = (f32[2,8,2048]{2,1,0:T(8,128)S(1)}, f32[2,8,2048]{2,1,0:T(8,128)S(1)}, u32[]{:S(2)}, u32[]{:S(2)}) collective-permute-start(f32[2,8,2048]{2,1,0:T(8,128)S(1)} %shard_map.184), channel_id=1, source_target_pairs={{0,16},{1,17},{2,18},{3,19},{4,12},{5,13},{6,14},{7,15},{8,24},{9,... | collective-permute-start | bytes 393224 | tf_op jit(solution)/shard_map/ppermute | solution.py:482
  34.3 4.5 %collective-permute-start.21 = (f32[2,8,2048]{2,1,0:T(8,128)S(1)}, f32[2,8,2048]{2,1,0:T(8,128)S(1)}, u32[]{:S(2)}, u32[]{:S(2)}) collective-permute-start(f32[2,8,2048]{2,1,0:T(8,128)S(1)} %shard_map.185.refs_4_), channel_id=1, source_target_pairs={{0,4},{1,5},{2,6},{3,7},{4,0},{5,1},{6,2},{7,3},{8,12},{9,13},{10,... | collective-permute-start | bytes 393224 | tf_op jit(solution)/shard_map/ppermute | solution.py:482
  34.4 9.8 %collective-permute-start.12 = (f32[64,256]{1,0:T(8,128)S(1)}, f32[64,256]{1,0:T(8,128)S(1)}, u32[]{:S(2)}, u32[]{:S(2)}) collective-permute-start(f32[64,256]{1,0:T(8,128)S(1)} %get-tuple-element.123), channel_id=1, source_target_pairs={{0,1},{1,0},{2,3},{3,2},{4,5},{5,4},{6,7},{7,6},{8,9},{9,8},{10,11... | collective-permute-start | bytes 196616 | tf_op jit(solution)/shard_map/ppermute | solution.py:486
  36.1 8.2 %collective-permute-start.13 = (f32[64,256]{1,0:T(8,128)S(1)}, f32[64,256]{1,0:T(8,128)S(1)}, u32[]{:S(2)}, u32[]{:S(2)}) collective-permute-start(f32[64,256]{1,0:T(8,128)S(1)} %get-tuple-element.124), channel_id=1, source_target_pairs={{0,2},{1,3},{2,0},{3,1},{4,6},{5,7},{6,4},{7,5},{8,10},{9,11},{10,... | collective-permute-start | bytes 196616 | tf_op jit(solution)/shard_map/ppermute | solution.py:486
  38.7 6.8 %collective-permute-start.14 = (f32[64,256]{1,0:T(8,128)S(1)}, f32[64,256]{1,0:T(8,128)S(1)}, u32[]{:S(2)}, u32[]{:S(2)}) collective-permute-start(f32[64,256]{1,0:T(8,128)S(1)} %get-tuple-element.125), channel_id=1, source_target_pairs={{0,3},{1,2},{2,1},{3,0},{4,7},{5,6},{6,5},{7,4},{8,11},{9,10},{10,... | collective-permute-start | bytes 196616 | tf_op jit(solution)/shard_map/ppermute | solution.py:486
  39.8 10.5 %collective-permute-start.22 = (f32[64,256]{1,0:T(8,128)S(1)}, f32[64,256]{1,0:T(8,128)S(1)}, u32[]{:S(2)}, u32[]{:S(2)}) collective-permute-start(f32[64,256]{1,0:T(8,128)S(1)} %get-tuple-element.130), channel_id=1, source_target_pairs={{0,1},{1,0},{2,3},{3,2},{4,5},{5,4},{6,7},{7,6},{8,9},{9,8},{10,11... | collective-permute-start | bytes 196616 | tf_op jit(solution)/shard_map/ppermute | solution.py:486
  40.7 9.7 %collective-permute-start.23 = (f32[64,256]{1,0:T(8,128)S(1)}, f32[64,256]{1,0:T(8,128)S(1)}, u32[]{:S(2)}, u32[]{:S(2)}) collective-permute-start(f32[64,256]{1,0:T(8,128)S(1)} %get-tuple-element.131), channel_id=1, source_target_pairs={{0,2},{1,3},{2,0},{3,1},{4,6},{5,7},{6,4},{7,5},{8,10},{9,11},{10,... | collective-permute-start | bytes 196616 | tf_op jit(solution)/shard_map/ppermute | solution.py:486
  44.1 6.2 %collective-permute-start.24 = (f32[64,256]{1,0:T(8,128)S(1)}, f32[64,256]{1,0:T(8,128)S(1)}, u32[]{:S(2)}, u32[]{:S(2)}) collective-permute-start(f32[64,256]{1,0:T(8,128)S(1)} %get-tuple-element.132), channel_id=1, source_target_pairs={{0,3},{1,2},{2,1},{3,0},{4,7},{5,6},{6,5},{7,4},{8,11},{9,10},{10,... | collective-permute-start | bytes 196616 | tf_op jit(solution)/shard_map/ppermute | solution.py:486
  47.3 7.9 %collective-permute-start.16 = (f32[8,4096]{1,0:T(8,128)S(1)}, f32[8,4096]{1,0:T(8,128)S(1)}, u32[]{:S(2)}, u32[]{:S(2)}) collective-permute-start(f32[8,4096]{1,0:T(8,128)S(1)} %shard_map.182.refs_18_), channel_id=1, source_target_pairs={{0,16},{1,17},{2,18},{3,19},{4,12},{5,13},{6,14},{7,15},{8,24},{9,... | collective-permute-start | bytes 393224 | tf_op jit(solution)/shard_map/ppermute | solution.py:482
  48.8 6.3 %collective-permute-start.15 = (f32[8,4096]{1,0:T(8,128)S(1)}, f32[8,4096]{1,0:T(8,128)S(1)}, u32[]{:S(2)}, u32[]{:S(2)}) collective-permute-start(f32[8,4096]{1,0:T(8,128)S(1)} %shard_map.182.refs_18_), channel_id=1, source_target_pairs={{0,8},{1,9},{2,10},{3,11},{4,20},{5,21},{6,22},{7,23},{8,0},{9,1},... | collective-permute-start | bytes 393224 | tf_op jit(solution)/shard_map/ppermute | solution.py:482
  52.1 5.0 %collective-permute-start.26 = (f32[8,4096]{1,0:T(8,128)S(1)}, f32[8,4096]{1,0:T(8,128)S(1)}, u32[]{:S(2)}, u32[]{:S(2)}) collective-permute-start(f32[8,4096]{1,0:T(8,128)S(1)} %shard_map.187), channel_id=1, source_target_pairs={{0,16},{1,17},{2,18},{3,19},{4,12},{5,13},{6,14},{7,15},{8,24},{9,... | collective-permute-start | bytes 393224 | tf_op jit(solution)/shard_map/ppermute | solution.py:482
  53.6 5.0 %collective-permute-start.25 = (f32[8,4096]{1,0:T(8,128)S(1)}, f32[8,4096]{1,0:T(8,128)S(1)}, u32[]{:S(2)}, u32[]{:S(2)}) collective-permute-start(f32[8,4096]{1,0:T(8,128)S(1)} %shard_map.187), channel_id=1, source_target_pairs={{0,8},{1,9},{2,10},{3,11},{4,20},{5,21},{6,22},{7,23},{8,0},{9,1},... | collective-permute-start | bytes 393224 | tf_op jit(solution)/shard_map/ppermute | solution.py:482
  55.2 5.4 %collective-permute-start.18 = (f32[2,8,4096]{2,1,0:T(8,128)S(1)}, f32[2,8,4096]{2,1,0:T(8,128)S(1)}, u32[]{:S(2)}, u32[]{:S(2)}) collective-permute-start(f32[2,8,4096]{2,1,0:T(8,128)S(1)} %shard_map.183), channel_id=1, source_target_pairs={{0,4},{1,5},{2,6},{3,7},{4,0},{5,1},{6,2},{7,3},{8,12},{9,13},{10,... | collective-permute-start | bytes 786440 | tf_op jit(solution)/shard_map/ppermute | solution.py:482
  58.6 2.0 %collective-permute-start.28 = (f32[2,8,4096]{2,1,0:T(8,128)S(1)}, f32[2,8,4096]{2,1,0:T(8,128)S(1)}, u32[]{:S(2)}, u32[]{:S(2)}) collective-permute-start(f32[2,8,4096]{2,1,0:T(8,128)S(1)} %shard_map.188), channel_id=1, source_target_pairs={{0,4},{1,5},{2,6},{3,7},{4,0},{5,1},{6,2},{7,3},{8,12},{9,13},{10,... | collective-permute-start | bytes 786440 | tf_op jit(solution)/shard_map/ppermute | solution.py:482
  58.7 1.7 %collective-permute-start.17 = (f32[8,4096]{1,0:T(8,128)S(1)}, f32[8,4096]{1,0:T(8,128)S(1)}, u32[]{:S(2)}, u32[]{:S(2)}) collective-permute-start(f32[8,4096]{1,0:T(8,128)S(1)} %shard_map.182.refs_18_), channel_id=1, source_target_pairs={{0,4},{1,5},{2,6},{3,7},{4,0},{5,1},{6,2},{7,3},{8,12},{9,13},{10,... | collective-permute-start | bytes 393224 | tf_op jit(solution)/shard_map/ppermute | solution.py:482
  59.2 1.4 %collective-permute-start.27 = (f32[8,4096]{1,0:T(8,128)S(1)}, f32[8,4096]{1,0:T(8,128)S(1)}, u32[]{:S(2)}, u32[]{:S(2)}) collective-permute-start(f32[8,4096]{1,0:T(8,128)S(1)} %shard_map.187), channel_id=1, source_target_pairs={{0,4},{1,5},{2,6},{3,7},{4,0},{5,1},{6,2},{7,3},{8,12},{9,13},{10,... | collective-permute-start | bytes 393224 | tf_op jit(solution)/shard_map/ppermute | solution.py:482
where the time goes:
time: 62.6 us; the launch traced here: 61.3 us
  starting transfers between devices  28.8 us (46%)
  waiting for transfers between devices  17.2 us (27%)
  Pallas kernels  14.2 us (23%)
  between operations  0.96 us (2%)
    ppermute x19, starting transfers between devices, swap(): return lax.ppermute(x, axes, moves)  19.9 us
    ppermute x19, waiting for transfers between devices, swap(): return lax.ppermute(x, axes, moves)  16 us
    ppermute x6, starting transfers between devices, cross(): return lax.ppermute(x, axes, moves)  8.9 us
    pallas_call x2, Pallas kernels, tile_device(): pl.pallas_call(functools.partial(backward_kernel, u, (CHUNKS, CHUNKS, len...  3.5 us
    pallas_call x1, Pallas kernels, tile_device(): pl.pallas_call(functools.partial(ready_kernel, per_device, n_grid), out_s...  2.71 us
    pallas_call x1, Pallas kernels, tile_device(): pl.pallas_call(functools.partial(setup_kernel, per_device), out_shape=[pa...  2.29 us
    pallas_call x2, Pallas kernels, tile_device(): pl.pallas_call(functools.partial(forward_kernel, u, counts + (n_grid - 1,...  2 us
    pallas_call x3, Pallas kernels, rotate(): pl.pallas_call(functools.partial(rotate_kernel, first * SUB), out_shape=(...  1.67 us
  transfers between devices with their start and end apart: 25, of which 11 were waited for; matrix products, arithmetic and copies ran while one was open for 0% of the time, Pallas kernels for 20%

commit v1 on v0

--- a/solution.py
+++ b/solution.py
@@ -117,24 +117,10 @@
     return o, lax.rem(o, 2), lax.div(o, 2)
 
 
-def fetch(source, out, sem, side, start, number):
-    at = pl.multiple_of(side * (source.shape[2] // 2) + start, LANES)
-    step = out.shape[0] // number
-    return [
-        pltpu.make_async_copy(
-            source.at[pl.ds(n * step, step), :, pl.ds(at, out.shape[2])], out.at[pl.ds(n * step, step)], sem.at[n]
-        )
-        for n in range(number)
-    ]
-
-
 def take_kernel(start, source, *rest):
-    out, sem = rest[-2:]
-    copies = fetch(source, out, sem, 1 - my_core(), start, sem.shape[0])
-    for copy in copies:
-        copy.start()
-    for copy in copies:
-        copy.wait()
+    out = rest[-1]
+    at = (1 - my_core()) * (source.shape[2] // 2) + start
+    out[...] = source[:, :, pl.ds(pl.multiple_of(at, LANES), out.shape[2])]
 
 
 class Place:
@@ -159,13 +145,13 @@
         return BLK * self.tiles[tile, 0], BLK * self.tiles[tile, 1]
 
 
-def setup_kernel(per_device, tiles, host, rotation, source, after, *rest):
-    fetched, (high, low, sem) = rest[:-3], rest[-3:]
+def setup_kernel(per_device, tiles, host, rotation, source, loaded, high, low, sem):
     core = my_core()
-    copies = []
-    for n, out in enumerate(fetched):
-        side, chunk = (1 - core, n + 1) if n < CHUNKS - 1 else (core, n - CHUNKS + 1)
-        copies += fetch(source, out, sem.at[n], side, chunk * out.shape[2], sem.shape[1])
+    step = per_device // sem.shape[0]
+    copies = [
+        pltpu.make_async_copy(source.at[pl.ds(n * step, step)], loaded.at[pl.ds(n * step, step)], sem.at[n])
+        for n in range(sem.shape[0])
+    ]
     for copy in copies:
         copy.start()
     at = Place(per_device, tiles, host)
@@ -247,8 +233,9 @@
     out[1] = y[...]
 
 
-def rotate_kernel(first, high, low, *rest):
+def rotate_kernel(first, start, high, low, mine, *rest):
     send, keep = rest[-2:]
+    begin = my_core() * (mine.shape[2] // 2) + start
     rows = send.shape[0] * SUB
     part = pl.ds(first, 2 * rows)
     table = (high[part, :], low[part, :])
@@ -257,10 +244,12 @@
     while at < send.shape[2]:
         width = rest[0].shape[2]
         n, inner = at // width, at % width
-        lanes = slice(inner, inner + step)
-        mine, theirs = rest[2 * n], rest[2 * n + 1]
-        depth = mine.shape[0] * SUB
-        cells = jnp.concatenate([mine[:, :, lanes].reshape(depth, step), theirs[:, :, lanes].reshape(depth, step)])
+        theirs = rest[n]
+        depth = theirs.shape[0] * SUB
+        own = pl.ds(pl.multiple_of(begin + at, LANES), step)
+        cells = jnp.concatenate([
+            mine[:, :, own].reshape(depth, step), theirs[:, :, inner:inner + step].reshape(depth, step)
+        ])
         total = dot3(table, split(cells))
         lanes = slice(at, at + step)
         send[:, :, lanes] = total[:rows].reshape(send.shape[0], SUB, step)
@@ -422,7 +411,7 @@
                 out[:, pl.ds(pl.multiple_of(at * LANES, LANES), LANES)] = -total
 
 
-def place_kernel(stride, match, *refs):
+def place_kernel(stride, sides, match, *refs):
     parts, (out, rows, sem) = refs[:-4], refs[-3:]
     pair = BLK // 2
     blocks = out.shape[0] // BLK
@@ -430,40 +419,37 @@
     values = []
     for part in parts:
         values += [part] if len(part.shape) == 2 else [part.at[n] for n in range(part.shape[0])]
-    parts, count = values, len(values) // pair
+    count = len(values) // (pair * len(sides))
 
     def hits(b, side):
-        return [(match[b * stride + side * stride // 2 + n], side * count // 2 + n) for n in range(count // 2)]
-
-    def found(b, side):
-        return sum(hit for hit, n in hits(b, side)) > 0
-
-    def move(b, side):
-        which = core if side == 0 else 1 - core
-        at = b * BLK + which * pair
-        return pltpu.make_async_copy(rows.at[b, side], out.at[pl.ds(at, pair)], sem.at[b, side])
+        return [match[b * stride + side * stride // 2 + n] for n in range(count)]
+
+    def move(b, at):
+        which = core if sides[at] == 0 else 1 - core
+        begin = b * BLK + which * pair
+        return pltpu.make_async_copy(rows.at[b, at], out.at[pl.ds(begin, pair)], sem.at[b, at])
 
     for b in range(blocks):
-        for side in range(2):
-
-            @pl.when(found(b, side))
+        for at, side in enumerate(sides):
+
+            @pl.when(sum(hits(b, side)) > 0)
             def _():
-                rows[b, side] = jnp.zeros(rows.shape[2:], f32)
-                for hit, n in hits(b, side):
+                rows[b, at] = jnp.zeros(rows.shape[2:], f32)
+                for n, hit in enumerate(hits(b, side)):
 
                     @pl.when(hit > 0)
                     def _():
                         for u in range(pair):
-                            rows[b, side, u] += parts[u * count + n][...]
-
-                move(b, side).start()
+                            rows[b, at, u] += values[(at * pair + u) * count + n][...]
+
+                move(b, at).start()
 
     for b in range(blocks):
-        for side in range(2):
-
-            @pl.when(found(b, side))
+        for at, side in enumerate(sides):
+
+            @pl.when(sum(hits(b, side)) > 0)
             def _():
-                move(b, side).wait()
+                move(b, at).wait()
 
 
 def tile_device(orbitals, rotation, tile_list, pair_mask):
@@ -487,14 +473,7 @@
 
     chunk = half // CHUNKS
     orbitals = pltpu.with_memory_space_constraint(orbitals, pltpu.HBM)
-
     part = jax.ShapeDtypeStruct((per_device, planes, chunk), f32)
-    copies = per_device // 2
-    taken = pl.pallas_call(
-        functools.partial(take_kernel, 0), out_shape=part, in_specs=[HBM], out_specs=VM,
-        scratch_shapes=[DMA((copies,))], name="take", compiler_params=grant(4),
-    )(orbitals)
-    theirs = [swap(taken, 1, 1)]
 
     pair = BLK // 2
     firsts = (BLK + 2) * chips
@@ -504,31 +483,35 @@
     c, r = line_np()
     c, r = line_np()
     host = jnp.asarray(host_np(chips).reshape(-1))
-    *fetched, high, low = pl.pallas_call(
+    loaded, high, low = pl.pallas_call(
         functools.partial(setup_kernel, per_device),
-        out_shape=[part] * (2 * CHUNKS - 1) + [wide_table] * 2,
-        in_specs=[SM, SM, VM, HBM, ANY], out_specs=[VM] * (2 * CHUNKS + 1),
-        scratch_shapes=[DMA((2 * CHUNKS - 1, copies))], name="setup", compiler_params=grant(8),
-    )(tile_list, host, rotation, orbitals, taken)
-    mine = fetched[CHUNKS - 1:]
-    for n, taken in enumerate(fetched[:CHUNKS - 1], 1):
+        out_shape=[jax.ShapeDtypeStruct(shape, f32)] + [wide_table] * 2,
+        in_specs=[SM, SM, VM, HBM], out_specs=[VM] * 3, scratch_shapes=[DMA((4,))], name="setup",
+        compiler_params=grant(8),
+    )(tile_list, host, rotation, orbitals)
+    theirs, last = [], ()
+    for n in range(CHUNKS):
+        taken = pl.pallas_call(
+            functools.partial(take_kernel, n * chunk), out_shape=part, in_specs=[VM] + [ANY] * len(last), out_specs=VM,
+            compiler_params=grant(8),
+        )(loaded, *last)
         theirs.append(swap(taken, 1, 1))
-
-    def rotate(first, count, fields, *after):
-        part = jax.ShapeDtypeStruct((count, planes, chunk * (len(fields) // 2)), f32)
+        last = (taken,)
+
+    def rotate(first, count, start, fields, *after):
+        part = jax.ShapeDtypeStruct((count, planes, chunk * len(fields)), f32)
         send, keep = pl.pallas_call(
-            functools.partial(rotate_kernel, first * SUB), out_shape=(part, part),
-            in_specs=[VM] * (2 + len(fields)) + [ANY] * len(after),
+            functools.partial(rotate_kernel, first * SUB, start), out_shape=(part, part),
+            in_specs=[VM] * (3 + len(fields)) + [ANY] * len(after),
             out_specs=(VM, VM), compiler_params=grant(8),
-        )(high, low, *fields, *after)
+        )(high, low, loaded, *fields, *after)
         return send, keep, swap(send, 2, 4)
 
     sums, last = [], ()
     for n in range(CHUNKS):
-        sums.append(rotate(0, firsts // 2, [mine[n], theirs[n]], *last))
+        sums.append(rotate(0, firsts // 2, n * chunk, [theirs[n]], *last))
         last = (sums[-1][0],)
-    both = [x for n in range(CHUNKS) for x in (mine[n], theirs[n])]
-    sums.append(rotate(firsts, (pair - 1) * chips, both, *last))
+    sums.append(rotate(firsts, (pair - 1) * chips, 0, theirs, *last))
     empty, powers, flags, match, alone = pl.pallas_call(
         functools.partial(ready_kernel, per_device, n_grid),
         out_shape=(pltpu.HBM(shape, f32), jax.ShapeDtypeStruct((6, NY, LANES), f32),
@@ -564,7 +547,7 @@
         step = pass_on(n, step)
     for n in range(CHUNKS):
         step = finish(n, step)
-    last = (step,)
+    last = (pass_on(CHUNKS, step),)
 
     sine_x, eigen_x = sine_np(planes), eigen_np(planes)
     ends = jnp.asarray(np.einsum("jp,pkl->kjl", sine_x, r[None] ** np.arange(planes - 1, -1, -1)[:, None, None])
@@ -585,7 +568,6 @@
     base_own, base_other = own[:CHUNKS], other[:CHUNKS]
     for u in range(pair):
         if u:
-            pass_on(CHUNKS, *last)
             finish(CHUNKS, *last)
         more_own, more_other = own[CHUNKS:][:u], other[CHUNKS:][:u]
         counts = (CHUNKS, CHUNKS, len(more_own), len(more_other))
@@ -630,26 +612,27 @@
         given = swap(term, 1, 1)
         sib_parts.append([given, swap(joined, 1, 1)])
 
-    def place(target, groups):
+    def place(target, sides, groups):
         parts = [part for group in groups for part in group]
         return pl.pallas_call(
-            functools.partial(place_kernel, 8),
+            functools.partial(place_kernel, 8, sides),
             out_shape=pltpu.HBM(shape, f32),
             in_specs=[SM] + [VM] * len(parts) + [HBM],
             out_specs=HBM,
             input_output_aliases={len(parts) + 1: 0},
-            scratch_shapes=[pltpu.VMEM((blocks, 2, pair, planes, width), f32), DMA((blocks, 2))],
-            name="place",
+            scratch_shapes=[pltpu.VMEM((blocks, len(sides), pair, planes, width), f32), DMA((blocks, len(sides)))],
             compiler_params=grant(8),
         )(match, *parts, target)
 
     def place_near(target, mine, sibs):
-        return place(target, [a + b for a, b in zip(mine, sibs)])
+        return place(target, (1,), sibs)
 
     def place_far(target, mine, sibs):
         far = [swap(group[1], 4, 2) for group in mine]
-        return place(target, [a + [x] + b + [swap(x, 1, 1)] for a, b, x in zip(mine, sibs, far)])
-
+        groups = [a + [x] for a, x in zip(mine, far)] + [b + [swap(x, 1, 1)] for b, x in zip(sibs, far)]
+        return place(target, (0, 1), groups)
+
+    empty = place(empty, (0,), own_parts)
     return lax.cond(alone[0] != 0, place_far, place_near, empty, own_parts, sib_parts)
 
 

time: 62.6 us -> 63.7 us (1.018)
  the two profiles are of different devices: /device:TPU:0 before, /device:TPU:17 now
where the time goes in v1:
time: 63.7 us; the launch traced here: 63.5 us
  starting transfers between devices  33.4 us (52%)
  Pallas kernels  13.7 us (22%)
  waiting for transfers between devices  13 us (20%)
  local copies, waits for them, and re-layouts  2.39 us (4%)
  between operations  0.99 us (2%)
    ppermute x19, starting transfers between devices, swap(): return lax.ppermute(x, axes, moves)  27.2 us
    ppermute x19, waiting for transfers between devices, swap(): return lax.ppermute(x, axes, moves)  9.47 us
    ppermute x6, starting transfers between devices, cross(): return lax.ppermute(x, axes, moves)  6.17 us
    ppermute x6, waiting for transfers between devices, cross(): return lax.ppermute(x, axes, moves)  3.51 us
    pallas_call x2, Pallas kernels, tile_device(): pl.pallas_call(functools.partial(backward_kernel, u, (CHUNKS, CHUNKS, len...  3.49 us
    pallas_call x1, Pallas kernels, tile_device(): pl.pallas_call(functools.partial(ready_kernel, per_device, n_grid), out_s...  2.71 us
    unnamed x35, local copies, waits for them, and re-layouts  2.39 us
    pallas_call x1, Pallas kernels, tile_device(): pl.pallas_call(functools.partial(setup_kernel, per_device), out_shape=[ja...  2.21 us
  transfers between devices with their start and end apart: 25, of which 9 were waited for; matrix products, arithmetic and copies ran while one was open for 0% of the time, Pallas kernels for 17%

profile of v1, /device:TPU:17, one launch (start us, length us, event | category | flops | bytes accessed | tf_op | source)
XLA Modules:
  0.0 63.5 jit_solution(4974531330305600351)
XLA Ops:
  0.0 0.8 %copy.25.tiles = s32[4,2]{1,0:T(4,128)S(1)} copy(s32[4,2]{0,1:T(2,128)} %param.22) | data formatting | bytes 64 | tf_op args[2]
  0.8 0.8 %copy-done.11 = f32[128,128]{1,0:T(8,128)S(1)} copy-done((f32[128,128]{1,0:T(8,128)S(1)}, f32[128,128]{1,0:T(8,128)}, u32[]{:S(2)}) %copy-start.11) | copy-done | bytes 65560
  1.6 0.7 %copy-done.15 = s32[1024]{0:T(1024)S(1)} copy-done((s32[1024]{0:T(1024)S(1)}, s32[1024]{0:T(1024)}, u32[]{:S(2)}) %copy-start.15) | copy-done | bytes 4120
  2.3 2.2 %setup.1 = (f32[16,8,4096]{2,1,0:T(8,128)S(1)}, bf16[256,256]{1,0:T(8,128)(2,1)S(1)}, bf16[256,256]{1,0:T(8,128)(2,1)S(1)}) custom-call(s32[4,2]{1,0:T(4,128)S(1)} %copy.25.tiles, s32[1024]{0:T(1024)S(1)} %copy-done.15, f32[128,128]{1,0:T(8,128)S(1)} %copy-done.11, f32[16,8,4096]{2,1,0:T(8,128)} %source.1), custom_call_target="tpu_custom_call" | custom-call | tf_op jit(solution)/shard_map/setup/pallas_call | solution.py:486
  4.6 0.7 %collective-permute-start.4 = (f32[16,8,1024]{2,1,0:T(8,128)S(1)}, f32[16,8,1024]{2,1,0:T(8,128)S(1)}, u32[]{:S(2)}, u32[]{:S(2)}) collective-permute-start(f32[16,8,1024]{2,1,0:T(8,128)S(1)} %shard_map.174.rest_0_), channel_id=1, source_target_pairs={{0,4},{1,5},{2,6},{3,7},{4,0},{5,1},{6,2},{7,3},{8,12},{9,13},{10,... | collective-permute-start | bytes 1572872 | tf_op jit(solution)/shard_map/ppermute | solution.py:468
  5.4 0.1 collective-permute-start.5
  5.5 1.4 %collective-permute-done.4.rest_0_ = f32[16,8,1024]{2,1,0:T(8,128)S(1)} collective-permute-done((f32[16,8,1024]{2,1,0:T(8,128)S(1)}, f32[16,8,1024]{2,1,0:T(8,128)S(1)}, u32[]{:S(2)}, u32[]{:S(2)}) %collective-permute-start.4) | collective-permute-done | bytes 524320 | tf_op jit(solution)/shard_map/ppermute | solution.py:468
  6.9 0.5 shard_map.176
  7.4 1.3 %collective-permute-start.6 = (f32[12,8,1024]{2,1,0:T(8,128)S(1)}, f32[12,8,1024]{2,1,0:T(8,128)S(1)}, u32[]{:S(2)}, u32[]{:S(2)}) collective-permute-start(f32[12,8,1024]{2,1,0:T(8,128)S(1)} %get-tuple-element.91.rest_1_), channel_id=1, source_target_pairs={{0,8},{1,9},{2,10},{3,11},{4,20},{5,21},{6,22},{7,23},{8,0},{9,1},... | collective-permute-start | bytes 1179656 | tf_op jit(solution)/shard_map/ppermute | solution.py:468
  8.7 0.5 shard_map.177
  9.2 0.3 collective-permute-start.8
  9.5 0.7 %shard_map.178 = (f32[4,8,2048]{2,1,0:T(8,128)S(1)}, f32[4,8,2048]{2,1,0:T(8,128)S(1)}) custom-call(bf16[256,256]{1,0:T(8,128)(2,1)S(1)} %get-tuple-element.88.high, bf16[256,256]{1,0:T(8,128)(2,1)S(1)} %get-tuple-element.89.low, f32[16,8,4096]{2,1,0:T(8,128)S(1)} %get-tuple-element.90.source.mine, f32[16,8,1024]{2,1,0:T(8,128)S(1)} %collective-permute-done.4.rest_0_, ...), custom_call_target="tpu_custom_call" | custom-call | tf_op jit(solution)/shard_map/pallas_call | solution.py:503
  10.3 2.7 %ready.1 = (f32[16,8,4096]{2,1,0:T(8,128)}, f32[6,64,128]{2,1,0:T(8,128)S(1)}, f32[8]{0:T(128)S(1)}, s32[32]{0:T(128)S(1)}, s32[1]{0:T(128)}) custom-call(s32[4,2]{1,0:T(4,128)S(1)} %copy.25.tiles, s32[1024]{0:T(1024)S(1)} %copy-done.16, s32[128,128]{1,0:T(8,128)S(1)} %copy-done.12, f32[64,128]{1,0:T(8,128)S(1)} %copy-done.13, ...), custom_call_target="tpu_custom_call" | custom-call | tf_op jit(solution)/shard_map/ready/pallas_call | solution.py:515
  13.0 1.4 %collective-permute-done.6.got = f32[12,8,1024]{2,1,0:T(8,128)S(1)} collective-permute-done((f32[12,8,1024]{2,1,0:T(8,128)S(1)}, f32[12,8,1024]{2,1,0:T(8,128)S(1)}, u32[]{:S(2)}, u32[]{:S(2)}) %collective-permute-start.6) | collective-permute-done | bytes 393248 | tf_op jit(solution)/shard_map/ppermute | solution.py:468
  14.4 1.3 %collective-permute-start.7 = (f32[6,8,1024]{2,1,0:T(8,128)S(1)}, f32[6,8,1024]{2,1,0:T(8,128)S(1)}, u32[]{:S(2)}, u32[]{:S(2)}) collective-permute-start(f32[6,8,1024]{2,1,0:T(8,128)S(1)} %shard_map.179.rest_0_), channel_id=1, source_target_pairs={{0,16},{1,17},{2,18},{3,19},{4,12},{5,13},{6,14},{7,15},{8,24},{9,... | collective-permute-start | bytes 589832 | tf_op jit(solution)/shard_map/ppermute | solution.py:468
  15.7 2.9 %collective-permute-done.8.got = f32[12,8,1024]{2,1,0:T(8,128)S(1)} collective-permute-done((f32[12,8,1024]{2,1,0:T(8,128)S(1)}, f32[12,8,1024]{2,1,0:T(8,128)S(1)}, u32[]{:S(2)}, u32[]{:S(2)}) %collective-permute-start.8) | collective-permute-done | bytes 393248 | tf_op jit(solution)/shard_map/ppermute | solution.py:468
  18.7 1.3 %collective-permute-start.9 = (f32[6,8,1024]{2,1,0:T(8,128)S(1)}, f32[6,8,1024]{2,1,0:T(8,128)S(1)}, u32[]{:S(2)}, u32[]{:S(2)}) collective-permute-start(f32[6,8,1024]{2,1,0:T(8,128)S(1)} %shard_map.180.rest_0_), channel_id=1, source_target_pairs={{0,16},{1,17},{2,18},{3,19},{4,12},{5,13},{6,14},{7,15},{8,24},{9,... | collective-permute-start | bytes 589832 | tf_op jit(solution)/shard_map/ppermute | solution.py:468
  19.9 1.2 %collective-permute-start.12 = (f32[4,8,2048]{2,1,0:T(8,128)S(1)}, f32[4,8,2048]{2,1,0:T(8,128)S(1)}, u32[]{:S(2)}, u32[]{:S(2)}) collective-permute-start(f32[4,8,2048]{2,1,0:T(8,128)S(1)} %get-tuple-element.93.rest_0_), channel_id=1, source_target_pairs={{0,8},{1,9},{2,10},{3,11},{4,20},{5,21},{6,22},{7,23},{8,0},{9,1},... | collective-permute-start | bytes 786440 | tf_op jit(solution)/shard_map/ppermute | solution.py:468
  21.2 0.2 collective-permute-done.7.passed
  21.4 1.9 %collective-permute-done.9.passed = f32[6,8,1024]{2,1,0:T(8,128)S(1)} collective-permute-done((f32[6,8,1024]{2,1,0:T(8,128)S(1)}, f32[6,8,1024]{2,1,0:T(8,128)S(1)}, u32[]{:S(2)}, u32[]{:S(2)}) %collective-permute-start.9) | collective-permute-done | bytes 196640 | tf_op jit(solution)/shard_map/ppermute | solution.py:468
  23.4 4.7 %collective-permute-start.11 = (f32[6,8,1024]{2,1,0:T(8,128)S(1)}, f32[6,8,1024]{2,1,0:T(8,128)S(1)}, u32[]{:S(2)}, u32[]{:S(2)}) collective-permute-start(f32[6,8,1024]{2,1,0:T(8,128)S(1)} %shard_map.182.rest_0_.refs_1_), channel_id=1, source_target_pairs={{0,4},{1,5},{2,6},{3,7},{4,0},{5,1},{6,2},{7,3},{8,12},{9,13},{10,... | collective-permute-start | bytes 589832 | tf_op jit(solution)/shard_map/ppermute | solution.py:468
  28.0 0.1 collective-permute-start.10
  28.2 1.1 %collective-permute-start.20 = (f32[2,8,2048]{2,1,0:T(8,128)S(1)}, f32[2,8,2048]{2,1,0:T(8,128)S(1)}, u32[]{:S(2)}, u32[]{:S(2)}) collective-permute-start(f32[2,8,2048]{2,1,0:T(8,128)S(1)} %shard_map.183.refs_10_), channel_id=1, source_target_pairs={{0,16},{1,17},{2,18},{3,19},{4,12},{5,13},{6,14},{7,15},{8,24},{9,... | collective-permute-start | bytes 393224 | tf_op jit(solution)/shard_map/ppermute | solution.py:468
  29.3 0.2 collective-permute-done.10.refs_2_
  29.5 1.0 %shard_map.184 = (f32[64,256]{1,0:T(8,128)S(1)}, f32[64,256]{1,0:T(8,128)S(1)}, f32[64,256]{1,0:T(8,128)S(1)}, f32[512,256]{1,0:T(8,128)S(1)}, f32[64,256]{1,0:T(8,128)S(1)}, /*index=5*/f32[64,256]{1,0:T(8,128)S(1)}) custom-call(f32[6,8,1024]{2,1,0:T(8,128)S(1)} %shard_map.181.rest_0_.refs_0_, f32[6,8,1024]{2,1,0:T(8,128)S(1)} %shard_map.182.rest_0_.refs_1_, ...), custom_call_target="tpu_custom_call" | custom-call | tf_op jit(solution)/shard_map/pallas_call | solution.py:575
  30.6 1.4 %collective-permute-done.20.passed = f32[2,8,2048]{2,1,0:T(8,128)S(1)} collective-permute-done((f32[2,8,2048]{2,1,0:T(8,128)S(1)}, f32[2,8,2048]{2,1,0:T(8,128)S(1)}, u32[]{:S(2)}, u32[]{:S(2)}) %collective-permute-start.20) | collective-permute-done | bytes 131104 | tf_op jit(solution)/shard_map/ppermute | solution.py:468
  32.1 3.1 %collective-permute-start.21 = (f32[2,8,2048]{2,1,0:T(8,128)S(1)}, f32[2,8,2048]{2,1,0:T(8,128)S(1)}, u32[]{:S(2)}, u32[]{:S(2)}) collective-permute-start(f32[2,8,2048]{2,1,0:T(8,128)S(1)} %shard_map.187.refs_4_), channel_id=1, source_target_pairs={{0,4},{1,5},{2,6},{3,7},{4,0},{5,1},{6,2},{7,3},{8,12},{9,13},{10,... | collective-permute-start | bytes 393224 | tf_op jit(solution)/shard_map/ppermute | solution.py:468
  35.2 1.3 %collective-permute-start.13 = (f32[64,256]{1,0:T(8,128)S(1)}, f32[64,256]{1,0:T(8,128)S(1)}, u32[]{:S(2)}, u32[]{:S(2)}) collective-permute-start(f32[64,256]{1,0:T(8,128)S(1)} %get-tuple-element.102), channel_id=1, source_target_pairs={{0,1},{1,0},{2,3},{3,2},{4,5},{5,4},{6,7},{7,6},{8,9},{9,8},{10,11... | collective-permute-start | bytes 196616 | tf_op jit(solution)/shard_map/ppermute | solution.py:472
  36.5 0.1 collective-permute-start.14
  36.5 1.3 %collective-permute-start.15 = (f32[64,256]{1,0:T(8,128)S(1)}, f32[64,256]{1,0:T(8,128)S(1)}, u32[]{:S(2)}, u32[]{:S(2)}) collective-permute-start(f32[64,256]{1,0:T(8,128)S(1)} %get-tuple-element.104), channel_id=1, source_target_pairs={{0,3},{1,2},{2,1},{3,0},{4,7},{5,6},{6,5},{7,4},{8,11},{9,10},{10,... | collective-permute-start | bytes 196616 | tf_op jit(solution)/shard_map/ppermute | solution.py:472
  37.8 1.0 %shard_map.188 = (f32[64,256]{1,0:T(8,128)S(1)}, f32[64,256]{1,0:T(8,128)S(1)}, f32[64,256]{1,0:T(8,128)S(1)}, f32[512,256]{1,0:T(8,128)S(1)}, f32[64,256]{1,0:T(8,128)S(1)}, /*index=5*/f32[64,256]{1,0:T(8,128)S(1)}) custom-call(f32[6,8,1024]{2,1,0:T(8,128)S(1)} %shard_map.181.rest_0_.refs_0_, f32[6,8,1024]{2,1,0:T(8,128)S(1)} %shard_map.182.rest_0_.refs_1_, ...), custom_call_target="tpu_custom_call" | custom-call | tf_op jit(solution)/shard_map/pallas_call | solution.py:575
  38.8 2.3 %collective-permute-start.22 = (f32[64,256]{1,0:T(8,128)S(1)}, f32[64,256]{1,0:T(8,128)S(1)}, u32[]{:S(2)}, u32[]{:S(2)}) collective-permute-start(f32[64,256]{1,0:T(8,128)S(1)} %get-tuple-element.108), channel_id=1, source_target_pairs={{0,1},{1,0},{2,3},{3,2},{4,5},{5,4},{6,7},{7,6},{8,9},{9,8},{10,11... | collective-permute-start | bytes 196616 | tf_op jit(solution)/shard_map/ppermute | solution.py:472
  41.1 1.3 %collective-permute-start.24 = (f32[64,256]{1,0:T(8,128)S(1)}, f32[64,256]{1,0:T(8,128)S(1)}, u32[]{:S(2)}, u32[]{:S(2)}) collective-permute-start(f32[64,256]{1,0:T(8,128)S(1)} %get-tuple-element.110), channel_id=1, source_target_pairs={{0,3},{1,2},{2,1},{3,0},{4,7},{5,6},{6,5},{7,4},{8,11},{9,10},{10,... | collective-permute-start | bytes 196616 | tf_op jit(solution)/shard_map/ppermute | solution.py:472
  42.3 1.5 %collective-permute-done.15.refs_6_ = f32[64,256]{1,0:T(8,128)S(1)} collective-permute-done((f32[64,256]{1,0:T(8,128)S(1)}, f32[64,256]{1,0:T(8,128)S(1)}, u32[]{:S(2)}, u32[]{:S(2)}) %collective-permute-start.15) | collective-permute-done | bytes 65568 | tf_op jit(solution)/shard_map/ppermute | solution.py:472
  43.9 1.8 %shard_map.185.refs_18_.refs_0_ = f32[8,4096]{1,0:T(8,128)S(1)} custom-call(f32[8]{0:T(128)S(1)} %get-tuple-element.96.flags, f32[6,8,1024]{2,1,0:T(8,128)S(1)} %shard_map.181.rest_0_.refs_0_, f32[6,8,1024]{2,1,0:T(8,128)S(1)} %shard_map.182.rest_0_.refs_1_, f32[6,8,1024]{2,1,0:T(8,128)S(1)} %collective-permute-done.10.refs_2_, ...), custom_call_target="tpu_custom_call" | custom-call | tf_op jit(solution)/shard_map/pallas_call | solution.py:593
  45.7 1.3 %collective-permute-start.18 = (f32[8,4096]{1,0:T(8,128)S(1)}, f32[8,4096]{1,0:T(8,128)S(1)}, u32[]{:S(2)}, u32[]{:S(2)}) collective-permute-start(f32[8,4096]{1,0:T(8,128)S(1)} %shard_map.185.refs_18_.refs_0_), channel_id=1, source_target_pairs={{0,16},{1,17},{2,18},{3,19},{4,12},{5,13},{6,14},{7,15},{8,24},{9,... | collective-permute-start | bytes 393224 | tf_op jit(solution)/shard_map/ppermute | solution.py:468
  46.9 0.2 collective-permute-start.17
  47.2 2.0 %collective-permute-done.24.refs_6_ = f32[64,256]{1,0:T(8,128)S(1)} collective-permute-done((f32[64,256]{1,0:T(8,128)S(1)}, f32[64,256]{1,0:T(8,128)S(1)}, u32[]{:S(2)}, u32[]{:S(2)}) %collective-permute-start.24) | collective-permute-done | bytes 65568 | tf_op jit(solution)/shard_map/ppermute | solution.py:472
  49.2 1.7 %shard_map.189.refs_3_ = f32[8,4096]{1,0:T(8,128)S(1)} custom-call(f32[8]{0:T(128)S(1)} %get-tuple-element.96.flags, f32[6,8,1024]{2,1,0:T(8,128)S(1)} %shard_map.181.rest_0_.refs_0_, f32[6,8,1024]{2,1,0:T(8,128)S(1)} %shard_map.182.rest_0_.refs_1_, f32[6,8,1024]{2,1,0:T(8,128)S(1)} %collective-permute-done.10.refs_2_, ...), custom_call_target="tpu_custom_call" | custom-call | tf_op jit(solution)/shard_map/pallas_call | solution.py:593
  50.9 1.3 %collective-permute-start.27 = (f32[8,4096]{1,0:T(8,128)S(1)}, f32[8,4096]{1,0:T(8,128)S(1)}, u32[]{:S(2)}, u32[]{:S(2)}) collective-permute-start(f32[8,4096]{1,0:T(8,128)S(1)} %shard_map.189.refs_3_), channel_id=1, source_target_pairs={{0,16},{1,17},{2,18},{3,19},{4,12},{5,13},{6,14},{7,15},{8,24},{9,... | collective-permute-start | bytes 393224 | tf_op jit(solution)/shard_map/ppermute | solution.py:468
  52.2 0.2 collective-permute-start.26
  52.4 4.5 %collective-permute-start.19 = (f32[2,8,4096]{2,1,0:T(8,128)S(1)}, f32[2,8,4096]{2,1,0:T(8,128)S(1)}, u32[]{:S(2)}, u32[]{:S(2)}) collective-permute-start(f32[2,8,4096]{2,1,0:T(8,128)S(1)} %shard_map.186), channel_id=1, source_target_pairs={{0,4},{1,5},{2,6},{3,7},{4,0},{5,1},{6,2},{7,3},{8,12},{9,13},{10,... | collective-permute-start | bytes 786440 | tf_op jit(solution)/shard_map/ppermute | solution.py:468
  57.0 4.0 %collective-permute-start.28 = (f32[2,8,4096]{2,1,0:T(8,128)S(1)}, f32[2,8,4096]{2,1,0:T(8,128)S(1)}, u32[]{:S(2)}, u32[]{:S(2)}) collective-permute-start(f32[2,8,4096]{2,1,0:T(8,128)S(1)} %shard_map.190), channel_id=1, source_target_pairs={{0,4},{1,5},{2,6},{3,7},{4,0},{5,1},{6,2},{7,3},{8,12},{9,13},{10,... | collective-permute-start | bytes 786440 | tf_op jit(solution)/shard_map/ppermute | solution.py:468
  61.0 0.1 collective-permute-start.16
  61.1 0.4 collective-permute-start.25
  62.1 0.6 %shard_map.191 = f32[16,8,4096]{2,1,0:T(8,128)} custom-call(s32[32]{0:T(128)S(1)} %get-tuple-element.95.match, f32[8,4096]{1,0:T(8,128)S(1)} %shard_map.185.refs_18_.refs_0_, f32[8,4096]{1,0:T(8,128)S(1)} %collective-permute-done.17.x.refs_1_, f32[8,4096]{1,0:T(8,128)S(1)} %collective-permute-done.18.y.refs_2_, ...), custom_call_target="tpu_custom_call", output_to_operand_aliasing={{}: (7, {})} | custom-call | tf_op jit(solution)/shard_map/pallas_call | solution.py:617
  62.8 0.7 %conditional.1 = (f32[16,8,4096]{2,1,0:T(8,128)}) conditional(s32[]{:T(128)} %bitcast, (s32[32]{0:T(128)S(1)}, f32[8,4096]{1,0:T(8,128)S(1)}, f32[2,8,4096]{2,1,0:T(8,128)S(1)}, f32[8,4096]{1,0:T(8,128)S(1)}, f32[2,8,4096]{2,1,0:T(8,128)S(1)}, /*index=5*/f32[16,8,4096]{2,1,0:T(8,128)}) %tuple.11, (f32[8,4096]{1,0:T(8,128)S(1)}, ...), branch_computations={%region_0.0_spmd, %region_1.0_spmd} | conditional | bytes 2097320 | solution.py:636
  62.8 0.6 %branch_0_fun.1 = f32[16,8,4096]{2,1,0:T(8,128)} custom-call(s32[32]{0:T(128)S(1)} %get-tuple-element.44.match, f32[8,4096]{1,0:T(8,128)S(1)} %get-tuple-element.45.refs_0_, f32[2,8,4096]{2,1,0:T(8,128)S(1)} %get-tuple-element.46.refs_1_, f32[8,4096]{1,0:T(8,128)S(1)} %get-tuple-element.47.refs_2_, ...), custom_call_target="tpu_custom_call", output_to_operand_aliasing={{}: (5, {})} | custom-call | tf_op jit(solution)/shard_map/cond/branch_0_fun/pallas_call | solution.py:617
  (59 shorter events, 0.4 us)
Async XLA Ops:
  0.8 0.8 %copy-start.11 = (f32[128,128]{1,0:T(8,128)S(1)}, f32[128,128]{1,0:T(8,128)}, u32[]{:S(2)}) copy-start(f32[128,128]{1,0:T(8,128)} %rotation.1) | copy-start | bytes 196612
  1.6 0.7 %copy-start.15 = (s32[1024]{0:T(1024)S(1)}, s32[1024]{0:T(1024)}, u32[]{:S(2)}) copy-start(s32[1024]{0:T(1024)} %constant.31.clone.host) | copy-start | bytes 12292
  4.6 2.3 %collective-permute-start.4 = (f32[16,8,1024]{2,1,0:T(8,128)S(1)}, f32[16,8,1024]{2,1,0:T(8,128)S(1)}, u32[]{:S(2)}, u32[]{:S(2)}) collective-permute-start(f32[16,8,1024]{2,1,0:T(8,128)S(1)} %shard_map.174.rest_0_), channel_id=1, source_target_pairs={{0,4},{1,5},{2,6},{3,7},{4,0},{5,1},{6,2},{7,3},{8,12},{9,13},{10,... | collective-permute-start | bytes 1572872 | tf_op jit(solution)/shard_map/ppermute | solution.py:468
  5.4 3.3 %collective-permute-start.5 = (f32[16,8,1024]{2,1,0:T(8,128)S(1)}, f32[16,8,1024]{2,1,0:T(8,128)S(1)}, u32[]{:S(2)}, u32[]{:S(2)}) collective-permute-start(f32[16,8,1024]{2,1,0:T(8,128)S(1)} %shard_map.175), channel_id=1, source_target_pairs={{0,4},{1,5},{2,6},{3,7},{4,0},{5,1},{6,2},{7,3},{8,12},{9,13},{10,... | collective-permute-start | bytes 1572872 | tf_op jit(solution)/shard_map/ppermute | solution.py:468
  7.4 7.0 %collective-permute-start.6 = (f32[12,8,1024]{2,1,0:T(8,128)S(1)}, f32[12,8,1024]{2,1,0:T(8,128)S(1)}, u32[]{:S(2)}, u32[]{:S(2)}) collective-permute-start(f32[12,8,1024]{2,1,0:T(8,128)S(1)} %get-tuple-element.91.rest_1_), channel_id=1, source_target_pairs={{0,8},{1,9},{2,10},{3,11},{4,20},{5,21},{6,22},{7,23},{8,0},{9,1},... | collective-permute-start | bytes 1179656 | tf_op jit(solution)/shard_map/ppermute | solution.py:468
  9.2 1.0 %copy-start.12 = (s32[128,128]{1,0:T(8,128)S(1)}, s32[128,128]{1,0:T(8,128)}, u32[]{:S(2)}) copy-start(s32[128,128]{1,0:T(8,128)} %mask.1) | copy-start | bytes 196612
  9.2 1.0 %copy-start.13 = (f32[64,128]{1,0:T(8,128)S(1)}, f32[64,128]{1,0:T(8,128)}, u32[]{:S(2)}) copy-start(f32[64,128]{1,0:T(8,128)} %constant.32.clone.log_r) | copy-start | bytes 98308
  9.2 1.0 %copy-start.16 = (s32[1024]{0:T(1024)S(1)}, s32[1024]{0:T(1024)}, u32[]{:S(2)}) copy-start(s32[1024]{0:T(1024)} %constant.31.clone.host) | copy-start | bytes 12292
  9.2 9.3 %collective-permute-start.8 = (f32[12,8,1024]{2,1,0:T(8,128)S(1)}, f32[12,8,1024]{2,1,0:T(8,128)S(1)}, u32[]{:S(2)}, u32[]{:S(2)}) collective-permute-start(f32[12,8,1024]{2,1,0:T(8,128)S(1)} %get-tuple-element.92.rest_2_), channel_id=1, source_target_pairs={{0,8},{1,9},{2,10},{3,11},{4,20},{5,21},{6,22},{7,23},{8,0},{9,1},... | collective-permute-start | bytes 1179656 | tf_op jit(solution)/shard_map/ppermute | solution.py:468
  14.4 7.0 %collective-permute-start.7 = (f32[6,8,1024]{2,1,0:T(8,128)S(1)}, f32[6,8,1024]{2,1,0:T(8,128)S(1)}, u32[]{:S(2)}, u32[]{:S(2)}) collective-permute-start(f32[6,8,1024]{2,1,0:T(8,128)S(1)} %shard_map.179.rest_0_), channel_id=1, source_target_pairs={{0,16},{1,17},{2,18},{3,19},{4,12},{5,13},{6,14},{7,15},{8,24},{9,... | collective-permute-start | bytes 589832 | tf_op jit(solution)/shard_map/ppermute | solution.py:468
  18.6 10.9 %copy-start = (bf16[2,256,256]{2,1,0:T(8,128)(2,1)S(1)}, bf16[2,256,256]{2,1,0:T(8,128)(2,1)}, u32[]{:S(2)}) copy-start(bf16[2,256,256]{2,1,0:T(8,128)(2,1)} %constant.38.clone.refs_5_.refs_7_) | copy-start | bytes 786436
  18.6 10.9 %copy-start.1 = (bf16[2,256,256]{2,1,0:T(8,128)(2,1)S(1)}, bf16[2,256,256]{2,1,0:T(8,128)(2,1)}, u32[]{:S(2)}) copy-start(bf16[2,256,256]{2,1,0:T(8,128)(2,1)} %constant.37.clone.refs_4_.refs_6_) | copy-start | bytes 786436
  18.6 10.9 %copy-start.2 = (f32[512,128]{1,0:T(8,128)S(1)}, f32[512,128]{1,0:T(8,128)}, u32[]{:S(2)}) copy-start(f32[512,128]{1,0:T(8,128)} %constant.33.clone.refs_8_.refs_10_) | copy-start | bytes 786436
  18.6 10.9 %copy-start.6 = (bf16[256,256]{1,0:T(8,128)(2,1)S(1)}, bf16[256,256]{1,0:T(8,128)(2,1)}, u32[]{:S(2)}) copy-start(bf16[256,256]{1,0:T(8,128)(2,1)} %constant.42.clone.refs_7_.refs_9_) | copy-start | bytes 393220
  18.6 10.9 %copy-start.7 = (bf16[256,256]{1,0:T(8,128)(2,1)S(1)}, bf16[256,256]{1,0:T(8,128)(2,1)}, u32[]{:S(2)}) copy-start(bf16[256,256]{1,0:T(8,128)(2,1)} %constant.41.clone.refs_6_.refs_8_) | copy-start | bytes 393220
  18.7 4.7 %collective-permute-start.9 = (f32[6,8,1024]{2,1,0:T(8,128)S(1)}, f32[6,8,1024]{2,1,0:T(8,128)S(1)}, u32[]{:S(2)}, u32[]{:S(2)}) collective-permute-start(f32[6,8,1024]{2,1,0:T(8,128)S(1)} %shard_map.180.rest_0_), channel_id=1, source_target_pairs={{0,16},{1,17},{2,18},{3,19},{4,12},{5,13},{6,14},{7,15},{8,24},{9,... | collective-permute-start | bytes 589832 | tf_op jit(solution)/shard_map/ppermute | solution.py:468
  19.9 8.2 %collective-permute-start.12 = (f32[4,8,2048]{2,1,0:T(8,128)S(1)}, f32[4,8,2048]{2,1,0:T(8,128)S(1)}, u32[]{:S(2)}, u32[]{:S(2)}) collective-permute-start(f32[4,8,2048]{2,1,0:T(8,128)S(1)} %get-tuple-element.93.rest_0_), channel_id=1, source_target_pairs={{0,8},{1,9},{2,10},{3,11},{4,20},{5,21},{6,22},{7,23},{8,0},{9,1},... | collective-permute-start | bytes 786440 | tf_op jit(solution)/shard_map/ppermute | solution.py:468
  23.4 5.9 %collective-permute-start.11 = (f32[6,8,1024]{2,1,0:T(8,128)S(1)}, f32[6,8,1024]{2,1,0:T(8,128)S(1)}, u32[]{:S(2)}, u32[]{:S(2)}) collective-permute-start(f32[6,8,1024]{2,1,0:T(8,128)S(1)} %shard_map.182.rest_0_.refs_1_), channel_id=1, source_target_pairs={{0,4},{1,5},{2,6},{3,7},{4,0},{5,1},{6,2},{7,3},{8,12},{9,13},{10,... | collective-permute-start | bytes 589832 | tf_op jit(solution)/shard_map/ppermute | solution.py:468
  28.0 1.4 %collective-permute-start.10 = (f32[6,8,1024]{2,1,0:T(8,128)S(1)}, f32[6,8,1024]{2,1,0:T(8,128)S(1)}, u32[]{:S(2)}, u32[]{:S(2)}) collective-permute-start(f32[6,8,1024]{2,1,0:T(8,128)S(1)} %shard_map.181.rest_0_.refs_0_), channel_id=1, source_target_pairs={{0,4},{1,5},{2,6},{3,7},{4,0},{5,1},{6,2},{7,3},{8,12},{9,13},{10,... | collective-permute-start | bytes 589832 | tf_op jit(solution)/shard_map/ppermute | solution.py:468
  28.2 3.9 %collective-permute-start.20 = (f32[2,8,2048]{2,1,0:T(8,128)S(1)}, f32[2,8,2048]{2,1,0:T(8,128)S(1)}, u32[]{:S(2)}, u32[]{:S(2)}) collective-permute-start(f32[2,8,2048]{2,1,0:T(8,128)S(1)} %shard_map.183.refs_10_), channel_id=1, source_target_pairs={{0,16},{1,17},{2,18},{3,19},{4,12},{5,13},{6,14},{7,15},{8,24},{9,... | collective-permute-start | bytes 393224 | tf_op jit(solution)/shard_map/ppermute | solution.py:468
  30.5 13.3 %copy-start.3 = (bf16[2,256,256]{2,1,0:T(8,128)(2,1)S(1)}, bf16[2,256,256]{2,1,0:T(8,128)(2,1)}, u32[]{:S(2)}) copy-start(bf16[2,256,256]{2,1,0:T(8,128)(2,1)} %constant.40.clone.refs_8_) | copy-start | bytes 786436
  30.5 13.3 %copy-start.4 = (bf16[2,256,256]{2,1,0:T(8,128)(2,1)S(1)}, bf16[2,256,256]{2,1,0:T(8,128)(2,1)}, u32[]{:S(2)}) copy-start(bf16[2,256,256]{2,1,0:T(8,128)(2,1)} %constant.39.clone.refs_7_) | copy-start | bytes 786436
  30.6 13.3 %copy-start.5 = (f32[512,128]{1,0:T(8,128)S(1)}, f32[512,128]{1,0:T(8,128)}, u32[]{:S(2)}) copy-start(f32[512,128]{1,0:T(8,128)} %constant.34.clone.refs_11_) | copy-start | bytes 786436
  30.6 13.3 %copy-start.8 = (bf16[256,256]{1,0:T(8,128)(2,1)S(1)}, bf16[256,256]{1,0:T(8,128)(2,1)}, u32[]{:S(2)}) copy-start(bf16[256,256]{1,0:T(8,128)(2,1)} %constant.44.clone.refs_10_) | copy-start | bytes 393220
  30.6 13.3 %copy-start.9 = (bf16[256,256]{1,0:T(8,128)(2,1)S(1)}, bf16[256,256]{1,0:T(8,128)(2,1)}, u32[]{:S(2)}) copy-start(bf16[256,256]{1,0:T(8,128)(2,1)} %constant.43.clone.refs_9_) | copy-start | bytes 393220
  30.6 13.3 %copy-start.10 = (f32[3,64,128]{2,1,0:T(8,128)S(1)}, f32[3,64,128]{2,1,0:T(8,128)}, u32[]{:S(2)}) copy-start(f32[3,64,128]{2,1,0:T(8,128)} %constant.36.clone.refs_14_) | copy-start | bytes 294916
  30.6 13.3 %copy-start.14 = (f32[2,8,128]{2,1,0:T(8,128)S(1)}, f32[2,8,128]{2,1,0:T(8,128)}, u32[]{:S(2)}) copy-start(f32[2,8,128]{2,1,0:T(8,128)} %constant.35.clone.refs_12_) | copy-start | bytes 24580
  32.1 5.8 %collective-permute-start.21 = (f32[2,8,2048]{2,1,0:T(8,128)S(1)}, f32[2,8,2048]{2,1,0:T(8,128)S(1)}, u32[]{:S(2)}, u32[]{:S(2)}) collective-permute-start(f32[2,8,2048]{2,1,0:T(8,128)S(1)} %shard_map.187.refs_4_), channel_id=1, source_target_pairs={{0,4},{1,5},{2,6},{3,7},{4,0},{5,1},{6,2},{7,3},{8,12},{9,13},{10,... | collective-permute-start | bytes 393224 | tf_op jit(solution)/shard_map/ppermute | solution.py:468
  35.2 5.9 %collective-permute-start.13 = (f32[64,256]{1,0:T(8,128)S(1)}, f32[64,256]{1,0:T(8,128)S(1)}, u32[]{:S(2)}, u32[]{:S(2)}) collective-permute-start(f32[64,256]{1,0:T(8,128)S(1)} %get-tuple-element.102), channel_id=1, source_target_pairs={{0,1},{1,0},{2,3},{3,2},{4,5},{5,4},{6,7},{7,6},{8,9},{9,8},{10,11... | collective-permute-start | bytes 196616 | tf_op jit(solution)/shard_map/ppermute | solution.py:472
  36.5 5.9 %collective-permute-start.14 = (f32[64,256]{1,0:T(8,128)S(1)}, f32[64,256]{1,0:T(8,128)S(1)}, u32[]{:S(2)}, u32[]{:S(2)}) collective-permute-start(f32[64,256]{1,0:T(8,128)S(1)} %get-tuple-element.103), channel_id=1, source_target_pairs={{0,2},{1,3},{2,0},{3,1},{4,6},{5,7},{6,4},{7,5},{8,10},{9,11},{10,... | collective-permute-start | bytes 196616 | tf_op jit(solution)/shard_map/ppermute | solution.py:472
  36.5 7.3 %collective-permute-start.15 = (f32[64,256]{1,0:T(8,128)S(1)}, f32[64,256]{1,0:T(8,128)S(1)}, u32[]{:S(2)}, u32[]{:S(2)}) collective-permute-start(f32[64,256]{1,0:T(8,128)S(1)} %get-tuple-element.104), channel_id=1, source_target_pairs={{0,3},{1,2},{2,1},{3,0},{4,7},{5,6},{6,5},{7,4},{8,11},{9,10},{10,... | collective-permute-start | bytes 196616 | tf_op jit(solution)/shard_map/ppermute | solution.py:472
  38.8 8.3 %collective-permute-start.22 = (f32[64,256]{1,0:T(8,128)S(1)}, f32[64,256]{1,0:T(8,128)S(1)}, u32[]{:S(2)}, u32[]{:S(2)}) collective-permute-start(f32[64,256]{1,0:T(8,128)S(1)} %get-tuple-element.108), channel_id=1, source_target_pairs={{0,1},{1,0},{2,3},{3,2},{4,5},{5,4},{6,7},{7,6},{8,9},{9,8},{10,11... | collective-permute-start | bytes 196616 | tf_op jit(solution)/shard_map/ppermute | solution.py:472
  41.1 6.1 %collective-permute-start.23 = (f32[64,256]{1,0:T(8,128)S(1)}, f32[64,256]{1,0:T(8,128)S(1)}, u32[]{:S(2)}, u32[]{:S(2)}) collective-permute-start(f32[64,256]{1,0:T(8,128)S(1)} %get-tuple-element.109), channel_id=1, source_target_pairs={{0,2},{1,3},{2,0},{3,1},{4,6},{5,7},{6,4},{7,5},{8,10},{9,11},{10,... | collective-permute-start | bytes 196616 | tf_op jit(solution)/shard_map/ppermute | solution.py:472
  41.1 8.1 %collective-permute-start.24 = (f32[64,256]{1,0:T(8,128)S(1)}, f32[64,256]{1,0:T(8,128)S(1)}, u32[]{:S(2)}, u32[]{:S(2)}) collective-permute-start(f32[64,256]{1,0:T(8,128)S(1)} %get-tuple-element.110), channel_id=1, source_target_pairs={{0,3},{1,2},{2,1},{3,0},{4,7},{5,6},{6,5},{7,4},{8,11},{9,10},{10,... | collective-permute-start | bytes 196616 | tf_op jit(solution)/shard_map/ppermute | solution.py:472
  45.7 6.8 %collective-permute-start.18 = (f32[8,4096]{1,0:T(8,128)S(1)}, f32[8,4096]{1,0:T(8,128)S(1)}, u32[]{:S(2)}, u32[]{:S(2)}) collective-permute-start(f32[8,4096]{1,0:T(8,128)S(1)} %shard_map.185.refs_18_.refs_0_), channel_id=1, source_target_pairs={{0,16},{1,17},{2,18},{3,19},{4,12},{5,13},{6,14},{7,15},{8,24},{9,... | collective-permute-start | bytes 393224 | tf_op jit(solution)/shard_map/ppermute | solution.py:468
  46.9 5.5 %collective-permute-start.17 = (f32[8,4096]{1,0:T(8,128)S(1)}, f32[8,4096]{1,0:T(8,128)S(1)}, u32[]{:S(2)}, u32[]{:S(2)}) collective-permute-start(f32[8,4096]{1,0:T(8,128)S(1)} %shard_map.185.refs_18_.refs_0_), channel_id=1, source_target_pairs={{0,8},{1,9},{2,10},{3,11},{4,20},{5,21},{6,22},{7,23},{8,0},{9,1},... | collective-permute-start | bytes 393224 | tf_op jit(solution)/shard_map/ppermute | solution.py:468
  50.9 6.1 %collective-permute-start.27 = (f32[8,4096]{1,0:T(8,128)S(1)}, f32[8,4096]{1,0:T(8,128)S(1)}, u32[]{:S(2)}, u32[]{:S(2)}) collective-permute-start(f32[8,4096]{1,0:T(8,128)S(1)} %shard_map.189.refs_3_), channel_id=1, source_target_pairs={{0,16},{1,17},{2,18},{3,19},{4,12},{5,13},{6,14},{7,15},{8,24},{9,... | collective-permute-start | bytes 393224 | tf_op jit(solution)/shard_map/ppermute | solution.py:468
  52.2 4.8 %collective-permute-start.26 = (f32[8,4096]{1,0:T(8,128)S(1)}, f32[8,4096]{1,0:T(8,128)S(1)}, u32[]{:S(2)}, u32[]{:S(2)}) collective-permute-start(f32[8,4096]{1,0:T(8,128)S(1)} %shard_map.189.refs_3_), channel_id=1, source_target_pairs={{0,8},{1,9},{2,10},{3,11},{4,20},{5,21},{6,22},{7,23},{8,0},{9,1},... | collective-permute-start | bytes 393224 | tf_op jit(solution)/shard_map/ppermute | solution.py:468
  52.4 10.3 %collective-permute-start.19 = (f32[2,8,4096]{2,1,0:T(8,128)S(1)}, f32[2,8,4096]{2,1,0:T(8,128)S(1)}, u32[]{:S(2)}, u32[]{:S(2)}) collective-permute-start(f32[2,8,4096]{2,1,0:T(8,128)S(1)} %shard_map.186), channel_id=1, source_target_pairs={{0,4},{1,5},{2,6},{3,7},{4,0},{5,1},{6,2},{7,3},{8,12},{9,13},{10,... | collective-permute-start | bytes 786440 | tf_op jit(solution)/shard_map/ppermute | solution.py:468
  57.0 5.8 %collective-permute-start.28 = (f32[2,8,4096]{2,1,0:T(8,128)S(1)}, f32[2,8,4096]{2,1,0:T(8,128)S(1)}, u32[]{:S(2)}, u32[]{:S(2)}) collective-permute-start(f32[2,8,4096]{2,1,0:T(8,128)S(1)} %shard_map.190), channel_id=1, source_target_pairs={{0,4},{1,5},{2,6},{3,7},{4,0},{5,1},{6,2},{7,3},{8,12},{9,13},{10,... | collective-permute-start | bytes 786440 | tf_op jit(solution)/shard_map/ppermute | solution.py:468
  61.0 1.8 %collective-permute-start.16 = (f32[8,4096]{1,0:T(8,128)S(1)}, f32[8,4096]{1,0:T(8,128)S(1)}, u32[]{:S(2)}, u32[]{:S(2)}) collective-permute-start(f32[8,4096]{1,0:T(8,128)S(1)} %shard_map.185.refs_18_.refs_0_), channel_id=1, source_target_pairs={{0,4},{1,5},{2,6},{3,7},{4,0},{5,1},{6,2},{7,3},{8,12},{9,13},{10,... | collective-permute-start | bytes 393224 | tf_op jit(solution)/shard_map/ppermute | solution.py:468
  61.1 1.7 %collective-permute-start.25 = (f32[8,4096]{1,0:T(8,128)S(1)}, f32[8,4096]{1,0:T(8,128)S(1)}, u32[]{:S(2)}, u32[]{:S(2)}) collective-permute-start(f32[8,4096]{1,0:T(8,128)S(1)} %shard_map.189.refs_3_), channel_id=1, source_target_pairs={{0,4},{1,5},{2,6},{3,7},{4,0},{5,1},{6,2},{7,3},{8,12},{9,13},{10,... | collective-permute-start | bytes 393224 | tf_op jit(solution)/shard_map/ppermute | solution.py:468

commit v2 on v0

--- a/solution.py
+++ b/solution.py
@@ -117,24 +117,22 @@
     return o, lax.rem(o, 2), lax.div(o, 2)
 
 
-def fetch(source, out, sem, side, start, number):
-    at = pl.multiple_of(side * (source.shape[2] // 2) + start, LANES)
-    step = out.shape[0] // number
-    return [
-        pltpu.make_async_copy(
-            source.at[pl.ds(n * step, step), :, pl.ds(at, out.shape[2])], out.at[pl.ds(n * step, step)], sem.at[n]
-        )
-        for n in range(number)
+def fetch_kernel(source, out, sem):
+    step = out.shape[0] // sem.shape[0]
+    copies = [
+        pltpu.make_async_copy(source.at[pl.ds(n * step, step)], out.at[pl.ds(n * step, step)], sem.at[n])
+        for n in range(sem.shape[0])
     ]
-
-
-def take_kernel(start, source, *rest):
-    out, sem = rest[-2:]
-    copies = fetch(source, out, sem, 1 - my_core(), start, sem.shape[0])
     for copy in copies:
         copy.start()
     for copy in copies:
         copy.wait()
+
+
+def take_kernel(start, source, *rest):
+    out = rest[-1]
+    at = (1 - my_core()) * (source.shape[2] // 2) + start
+    out[...] = source[:, :, pl.ds(pl.multiple_of(at, LANES), out.shape[2])]
 
 
 class Place:
@@ -159,15 +157,8 @@
         return BLK * self.tiles[tile, 0], BLK * self.tiles[tile, 1]
 
 
-def setup_kernel(per_device, tiles, host, rotation, source, after, *rest):
-    fetched, (high, low, sem) = rest[:-3], rest[-3:]
+def setup_kernel(per_device, tiles, host, rotation, after, high, low):
     core = my_core()
-    copies = []
-    for n, out in enumerate(fetched):
-        side, chunk = (1 - core, n + 1) if n < CHUNKS - 1 else (core, n - CHUNKS + 1)
-        copies += fetch(source, out, sem.at[n], side, chunk * out.shape[2], sem.shape[1])
-    for copy in copies:
-        copy.start()
     at = Place(per_device, tiles, host)
     pair = BLK // 2
     heads = [at.heads(chip) for chip in (at.chip ^ 3, at.chip ^ at.bit_1, at.chip ^ at.bit_2, at.chip)]
@@ -193,8 +184,6 @@
         picked = lax.dot_general(chosen, values, (((1,), (1,)), ((), ())), preferred_element_type=f32).astype(bf16)
         for e in range(2):
             out[:, e * LANES:(e + 1) * LANES] = jnp.where(keep, dot(picked, columns[e]), 0.0).astype(bf16)
-    for copy in copies:
-        copy.wait()
 
 
 def ready_kernel(per_device, n_grid, tiles, host, mask, log_r, *rest):
@@ -237,7 +226,10 @@
             hit = home == at.o * blocks + block
             if n % 4 == 3:
                 hit = hit & at.same
-            match[block * len(parts) + n] = hit.astype(jnp.int32)
+            found = hit.astype(jnp.int32)
+            match[block * len(parts) + n] = found
+            total = blocks * len(parts) + 2 * block + n // 4
+            match[total] = found if n % 4 == 0 else match[total] + found
     for copy in copies:
         copy.wait()
 
@@ -247,8 +239,9 @@
     out[1] = y[...]
 
 
-def rotate_kernel(first, high, low, *rest):
+def rotate_kernel(first, start, high, low, mine, *rest):
     send, keep = rest[-2:]
+    begin = my_core() * (mine.shape[2] // 2) + start
     rows = send.shape[0] * SUB
     part = pl.ds(first, 2 * rows)
     table = (high[part, :], low[part, :])
@@ -257,10 +250,12 @@
     while at < send.shape[2]:
         width = rest[0].shape[2]
         n, inner = at // width, at % width
-        lanes = slice(inner, inner + step)
-        mine, theirs = rest[2 * n], rest[2 * n + 1]
-        depth = mine.shape[0] * SUB
-        cells = jnp.concatenate([mine[:, :, lanes].reshape(depth, step), theirs[:, :, lanes].reshape(depth, step)])
+        theirs = rest[n]
+        depth = theirs.shape[0] * SUB
+        own = pl.ds(pl.multiple_of(begin + at, LANES), step)
+        cells = jnp.concatenate([
+            mine[:, :, own].reshape(depth, step), theirs[:, :, inner:inner + step].reshape(depth, step)
+        ])
         total = dot3(table, split(cells))
         lanes = slice(at, at + step)
         send[:, :, lanes] = total[:rows].reshape(send.shape[0], SUB, step)
@@ -436,7 +431,7 @@
         return [(match[b * stride + side * stride // 2 + n], side * count // 2 + n) for n in range(count // 2)]
 
     def found(b, side):
-        return sum(hit for hit, n in hits(b, side)) > 0
+        return match[blocks * stride + 2 * b + side] > 0
 
     def move(b, side):
         which = core if side == 0 else 1 - core
@@ -489,12 +484,18 @@
     orbitals = pltpu.with_memory_space_constraint(orbitals, pltpu.HBM)
 
     part = jax.ShapeDtypeStruct((per_device, planes, chunk), f32)
-    copies = per_device // 2
-    taken = pl.pallas_call(
-        functools.partial(take_kernel, 0), out_shape=part, in_specs=[HBM], out_specs=VM,
-        scratch_shapes=[DMA((copies,))], name="take", compiler_params=grant(4),
+    loaded = pl.pallas_call(
+        fetch_kernel, out_shape=jax.ShapeDtypeStruct(shape, f32), in_specs=[HBM], out_specs=VM,
+        scratch_shapes=[DMA((4,))], name="fetch", compiler_params=grant(8),
     )(orbitals)
-    theirs = [swap(taken, 1, 1)]
+    theirs, last = [], ()
+    for n in range(CHUNKS):
+        taken = pl.pallas_call(
+            functools.partial(take_kernel, n * chunk), out_shape=part, in_specs=[VM] + [ANY] * len(last), out_specs=VM,
+            compiler_params=grant(8),
+        )(loaded, *last)
+        theirs.append(swap(taken, 1, 1))
+        last = (taken,)
 
     pair = BLK // 2
     firsts = (BLK + 2) * chips
@@ -504,40 +505,25 @@
     c, r = line_np()
     c, r = line_np()
     host = jnp.asarray(host_np(chips).reshape(-1))
-    *fetched, high, low = pl.pallas_call(
-        functools.partial(setup_kernel, per_device),
-        out_shape=[part] * (2 * CHUNKS - 1) + [wide_table] * 2,
-        in_specs=[SM, SM, VM, HBM, ANY], out_specs=[VM] * (2 * CHUNKS + 1),
-        scratch_shapes=[DMA((2 * CHUNKS - 1, copies))], name="setup", compiler_params=grant(8),
-    )(tile_list, host, rotation, orbitals, taken)
-    mine = fetched[CHUNKS - 1:]
-    for n, taken in enumerate(fetched[:CHUNKS - 1], 1):
-        theirs.append(swap(taken, 1, 1))
-
-    def rotate(first, count, fields, *after):
-        part = jax.ShapeDtypeStruct((count, planes, chunk * (len(fields) // 2)), f32)
+    high, low = pl.pallas_call(
+        functools.partial(setup_kernel, per_device), out_shape=[wide_table] * 2,
+        in_specs=[SM, SM, VM, ANY], out_specs=[VM] * 2, name="setup", compiler_params=grant(8),
+    )(tile_list, host, rotation, taken)
+
+    def rotate(first, count, start, fields, *after):
+        part = jax.ShapeDtypeStruct((count, planes, chunk * len(fields)), f32)
         send, keep = pl.pallas_call(
-            functools.partial(rotate_kernel, first * SUB), out_shape=(part, part),
-            in_specs=[VM] * (2 + len(fields)) + [ANY] * len(after),
+            functools.partial(rotate_kernel, first * SUB, start), out_shape=(part, part),
+            in_specs=[VM] * (3 + len(fields)) + [ANY] * len(after),
             out_specs=(VM, VM), compiler_params=grant(8),
-        )(high, low, *fields, *after)
+        )(high, low, loaded, *fields, *after)
         return send, keep, swap(send, 2, 4)
 
     sums, last = [], ()
     for n in range(CHUNKS):
-        sums.append(rotate(0, firsts // 2, [mine[n], theirs[n]], *last))
+        sums.append(rotate(0, firsts // 2, n * chunk, [theirs[n]], *last))
         last = (sums[-1][0],)
-    both = [x for n in range(CHUNKS) for x in (mine[n], theirs[n])]
-    sums.append(rotate(firsts, (pair - 1) * chips, both, *last))
-    empty, powers, flags, match, alone = pl.pallas_call(
-        functools.partial(ready_kernel, per_device, n_grid),
-        out_shape=(pltpu.HBM(shape, f32), jax.ShapeDtypeStruct((6, NY, LANES), f32),
-                   jax.ShapeDtypeStruct((pair * BLK,), f32), jax.ShapeDtypeStruct((blocks * 8,), jnp.int32),
-                   jax.ShapeDtypeStruct((1,), jnp.int32)),
-        in_specs=[SM, SM, VM, VM, ANY], out_specs=(HBM, VM, SM, SM, SM),
-        scratch_shapes=[pltpu.VMEM((pair, planes, width), f32), DMA((per_device // pair,))], name="ready",
-        compiler_params=grant(4),
-    )(tile_list, host, pair_mask, jnp.asarray(np.log(r), f32), sums[-1][0])
+    sums.append(rotate(firsts, (pair - 1) * chips, 0, theirs, *last))
     passing, own, other = [], [], []
 
     def pass_on(n, *after, spec=ANY):
@@ -559,12 +545,22 @@
         other.append(swap(own[-1], 1, 1))
         return own[-1]
 
-    step = pass_on(0, empty, spec=HBM)
-    for n in range(1, CHUNKS):
+    step = pass_on(0, sums[-1][0])
+    empty, powers, flags, match, alone = pl.pallas_call(
+        functools.partial(ready_kernel, per_device, n_grid),
+        out_shape=(pltpu.HBM(shape, f32), jax.ShapeDtypeStruct((6, NY, LANES), f32),
+                   jax.ShapeDtypeStruct((pair * BLK,), f32), jax.ShapeDtypeStruct((blocks * 10,), jnp.int32),
+                   jax.ShapeDtypeStruct((1,), jnp.int32)),
+        in_specs=[SM, SM, VM, VM, ANY], out_specs=(HBM, VM, SM, SM, SM),
+        scratch_shapes=[pltpu.VMEM((pair, planes, width), f32), DMA((per_device // pair,))], name="ready",
+        compiler_params=grant(4),
+    )(tile_list, host, pair_mask, jnp.asarray(np.log(r), f32), step)
+    step = pass_on(1, empty, spec=HBM)
+    for n in range(2, CHUNKS):
         step = pass_on(n, step)
     for n in range(CHUNKS):
         step = finish(n, step)
-    last = (step,)
+    last = (pass_on(CHUNKS, step),)
 
     sine_x, eigen_x = sine_np(planes), eigen_np(planes)
     ends = jnp.asarray(np.einsum("jp,pkl->kjl", sine_x, r[None] ** np.arange(planes - 1, -1, -1)[:, None, None])
@@ -585,7 +581,6 @@
     base_own, base_other = own[:CHUNKS], other[:CHUNKS]
     for u in range(pair):
         if u:
-            pass_on(CHUNKS, *last)
             finish(CHUNKS, *last)
         more_own, more_other = own[CHUNKS:][:u], other[CHUNKS:][:u]
         counts = (CHUNKS, CHUNKS, len(more_own), len(more_other))

time: 62.6 us -> 61.8 us (0.987)
  the two profiles are of different devices: /device:TPU:0 before, /device:TPU:17 now
where the time goes in v2:
time: 61.8 us; the launch traced here: 61.5 us
  starting transfers between devices  35.3 us (57%)
  Pallas kernels  16.7 us (27%)
  waiting for transfers between devices  8.28 us (13%)
  between operations  0.97 us (2%)
    ppermute x19, starting transfers between devices, swap(): return lax.ppermute(x, axes, moves)  29.1 us
    ppermute x6, starting transfers between devices, cross(): return lax.ppermute(x, axes, moves)  6.18 us
    pallas_call x3, Pallas kernels, rotate(): pl.pallas_call(functools.partial(rotate_kernel, first * SUB, start), out_...  4.98 us
    ppermute x19, waiting for transfers between devices, swap(): return lax.ppermute(x, axes, moves)  4.77 us
    ppermute x6, waiting for transfers between devices, cross(): return lax.ppermute(x, axes, moves)  3.51 us
    pallas_call x2, Pallas kernels, tile_device(): pl.pallas_call(functools.partial(backward_kernel, u, (CHUNKS, CHUNKS, len...  3.49 us
    pallas_call x1, Pallas kernels, tile_device(): pl.pallas_call(functools.partial(ready_kernel, per_device, n_grid), out_s...  2.71 us
    pallas_call x2, Pallas kernels, tile_device(): pl.pallas_call(functools.partial(forward_kernel, u, counts + (n_grid - 1,...  2 us
  transfers between devices with their start and end apart: 25, of which 9 were waited for; matrix products, arithmetic and copies ran while one was open for 0% of the time, Pallas kernels for 23%

profile of v2, /device:TPU:17, one launch (start us, length us, event | category | flops | bytes accessed | tf_op | source)
XLA Modules:
  0.0 61.5 jit_solution(17235051706086647773)
XLA Ops:
  0.0 1.5 %fetch.1.source.mine = f32[16,8,4096]{2,1,0:T(8,128)S(1)} custom-call(f32[16,8,4096]{2,1,0:T(8,128)} %source.1), custom_call_target="tpu_custom_call" | custom-call | tf_op jit(solution)/shard_map/fetch/pallas_call | solution.py:487
  1.6 0.1 shard_map.174.rest_0_
  1.6 0.0 copy-start.15
  1.7 0.7 %collective-permute-start.4 = (f32[16,8,1024]{2,1,0:T(8,128)S(1)}, f32[16,8,1024]{2,1,0:T(8,128)}, u32[]{:S(2)}, u32[]{:S(2)}) collective-permute-start(f32[16,8,1024]{2,1,0:T(8,128)S(1)} %shard_map.174.rest_0_), channel_id=1, source_target_pairs={{0,4},{1,5},{2,6},{3,7},{4,0},{5,1},{6,2},{7,3},{8,12},{9,13},{10,... | collective-permute-start | bytes 1572872 | tf_op jit(solution)/shard_map/ppermute | solution.py:477
  2.4 0.1 collective-permute-start.6
  2.5 0.1 copy.24.tiles
  2.6 1.0 %setup.1 = (bf16[256,256]{1,0:T(8,128)(2,1)S(1)}, bf16[256,256]{1,0:T(8,128)(2,1)S(1)}) custom-call(s32[4,2]{1,0:T(4,128)S(1)} %copy.24.tiles, s32[1024]{0:T(1024)S(1)} %copy-done.15, f32[128,128]{1,0:T(8,128)S(1)} %copy-done.11, f32[16,8,1024]{2,1,0:T(8,128)S(1)} %shard_map.175.after), custom_call_target="tpu_custom_call" | custom-call | tf_op jit(solution)/shard_map/setup/pallas_call | solution.py:508
  3.7 0.4 collective-permute-done.4.rest_0_
  4.1 1.5 %shard_map.176 = (f32[12,8,1024]{2,1,0:T(8,128)S(1)}, f32[12,8,1024]{2,1,0:T(8,128)S(1)}) custom-call(bf16[256,256]{1,0:T(8,128)(2,1)S(1)} %get-tuple-element.105.high, bf16[256,256]{1,0:T(8,128)(2,1)S(1)} %get-tuple-element.106.low, f32[16,8,4096]{2,1,0:T(8,128)S(1)} %fetch.1.source.mine, f32[16,8,1024]{2,1,0:T(8,128)} %collective-permute-done.4.rest_0_), custom_call_target="tpu_custom_call" | custom-call | tf_op jit(solution)/shard_map/pallas_call | solution.py:515
  5.6 1.3 %collective-permute-start.5 = (f32[12,8,1024]{2,1,0:T(8,128)S(1)}, f32[12,8,1024]{2,1,0:T(8,128)S(1)}, u32[]{:S(2)}, u32[]{:S(2)}) collective-permute-start(f32[12,8,1024]{2,1,0:T(8,128)S(1)} %get-tuple-element.108.rest_1_), channel_id=1, source_target_pairs={{0,8},{1,9},{2,10},{3,11},{4,20},{5,21},{6,22},{7,23},{8,0},{9,1},... | collective-permute-start | bytes 1179656 | tf_op jit(solution)/shard_map/ppermute | solution.py:477
  6.9 1.5 %shard_map.177 = (f32[12,8,1024]{2,1,0:T(8,128)S(1)}, f32[12,8,1024]{2,1,0:T(8,128)S(1)}) custom-call(bf16[256,256]{1,0:T(8,128)(2,1)S(1)} %get-tuple-element.105.high, bf16[256,256]{1,0:T(8,128)(2,1)S(1)} %get-tuple-element.106.low, f32[16,8,4096]{2,1,0:T(8,128)S(1)} %fetch.1.source.mine, f32[16,8,1024]{2,1,0:T(8,128)} %collective-permute-done.6.rest_0_.rest_1_, ...), custom_call_target="tpu_custom_call" | custom-call | tf_op jit(solution)/shard_map/pallas_call | solution.py:515
  8.5 0.3 collective-permute-start.8
  8.8 1.9 %shard_map.178 = (f32[4,8,2048]{2,1,0:T(8,128)S(1)}, f32[4,8,2048]{2,1,0:T(8,128)S(1)}) custom-call(bf16[256,256]{1,0:T(8,128)(2,1)S(1)} %get-tuple-element.105.high, bf16[256,256]{1,0:T(8,128)(2,1)S(1)} %get-tuple-element.106.low, f32[16,8,4096]{2,1,0:T(8,128)S(1)} %fetch.1.source.mine, f32[16,8,1024]{2,1,0:T(8,128)} %collective-permute-done.4.rest_0_, ...), custom_call_target="tpu_custom_call" | custom-call | tf_op jit(solution)/shard_map/pallas_call | solution.py:515
  10.7 1.9 %collective-permute-done.5.got = f32[12,8,1024]{2,1,0:T(8,128)S(1)} collective-permute-done((f32[12,8,1024]{2,1,0:T(8,128)S(1)}, f32[12,8,1024]{2,1,0:T(8,128)S(1)}, u32[]{:S(2)}, u32[]{:S(2)}) %collective-permute-start.5) | collective-permute-done | bytes 393248 | tf_op jit(solution)/shard_map/ppermute | solution.py:477
  12.6 1.3 %collective-permute-start.7 = (f32[6,8,1024]{2,1,0:T(8,128)S(1)}, f32[6,8,1024]{2,1,0:T(8,128)S(1)}, u32[]{:S(2)}, u32[]{:S(2)}) collective-permute-start(f32[6,8,1024]{2,1,0:T(8,128)S(1)} %shard_map.179.rest_0_), channel_id=1, source_target_pairs={{0,16},{1,17},{2,18},{3,19},{4,12},{5,13},{6,14},{7,15},{8,24},{9,... | collective-permute-start | bytes 589832 | tf_op jit(solution)/shard_map/ppermute | solution.py:477
  13.9 2.7 %ready.1 = (f32[16,8,4096]{2,1,0:T(8,128)}, f32[6,64,128]{2,1,0:T(8,128)S(1)}, f32[8]{0:T(128)S(1)}, s32[40]{0:T(128)S(1)}, s32[1]{0:T(128)}) custom-call(s32[4,2]{1,0:T(4,128)S(1)} %copy.24.tiles, s32[1024]{0:T(1024)S(1)} %copy-done.15, s32[128,128]{1,0:T(8,128)S(1)} %copy-done.12, f32[64,128]{1,0:T(8,128)S(1)} %copy-done.13, ...), custom_call_target="tpu_custom_call" | custom-call | tf_op jit(solution)/shard_map/ready/pallas_call | solution.py:549
  16.6 0.2 collective-permute-done.8.got
  16.9 1.3 %collective-permute-start.9 = (f32[6,8,1024]{2,1,0:T(8,128)S(1)}, f32[6,8,1024]{2,1,0:T(8,128)S(1)}, u32[]{:S(2)}, u32[]{:S(2)}) collective-permute-start(f32[6,8,1024]{2,1,0:T(8,128)S(1)} %shard_map.180.rest_0_), channel_id=1, source_target_pairs={{0,16},{1,17},{2,18},{3,19},{4,12},{5,13},{6,14},{7,15},{8,24},{9,... | collective-permute-start | bytes 589832 | tf_op jit(solution)/shard_map/ppermute | solution.py:477
  18.2 1.2 %collective-permute-start.12 = (f32[4,8,2048]{2,1,0:T(8,128)S(1)}, f32[4,8,2048]{2,1,0:T(8,128)S(1)}, u32[]{:S(2)}, u32[]{:S(2)}) collective-permute-start(f32[4,8,2048]{2,1,0:T(8,128)S(1)} %get-tuple-element.110.rest_0_), channel_id=1, source_target_pairs={{0,8},{1,9},{2,10},{3,11},{4,20},{5,21},{6,22},{7,23},{8,0},{9,1},... | collective-permute-start | bytes 786440 | tf_op jit(solution)/shard_map/ppermute | solution.py:477
  19.4 0.2 collective-permute-done.7.passed
  19.7 3.8 %collective-permute-start.10 = (f32[6,8,1024]{2,1,0:T(8,128)S(1)}, f32[6,8,1024]{2,1,0:T(8,128)S(1)}, u32[]{:S(2)}, u32[]{:S(2)}) collective-permute-start(f32[6,8,1024]{2,1,0:T(8,128)S(1)} %shard_map.181.rest_0_.refs_0_), channel_id=1, source_target_pairs={{0,4},{1,5},{2,6},{3,7},{4,0},{5,1},{6,2},{7,3},{8,12},{9,13},{10,... | collective-permute-start | bytes 589832 | tf_op jit(solution)/shard_map/ppermute | solution.py:477
  23.5 2.8 %collective-permute-start.11 = (f32[6,8,1024]{2,1,0:T(8,128)S(1)}, f32[6,8,1024]{2,1,0:T(8,128)S(1)}, u32[]{:S(2)}, u32[]{:S(2)}) collective-permute-start(f32[6,8,1024]{2,1,0:T(8,128)S(1)} %shard_map.182.rest_0_.refs_1_), channel_id=1, source_target_pairs={{0,4},{1,5},{2,6},{3,7},{4,0},{5,1},{6,2},{7,3},{8,12},{9,13},{10,... | collective-permute-start | bytes 589832 | tf_op jit(solution)/shard_map/ppermute | solution.py:477
  26.3 1.1 %collective-permute-start.20 = (f32[2,8,2048]{2,1,0:T(8,128)S(1)}, f32[2,8,2048]{2,1,0:T(8,128)S(1)}, u32[]{:S(2)}, u32[]{:S(2)}) collective-permute-start(f32[2,8,2048]{2,1,0:T(8,128)S(1)} %shard_map.183.refs_10_), channel_id=1, source_target_pairs={{0,16},{1,17},{2,18},{3,19},{4,12},{5,13},{6,14},{7,15},{8,24},{9,... | collective-permute-start | bytes 393224 | tf_op jit(solution)/shard_map/ppermute | solution.py:477
  27.5 1.0 %shard_map.184 = (f32[64,256]{1,0:T(8,128)S(1)}, f32[64,256]{1,0:T(8,128)S(1)}, f32[64,256]{1,0:T(8,128)S(1)}, f32[512,256]{1,0:T(8,128)S(1)}, f32[64,256]{1,0:T(8,128)S(1)}, /*index=5*/f32[64,256]{1,0:T(8,128)S(1)}) custom-call(f32[6,8,1024]{2,1,0:T(8,128)S(1)} %shard_map.181.rest_0_.refs_0_, f32[6,8,1024]{2,1,0:T(8,128)S(1)} %shard_map.182.rest_0_.refs_1_, ...), custom_call_target="tpu_custom_call" | custom-call | tf_op jit(solution)/shard_map/pallas_call | solution.py:588
  28.6 1.6 %collective-permute-done.20.passed = f32[2,8,2048]{2,1,0:T(8,128)S(1)} collective-permute-done((f32[2,8,2048]{2,1,0:T(8,128)S(1)}, f32[2,8,2048]{2,1,0:T(8,128)S(1)}, u32[]{:S(2)}, u32[]{:S(2)}) %collective-permute-start.20) | collective-permute-done | bytes 131104 | tf_op jit(solution)/shard_map/ppermute | solution.py:477
  30.2 3.2 %collective-permute-start.21 = (f32[2,8,2048]{2,1,0:T(8,128)S(1)}, f32[2,8,2048]{2,1,0:T(8,128)S(1)}, u32[]{:S(2)}, u32[]{:S(2)}) collective-permute-start(f32[2,8,2048]{2,1,0:T(8,128)S(1)} %shard_map.187.refs_4_), channel_id=1, source_target_pairs={{0,4},{1,5},{2,6},{3,7},{4,0},{5,1},{6,2},{7,3},{8,12},{9,13},{10,... | collective-permute-start | bytes 393224 | tf_op jit(solution)/shard_map/ppermute | solution.py:477
  33.4 1.3 %collective-permute-start.13 = (f32[64,256]{1,0:T(8,128)S(1)}, f32[64,256]{1,0:T(8,128)S(1)}, u32[]{:S(2)}, u32[]{:S(2)}) collective-permute-start(f32[64,256]{1,0:T(8,128)S(1)} %get-tuple-element.118), channel_id=1, source_target_pairs={{0,1},{1,0},{2,3},{3,2},{4,5},{5,4},{6,7},{7,6},{8,9},{9,8},{10,11... | collective-permute-start | bytes 196616 | tf_op jit(solution)/shard_map/ppermute | solution.py:481
  34.7 0.0 collective-permute-start.14
  34.8 1.3 %collective-permute-start.15 = (f32[64,256]{1,0:T(8,128)S(1)}, f32[64,256]{1,0:T(8,128)S(1)}, u32[]{:S(2)}, u32[]{:S(2)}) collective-permute-start(f32[64,256]{1,0:T(8,128)S(1)} %get-tuple-element.120), channel_id=1, source_target_pairs={{0,3},{1,2},{2,1},{3,0},{4,7},{5,6},{6,5},{7,4},{8,11},{9,10},{10,... | collective-permute-start | bytes 196616 | tf_op jit(solution)/shard_map/ppermute | solution.py:481
  36.1 1.0 %shard_map.188 = (f32[64,256]{1,0:T(8,128)S(1)}, f32[64,256]{1,0:T(8,128)S(1)}, f32[64,256]{1,0:T(8,128)S(1)}, f32[512,256]{1,0:T(8,128)S(1)}, f32[64,256]{1,0:T(8,128)S(1)}, /*index=5*/f32[64,256]{1,0:T(8,128)S(1)}) custom-call(f32[6,8,1024]{2,1,0:T(8,128)S(1)} %shard_map.181.rest_0_.refs_0_, f32[6,8,1024]{2,1,0:T(8,128)S(1)} %shard_map.182.rest_0_.refs_1_, ...), custom_call_target="tpu_custom_call" | custom-call | tf_op jit(solution)/shard_map/pallas_call | solution.py:588
  37.1 2.3 %collective-permute-start.22 = (f32[64,256]{1,0:T(8,128)S(1)}, f32[64,256]{1,0:T(8,128)S(1)}, u32[]{:S(2)}, u32[]{:S(2)}) collective-permute-start(f32[64,256]{1,0:T(8,128)S(1)} %get-tuple-element.124), channel_id=1, source_target_pairs={{0,1},{1,0},{2,3},{3,2},{4,5},{5,4},{6,7},{7,6},{8,9},{9,8},{10,11... | collective-permute-start | bytes 196616 | tf_op jit(solution)/shard_map/ppermute | solution.py:481
  39.3 1.3 %collective-permute-start.24 = (f32[64,256]{1,0:T(8,128)S(1)}, f32[64,256]{1,0:T(8,128)S(1)}, u32[]{:S(2)}, u32[]{:S(2)}) collective-permute-start(f32[64,256]{1,0:T(8,128)S(1)} %get-tuple-element.126), channel_id=1, source_target_pairs={{0,3},{1,2},{2,1},{3,0},{4,7},{5,6},{6,5},{7,4},{8,11},{9,10},{10,... | collective-permute-start | bytes 196616 | tf_op jit(solution)/shard_map/ppermute | solution.py:481
  40.6 1.5 %collective-permute-done.15.refs_6_ = f32[64,256]{1,0:T(8,128)S(1)} collective-permute-done((f32[64,256]{1,0:T(8,128)S(1)}, f32[64,256]{1,0:T(8,128)S(1)}, u32[]{:S(2)}, u32[]{:S(2)}) %collective-permute-start.15) | collective-permute-done | bytes 65568 | tf_op jit(solution)/shard_map/ppermute | solution.py:481
  42.1 1.8 %shard_map.185.refs_18_ = f32[8,4096]{1,0:T(8,128)S(1)} custom-call(f32[8]{0:T(128)S(1)} %get-tuple-element.113.flags, f32[6,8,1024]{2,1,0:T(8,128)S(1)} %shard_map.181.rest_0_.refs_0_, f32[6,8,1024]{2,1,0:T(8,128)S(1)} %shard_map.182.rest_0_.refs_1_, f32[6,8,1024]{2,1,0:T(8,128)S(1)} %collective-permute-done.10.refs_2_, ...), custom_call_target="tpu_custom_call" | custom-call | tf_op jit(solution)/shard_map/pallas_call | solution.py:606
  43.9 1.3 %collective-permute-start.17 = (f32[8,4096]{1,0:T(8,128)S(1)}, f32[8,4096]{1,0:T(8,128)S(1)}, u32[]{:S(2)}, u32[]{:S(2)}) collective-permute-start(f32[8,4096]{1,0:T(8,128)S(1)} %shard_map.185.refs_18_), channel_id=1, source_target_pairs={{0,16},{1,17},{2,18},{3,19},{4,12},{5,13},{6,14},{7,15},{8,24},{9,... | collective-permute-start | bytes 393224 | tf_op jit(solution)/shard_map/ppermute | solution.py:477
  45.2 0.2 collective-permute-start.16
  45.4 2.0 %collective-permute-done.24.refs_6_ = f32[64,256]{1,0:T(8,128)S(1)} collective-permute-done((f32[64,256]{1,0:T(8,128)S(1)}, f32[64,256]{1,0:T(8,128)S(1)}, u32[]{:S(2)}, u32[]{:S(2)}) %collective-permute-start.24) | collective-permute-done | bytes 65568 | tf_op jit(solution)/shard_map/ppermute | solution.py:481
  47.4 1.7 %shard_map.189 = f32[8,4096]{1,0:T(8,128)S(1)} custom-call(f32[8]{0:T(128)S(1)} %get-tuple-element.113.flags, f32[6,8,1024]{2,1,0:T(8,128)S(1)} %shard_map.181.rest_0_.refs_0_, f32[6,8,1024]{2,1,0:T(8,128)S(1)} %shard_map.182.rest_0_.refs_1_, f32[6,8,1024]{2,1,0:T(8,128)S(1)} %collective-permute-done.10.refs_2_, ...), custom_call_target="tpu_custom_call" | custom-call | tf_op jit(solution)/shard_map/pallas_call | solution.py:606
  49.2 1.3 %collective-permute-start.26 = (f32[8,4096]{1,0:T(8,128)S(1)}, f32[8,4096]{1,0:T(8,128)S(1)}, u32[]{:S(2)}, u32[]{:S(2)}) collective-permute-start(f32[8,4096]{1,0:T(8,128)S(1)} %shard_map.189), channel_id=1, source_target_pairs={{0,16},{1,17},{2,18},{3,19},{4,12},{5,13},{6,14},{7,15},{8,24},{9,... | collective-permute-start | bytes 393224 | tf_op jit(solution)/shard_map/ppermute | solution.py:477
  50.4 0.2 collective-permute-start.25
  50.7 4.5 %collective-permute-start.19 = (f32[2,8,4096]{2,1,0:T(8,128)S(1)}, f32[2,8,4096]{2,1,0:T(8,128)S(1)}, u32[]{:S(2)}, u32[]{:S(2)}) collective-permute-start(f32[2,8,4096]{2,1,0:T(8,128)S(1)} %shard_map.186), channel_id=1, source_target_pairs={{0,4},{1,5},{2,6},{3,7},{4,0},{5,1},{6,2},{7,3},{8,12},{9,13},{10,... | collective-permute-start | bytes 786440 | tf_op jit(solution)/shard_map/ppermute | solution.py:477
  55.3 4.0 %collective-permute-start.28 = (f32[2,8,4096]{2,1,0:T(8,128)S(1)}, f32[2,8,4096]{2,1,0:T(8,128)S(1)}, u32[]{:S(2)}, u32[]{:S(2)}) collective-permute-start(f32[2,8,4096]{2,1,0:T(8,128)S(1)} %shard_map.190), channel_id=1, source_target_pairs={{0,4},{1,5},{2,6},{3,7},{4,0},{5,1},{6,2},{7,3},{8,12},{9,13},{10,... | collective-permute-start | bytes 786440 | tf_op jit(solution)/shard_map/ppermute | solution.py:477
  59.2 0.1 collective-permute-start.18
  59.3 0.4 collective-permute-start.27
  60.4 0.2 collective-permute-done.18
  60.6 0.2 collective-permute-done.27
  60.8 0.7 %conditional.1 = (f32[16,8,4096]{2,1,0:T(8,128)}) conditional(s32[]{:T(128)} %bitcast, (s32[40]{0:T(128)S(1)}, f32[8,4096]{1,0:T(8,128)S(1)}, f32[8,4096]{1,0:T(8,128)S(1)}, f32[8,4096]{1,0:T(8,128)S(1)}, f32[8,4096]{1,0:T(8,128)S(1)}, /*index=5*/f32[2,8,4096]{2,1,0:T(8,128)S(1)}, f32[8,4096]{1,0:T(8,128)S(1)}, f32[8,4096]{1,0:T(8,128)S(1)}, ...), branch_computations={%region_0.0_spmd, %region_1.0_spmd} | conditional | bytes 2097320 | solution.py:648
  60.8 0.7 %place.2 = f32[16,8,4096]{2,1,0:T(8,128)} custom-call(s32[40]{0:T(128)S(1)} %get-tuple-element.56.match, f32[8,4096]{1,0:T(8,128)S(1)} %get-tuple-element.57.refs_0_, f32[8,4096]{1,0:T(8,128)S(1)} %get-tuple-element.58.refs_1_, f32[8,4096]{1,0:T(8,128)S(1)} %get-tuple-element.59.refs_2_, ...), custom_call_target="tpu_custom_call", output_to_operand_aliasing={{}: (11, {})} | custom-call | tf_op jit(solution)/shard_map/cond/branch_0_fun/place/pallas_call | solution.py:630
  (59 shorter events, 0.4 us)
Async XLA Ops:
  1.6 0.9 %copy-start.16 = (s32[4,2]{0,1:T(2,128)S(1)}, s32[4,2]{0,1:T(2,128)}, u32[]{:S(2)}) copy-start(s32[4,2]{0,1:T(2,128)} %param.22) | copy-start | bytes 100
  1.6 1.0 %copy-start.11 = (f32[128,128]{1,0:T(8,128)S(1)}, f32[128,128]{1,0:T(8,128)}, u32[]{:S(2)}) copy-start(f32[128,128]{1,0:T(8,128)} %rotation.1) | copy-start | bytes 196612
  1.6 1.0 %copy-start.15 = (s32[1024]{0:T(1024)S(1)}, s32[1024]{0:T(1024)}, u32[]{:S(2)}) copy-start(s32[1024]{0:T(1024)} %constant.31.clone.host) | copy-start | bytes 12292
  1.7 2.4 %collective-permute-start.4 = (f32[16,8,1024]{2,1,0:T(8,128)S(1)}, f32[16,8,1024]{2,1,0:T(8,128)}, u32[]{:S(2)}, u32[]{:S(2)}) collective-permute-start(f32[16,8,1024]{2,1,0:T(8,128)S(1)} %shard_map.174.rest_0_), channel_id=1, source_target_pairs={{0,4},{1,5},{2,6},{3,7},{4,0},{5,1},{6,2},{7,3},{8,12},{9,13},{10,... | collective-permute-start | bytes 1572872 | tf_op jit(solution)/shard_map/ppermute | solution.py:477
  2.4 4.5 %collective-permute-start.6 = (f32[16,8,1024]{2,1,0:T(8,128)S(1)}, f32[16,8,1024]{2,1,0:T(8,128)}, u32[]{:S(2)}, u32[]{:S(2)}) collective-permute-start(f32[16,8,1024]{2,1,0:T(8,128)S(1)} %shard_map.175.after), channel_id=1, source_target_pairs={{0,4},{1,5},{2,6},{3,7},{4,0},{5,1},{6,2},{7,3},{8,12},{9,13},{10,... | collective-permute-start | bytes 1572872 | tf_op jit(solution)/shard_map/ppermute | solution.py:477
  5.6 7.0 %collective-permute-start.5 = (f32[12,8,1024]{2,1,0:T(8,128)S(1)}, f32[12,8,1024]{2,1,0:T(8,128)S(1)}, u32[]{:S(2)}, u32[]{:S(2)}) collective-permute-start(f32[12,8,1024]{2,1,0:T(8,128)S(1)} %get-tuple-element.108.rest_1_), channel_id=1, source_target_pairs={{0,8},{1,9},{2,10},{3,11},{4,20},{5,21},{6,22},{7,23},{8,0},{9,1},... | collective-permute-start | bytes 1179656 | tf_op jit(solution)/shard_map/ppermute | solution.py:477
  8.5 5.4 %copy-start.12 = (s32[128,128]{1,0:T(8,128)S(1)}, s32[128,128]{1,0:T(8,128)}, u32[]{:S(2)}) copy-start(s32[128,128]{1,0:T(8,128)} %mask.1) | copy-start | bytes 196612
  8.5 5.4 %copy-start.13 = (f32[64,128]{1,0:T(8,128)S(1)}, f32[64,128]{1,0:T(8,128)}, u32[]{:S(2)}) copy-start(f32[64,128]{1,0:T(8,128)} %constant.32.clone.log_r) | copy-start | bytes 98308
  8.5 8.3 %collective-permute-start.8 = (f32[12,8,1024]{2,1,0:T(8,128)S(1)}, f32[12,8,1024]{2,1,0:T(8,128)S(1)}, u32[]{:S(2)}, u32[]{:S(2)}) collective-permute-start(f32[12,8,1024]{2,1,0:T(8,128)S(1)} %get-tuple-element.109.rest_2_), channel_id=1, source_target_pairs={{0,8},{1,9},{2,10},{3,11},{4,20},{5,21},{6,22},{7,23},{8,0},{9,1},... | collective-permute-start | bytes 1179656 | tf_op jit(solution)/shard_map/ppermute | solution.py:477
  12.6 7.0 %collective-permute-start.7 = (f32[6,8,1024]{2,1,0:T(8,128)S(1)}, f32[6,8,1024]{2,1,0:T(8,128)S(1)}, u32[]{:S(2)}, u32[]{:S(2)}) collective-permute-start(f32[6,8,1024]{2,1,0:T(8,128)S(1)} %shard_map.179.rest_0_), channel_id=1, source_target_pairs={{0,16},{1,17},{2,18},{3,19},{4,12},{5,13},{6,14},{7,15},{8,24},{9,... | collective-permute-start | bytes 589832 | tf_op jit(solution)/shard_map/ppermute | solution.py:477
  16.8 10.6 %copy-start = (bf16[2,256,256]{2,1,0:T(8,128)(2,1)S(1)}, bf16[2,256,256]{2,1,0:T(8,128)(2,1)}, u32[]{:S(2)}) copy-start(bf16[2,256,256]{2,1,0:T(8,128)(2,1)} %constant.38.clone.refs_5_.refs_7_) | copy-start | bytes 786436
  16.9 10.6 %copy-start.1 = (bf16[2,256,256]{2,1,0:T(8,128)(2,1)S(1)}, bf16[2,256,256]{2,1,0:T(8,128)(2,1)}, u32[]{:S(2)}) copy-start(bf16[2,256,256]{2,1,0:T(8,128)(2,1)} %constant.37.clone.refs_4_.refs_6_) | copy-start | bytes 786436
  16.9 10.6 %copy-start.2 = (f32[512,128]{1,0:T(8,128)S(1)}, f32[512,128]{1,0:T(8,128)}, u32[]{:S(2)}) copy-start(f32[512,128]{1,0:T(8,128)} %constant.33.clone.refs_8_.refs_10_) | copy-start | bytes 786436
  16.9 10.6 %copy-start.6 = (bf16[256,256]{1,0:T(8,128)(2,1)S(1)}, bf16[256,256]{1,0:T(8,128)(2,1)}, u32[]{:S(2)}) copy-start(bf16[256,256]{1,0:T(8,128)(2,1)} %constant.42.clone.refs_7_.refs_9_) | copy-start | bytes 393220
  16.9 10.6 %copy-start.7 = (bf16[256,256]{1,0:T(8,128)(2,1)S(1)}, bf16[256,256]{1,0:T(8,128)(2,1)}, u32[]{:S(2)}) copy-start(bf16[256,256]{1,0:T(8,128)(2,1)} %constant.41.clone.refs_6_.refs_8_) | copy-start | bytes 393220
  16.9 6.6 %collective-permute-start.9 = (f32[6,8,1024]{2,1,0:T(8,128)S(1)}, f32[6,8,1024]{2,1,0:T(8,128)S(1)}, u32[]{:S(2)}, u32[]{:S(2)}) collective-permute-start(f32[6,8,1024]{2,1,0:T(8,128)S(1)} %shard_map.180.rest_0_), channel_id=1, source_target_pairs={{0,16},{1,17},{2,18},{3,19},{4,12},{5,13},{6,14},{7,15},{8,24},{9,... | collective-permute-start | bytes 589832 | tf_op jit(solution)/shard_map/ppermute | solution.py:477
  18.2 8.1 %collective-permute-start.12 = (f32[4,8,2048]{2,1,0:T(8,128)S(1)}, f32[4,8,2048]{2,1,0:T(8,128)S(1)}, u32[]{:S(2)}, u32[]{:S(2)}) collective-permute-start(f32[4,8,2048]{2,1,0:T(8,128)S(1)} %get-tuple-element.110.rest_0_), channel_id=1, source_target_pairs={{0,8},{1,9},{2,10},{3,11},{4,20},{5,21},{6,22},{7,23},{8,0},{9,1},... | collective-permute-start | bytes 786440 | tf_op jit(solution)/shard_map/ppermute | solution.py:477
  19.7 7.8 %collective-permute-start.10 = (f32[6,8,1024]{2,1,0:T(8,128)S(1)}, f32[6,8,1024]{2,1,0:T(8,128)S(1)}, u32[]{:S(2)}, u32[]{:S(2)}) collective-permute-start(f32[6,8,1024]{2,1,0:T(8,128)S(1)} %shard_map.181.rest_0_.refs_0_), channel_id=1, source_target_pairs={{0,4},{1,5},{2,6},{3,7},{4,0},{5,1},{6,2},{7,3},{8,12},{9,13},{10,... | collective-permute-start | bytes 589832 | tf_op jit(solution)/shard_map/ppermute | solution.py:477
  23.5 3.9 %collective-permute-start.11 = (f32[6,8,1024]{2,1,0:T(8,128)S(1)}, f32[6,8,1024]{2,1,0:T(8,128)S(1)}, u32[]{:S(2)}, u32[]{:S(2)}) collective-permute-start(f32[6,8,1024]{2,1,0:T(8,128)S(1)} %shard_map.182.rest_0_.refs_1_), channel_id=1, source_target_pairs={{0,4},{1,5},{2,6},{3,7},{4,0},{5,1},{6,2},{7,3},{8,12},{9,13},{10,... | collective-permute-start | bytes 589832 | tf_op jit(solution)/shard_map/ppermute | solution.py:477
  26.3 3.9 %collective-permute-start.20 = (f32[2,8,2048]{2,1,0:T(8,128)S(1)}, f32[2,8,2048]{2,1,0:T(8,128)S(1)}, u32[]{:S(2)}, u32[]{:S(2)}) collective-permute-start(f32[2,8,2048]{2,1,0:T(8,128)S(1)} %shard_map.183.refs_10_), channel_id=1, source_target_pairs={{0,16},{1,17},{2,18},{3,19},{4,12},{5,13},{6,14},{7,15},{8,24},{9,... | collective-permute-start | bytes 393224 | tf_op jit(solution)/shard_map/ppermute | solution.py:477
  28.5 13.6 %copy-start.3 = (bf16[2,256,256]{2,1,0:T(8,128)(2,1)S(1)}, bf16[2,256,256]{2,1,0:T(8,128)(2,1)}, u32[]{:S(2)}) copy-start(bf16[2,256,256]{2,1,0:T(8,128)(2,1)} %constant.40.clone.refs_8_) | copy-start | bytes 786436
  28.5 13.6 %copy-start.4 = (bf16[2,256,256]{2,1,0:T(8,128)(2,1)S(1)}, bf16[2,256,256]{2,1,0:T(8,128)(2,1)}, u32[]{:S(2)}) copy-start(bf16[2,256,256]{2,1,0:T(8,128)(2,1)} %constant.39.clone.refs_7_) | copy-start | bytes 786436
  28.5 13.6 %copy-start.5 = (f32[512,128]{1,0:T(8,128)S(1)}, f32[512,128]{1,0:T(8,128)}, u32[]{:S(2)}) copy-start(f32[512,128]{1,0:T(8,128)} %constant.34.clone.refs_11_) | copy-start | bytes 786436
  28.5 13.6 %copy-start.8 = (bf16[256,256]{1,0:T(8,128)(2,1)S(1)}, bf16[256,256]{1,0:T(8,128)(2,1)}, u32[]{:S(2)}) copy-start(bf16[256,256]{1,0:T(8,128)(2,1)} %constant.44.clone.refs_10_) | copy-start | bytes 393220
  28.6 13.6 %copy-start.9 = (bf16[256,256]{1,0:T(8,128)(2,1)S(1)}, bf16[256,256]{1,0:T(8,128)(2,1)}, u32[]{:S(2)}) copy-start(bf16[256,256]{1,0:T(8,128)(2,1)} %constant.43.clone.refs_9_) | copy-start | bytes 393220
  28.6 13.6 %copy-start.10 = (f32[3,64,128]{2,1,0:T(8,128)S(1)}, f32[3,64,128]{2,1,0:T(8,128)}, u32[]{:S(2)}) copy-start(f32[3,64,128]{2,1,0:T(8,128)} %constant.36.clone.refs_14_) | copy-start | bytes 294916
  28.6 13.6 %copy-start.14 = (f32[2,8,128]{2,1,0:T(8,128)S(1)}, f32[2,8,128]{2,1,0:T(8,128)}, u32[]{:S(2)}) copy-start(f32[2,8,128]{2,1,0:T(8,128)} %constant.35.clone.refs_12_) | copy-start | bytes 24580
  30.2 5.8 %collective-permute-start.21 = (f32[2,8,2048]{2,1,0:T(8,128)S(1)}, f32[2,8,2048]{2,1,0:T(8,128)S(1)}, u32[]{:S(2)}, u32[]{:S(2)}) collective-permute-start(f32[2,8,2048]{2,1,0:T(8,128)S(1)} %shard_map.187.refs_4_), channel_id=1, source_target_pairs={{0,4},{1,5},{2,6},{3,7},{4,0},{5,1},{6,2},{7,3},{8,12},{9,13},{10,... | collective-permute-start | bytes 393224 | tf_op jit(solution)/shard_map/ppermute | solution.py:477
  33.4 5.9 %collective-permute-start.13 = (f32[64,256]{1,0:T(8,128)S(1)}, f32[64,256]{1,0:T(8,128)S(1)}, u32[]{:S(2)}, u32[]{:S(2)}) collective-permute-start(f32[64,256]{1,0:T(8,128)S(1)} %get-tuple-element.118), channel_id=1, source_target_pairs={{0,1},{1,0},{2,3},{3,2},{4,5},{5,4},{6,7},{7,6},{8,9},{9,8},{10,11... | collective-permute-start | bytes 196616 | tf_op jit(solution)/shard_map/ppermute | solution.py:481
  34.7 5.9 %collective-permute-start.14 = (f32[64,256]{1,0:T(8,128)S(1)}, f32[64,256]{1,0:T(8,128)S(1)}, u32[]{:S(2)}, u32[]{:S(2)}) collective-permute-start(f32[64,256]{1,0:T(8,128)S(1)} %get-tuple-element.119), channel_id=1, source_target_pairs={{0,2},{1,3},{2,0},{3,1},{4,6},{5,7},{6,4},{7,5},{8,10},{9,11},{10,... | collective-permute-start | bytes 196616 | tf_op jit(solution)/shard_map/ppermute | solution.py:481
  34.8 7.3 %collective-permute-start.15 = (f32[64,256]{1,0:T(8,128)S(1)}, f32[64,256]{1,0:T(8,128)S(1)}, u32[]{:S(2)}, u32[]{:S(2)}) collective-permute-start(f32[64,256]{1,0:T(8,128)S(1)} %get-tuple-element.120), channel_id=1, source_target_pairs={{0,3},{1,2},{2,1},{3,0},{4,7},{5,6},{6,5},{7,4},{8,11},{9,10},{10,... | collective-permute-start | bytes 196616 | tf_op jit(solution)/shard_map/ppermute | solution.py:481
  37.1 8.3 %collective-permute-start.22 = (f32[64,256]{1,0:T(8,128)S(1)}, f32[64,256]{1,0:T(8,128)S(1)}, u32[]{:S(2)}, u32[]{:S(2)}) collective-permute-start(f32[64,256]{1,0:T(8,128)S(1)} %get-tuple-element.124), channel_id=1, source_target_pairs={{0,1},{1,0},{2,3},{3,2},{4,5},{5,4},{6,7},{7,6},{8,9},{9,8},{10,11... | collective-permute-start | bytes 196616 | tf_op jit(solution)/shard_map/ppermute | solution.py:481
  39.3 6.1 %collective-permute-start.23 = (f32[64,256]{1,0:T(8,128)S(1)}, f32[64,256]{1,0:T(8,128)S(1)}, u32[]{:S(2)}, u32[]{:S(2)}) collective-permute-start(f32[64,256]{1,0:T(8,128)S(1)} %get-tuple-element.125), channel_id=1, source_target_pairs={{0,2},{1,3},{2,0},{3,1},{4,6},{5,7},{6,4},{7,5},{8,10},{9,11},{10,... | collective-permute-start | bytes 196616 | tf_op jit(solution)/shard_map/ppermute | solution.py:481
  39.3 8.1 %collective-permute-start.24 = (f32[64,256]{1,0:T(8,128)S(1)}, f32[64,256]{1,0:T(8,128)S(1)}, u32[]{:S(2)}, u32[]{:S(2)}) collective-permute-start(f32[64,256]{1,0:T(8,128)S(1)} %get-tuple-element.126), channel_id=1, source_target_pairs={{0,3},{1,2},{2,1},{3,0},{4,7},{5,6},{6,5},{7,4},{8,11},{9,10},{10,... | collective-permute-start | bytes 196616 | tf_op jit(solution)/shard_map/ppermute | solution.py:481
  43.9 6.8 %collective-permute-start.17 = (f32[8,4096]{1,0:T(8,128)S(1)}, f32[8,4096]{1,0:T(8,128)S(1)}, u32[]{:S(2)}, u32[]{:S(2)}) collective-permute-start(f32[8,4096]{1,0:T(8,128)S(1)} %shard_map.185.refs_18_), channel_id=1, source_target_pairs={{0,16},{1,17},{2,18},{3,19},{4,12},{5,13},{6,14},{7,15},{8,24},{9,... | collective-permute-start | bytes 393224 | tf_op jit(solution)/shard_map/ppermute | solution.py:477
  45.2 5.5 %collective-permute-start.16 = (f32[8,4096]{1,0:T(8,128)S(1)}, f32[8,4096]{1,0:T(8,128)S(1)}, u32[]{:S(2)}, u32[]{:S(2)}) collective-permute-start(f32[8,4096]{1,0:T(8,128)S(1)} %shard_map.185.refs_18_), channel_id=1, source_target_pairs={{0,8},{1,9},{2,10},{3,11},{4,20},{5,21},{6,22},{7,23},{8,0},{9,1},... | collective-permute-start | bytes 393224 | tf_op jit(solution)/shard_map/ppermute | solution.py:477
  49.2 6.1 %collective-permute-start.26 = (f32[8,4096]{1,0:T(8,128)S(1)}, f32[8,4096]{1,0:T(8,128)S(1)}, u32[]{:S(2)}, u32[]{:S(2)}) collective-permute-start(f32[8,4096]{1,0:T(8,128)S(1)} %shard_map.189), channel_id=1, source_target_pairs={{0,16},{1,17},{2,18},{3,19},{4,12},{5,13},{6,14},{7,15},{8,24},{9,... | collective-permute-start | bytes 393224 | tf_op jit(solution)/shard_map/ppermute | solution.py:477
  50.4 4.8 %collective-permute-start.25 = (f32[8,4096]{1,0:T(8,128)S(1)}, f32[8,4096]{1,0:T(8,128)S(1)}, u32[]{:S(2)}, u32[]{:S(2)}) collective-permute-start(f32[8,4096]{1,0:T(8,128)S(1)} %shard_map.189), channel_id=1, source_target_pairs={{0,8},{1,9},{2,10},{3,11},{4,20},{5,21},{6,22},{7,23},{8,0},{9,1},... | collective-permute-start | bytes 393224 | tf_op jit(solution)/shard_map/ppermute | solution.py:477
  50.7 10.1 %collective-permute-start.19 = (f32[2,8,4096]{2,1,0:T(8,128)S(1)}, f32[2,8,4096]{2,1,0:T(8,128)S(1)}, u32[]{:S(2)}, u32[]{:S(2)}) collective-permute-start(f32[2,8,4096]{2,1,0:T(8,128)S(1)} %shard_map.186), channel_id=1, source_target_pairs={{0,4},{1,5},{2,6},{3,7},{4,0},{5,1},{6,2},{7,3},{8,12},{9,13},{10,... | collective-permute-start | bytes 786440 | tf_op jit(solution)/shard_map/ppermute | solution.py:477
  55.3 5.5 %collective-permute-start.28 = (f32[2,8,4096]{2,1,0:T(8,128)S(1)}, f32[2,8,4096]{2,1,0:T(8,128)S(1)}, u32[]{:S(2)}, u32[]{:S(2)}) collective-permute-start(f32[2,8,4096]{2,1,0:T(8,128)S(1)} %shard_map.190), channel_id=1, source_target_pairs={{0,4},{1,5},{2,6},{3,7},{4,0},{5,1},{6,2},{7,3},{8,12},{9,13},{10,... | collective-permute-start | bytes 786440 | tf_op jit(solution)/shard_map/ppermute | solution.py:477
  59.2 1.3 %collective-permute-start.18 = (f32[8,4096]{1,0:T(8,128)S(1)}, f32[8,4096]{1,0:T(8,128)S(1)}, u32[]{:S(2)}, u32[]{:S(2)}) collective-permute-start(f32[8,4096]{1,0:T(8,128)S(1)} %shard_map.185.refs_18_), channel_id=1, source_target_pairs={{0,4},{1,5},{2,6},{3,7},{4,0},{5,1},{6,2},{7,3},{8,12},{9,13},{10,... | collective-permute-start | bytes 393224 | tf_op jit(solution)/shard_map/ppermute | solution.py:477
  59.3 1.5 %collective-permute-start.27 = (f32[8,4096]{1,0:T(8,128)S(1)}, f32[8,4096]{1,0:T(8,128)S(1)}, u32[]{:S(2)}, u32[]{:S(2)}) collective-permute-start(f32[8,4096]{1,0:T(8,128)S(1)} %shard_map.189), channel_id=1, source_target_pairs={{0,4},{1,5},{2,6},{3,7},{4,0},{5,1},{6,2},{7,3},{8,12},{9,13},{10,... | collective-permute-start | bytes 393224 | tf_op jit(solution)/shard_map/ppermute | solution.py:477

commit v3 on v2

--- a/solution.py
+++ b/solution.py
@@ -129,10 +129,13 @@
         copy.wait()
 
 
-def take_kernel(start, source, *rest):
-    out = rest[-1]
-    at = (1 - my_core()) * (source.shape[2] // 2) + start
-    out[...] = source[:, :, pl.ds(pl.multiple_of(at, LANES), out.shape[2])]
+def take_kernel(flip, start, source, *rest):
+    out, sem = rest[-2:]
+    core = my_core()
+    at = (1 - core if flip else core) * (source.shape[2] // 2) + start
+    copy = pltpu.make_async_copy(source.at[:, :, pl.ds(pl.multiple_of(at, LANES), out.shape[2])], out, sem)
+    copy.start()
+    copy.wait()
 
 
 class Place:
@@ -239,9 +242,8 @@
     out[1] = y[...]
 
 
-def rotate_kernel(first, start, high, low, mine, *rest):
+def rotate_kernel(first, high, low, *rest):
     send, keep = rest[-2:]
-    begin = my_core() * (mine.shape[2] // 2) + start
     rows = send.shape[0] * SUB
     part = pl.ds(first, 2 * rows)
     table = (high[part, :], low[part, :])
@@ -250,12 +252,10 @@
     while at < send.shape[2]:
         width = rest[0].shape[2]
         n, inner = at // width, at % width
-        theirs = rest[n]
-        depth = theirs.shape[0] * SUB
-        own = pl.ds(pl.multiple_of(begin + at, LANES), step)
-        cells = jnp.concatenate([
-            mine[:, :, own].reshape(depth, step), theirs[:, :, inner:inner + step].reshape(depth, step)
-        ])
+        lanes = slice(inner, inner + step)
+        mine, theirs = rest[2 * n], rest[2 * n + 1]
+        depth = mine.shape[0] * SUB
+        cells = jnp.concatenate([mine[:, :, lanes].reshape(depth, step), theirs[:, :, lanes].reshape(depth, step)])
         total = dot3(table, split(cells))
         lanes = slice(at, at + step)
         send[:, :, lanes] = total[:rows].reshape(send.shape[0], SUB, step)
@@ -488,14 +488,19 @@
         fetch_kernel, out_shape=jax.ShapeDtypeStruct(shape, f32), in_specs=[HBM], out_specs=VM,
         scratch_shapes=[DMA((4,))], name="fetch", compiler_params=grant(8),
     )(orbitals)
+
+    def take(flip, n, *after):
+        return pl.pallas_call(
+            functools.partial(take_kernel, flip, n * chunk), out_shape=part, in_specs=[VM] + [ANY] * len(after),
+            out_specs=VM, scratch_shapes=[DMA], compiler_params=grant(8),
+        )(loaded, *after)
+
     theirs, last = [], ()
     for n in range(CHUNKS):
-        taken = pl.pallas_call(
-            functools.partial(take_kernel, n * chunk), out_shape=part, in_specs=[VM] + [ANY] * len(last), out_specs=VM,
-            compiler_params=grant(8),
-        )(loaded, *last)
+        taken = take(True, n, *last)
         theirs.append(swap(taken, 1, 1))
         last = (taken,)
+    mine = [take(False, n, taken) for n in range(CHUNKS)]
 
     pair = BLK // 2
     firsts = (BLK + 2) * chips
@@ -510,20 +515,21 @@
         in_specs=[SM, SM, VM, ANY], out_specs=[VM] * 2, name="setup", compiler_params=grant(8),
     )(tile_list, host, rotation, taken)
 
-    def rotate(first, count, start, fields, *after):
-        part = jax.ShapeDtypeStruct((count, planes, chunk * len(fields)), f32)
+    def rotate(first, count, fields, *after):
+        part = jax.ShapeDtypeStruct((count, planes, chunk * (len(fields) // 2)), f32)
         send, keep = pl.pallas_call(
-            functools.partial(rotate_kernel, first * SUB, start), out_shape=(part, part),
-            in_specs=[VM] * (3 + len(fields)) + [ANY] * len(after),
+            functools.partial(rotate_kernel, first * SUB), out_shape=(part, part),
+            in_specs=[VM] * (2 + len(fields)) + [ANY] * len(after),
             out_specs=(VM, VM), compiler_params=grant(8),
-        )(high, low, loaded, *fields, *after)
+        )(high, low, *fields, *after)
         return send, keep, swap(send, 2, 4)
 
     sums, last = [], ()
     for n in range(CHUNKS):
-        sums.append(rotate(0, firsts // 2, n * chunk, [theirs[n]], *last))
+        sums.append(rotate(0, firsts // 2, [mine[n], theirs[n]], *last))
         last = (sums[-1][0],)
-    sums.append(rotate(firsts, (pair - 1) * chips, 0, theirs, *last))
+    both = [x for n in range(CHUNKS) for x in (mine[n], theirs[n])]
+    sums.append(rotate(firsts, (pair - 1) * chips, both, *last))
     passing, own, other = [], [], []
 
     def pass_on(n, *after, spec=ANY):

time: 61.8 us -> 62.7 us (1.015)
  Pallas kernels: 16.7 us -> 17.6 us
    pallas_call x5 -> x7, Pallas kernels: 5.06 us -> 5.95 us  [the longest x3 4.96 us: rotate(): pl.pallas_call(functools.partial(rotate_kernel, first * SUB), out_shape=(...]
  transfers between devices with their start and end apart: 25 -> 25, of which waited for: 9 -> 8; matrix products, arithmetic and copies ran while one was open for 0% -> 0% of each run, Pallas kernels for 23% -> 23%
where the time goes in v3:
time: 62.7 us; the launch traced here: 62.4 us
  starting transfers between devices  35.1 us (56%)
  Pallas kernels  17.6 us (28%)
  waiting for transfers between devices  7.97 us (13%)
  between operations  0.97 us (2%)
  local copies, waits for them, and re-layouts  0.78 us (1%)
    ppermute x19, starting transfers between devices, swap(): return lax.ppermute(x, axes, moves)  28.9 us
    ppermute x6, starting transfers between devices, cross(): return lax.ppermute(x, axes, moves)  6.16 us
    pallas_call x3, Pallas kernels, rotate(): pl.pallas_call(functools.partial(rotate_kernel, first * SUB), out_shape=(...  4.96 us
    ppermute x19, waiting for transfers between devices, swap(): return lax.ppermute(x, axes, moves)  4.46 us
    ppermute x6, waiting for transfers between devices, cross(): return lax.ppermute(x, axes, moves)  3.52 us
    pallas_call x2, Pallas kernels, tile_device(): pl.pallas_call(functools.partial(backward_kernel, u, (CHUNKS, CHUNKS, len...  3.49 us
    pallas_call x1, Pallas kernels, tile_device(): pl.pallas_call(functools.partial(ready_kernel, per_device, n_grid), out_s...  2.71 us
    pallas_call x2, Pallas kernels, tile_device(): pl.pallas_call(functools.partial(forward_kernel, u, counts + (n_grid - 1,...  2 us
  transfers between devices with their start and end apart: 25, of which 8 were waited for; matrix products, arithmetic and copies ran while one was open for 0% of the time, Pallas kernels for 23%

profile of v3, /device:TPU:17, one launch (start us, length us, event | category | flops | bytes accessed | tf_op | source)
XLA Modules:
  0.0 62.4 jit_solution(3041953462834526492)
XLA Ops:
  0.0 1.5 %fetch.1.source = f32[16,8,4096]{2,1,0:T(8,128)S(1)} custom-call(f32[16,8,4096]{2,1,0:T(8,128)} %source.1), custom_call_target="tpu_custom_call" | custom-call | tf_op jit(solution)/shard_map/fetch/pallas_call | solution.py:487
  1.6 0.9 %shard_map.174.rest_0_ = f32[16,8,1024]{2,1,0:T(8,128)} custom-call(f32[16,8,4096]{2,1,0:T(8,128)S(1)} %fetch.1.source), custom_call_target="tpu_custom_call" | custom-call | tf_op jit(solution)/shard_map/pallas_call | solution.py:493
  2.4 0.7 %collective-permute-start.4 = (f32[16,8,1024]{2,1,0:T(8,128)}, f32[16,8,1024]{2,1,0:T(8,128)}, u32[]{:S(2)}, u32[]{:S(2)}) collective-permute-start(f32[16,8,1024]{2,1,0:T(8,128)} %shard_map.174.rest_0_), channel_id=1, source_target_pairs={{0,4},{1,5},{2,6},{3,7},{4,0},{5,1},{6,2},{7,3},{8,12},{9,13},{10,... | collective-permute-start | bytes 1572872 | tf_op jit(solution)/shard_map/ppermute | solution.py:477
  3.2 0.1 collective-permute-start.6
  3.4 0.5 copy-done.16
  3.9 0.1 copy.24.tiles
  4.0 0.1 copy-done.11
  4.1 1.0 %setup.1 = (bf16[256,256]{1,0:T(8,128)(2,1)S(1)}, bf16[256,256]{1,0:T(8,128)(2,1)S(1)}) custom-call(s32[4,2]{1,0:T(4,128)S(1)} %copy.24.tiles, s32[1024]{0:T(1024)S(1)} %copy-done.15, f32[128,128]{1,0:T(8,128)S(1)} %copy-done.11, f32[16,8,1024]{2,1,0:T(8,128)S(1)} %shard_map.175.after.rest_0_), custom_call_target="tpu_custom_call" | custom-call | tf_op jit(solution)/shard_map/setup/pallas_call | solution.py:513
  5.1 1.5 %shard_map.177 = (f32[12,8,1024]{2,1,0:T(8,128)S(1)}, f32[12,8,1024]{2,1,0:T(8,128)S(1)}) custom-call(bf16[256,256]{1,0:T(8,128)(2,1)S(1)} %get-tuple-element.105.high, bf16[256,256]{1,0:T(8,128)(2,1)S(1)} %get-tuple-element.106.low, f32[16,8,1024]{2,1,0:T(8,128)S(1)} %shard_map.176.rest_0_, f32[16,8,1024]{2,1,0:T(8,128)} %collective-permute-done.4.rest_1_), custom_call_target="tpu_custom_call" | custom-call | tf_op jit(solution)/shard_map/pallas_call | solution.py:520
  6.6 1.3 %collective-permute-start.5 = (f32[12,8,1024]{2,1,0:T(8,128)S(1)}, f32[12,8,1024]{2,1,0:T(8,128)S(1)}, u32[]{:S(2)}, u32[]{:S(2)}) collective-permute-start(f32[12,8,1024]{2,1,0:T(8,128)S(1)} %get-tuple-element.108.rest_2_), channel_id=1, source_target_pairs={{0,8},{1,9},{2,10},{3,11},{4,20},{5,21},{6,22},{7,23},{8,0},{9,1},... | collective-permute-start | bytes 1179656 | tf_op jit(solution)/shard_map/ppermute | solution.py:477
  8.0 1.5 %shard_map.179 = (f32[12,8,1024]{2,1,0:T(8,128)S(1)}, f32[12,8,1024]{2,1,0:T(8,128)S(1)}) custom-call(bf16[256,256]{1,0:T(8,128)(2,1)S(1)} %get-tuple-element.105.high, bf16[256,256]{1,0:T(8,128)(2,1)S(1)} %get-tuple-element.106.low, f32[16,8,1024]{2,1,0:T(8,128)S(1)} %shard_map.178.rest_0_.rest_2_, f32[16,8,1024]{2,1,0:T(8,128)} %collective-permute-done.6.rest_1_.rest_3_, ...), custom_call_target="tpu_custom_call" | custom-call | tf_op jit(solution)/shard_map/pallas_call | solution.py:520
  9.6 0.3 collective-permute-start.8
  9.9 1.9 %shard_map.180 = (f32[4,8,2048]{2,1,0:T(8,128)S(1)}, f32[4,8,2048]{2,1,0:T(8,128)S(1)}) custom-call(bf16[256,256]{1,0:T(8,128)(2,1)S(1)} %get-tuple-element.105.high, bf16[256,256]{1,0:T(8,128)(2,1)S(1)} %get-tuple-element.106.low, f32[16,8,1024]{2,1,0:T(8,128)S(1)} %shard_map.176.rest_0_, f32[16,8,1024]{2,1,0:T(8,128)} %collective-permute-done.4.rest_1_, ...), custom_call_target="tpu_custom_call" | custom-call | tf_op jit(solution)/shard_map/pallas_call | solution.py:520
  11.8 1.9 %collective-permute-done.5.got = f32[12,8,1024]{2,1,0:T(8,128)S(1)} collective-permute-done((f32[12,8,1024]{2,1,0:T(8,128)S(1)}, f32[12,8,1024]{2,1,0:T(8,128)S(1)}, u32[]{:S(2)}, u32[]{:S(2)}) %collective-permute-start.5) | collective-permute-done | bytes 393248 | tf_op jit(solution)/shard_map/ppermute | solution.py:477
  13.7 1.3 %collective-permute-start.7 = (f32[6,8,1024]{2,1,0:T(8,128)S(1)}, f32[6,8,1024]{2,1,0:T(8,128)S(1)}, u32[]{:S(2)}, u32[]{:S(2)}) collective-permute-start(f32[6,8,1024]{2,1,0:T(8,128)S(1)} %shard_map.181.rest_0_), channel_id=1, source_target_pairs={{0,16},{1,17},{2,18},{3,19},{4,12},{5,13},{6,14},{7,15},{8,24},{9,... | collective-permute-start | bytes 589832 | tf_op jit(solution)/shard_map/ppermute | solution.py:477
  14.9 2.7 %ready.1 = (f32[16,8,4096]{2,1,0:T(8,128)}, f32[6,64,128]{2,1,0:T(8,128)S(1)}, f32[8]{0:T(128)S(1)}, s32[40]{0:T(128)S(1)}, s32[1]{0:T(128)}) custom-call(s32[4,2]{1,0:T(4,128)S(1)} %copy.24.tiles, s32[1024]{0:T(1024)S(1)} %copy-done.15, s32[128,128]{1,0:T(8,128)S(1)} %copy-done.12, f32[64,128]{1,0:T(8,128)S(1)} %copy-done.13, ...), custom_call_target="tpu_custom_call" | custom-call | tf_op jit(solution)/shard_map/ready/pallas_call | solution.py:555
  17.7 0.2 collective-permute-done.8.got
  17.9 1.3 %collective-permute-start.9 = (f32[6,8,1024]{2,1,0:T(8,128)S(1)}, f32[6,8,1024]{2,1,0:T(8,128)S(1)}, u32[]{:S(2)}, u32[]{:S(2)}) collective-permute-start(f32[6,8,1024]{2,1,0:T(8,128)S(1)} %shard_map.182.rest_0_), channel_id=1, source_target_pairs={{0,16},{1,17},{2,18},{3,19},{4,12},{5,13},{6,14},{7,15},{8,24},{9,... | collective-permute-start | bytes 589832 | tf_op jit(solution)/shard_map/ppermute | solution.py:477
  19.2 1.2 %collective-permute-start.12 = (f32[4,8,2048]{2,1,0:T(8,128)S(1)}, f32[4,8,2048]{2,1,0:T(8,128)S(1)}, u32[]{:S(2)}, u32[]{:S(2)}) collective-permute-start(f32[4,8,2048]{2,1,0:T(8,128)S(1)} %get-tuple-element.110.rest_0_), channel_id=1, source_target_pairs={{0,8},{1,9},{2,10},{3,11},{4,20},{5,21},{6,22},{7,23},{8,0},{9,1},... | collective-permute-start | bytes 786440 | tf_op jit(solution)/shard_map/ppermute | solution.py:477
  20.5 0.2 collective-permute-done.7.passed
  20.7 3.7 %collective-permute-start.10 = (f32[6,8,1024]{2,1,0:T(8,128)S(1)}, f32[6,8,1024]{2,1,0:T(8,128)S(1)}, u32[]{:S(2)}, u32[]{:S(2)}) collective-permute-start(f32[6,8,1024]{2,1,0:T(8,128)S(1)} %shard_map.183.rest_0_.refs_0_), channel_id=1, source_target_pairs={{0,4},{1,5},{2,6},{3,7},{4,0},{5,1},{6,2},{7,3},{8,12},{9,13},{10,... | collective-permute-start | bytes 589832 | tf_op jit(solution)/shard_map/ppermute | solution.py:477
  24.4 2.9 %collective-permute-start.11 = (f32[6,8,1024]{2,1,0:T(8,128)S(1)}, f32[6,8,1024]{2,1,0:T(8,128)S(1)}, u32[]{:S(2)}, u32[]{:S(2)}) collective-permute-start(f32[6,8,1024]{2,1,0:T(8,128)S(1)} %shard_map.184.rest_0_.refs_1_), channel_id=1, source_target_pairs={{0,4},{1,5},{2,6},{3,7},{4,0},{5,1},{6,2},{7,3},{8,12},{9,13},{10,... | collective-permute-start | bytes 589832 | tf_op jit(solution)/shard_map/ppermute | solution.py:477
  27.4 1.0 %collective-permute-start.20 = (f32[2,8,2048]{2,1,0:T(8,128)S(1)}, f32[2,8,2048]{2,1,0:T(8,128)S(1)}, u32[]{:S(2)}, u32[]{:S(2)}) collective-permute-start(f32[2,8,2048]{2,1,0:T(8,128)S(1)} %shard_map.185.refs_10_), channel_id=1, source_target_pairs={{0,16},{1,17},{2,18},{3,19},{4,12},{5,13},{6,14},{7,15},{8,24},{9,... | collective-permute-start | bytes 393224 | tf_op jit(solution)/shard_map/ppermute | solution.py:477
  28.4 1.0 %shard_map.186 = (f32[64,256]{1,0:T(8,128)S(1)}, f32[64,256]{1,0:T(8,128)S(1)}, f32[64,256]{1,0:T(8,128)S(1)}, f32[512,256]{1,0:T(8,128)S(1)}, f32[64,256]{1,0:T(8,128)S(1)}, /*index=5*/f32[64,256]{1,0:T(8,128)S(1)}) custom-call(f32[6,8,1024]{2,1,0:T(8,128)S(1)} %shard_map.183.rest_0_.refs_0_, f32[6,8,1024]{2,1,0:T(8,128)S(1)} %shard_map.184.rest_0_.refs_1_, ...), custom_call_target="tpu_custom_call" | custom-call | tf_op jit(solution)/shard_map/pallas_call | solution.py:594
  29.5 1.7 %collective-permute-done.20.passed = f32[2,8,2048]{2,1,0:T(8,128)S(1)} collective-permute-done((f32[2,8,2048]{2,1,0:T(8,128)S(1)}, f32[2,8,2048]{2,1,0:T(8,128)S(1)}, u32[]{:S(2)}, u32[]{:S(2)}) %collective-permute-start.20) | collective-permute-done | bytes 131104 | tf_op jit(solution)/shard_map/ppermute | solution.py:477
  31.3 3.0 %collective-permute-start.21 = (f32[2,8,2048]{2,1,0:T(8,128)S(1)}, f32[2,8,2048]{2,1,0:T(8,128)S(1)}, u32[]{:S(2)}, u32[]{:S(2)}) collective-permute-start(f32[2,8,2048]{2,1,0:T(8,128)S(1)} %shard_map.189.refs_4_), channel_id=1, source_target_pairs={{0,4},{1,5},{2,6},{3,7},{4,0},{5,1},{6,2},{7,3},{8,12},{9,13},{10,... | collective-permute-start | bytes 393224 | tf_op jit(solution)/shard_map/ppermute | solution.py:477
  34.3 1.3 %collective-permute-start.13 = (f32[64,256]{1,0:T(8,128)S(1)}, f32[64,256]{1,0:T(8,128)S(1)}, u32[]{:S(2)}, u32[]{:S(2)}) collective-permute-start(f32[64,256]{1,0:T(8,128)S(1)} %get-tuple-element.118), channel_id=1, source_target_pairs={{0,1},{1,0},{2,3},{3,2},{4,5},{5,4},{6,7},{7,6},{8,9},{9,8},{10,11... | collective-permute-start | bytes 196616 | tf_op jit(solution)/shard_map/ppermute | solution.py:481
  35.6 0.1 collective-permute-start.14
  35.7 1.3 %collective-permute-start.15 = (f32[64,256]{1,0:T(8,128)S(1)}, f32[64,256]{1,0:T(8,128)S(1)}, u32[]{:S(2)}, u32[]{:S(2)}) collective-permute-start(f32[64,256]{1,0:T(8,128)S(1)} %get-tuple-element.120), channel_id=1, source_target_pairs={{0,3},{1,2},{2,1},{3,0},{4,7},{5,6},{6,5},{7,4},{8,11},{9,10},{10,... | collective-permute-start | bytes 196616 | tf_op jit(solution)/shard_map/ppermute | solution.py:481
  37.0 1.0 %shard_map.190 = (f32[64,256]{1,0:T(8,128)S(1)}, f32[64,256]{1,0:T(8,128)S(1)}, f32[64,256]{1,0:T(8,128)S(1)}, f32[512,256]{1,0:T(8,128)S(1)}, f32[64,256]{1,0:T(8,128)S(1)}, /*index=5*/f32[64,256]{1,0:T(8,128)S(1)}) custom-call(f32[6,8,1024]{2,1,0:T(8,128)S(1)} %shard_map.183.rest_0_.refs_0_, f32[6,8,1024]{2,1,0:T(8,128)S(1)} %shard_map.184.rest_0_.refs_1_, ...), custom_call_target="tpu_custom_call" | custom-call | tf_op jit(solution)/shard_map/pallas_call | solution.py:594
  38.0 2.3 %collective-permute-start.22 = (f32[64,256]{1,0:T(8,128)S(1)}, f32[64,256]{1,0:T(8,128)S(1)}, u32[]{:S(2)}, u32[]{:S(2)}) collective-permute-start(f32[64,256]{1,0:T(8,128)S(1)} %get-tuple-element.124), channel_id=1, source_target_pairs={{0,1},{1,0},{2,3},{3,2},{4,5},{5,4},{6,7},{7,6},{8,9},{9,8},{10,11... | collective-permute-start | bytes 196616 | tf_op jit(solution)/shard_map/ppermute | solution.py:481
  40.2 1.3 %collective-permute-start.24 = (f32[64,256]{1,0:T(8,128)S(1)}, f32[64,256]{1,0:T(8,128)S(1)}, u32[]{:S(2)}, u32[]{:S(2)}) collective-permute-start(f32[64,256]{1,0:T(8,128)S(1)} %get-tuple-element.126), channel_id=1, source_target_pairs={{0,3},{1,2},{2,1},{3,0},{4,7},{5,6},{6,5},{7,4},{8,11},{9,10},{10,... | collective-permute-start | bytes 196616 | tf_op jit(solution)/shard_map/ppermute | solution.py:481
  41.5 1.5 %collective-permute-done.15.refs_6_ = f32[64,256]{1,0:T(8,128)S(1)} collective-permute-done((f32[64,256]{1,0:T(8,128)S(1)}, f32[64,256]{1,0:T(8,128)S(1)}, u32[]{:S(2)}, u32[]{:S(2)}) %collective-permute-start.15) | collective-permute-done | bytes 65568 | tf_op jit(solution)/shard_map/ppermute | solution.py:481
  43.1 1.8 %shard_map.187.refs_18_ = f32[8,4096]{1,0:T(8,128)S(1)} custom-call(f32[8]{0:T(128)S(1)} %get-tuple-element.113.flags, f32[6,8,1024]{2,1,0:T(8,128)S(1)} %shard_map.183.rest_0_.refs_0_, f32[6,8,1024]{2,1,0:T(8,128)S(1)} %shard_map.184.rest_0_.refs_1_, f32[6,8,1024]{2,1,0:T(8,128)S(1)} %collective-permute-done.10.refs_2_, ...), custom_call_target="tpu_custom_call" | custom-call | tf_op jit(solution)/shard_map/pallas_call | solution.py:612
  44.8 1.3 %collective-permute-start.17 = (f32[8,4096]{1,0:T(8,128)S(1)}, f32[8,4096]{1,0:T(8,128)S(1)}, u32[]{:S(2)}, u32[]{:S(2)}) collective-permute-start(f32[8,4096]{1,0:T(8,128)S(1)} %shard_map.187.refs_18_), channel_id=1, source_target_pairs={{0,16},{1,17},{2,18},{3,19},{4,12},{5,13},{6,14},{7,15},{8,24},{9,... | collective-permute-start | bytes 393224 | tf_op jit(solution)/shard_map/ppermute | solution.py:477
  46.1 0.2 collective-permute-start.16
  46.3 2.0 %collective-permute-done.24.refs_6_ = f32[64,256]{1,0:T(8,128)S(1)} collective-permute-done((f32[64,256]{1,0:T(8,128)S(1)}, f32[64,256]{1,0:T(8,128)S(1)}, u32[]{:S(2)}, u32[]{:S(2)}) %collective-permute-start.24) | collective-permute-done | bytes 65568 | tf_op jit(solution)/shard_map/ppermute | solution.py:481
  48.3 1.7 %shard_map.191 = f32[8,4096]{1,0:T(8,128)S(1)} custom-call(f32[8]{0:T(128)S(1)} %get-tuple-element.113.flags, f32[6,8,1024]{2,1,0:T(8,128)S(1)} %shard_map.183.rest_0_.refs_0_, f32[6,8,1024]{2,1,0:T(8,128)S(1)} %shard_map.184.rest_0_.refs_1_, f32[6,8,1024]{2,1,0:T(8,128)S(1)} %collective-permute-done.10.refs_2_, ...), custom_call_target="tpu_custom_call" | custom-call | tf_op jit(solution)/shard_map/pallas_call | solution.py:612
  50.1 1.3 %collective-permute-start.26 = (f32[8,4096]{1,0:T(8,128)S(1)}, f32[8,4096]{1,0:T(8,128)S(1)}, u32[]{:S(2)}, u32[]{:S(2)}) collective-permute-start(f32[8,4096]{1,0:T(8,128)S(1)} %shard_map.191), channel_id=1, source_target_pairs={{0,16},{1,17},{2,18},{3,19},{4,12},{5,13},{6,14},{7,15},{8,24},{9,... | collective-permute-start | bytes 393224 | tf_op jit(solution)/shard_map/ppermute | solution.py:477
  51.4 0.2 collective-permute-start.25
  51.6 4.5 %collective-permute-start.19 = (f32[2,8,4096]{2,1,0:T(8,128)S(1)}, f32[2,8,4096]{2,1,0:T(8,128)S(1)}, u32[]{:S(2)}, u32[]{:S(2)}) collective-permute-start(f32[2,8,4096]{2,1,0:T(8,128)S(1)} %shard_map.188), channel_id=1, source_target_pairs={{0,4},{1,5},{2,6},{3,7},{4,0},{5,1},{6,2},{7,3},{8,12},{9,13},{10,... | collective-permute-start | bytes 786440 | tf_op jit(solution)/shard_map/ppermute | solution.py:477
  56.2 4.0 %collective-permute-start.28 = (f32[2,8,4096]{2,1,0:T(8,128)S(1)}, f32[2,8,4096]{2,1,0:T(8,128)S(1)}, u32[]{:S(2)}, u32[]{:S(2)}) collective-permute-start(f32[2,8,4096]{2,1,0:T(8,128)S(1)} %shard_map.192), channel_id=1, source_target_pairs={{0,4},{1,5},{2,6},{3,7},{4,0},{5,1},{6,2},{7,3},{8,12},{9,13},{10,... | collective-permute-start | bytes 786440 | tf_op jit(solution)/shard_map/ppermute | solution.py:477
  60.1 0.1 collective-permute-start.18
  60.2 0.4 collective-permute-start.27
  61.3 0.2 collective-permute-done.18
  61.5 0.2 collective-permute-done.27
  61.7 0.7 %conditional.1 = (f32[16,8,4096]{2,1,0:T(8,128)}) conditional(s32[]{:T(128)} %bitcast, (s32[40]{0:T(128)S(1)}, f32[8,4096]{1,0:T(8,128)S(1)}, f32[8,4096]{1,0:T(8,128)S(1)}, f32[8,4096]{1,0:T(8,128)S(1)}, f32[8,4096]{1,0:T(8,128)S(1)}, /*index=5*/f32[2,8,4096]{2,1,0:T(8,128)S(1)}, f32[8,4096]{1,0:T(8,128)S(1)}, f32[8,4096]{1,0:T(8,128)S(1)}, ...), branch_computations={%region_0.0_spmd, %region_1.0_spmd} | conditional | bytes 2097320 | solution.py:654
  61.7 0.7 %place.2 = f32[16,8,4096]{2,1,0:T(8,128)} custom-call(s32[40]{0:T(128)S(1)} %get-tuple-element.56.match, f32[8,4096]{1,0:T(8,128)S(1)} %get-tuple-element.57.refs_0_, f32[8,4096]{1,0:T(8,128)S(1)} %get-tuple-element.58.refs_1_, f32[8,4096]{1,0:T(8,128)S(1)} %get-tuple-element.59.refs_2_, ...), custom_call_target="tpu_custom_call", output_to_operand_aliasing={{}: (11, {})} | custom-call | tf_op jit(solution)/shard_map/cond/branch_0_fun/place/pallas_call | solution.py:636
  (61 shorter events, 0.5 us)
Async XLA Ops:
  2.4 2.7 %collective-permute-start.4 = (f32[16,8,1024]{2,1,0:T(8,128)}, f32[16,8,1024]{2,1,0:T(8,128)}, u32[]{:S(2)}, u32[]{:S(2)}) collective-permute-start(f32[16,8,1024]{2,1,0:T(8,128)} %shard_map.174.rest_0_), channel_id=1, source_target_pairs={{0,4},{1,5},{2,6},{3,7},{4,0},{5,1},{6,2},{7,3},{8,12},{9,13},{10,... | collective-permute-start | bytes 1572872 | tf_op jit(solution)/shard_map/ppermute | solution.py:477
  3.2 0.7 %copy-start.16 = (s32[4,2]{0,1:T(2,128)S(1)}, s32[4,2]{0,1:T(2,128)}, u32[]{:S(2)}) copy-start(s32[4,2]{0,1:T(2,128)} %param.22) | copy-start | bytes 100
  3.2 0.8 %copy-start.11 = (f32[128,128]{1,0:T(8,128)S(1)}, f32[128,128]{1,0:T(8,128)}, u32[]{:S(2)}) copy-start(f32[128,128]{1,0:T(8,128)} %rotation.1) | copy-start | bytes 196612
  3.2 0.8 %copy-start.15 = (s32[1024]{0:T(1024)S(1)}, s32[1024]{0:T(1024)}, u32[]{:S(2)}) copy-start(s32[1024]{0:T(1024)} %constant.31.clone.host) | copy-start | bytes 12292
  3.2 4.8 %collective-permute-start.6 = (f32[16,8,1024]{2,1,0:T(8,128)S(1)}, f32[16,8,1024]{2,1,0:T(8,128)}, u32[]{:S(2)}, u32[]{:S(2)}) collective-permute-start(f32[16,8,1024]{2,1,0:T(8,128)S(1)} %shard_map.175.after.rest_0_), channel_id=1, source_target_pairs={{0,4},{1,5},{2,6},{3,7},{4,0},{5,1},{6,2},{7,3},{8,12},{9,13},{10,... | collective-permute-start | bytes 1572872 | tf_op jit(solution)/shard_map/ppermute | solution.py:477
  6.6 7.0 %collective-permute-start.5 = (f32[12,8,1024]{2,1,0:T(8,128)S(1)}, f32[12,8,1024]{2,1,0:T(8,128)S(1)}, u32[]{:S(2)}, u32[]{:S(2)}) collective-permute-start(f32[12,8,1024]{2,1,0:T(8,128)S(1)} %get-tuple-element.108.rest_2_), channel_id=1, source_target_pairs={{0,8},{1,9},{2,10},{3,11},{4,20},{5,21},{6,22},{7,23},{8,0},{9,1},... | collective-permute-start | bytes 1179656 | tf_op jit(solution)/shard_map/ppermute | solution.py:477
  9.6 5.4 %copy-start.12 = (s32[128,128]{1,0:T(8,128)S(1)}, s32[128,128]{1,0:T(8,128)}, u32[]{:S(2)}) copy-start(s32[128,128]{1,0:T(8,128)} %mask.1) | copy-start | bytes 196612
  9.6 5.4 %copy-start.13 = (f32[64,128]{1,0:T(8,128)S(1)}, f32[64,128]{1,0:T(8,128)}, u32[]{:S(2)}) copy-start(f32[64,128]{1,0:T(8,128)} %constant.32.clone.log_r) | copy-start | bytes 98308
  9.6 8.3 %collective-permute-start.8 = (f32[12,8,1024]{2,1,0:T(8,128)S(1)}, f32[12,8,1024]{2,1,0:T(8,128)S(1)}, u32[]{:S(2)}, u32[]{:S(2)}) collective-permute-start(f32[12,8,1024]{2,1,0:T(8,128)S(1)} %get-tuple-element.109.rest_4_), channel_id=1, source_target_pairs={{0,8},{1,9},{2,10},{3,11},{4,20},{5,21},{6,22},{7,23},{8,0},{9,1},... | collective-permute-start | bytes 1179656 | tf_op jit(solution)/shard_map/ppermute | solution.py:477
  13.7 7.0 %collective-permute-start.7 = (f32[6,8,1024]{2,1,0:T(8,128)S(1)}, f32[6,8,1024]{2,1,0:T(8,128)S(1)}, u32[]{:S(2)}, u32[]{:S(2)}) collective-permute-start(f32[6,8,1024]{2,1,0:T(8,128)S(1)} %shard_map.181.rest_0_), channel_id=1, source_target_pairs={{0,16},{1,17},{2,18},{3,19},{4,12},{5,13},{6,14},{7,15},{8,24},{9,... | collective-permute-start | bytes 589832 | tf_op jit(solution)/shard_map/ppermute | solution.py:477
  17.9 10.5 %copy-start = (bf16[2,256,256]{2,1,0:T(8,128)(2,1)S(1)}, bf16[2,256,256]{2,1,0:T(8,128)(2,1)}, u32[]{:S(2)}) copy-start(bf16[2,256,256]{2,1,0:T(8,128)(2,1)} %constant.38.clone.refs_5_.refs_7_) | copy-start | bytes 786436
  17.9 10.5 %copy-start.1 = (bf16[2,256,256]{2,1,0:T(8,128)(2,1)S(1)}, bf16[2,256,256]{2,1,0:T(8,128)(2,1)}, u32[]{:S(2)}) copy-start(bf16[2,256,256]{2,1,0:T(8,128)(2,1)} %constant.37.clone.refs_4_.refs_6_) | copy-start | bytes 786436
  17.9 10.5 %copy-start.2 = (f32[512,128]{1,0:T(8,128)S(1)}, f32[512,128]{1,0:T(8,128)}, u32[]{:S(2)}) copy-start(f32[512,128]{1,0:T(8,128)} %constant.33.clone.refs_8_.refs_10_) | copy-start | bytes 786436
  17.9 10.5 %copy-start.6 = (bf16[256,256]{1,0:T(8,128)(2,1)S(1)}, bf16[256,256]{1,0:T(8,128)(2,1)}, u32[]{:S(2)}) copy-start(bf16[256,256]{1,0:T(8,128)(2,1)} %constant.42.clone.refs_7_.refs_9_) | copy-start | bytes 393220
  17.9 10.5 %copy-start.7 = (bf16[256,256]{1,0:T(8,128)(2,1)S(1)}, bf16[256,256]{1,0:T(8,128)(2,1)}, u32[]{:S(2)}) copy-start(bf16[256,256]{1,0:T(8,128)(2,1)} %constant.41.clone.refs_6_.refs_8_) | copy-start | bytes 393220
  17.9 6.5 %collective-permute-start.9 = (f32[6,8,1024]{2,1,0:T(8,128)S(1)}, f32[6,8,1024]{2,1,0:T(8,128)S(1)}, u32[]{:S(2)}, u32[]{:S(2)}) collective-permute-start(f32[6,8,1024]{2,1,0:T(8,128)S(1)} %shard_map.182.rest_0_), channel_id=1, source_target_pairs={{0,16},{1,17},{2,18},{3,19},{4,12},{5,13},{6,14},{7,15},{8,24},{9,... | collective-permute-start | bytes 589832 | tf_op jit(solution)/shard_map/ppermute | solution.py:477
  19.2 8.1 %collective-permute-start.12 = (f32[4,8,2048]{2,1,0:T(8,128)S(1)}, f32[4,8,2048]{2,1,0:T(8,128)S(1)}, u32[]{:S(2)}, u32[]{:S(2)}) collective-permute-start(f32[4,8,2048]{2,1,0:T(8,128)S(1)} %get-tuple-element.110.rest_0_), channel_id=1, source_target_pairs={{0,8},{1,9},{2,10},{3,11},{4,20},{5,21},{6,22},{7,23},{8,0},{9,1},... | collective-permute-start | bytes 786440 | tf_op jit(solution)/shard_map/ppermute | solution.py:477
  20.7 7.7 %collective-permute-start.10 = (f32[6,8,1024]{2,1,0:T(8,128)S(1)}, f32[6,8,1024]{2,1,0:T(8,128)S(1)}, u32[]{:S(2)}, u32[]{:S(2)}) collective-permute-start(f32[6,8,1024]{2,1,0:T(8,128)S(1)} %shard_map.183.rest_0_.refs_0_), channel_id=1, source_target_pairs={{0,4},{1,5},{2,6},{3,7},{4,0},{5,1},{6,2},{7,3},{8,12},{9,13},{10,... | collective-permute-start | bytes 589832 | tf_op jit(solution)/shard_map/ppermute | solution.py:477
  24.4 4.0 %collective-permute-start.11 = (f32[6,8,1024]{2,1,0:T(8,128)S(1)}, f32[6,8,1024]{2,1,0:T(8,128)S(1)}, u32[]{:S(2)}, u32[]{:S(2)}) collective-permute-start(f32[6,8,1024]{2,1,0:T(8,128)S(1)} %shard_map.184.rest_0_.refs_1_), channel_id=1, source_target_pairs={{0,4},{1,5},{2,6},{3,7},{4,0},{5,1},{6,2},{7,3},{8,12},{9,13},{10,... | collective-permute-start | bytes 589832 | tf_op jit(solution)/shard_map/ppermute | solution.py:477
  27.4 3.9 %collective-permute-start.20 = (f32[2,8,2048]{2,1,0:T(8,128)S(1)}, f32[2,8,2048]{2,1,0:T(8,128)S(1)}, u32[]{:S(2)}, u32[]{:S(2)}) collective-permute-start(f32[2,8,2048]{2,1,0:T(8,128)S(1)} %shard_map.185.refs_10_), channel_id=1, source_target_pairs={{0,16},{1,17},{2,18},{3,19},{4,12},{5,13},{6,14},{7,15},{8,24},{9,... | collective-permute-start | bytes 393224 | tf_op jit(solution)/shard_map/ppermute | solution.py:477
  29.4 13.6 %copy-start.3 = (bf16[2,256,256]{2,1,0:T(8,128)(2,1)S(1)}, bf16[2,256,256]{2,1,0:T(8,128)(2,1)}, u32[]{:S(2)}) copy-start(bf16[2,256,256]{2,1,0:T(8,128)(2,1)} %constant.40.clone.refs_8_) | copy-start | bytes 786436
  29.4 13.6 %copy-start.4 = (bf16[2,256,256]{2,1,0:T(8,128)(2,1)S(1)}, bf16[2,256,256]{2,1,0:T(8,128)(2,1)}, u32[]{:S(2)}) copy-start(bf16[2,256,256]{2,1,0:T(8,128)(2,1)} %constant.39.clone.refs_7_) | copy-start | bytes 786436
  29.5 13.6 %copy-start.5 = (f32[512,128]{1,0:T(8,128)S(1)}, f32[512,128]{1,0:T(8,128)}, u32[]{:S(2)}) copy-start(f32[512,128]{1,0:T(8,128)} %constant.34.clone.refs_11_) | copy-start | bytes 786436
  29.5 13.5 %copy-start.8 = (bf16[256,256]{1,0:T(8,128)(2,1)S(1)}, bf16[256,256]{1,0:T(8,128)(2,1)}, u32[]{:S(2)}) copy-start(bf16[256,256]{1,0:T(8,128)(2,1)} %constant.44.clone.refs_10_) | copy-start | bytes 393220
  29.5 13.5 %copy-start.9 = (bf16[256,256]{1,0:T(8,128)(2,1)S(1)}, bf16[256,256]{1,0:T(8,128)(2,1)}, u32[]{:S(2)}) copy-start(bf16[256,256]{1,0:T(8,128)(2,1)} %constant.43.clone.refs_9_) | copy-start | bytes 393220
  29.5 13.5 %copy-start.10 = (f32[3,64,128]{2,1,0:T(8,128)S(1)}, f32[3,64,128]{2,1,0:T(8,128)}, u32[]{:S(2)}) copy-start(f32[3,64,128]{2,1,0:T(8,128)} %constant.36.clone.refs_14_) | copy-start | bytes 294916
  29.5 13.5 %copy-start.14 = (f32[2,8,128]{2,1,0:T(8,128)S(1)}, f32[2,8,128]{2,1,0:T(8,128)}, u32[]{:S(2)}) copy-start(f32[2,8,128]{2,1,0:T(8,128)} %constant.35.clone.refs_12_) | copy-start | bytes 24580
  31.3 5.7 %collective-permute-start.21 = (f32[2,8,2048]{2,1,0:T(8,128)S(1)}, f32[2,8,2048]{2,1,0:T(8,128)S(1)}, u32[]{:S(2)}, u32[]{:S(2)}) collective-permute-start(f32[2,8,2048]{2,1,0:T(8,128)S(1)} %shard_map.189.refs_4_), channel_id=1, source_target_pairs={{0,4},{1,5},{2,6},{3,7},{4,0},{5,1},{6,2},{7,3},{8,12},{9,13},{10,... | collective-permute-start | bytes 393224 | tf_op jit(solution)/shard_map/ppermute | solution.py:477
  34.3 5.9 %collective-permute-start.13 = (f32[64,256]{1,0:T(8,128)S(1)}, f32[64,256]{1,0:T(8,128)S(1)}, u32[]{:S(2)}, u32[]{:S(2)}) collective-permute-start(f32[64,256]{1,0:T(8,128)S(1)} %get-tuple-element.118), channel_id=1, source_target_pairs={{0,1},{1,0},{2,3},{3,2},{4,5},{5,4},{6,7},{7,6},{8,9},{9,8},{10,11... | collective-permute-start | bytes 196616 | tf_op jit(solution)/shard_map/ppermute | solution.py:481
  35.6 5.9 %collective-permute-start.14 = (f32[64,256]{1,0:T(8,128)S(1)}, f32[64,256]{1,0:T(8,128)S(1)}, u32[]{:S(2)}, u32[]{:S(2)}) collective-permute-start(f32[64,256]{1,0:T(8,128)S(1)} %get-tuple-element.119), channel_id=1, source_target_pairs={{0,2},{1,3},{2,0},{3,1},{4,6},{5,7},{6,4},{7,5},{8,10},{9,11},{10,... | collective-permute-start | bytes 196616 | tf_op jit(solution)/shard_map/ppermute | solution.py:481
  35.7 7.3 %collective-permute-start.15 = (f32[64,256]{1,0:T(8,128)S(1)}, f32[64,256]{1,0:T(8,128)S(1)}, u32[]{:S(2)}, u32[]{:S(2)}) collective-permute-start(f32[64,256]{1,0:T(8,128)S(1)} %get-tuple-element.120), channel_id=1, source_target_pairs={{0,3},{1,2},{2,1},{3,0},{4,7},{5,6},{6,5},{7,4},{8,11},{9,10},{10,... | collective-permute-start | bytes 196616 | tf_op jit(solution)/shard_map/ppermute | solution.py:481
  38.0 8.3 %collective-permute-start.22 = (f32[64,256]{1,0:T(8,128)S(1)}, f32[64,256]{1,0:T(8,128)S(1)}, u32[]{:S(2)}, u32[]{:S(2)}) collective-permute-start(f32[64,256]{1,0:T(8,128)S(1)} %get-tuple-element.124), channel_id=1, source_target_pairs={{0,1},{1,0},{2,3},{3,2},{4,5},{5,4},{6,7},{7,6},{8,9},{9,8},{10,11... | collective-permute-start | bytes 196616 | tf_op jit(solution)/shard_map/ppermute | solution.py:481
  40.2 6.1 %collective-permute-start.23 = (f32[64,256]{1,0:T(8,128)S(1)}, f32[64,256]{1,0:T(8,128)S(1)}, u32[]{:S(2)}, u32[]{:S(2)}) collective-permute-start(f32[64,256]{1,0:T(8,128)S(1)} %get-tuple-element.125), channel_id=1, source_target_pairs={{0,2},{1,3},{2,0},{3,1},{4,6},{5,7},{6,4},{7,5},{8,10},{9,11},{10,... | collective-permute-start | bytes 196616 | tf_op jit(solution)/shard_map/ppermute | solution.py:481
  40.2 8.1 %collective-permute-start.24 = (f32[64,256]{1,0:T(8,128)S(1)}, f32[64,256]{1,0:T(8,128)S(1)}, u32[]{:S(2)}, u32[]{:S(2)}) collective-permute-start(f32[64,256]{1,0:T(8,128)S(1)} %get-tuple-element.126), channel_id=1, source_target_pairs={{0,3},{1,2},{2,1},{3,0},{4,7},{5,6},{6,5},{7,4},{8,11},{9,10},{10,... | collective-permute-start | bytes 196616 | tf_op jit(solution)/shard_map/ppermute | solution.py:481
  44.8 6.8 %collective-permute-start.17 = (f32[8,4096]{1,0:T(8,128)S(1)}, f32[8,4096]{1,0:T(8,128)S(1)}, u32[]{:S(2)}, u32[]{:S(2)}) collective-permute-start(f32[8,4096]{1,0:T(8,128)S(1)} %shard_map.187.refs_18_), channel_id=1, source_target_pairs={{0,16},{1,17},{2,18},{3,19},{4,12},{5,13},{6,14},{7,15},{8,24},{9,... | collective-permute-start | bytes 393224 | tf_op jit(solution)/shard_map/ppermute | solution.py:477
  46.1 5.5 %collective-permute-start.16 = (f32[8,4096]{1,0:T(8,128)S(1)}, f32[8,4096]{1,0:T(8,128)S(1)}, u32[]{:S(2)}, u32[]{:S(2)}) collective-permute-start(f32[8,4096]{1,0:T(8,128)S(1)} %shard_map.187.refs_18_), channel_id=1, source_target_pairs={{0,8},{1,9},{2,10},{3,11},{4,20},{5,21},{6,22},{7,23},{8,0},{9,1},... | collective-permute-start | bytes 393224 | tf_op jit(solution)/shard_map/ppermute | solution.py:477
  50.1 6.1 %collective-permute-start.26 = (f32[8,4096]{1,0:T(8,128)S(1)}, f32[8,4096]{1,0:T(8,128)S(1)}, u32[]{:S(2)}, u32[]{:S(2)}) collective-permute-start(f32[8,4096]{1,0:T(8,128)S(1)} %shard_map.191), channel_id=1, source_target_pairs={{0,16},{1,17},{2,18},{3,19},{4,12},{5,13},{6,14},{7,15},{8,24},{9,... | collective-permute-start | bytes 393224 | tf_op jit(solution)/shard_map/ppermute | solution.py:477
  51.4 4.8 %collective-permute-start.25 = (f32[8,4096]{1,0:T(8,128)S(1)}, f32[8,4096]{1,0:T(8,128)S(1)}, u32[]{:S(2)}, u32[]{:S(2)}) collective-permute-start(f32[8,4096]{1,0:T(8,128)S(1)} %shard_map.191), channel_id=1, source_target_pairs={{0,8},{1,9},{2,10},{3,11},{4,20},{5,21},{6,22},{7,23},{8,0},{9,1},... | collective-permute-start | bytes 393224 | tf_op jit(solution)/shard_map/ppermute | solution.py:477
  51.6 10.1 %collective-permute-start.19 = (f32[2,8,4096]{2,1,0:T(8,128)S(1)}, f32[2,8,4096]{2,1,0:T(8,128)S(1)}, u32[]{:S(2)}, u32[]{:S(2)}) collective-permute-start(f32[2,8,4096]{2,1,0:T(8,128)S(1)} %shard_map.188), channel_id=1, source_target_pairs={{0,4},{1,5},{2,6},{3,7},{4,0},{5,1},{6,2},{7,3},{8,12},{9,13},{10,... | collective-permute-start | bytes 786440 | tf_op jit(solution)/shard_map/ppermute | solution.py:477
  56.2 5.5 %collective-permute-start.28 = (f32[2,8,4096]{2,1,0:T(8,128)S(1)}, f32[2,8,4096]{2,1,0:T(8,128)S(1)}, u32[]{:S(2)}, u32[]{:S(2)}) collective-permute-start(f32[2,8,4096]{2,1,0:T(8,128)S(1)} %shard_map.192), channel_id=1, source_target_pairs={{0,4},{1,5},{2,6},{3,7},{4,0},{5,1},{6,2},{7,3},{8,12},{9,13},{10,... | collective-permute-start | bytes 786440 | tf_op jit(solution)/shard_map/ppermute | solution.py:477
  60.1 1.3 %collective-permute-start.18 = (f32[8,4096]{1,0:T(8,128)S(1)}, f32[8,4096]{1,0:T(8,128)S(1)}, u32[]{:S(2)}, u32[]{:S(2)}) collective-permute-start(f32[8,4096]{1,0:T(8,128)S(1)} %shard_map.187.refs_18_), channel_id=1, source_target_pairs={{0,4},{1,5},{2,6},{3,7},{4,0},{5,1},{6,2},{7,3},{8,12},{9,13},{10,... | collective-permute-start | bytes 393224 | tf_op jit(solution)/shard_map/ppermute | solution.py:477
  60.2 1.5 %collective-permute-start.27 = (f32[8,4096]{1,0:T(8,128)S(1)}, f32[8,4096]{1,0:T(8,128)S(1)}, u32[]{:S(2)}, u32[]{:S(2)}) collective-permute-start(f32[8,4096]{1,0:T(8,128)S(1)} %shard_map.191), channel_id=1, source_target_pairs={{0,4},{1,5},{2,6},{3,7},{4,0},{5,1},{6,2},{7,3},{8,12},{9,13},{10,... | collective-permute-start | bytes 393224 | tf_op jit(solution)/shard_map/ppermute | solution.py:477

commit v4 on v3

--- a/solution.py
+++ b/solution.py
@@ -117,25 +117,28 @@
     return o, lax.rem(o, 2), lax.div(o, 2)
 
 
-def fetch_kernel(source, out, sem):
-    step = out.shape[0] // sem.shape[0]
+def fetch_kernel(source, *rest):
+    outs, (whole, sem) = rest[:-2], rest[-2:]
+    step = whole.shape[0] // len(outs)
     copies = [
-        pltpu.make_async_copy(source.at[pl.ds(n * step, step)], out.at[pl.ds(n * step, step)], sem.at[n])
-        for n in range(sem.shape[0])
+        pltpu.make_async_copy(source.at[pl.ds(n * step, step)], whole.at[pl.ds(n * step, step)], sem.at[n])
+        for n in range(len(outs))
     ]
     for copy in copies:
         copy.start()
     for copy in copies:
         copy.wait()
-
-
-def take_kernel(flip, start, source, *rest):
-    out, sem = rest[-2:]
     core = my_core()
-    at = (1 - core if flip else core) * (source.shape[2] // 2) + start
-    copy = pltpu.make_async_copy(source.at[:, :, pl.ds(pl.multiple_of(at, LANES), out.shape[2])], out, sem)
-    copy.start()
-    copy.wait()
+    copies = []
+    for n, out in enumerate(outs):
+        side = 1 - core if n < CHUNKS else core
+        at = side * (whole.shape[2] // 2) + n % CHUNKS * out.shape[2]
+        lanes = pl.ds(pl.multiple_of(at, LANES), out.shape[2])
+        copies.append(pltpu.make_async_copy(whole.at[:, :, lanes], out, sem.at[n]))
+    for copy in copies:
+        copy.start()
+    for copy in copies:
+        copy.wait()
 
 
 class Place:
@@ -484,23 +487,13 @@
     orbitals = pltpu.with_memory_space_constraint(orbitals, pltpu.HBM)
 
     part = jax.ShapeDtypeStruct((per_device, planes, chunk), f32)
-    loaded = pl.pallas_call(
-        fetch_kernel, out_shape=jax.ShapeDtypeStruct(shape, f32), in_specs=[HBM], out_specs=VM,
-        scratch_shapes=[DMA((4,))], name="fetch", compiler_params=grant(8),
+    fetched = pl.pallas_call(
+        fetch_kernel, out_shape=[part] * (2 * CHUNKS), in_specs=[HBM], out_specs=[VM] * (2 * CHUNKS),
+        scratch_shapes=[pltpu.VMEM(shape, f32), DMA((2 * CHUNKS,))], name="fetch", compiler_params=grant(8),
     )(orbitals)
-
-    def take(flip, n, *after):
-        return pl.pallas_call(
-            functools.partial(take_kernel, flip, n * chunk), out_shape=part, in_specs=[VM] + [ANY] * len(after),
-            out_specs=VM, scratch_shapes=[DMA], compiler_params=grant(8),
-        )(loaded, *after)
-
-    theirs, last = [], ()
-    for n in range(CHUNKS):
-        taken = take(True, n, *last)
+    theirs, mine = [], fetched[CHUNKS:]
+    for taken in fetched[:CHUNKS]:
         theirs.append(swap(taken, 1, 1))
-        last = (taken,)
-    mine = [take(False, n, taken) for n in range(CHUNKS)]
 
     pair = BLK // 2
     firsts = (BLK + 2) * chips

time: 62.7 us -> 60.6 us (0.967)
  Pallas kernels: 17.6 us -> 13.5 us
  waiting for transfers between devices: 7.97 us -> 10.4 us
    pallas_call x3, Pallas kernels: 4.96 us -> 1.67 us  [rotate(): pl.pallas_call(functools.partial(rotate_kernel, first * SUB), out_shape=(...]
    ppermute x19, waiting for transfers between devices: 4.46 us -> 6.88 us  [swap(): return lax.ppermute(x, axes, moves)]
    pallas_call x5 -> x1, Pallas kernels: 2.54 us -> 1.74 us  [tile_device(): pl.pallas_call(fetch_kernel, out_shape=[part] * (2 * CHUNKS), in_specs=[H...]
  transfers between devices with their start and end apart: 25 -> 25, of which waited for: 8 -> 9; matrix products, arithmetic and copies ran while one was open for 0% -> 0% of each run, Pallas kernels for 23% -> 18%
where the time goes in v4:
time: 60.6 us; the launch traced here: 60.4 us
  starting transfers between devices  35.3 us (58%)
  Pallas kernels  13.5 us (22%)
  waiting for transfers between devices  10.4 us (17%)
  between operations  1 us (2%)
    ppermute x19, starting transfers between devices, swap(): return lax.ppermute(x, axes, moves)  29.1 us
    ppermute x19, waiting for transfers between devices, swap(): return lax.ppermute(x, axes, moves)  6.88 us
    ppermute x6, starting transfers between devices, cross(): return lax.ppermute(x, axes, moves)  6.16 us
    ppermute x6, waiting for transfers between devices, cross(): return lax.ppermute(x, axes, moves)  3.51 us
    pallas_call x2, Pallas kernels, tile_device(): pl.pallas_call(functools.partial(backward_kernel, u, (CHUNKS, CHUNKS, len...  3.49 us
    pallas_call x1, Pallas kernels, tile_device(): pl.pallas_call(functools.partial(ready_kernel, per_device, n_grid), out_s...  2.71 us
    pallas_call x2, Pallas kernels, tile_device(): pl.pallas_call(functools.partial(forward_kernel, u, counts + (n_grid - 1,...  2 us
    pallas_call x1, Pallas kernels, tile_device(): pl.pallas_call(fetch_kernel, out_shape=[part] * (2 * CHUNKS), in_specs=[H...  1.74 us
  transfers between devices with their start and end apart: 25, of which 9 were waited for; matrix products, arithmetic and copies ran while one was open for 0% of the time, Pallas kernels for 18%

profile of v4, /device:TPU:17, one launch (start us, length us, event | category | flops | bytes accessed | tf_op | source)
XLA Modules:
  0.0 60.4 jit_solution(12790154795340653139)
XLA Ops:
  0.0 1.7 %fetch.1 = (f32[16,8,1024]{2,1,0:T(8,128)S(1)}, f32[16,8,1024]{2,1,0:T(8,128)S(1)}, f32[16,8,1024]{2,1,0:T(8,128)S(1)}, f32[16,8,1024]{2,1,0:T(8,128)S(1)}) custom-call(f32[16,8,4096]{2,1,0:T(8,128)} %source.1), custom_call_target="tpu_custom_call" | custom-call | tf_op jit(solution)/shard_map/fetch/pallas_call | solution.py:490
  1.8 0.7 %collective-permute-start.4 = (f32[16,8,1024]{2,1,0:T(8,128)S(1)}, f32[16,8,1024]{2,1,0:T(8,128)S(1)}, u32[]{:S(2)}, u32[]{:S(2)}) collective-permute-start(f32[16,8,1024]{2,1,0:T(8,128)S(1)} %get-tuple-element.113), channel_id=1, source_target_pairs={{0,4},{1,5},{2,6},{3,7},{4,0},{5,1},{6,2},{7,3},{8,12},{9,13},{10,... | collective-permute-start | bytes 1572872 | tf_op jit(solution)/shard_map/ppermute | solution.py:480
  2.5 0.1 collective-permute-start.6
  2.6 0.1 copy.24.tiles
  2.7 1.0 %setup.1 = (bf16[256,256]{1,0:T(8,128)(2,1)S(1)}, bf16[256,256]{1,0:T(8,128)(2,1)S(1)}) custom-call(s32[4,2]{1,0:T(4,128)S(1)} %copy.24.tiles, s32[1024]{0:T(1024)S(1)} %copy-done.15, f32[128,128]{1,0:T(8,128)S(1)} %copy-done.11, f32[16,8,1024]{2,1,0:T(8,128)S(1)} %get-tuple-element.109.after), custom_call_target="tpu_custom_call" | custom-call | tf_op jit(solution)/shard_map/setup/pallas_call | solution.py:506
  3.7 0.3 collective-permute-done.4.rest_1_
  4.0 0.5 shard_map.174
  4.5 1.3 %collective-permute-start.5 = (f32[12,8,1024]{2,1,0:T(8,128)S(1)}, f32[12,8,1024]{2,1,0:T(8,128)S(1)}, u32[]{:S(2)}, u32[]{:S(2)}) collective-permute-start(f32[12,8,1024]{2,1,0:T(8,128)S(1)} %get-tuple-element.115.rest_2_), channel_id=1, source_target_pairs={{0,8},{1,9},{2,10},{3,11},{4,20},{5,21},{6,22},{7,23},{8,0},{9,1},... | collective-permute-start | bytes 1179656 | tf_op jit(solution)/shard_map/ppermute | solution.py:480
  5.8 0.5 shard_map.175
  6.4 0.0 copy-start.13
  6.4 0.3 collective-permute-start.8
  6.7 0.7 %shard_map.176 = (f32[4,8,2048]{2,1,0:T(8,128)S(1)}, f32[4,8,2048]{2,1,0:T(8,128)S(1)}) custom-call(bf16[256,256]{1,0:T(8,128)(2,1)S(1)} %get-tuple-element.110.high, bf16[256,256]{1,0:T(8,128)(2,1)S(1)} %get-tuple-element.111.low, f32[16,8,1024]{2,1,0:T(8,128)S(1)} %get-tuple-element.112.rest_0_, f32[16,8,1024]{2,1,0:T(8,128)S(1)} %collective-permute-done.4.rest_1_, ...), custom_call_target="tpu_custom_call" | custom-call | tf_op jit(solution)/shard_map/pallas_call | solution.py:513
  7.4 4.2 %collective-permute-done.5.got = f32[12,8,1024]{2,1,0:T(8,128)S(1)} collective-permute-done((f32[12,8,1024]{2,1,0:T(8,128)S(1)}, f32[12,8,1024]{2,1,0:T(8,128)S(1)}, u32[]{:S(2)}, u32[]{:S(2)}) %collective-permute-start.5) | collective-permute-done | bytes 393248 | tf_op jit(solution)/shard_map/ppermute | solution.py:480
  11.5 1.3 %collective-permute-start.7 = (f32[6,8,1024]{2,1,0:T(8,128)S(1)}, f32[6,8,1024]{2,1,0:T(8,128)S(1)}, u32[]{:S(2)}, u32[]{:S(2)}) collective-permute-start(f32[6,8,1024]{2,1,0:T(8,128)S(1)} %shard_map.177.rest_0_), channel_id=1, source_target_pairs={{0,16},{1,17},{2,18},{3,19},{4,12},{5,13},{6,14},{7,15},{8,24},{9,... | collective-permute-start | bytes 589832 | tf_op jit(solution)/shard_map/ppermute | solution.py:480
  12.8 2.7 %ready.1 = (f32[16,8,4096]{2,1,0:T(8,128)}, f32[6,64,128]{2,1,0:T(8,128)S(1)}, f32[8]{0:T(128)S(1)}, s32[40]{0:T(128)S(1)}, s32[1]{0:T(128)}) custom-call(s32[4,2]{1,0:T(4,128)S(1)} %copy.24.tiles, s32[1024]{0:T(1024)S(1)} %copy-done.15, s32[128,128]{1,0:T(8,128)S(1)} %copy-done.12, f32[64,128]{1,0:T(8,128)S(1)} %copy-done.13, ...), custom_call_target="tpu_custom_call" | custom-call | tf_op jit(solution)/shard_map/ready/pallas_call | solution.py:548
  15.5 0.2 collective-permute-done.8.got
  15.8 0.0 copy-start
  15.8 1.3 %collective-permute-start.9 = (f32[6,8,1024]{2,1,0:T(8,128)S(1)}, f32[6,8,1024]{2,1,0:T(8,128)S(1)}, u32[]{:S(2)}, u32[]{:S(2)}) collective-permute-start(f32[6,8,1024]{2,1,0:T(8,128)S(1)} %shard_map.178.rest_0_), channel_id=1, source_target_pairs={{0,16},{1,17},{2,18},{3,19},{4,12},{5,13},{6,14},{7,15},{8,24},{9,... | collective-permute-start | bytes 589832 | tf_op jit(solution)/shard_map/ppermute | solution.py:480
  17.1 1.2 %collective-permute-start.12 = (f32[4,8,2048]{2,1,0:T(8,128)S(1)}, f32[4,8,2048]{2,1,0:T(8,128)S(1)}, u32[]{:S(2)}, u32[]{:S(2)}) collective-permute-start(f32[4,8,2048]{2,1,0:T(8,128)S(1)} %get-tuple-element.118.rest_0_), channel_id=1, source_target_pairs={{0,8},{1,9},{2,10},{3,11},{4,20},{5,21},{6,22},{7,23},{8,0},{9,1},... | collective-permute-start | bytes 786440 | tf_op jit(solution)/shard_map/ppermute | solution.py:480
  18.3 0.2 collective-permute-done.7.passed
  18.6 3.8 %collective-permute-start.10 = (f32[6,8,1024]{2,1,0:T(8,128)S(1)}, f32[6,8,1024]{2,1,0:T(8,128)S(1)}, u32[]{:S(2)}, u32[]{:S(2)}) collective-permute-start(f32[6,8,1024]{2,1,0:T(8,128)S(1)} %shard_map.179.rest_0_.refs_0_), channel_id=1, source_target_pairs={{0,4},{1,5},{2,6},{3,7},{4,0},{5,1},{6,2},{7,3},{8,12},{9,13},{10,... | collective-permute-start | bytes 589832 | tf_op jit(solution)/shard_map/ppermute | solution.py:480
  22.5 2.8 %collective-permute-start.11 = (f32[6,8,1024]{2,1,0:T(8,128)S(1)}, f32[6,8,1024]{2,1,0:T(8,128)S(1)}, u32[]{:S(2)}, u32[]{:S(2)}) collective-permute-start(f32[6,8,1024]{2,1,0:T(8,128)S(1)} %shard_map.180.rest_0_.refs_1_), channel_id=1, source_target_pairs={{0,4},{1,5},{2,6},{3,7},{4,0},{5,1},{6,2},{7,3},{8,12},{9,13},{10,... | collective-permute-start | bytes 589832 | tf_op jit(solution)/shard_map/ppermute | solution.py:480
  25.2 1.1 %collective-permute-start.20 = (f32[2,8,2048]{2,1,0:T(8,128)S(1)}, f32[2,8,2048]{2,1,0:T(8,128)S(1)}, u32[]{:S(2)}, u32[]{:S(2)}) collective-permute-start(f32[2,8,2048]{2,1,0:T(8,128)S(1)} %shard_map.181.refs_10_), channel_id=1, source_target_pairs={{0,16},{1,17},{2,18},{3,19},{4,12},{5,13},{6,14},{7,15},{8,24},{9,... | collective-permute-start | bytes 393224 | tf_op jit(solution)/shard_map/ppermute | solution.py:480
  26.4 1.0 %shard_map.182 = (f32[64,256]{1,0:T(8,128)S(1)}, f32[64,256]{1,0:T(8,128)S(1)}, f32[64,256]{1,0:T(8,128)S(1)}, f32[512,256]{1,0:T(8,128)S(1)}, f32[64,256]{1,0:T(8,128)S(1)}, /*index=5*/f32[64,256]{1,0:T(8,128)S(1)}) custom-call(f32[6,8,1024]{2,1,0:T(8,128)S(1)} %shard_map.179.rest_0_.refs_0_, f32[6,8,1024]{2,1,0:T(8,128)S(1)} %shard_map.180.rest_0_.refs_1_, ...), custom_call_target="tpu_custom_call" | custom-call | tf_op jit(solution)/shard_map/pallas_call | solution.py:587
  27.5 1.6 %collective-permute-done.20.passed = f32[2,8,2048]{2,1,0:T(8,128)S(1)} collective-permute-done((f32[2,8,2048]{2,1,0:T(8,128)S(1)}, f32[2,8,2048]{2,1,0:T(8,128)S(1)}, u32[]{:S(2)}, u32[]{:S(2)}) %collective-permute-start.20) | collective-permute-done | bytes 131104 | tf_op jit(solution)/shard_map/ppermute | solution.py:480
  29.1 3.2 %collective-permute-start.21 = (f32[2,8,2048]{2,1,0:T(8,128)S(1)}, f32[2,8,2048]{2,1,0:T(8,128)S(1)}, u32[]{:S(2)}, u32[]{:S(2)}) collective-permute-start(f32[2,8,2048]{2,1,0:T(8,128)S(1)} %shard_map.185.refs_4_), channel_id=1, source_target_pairs={{0,4},{1,5},{2,6},{3,7},{4,0},{5,1},{6,2},{7,3},{8,12},{9,13},{10,... | collective-permute-start | bytes 393224 | tf_op jit(solution)/shard_map/ppermute | solution.py:480
  32.3 1.3 %collective-permute-start.13 = (f32[64,256]{1,0:T(8,128)S(1)}, f32[64,256]{1,0:T(8,128)S(1)}, u32[]{:S(2)}, u32[]{:S(2)}) collective-permute-start(f32[64,256]{1,0:T(8,128)S(1)} %get-tuple-element.126), channel_id=1, source_target_pairs={{0,1},{1,0},{2,3},{3,2},{4,5},{5,4},{6,7},{7,6},{8,9},{9,8},{10,11... | collective-permute-start | bytes 196616 | tf_op jit(solution)/shard_map/ppermute | solution.py:484
  33.6 0.1 collective-permute-start.14
  33.7 1.3 %collective-permute-start.15 = (f32[64,256]{1,0:T(8,128)S(1)}, f32[64,256]{1,0:T(8,128)S(1)}, u32[]{:S(2)}, u32[]{:S(2)}) collective-permute-start(f32[64,256]{1,0:T(8,128)S(1)} %get-tuple-element.128), channel_id=1, source_target_pairs={{0,3},{1,2},{2,1},{3,0},{4,7},{5,6},{6,5},{7,4},{8,11},{9,10},{10,... | collective-permute-start | bytes 196616 | tf_op jit(solution)/shard_map/ppermute | solution.py:484
  35.0 1.0 %shard_map.186 = (f32[64,256]{1,0:T(8,128)S(1)}, f32[64,256]{1,0:T(8,128)S(1)}, f32[64,256]{1,0:T(8,128)S(1)}, f32[512,256]{1,0:T(8,128)S(1)}, f32[64,256]{1,0:T(8,128)S(1)}, /*index=5*/f32[64,256]{1,0:T(8,128)S(1)}) custom-call(f32[6,8,1024]{2,1,0:T(8,128)S(1)} %shard_map.179.rest_0_.refs_0_, f32[6,8,1024]{2,1,0:T(8,128)S(1)} %shard_map.180.rest_0_.refs_1_, ...), custom_call_target="tpu_custom_call" | custom-call | tf_op jit(solution)/shard_map/pallas_call | solution.py:587
  36.0 2.3 %collective-permute-start.22 = (f32[64,256]{1,0:T(8,128)S(1)}, f32[64,256]{1,0:T(8,128)S(1)}, u32[]{:S(2)}, u32[]{:S(2)}) collective-permute-start(f32[64,256]{1,0:T(8,128)S(1)} %get-tuple-element.132), channel_id=1, source_target_pairs={{0,1},{1,0},{2,3},{3,2},{4,5},{5,4},{6,7},{7,6},{8,9},{9,8},{10,11... | collective-permute-start | bytes 196616 | tf_op jit(solution)/shard_map/ppermute | solution.py:484
  38.3 1.3 %collective-permute-start.24 = (f32[64,256]{1,0:T(8,128)S(1)}, f32[64,256]{1,0:T(8,128)S(1)}, u32[]{:S(2)}, u32[]{:S(2)}) collective-permute-start(f32[64,256]{1,0:T(8,128)S(1)} %get-tuple-element.134), channel_id=1, source_target_pairs={{0,3},{1,2},{2,1},{3,0},{4,7},{5,6},{6,5},{7,4},{8,11},{9,10},{10,... | collective-permute-start | bytes 196616 | tf_op jit(solution)/shard_map/ppermute | solution.py:484
  39.5 1.5 %collective-permute-done.15.refs_6_ = f32[64,256]{1,0:T(8,128)S(1)} collective-permute-done((f32[64,256]{1,0:T(8,128)S(1)}, f32[64,256]{1,0:T(8,128)S(1)}, u32[]{:S(2)}, u32[]{:S(2)}) %collective-permute-start.15) | collective-permute-done | bytes 65568 | tf_op jit(solution)/shard_map/ppermute | solution.py:484
  41.1 1.8 %shard_map.183.refs_18_ = f32[8,4096]{1,0:T(8,128)S(1)} custom-call(f32[8]{0:T(128)S(1)} %get-tuple-element.121.flags, f32[6,8,1024]{2,1,0:T(8,128)S(1)} %shard_map.179.rest_0_.refs_0_, f32[6,8,1024]{2,1,0:T(8,128)S(1)} %shard_map.180.rest_0_.refs_1_, f32[6,8,1024]{2,1,0:T(8,128)S(1)} %collective-permute-done.10.refs_2_, ...), custom_call_target="tpu_custom_call" | custom-call | tf_op jit(solution)/shard_map/pallas_call | solution.py:605
  42.8 1.3 %collective-permute-start.17 = (f32[8,4096]{1,0:T(8,128)S(1)}, f32[8,4096]{1,0:T(8,128)S(1)}, u32[]{:S(2)}, u32[]{:S(2)}) collective-permute-start(f32[8,4096]{1,0:T(8,128)S(1)} %shard_map.183.refs_18_), channel_id=1, source_target_pairs={{0,16},{1,17},{2,18},{3,19},{4,12},{5,13},{6,14},{7,15},{8,24},{9,... | collective-permute-start | bytes 393224 | tf_op jit(solution)/shard_map/ppermute | solution.py:480
  44.1 0.2 collective-permute-start.16
  44.3 2.0 %collective-permute-done.24.refs_6_ = f32[64,256]{1,0:T(8,128)S(1)} collective-permute-done((f32[64,256]{1,0:T(8,128)S(1)}, f32[64,256]{1,0:T(8,128)S(1)}, u32[]{:S(2)}, u32[]{:S(2)}) %collective-permute-start.24) | collective-permute-done | bytes 65568 | tf_op jit(solution)/shard_map/ppermute | solution.py:484
  46.3 1.7 %shard_map.187 = f32[8,4096]{1,0:T(8,128)S(1)} custom-call(f32[8]{0:T(128)S(1)} %get-tuple-element.121.flags, f32[6,8,1024]{2,1,0:T(8,128)S(1)} %shard_map.179.rest_0_.refs_0_, f32[6,8,1024]{2,1,0:T(8,128)S(1)} %shard_map.180.rest_0_.refs_1_, f32[6,8,1024]{2,1,0:T(8,128)S(1)} %collective-permute-done.10.refs_2_, ...), custom_call_target="tpu_custom_call" | custom-call | tf_op jit(solution)/shard_map/pallas_call | solution.py:605
  48.1 1.3 %collective-permute-start.26 = (f32[8,4096]{1,0:T(8,128)S(1)}, f32[8,4096]{1,0:T(8,128)S(1)}, u32[]{:S(2)}, u32[]{:S(2)}) collective-permute-start(f32[8,4096]{1,0:T(8,128)S(1)} %shard_map.187), channel_id=1, source_target_pairs={{0,16},{1,17},{2,18},{3,19},{4,12},{5,13},{6,14},{7,15},{8,24},{9,... | collective-permute-start | bytes 393224 | tf_op jit(solution)/shard_map/ppermute | solution.py:480
  49.4 0.2 collective-permute-start.25
  49.6 4.5 %collective-permute-start.19 = (f32[2,8,4096]{2,1,0:T(8,128)S(1)}, f32[2,8,4096]{2,1,0:T(8,128)S(1)}, u32[]{:S(2)}, u32[]{:S(2)}) collective-permute-start(f32[2,8,4096]{2,1,0:T(8,128)S(1)} %shard_map.184), channel_id=1, source_target_pairs={{0,4},{1,5},{2,6},{3,7},{4,0},{5,1},{6,2},{7,3},{8,12},{9,13},{10,... | collective-permute-start | bytes 786440 | tf_op jit(solution)/shard_map/ppermute | solution.py:480
  54.2 4.0 %collective-permute-start.28 = (f32[2,8,4096]{2,1,0:T(8,128)S(1)}, f32[2,8,4096]{2,1,0:T(8,128)S(1)}, u32[]{:S(2)}, u32[]{:S(2)}) collective-permute-start(f32[2,8,4096]{2,1,0:T(8,128)S(1)} %shard_map.188), channel_id=1, source_target_pairs={{0,4},{1,5},{2,6},{3,7},{4,0},{5,1},{6,2},{7,3},{8,12},{9,13},{10,... | collective-permute-start | bytes 786440 | tf_op jit(solution)/shard_map/ppermute | solution.py:480
  58.1 0.1 collective-permute-start.18
  58.2 0.4 collective-permute-start.27
  59.3 0.2 collective-permute-done.18
  59.5 0.2 collective-permute-done.27
  59.7 0.7 %conditional.1 = (f32[16,8,4096]{2,1,0:T(8,128)}) conditional(s32[]{:T(128)} %bitcast, (s32[40]{0:T(128)S(1)}, f32[8,4096]{1,0:T(8,128)S(1)}, f32[8,4096]{1,0:T(8,128)S(1)}, f32[8,4096]{1,0:T(8,128)S(1)}, f32[8,4096]{1,0:T(8,128)S(1)}, /*index=5*/f32[2,8,4096]{2,1,0:T(8,128)S(1)}, f32[8,4096]{1,0:T(8,128)S(1)}, f32[8,4096]{1,0:T(8,128)S(1)}, ...), branch_computations={%region_0.0_spmd, %region_1.0_spmd} | conditional | bytes 2097320 | solution.py:647
  59.7 0.7 %place.2 = f32[16,8,4096]{2,1,0:T(8,128)} custom-call(s32[40]{0:T(128)S(1)} %get-tuple-element.56.match, f32[8,4096]{1,0:T(8,128)S(1)} %get-tuple-element.57.refs_0_, f32[8,4096]{1,0:T(8,128)S(1)} %get-tuple-element.58.refs_1_, f32[8,4096]{1,0:T(8,128)S(1)} %get-tuple-element.59.refs_2_, ...), custom_call_target="tpu_custom_call", output_to_operand_aliasing={{}: (11, {})} | custom-call | tf_op jit(solution)/shard_map/cond/branch_0_fun/place/pallas_call | solution.py:629
  (57 shorter events, 0.3 us)
Async XLA Ops:
  0.0 2.7 %copy-start.15 = (s32[1024]{0:T(1024)S(1)}, s32[1024]{0:T(1024)}, u32[]{:S(2)}) copy-start(s32[1024]{0:T(1024)} %constant.31.clone.host) | copy-start | bytes 12292
  0.0 2.6 %copy-start.16 = (s32[4,2]{0,1:T(2,128)S(1)}, s32[4,2]{0,1:T(2,128)}, u32[]{:S(2)}) copy-start(s32[4,2]{0,1:T(2,128)} %param.22) | copy-start | bytes 100
  0.0 2.7 %copy-start.11 = (f32[128,128]{1,0:T(8,128)S(1)}, f32[128,128]{1,0:T(8,128)}, u32[]{:S(2)}) copy-start(f32[128,128]{1,0:T(8,128)} %rotation.1) | copy-start | bytes 196612
  1.8 2.3 %collective-permute-start.4 = (f32[16,8,1024]{2,1,0:T(8,128)S(1)}, f32[16,8,1024]{2,1,0:T(8,128)S(1)}, u32[]{:S(2)}, u32[]{:S(2)}) collective-permute-start(f32[16,8,1024]{2,1,0:T(8,128)S(1)} %get-tuple-element.113), channel_id=1, source_target_pairs={{0,4},{1,5},{2,6},{3,7},{4,0},{5,1},{6,2},{7,3},{8,12},{9,13},{10,... | collective-permute-start | bytes 1572872 | tf_op jit(solution)/shard_map/ppermute | solution.py:480
  2.5 3.3 %collective-permute-start.6 = (f32[16,8,1024]{2,1,0:T(8,128)S(1)}, f32[16,8,1024]{2,1,0:T(8,128)S(1)}, u32[]{:S(2)}, u32[]{:S(2)}) collective-permute-start(f32[16,8,1024]{2,1,0:T(8,128)S(1)} %get-tuple-element.109.after), channel_id=1, source_target_pairs={{0,4},{1,5},{2,6},{3,7},{4,0},{5,1},{6,2},{7,3},{8,12},{9,13},{10,... | collective-permute-start | bytes 1572872 | tf_op jit(solution)/shard_map/ppermute | solution.py:480
  4.5 7.0 %collective-permute-start.5 = (f32[12,8,1024]{2,1,0:T(8,128)S(1)}, f32[12,8,1024]{2,1,0:T(8,128)S(1)}, u32[]{:S(2)}, u32[]{:S(2)}) collective-permute-start(f32[12,8,1024]{2,1,0:T(8,128)S(1)} %get-tuple-element.115.rest_2_), channel_id=1, source_target_pairs={{0,8},{1,9},{2,10},{3,11},{4,20},{5,21},{6,22},{7,23},{8,0},{9,1},... | collective-permute-start | bytes 1179656 | tf_op jit(solution)/shard_map/ppermute | solution.py:480
  6.3 6.5 %copy-start.12 = (s32[128,128]{1,0:T(8,128)S(1)}, s32[128,128]{1,0:T(8,128)}, u32[]{:S(2)}) copy-start(s32[128,128]{1,0:T(8,128)} %mask.1) | copy-start | bytes 196612
  6.4 6.5 %copy-start.13 = (f32[64,128]{1,0:T(8,128)S(1)}, f32[64,128]{1,0:T(8,128)}, u32[]{:S(2)}) copy-start(f32[64,128]{1,0:T(8,128)} %constant.32.clone.log_r) | copy-start | bytes 98308
  6.4 9.4 %collective-permute-start.8 = (f32[12,8,1024]{2,1,0:T(8,128)S(1)}, f32[12,8,1024]{2,1,0:T(8,128)S(1)}, u32[]{:S(2)}, u32[]{:S(2)}) collective-permute-start(f32[12,8,1024]{2,1,0:T(8,128)S(1)} %get-tuple-element.117.rest_4_), channel_id=1, source_target_pairs={{0,8},{1,9},{2,10},{3,11},{4,20},{5,21},{6,22},{7,23},{8,0},{9,1},... | collective-permute-start | bytes 1179656 | tf_op jit(solution)/shard_map/ppermute | solution.py:480
  11.5 7.0 %collective-permute-start.7 = (f32[6,8,1024]{2,1,0:T(8,128)S(1)}, f32[6,8,1024]{2,1,0:T(8,128)S(1)}, u32[]{:S(2)}, u32[]{:S(2)}) collective-permute-start(f32[6,8,1024]{2,1,0:T(8,128)S(1)} %shard_map.177.rest_0_), channel_id=1, source_target_pairs={{0,16},{1,17},{2,18},{3,19},{4,12},{5,13},{6,14},{7,15},{8,24},{9,... | collective-permute-start | bytes 589832 | tf_op jit(solution)/shard_map/ppermute | solution.py:480
  15.8 10.6 %copy-start = (bf16[2,256,256]{2,1,0:T(8,128)(2,1)S(1)}, bf16[2,256,256]{2,1,0:T(8,128)(2,1)}, u32[]{:S(2)}) copy-start(bf16[2,256,256]{2,1,0:T(8,128)(2,1)} %constant.38.clone.refs_5_.refs_7_) | copy-start | bytes 786436
  15.8 10.6 %copy-start.1 = (bf16[2,256,256]{2,1,0:T(8,128)(2,1)S(1)}, bf16[2,256,256]{2,1,0:T(8,128)(2,1)}, u32[]{:S(2)}) copy-start(bf16[2,256,256]{2,1,0:T(8,128)(2,1)} %constant.37.clone.refs_4_.refs_6_) | copy-start | bytes 786436
  15.8 10.6 %copy-start.2 = (f32[512,128]{1,0:T(8,128)S(1)}, f32[512,128]{1,0:T(8,128)}, u32[]{:S(2)}) copy-start(f32[512,128]{1,0:T(8,128)} %constant.33.clone.refs_8_.refs_10_) | copy-start | bytes 786436
  15.8 10.6 %copy-start.6 = (bf16[256,256]{1,0:T(8,128)(2,1)S(1)}, bf16[256,256]{1,0:T(8,128)(2,1)}, u32[]{:S(2)}) copy-start(bf16[256,256]{1,0:T(8,128)(2,1)} %constant.42.clone.refs_7_.refs_9_) | copy-start | bytes 393220
  15.8 10.6 %copy-start.7 = (bf16[256,256]{1,0:T(8,128)(2,1)S(1)}, bf16[256,256]{1,0:T(8,128)(2,1)}, u32[]{:S(2)}) copy-start(bf16[256,256]{1,0:T(8,128)(2,1)} %constant.41.clone.refs_6_.refs_8_) | copy-start | bytes 393220
  15.8 6.6 %collective-permute-start.9 = (f32[6,8,1024]{2,1,0:T(8,128)S(1)}, f32[6,8,1024]{2,1,0:T(8,128)S(1)}, u32[]{:S(2)}, u32[]{:S(2)}) collective-permute-start(f32[6,8,1024]{2,1,0:T(8,128)S(1)} %shard_map.178.rest_0_), channel_id=1, source_target_pairs={{0,16},{1,17},{2,18},{3,19},{4,12},{5,13},{6,14},{7,15},{8,24},{9,... | collective-permute-start | bytes 589832 | tf_op jit(solution)/shard_map/ppermute | solution.py:480
  17.1 8.1 %collective-permute-start.12 = (f32[4,8,2048]{2,1,0:T(8,128)S(1)}, f32[4,8,2048]{2,1,0:T(8,128)S(1)}, u32[]{:S(2)}, u32[]{:S(2)}) collective-permute-start(f32[4,8,2048]{2,1,0:T(8,128)S(1)} %get-tuple-element.118.rest_0_), channel_id=1, source_target_pairs={{0,8},{1,9},{2,10},{3,11},{4,20},{5,21},{6,22},{7,23},{8,0},{9,1},... | collective-permute-start | bytes 786440 | tf_op jit(solution)/shard_map/ppermute | solution.py:480
  18.6 7.8 %collective-permute-start.10 = (f32[6,8,1024]{2,1,0:T(8,128)S(1)}, f32[6,8,1024]{2,1,0:T(8,128)S(1)}, u32[]{:S(2)}, u32[]{:S(2)}) collective-permute-start(f32[6,8,1024]{2,1,0:T(8,128)S(1)} %shard_map.179.rest_0_.refs_0_), channel_id=1, source_target_pairs={{0,4},{1,5},{2,6},{3,7},{4,0},{5,1},{6,2},{7,3},{8,12},{9,13},{10,... | collective-permute-start | bytes 589832 | tf_op jit(solution)/shard_map/ppermute | solution.py:480
  22.5 3.9 %collective-permute-start.11 = (f32[6,8,1024]{2,1,0:T(8,128)S(1)}, f32[6,8,1024]{2,1,0:T(8,128)S(1)}, u32[]{:S(2)}, u32[]{:S(2)}) collective-permute-start(f32[6,8,1024]{2,1,0:T(8,128)S(1)} %shard_map.180.rest_0_.refs_1_), channel_id=1, source_target_pairs={{0,4},{1,5},{2,6},{3,7},{4,0},{5,1},{6,2},{7,3},{8,12},{9,13},{10,... | collective-permute-start | bytes 589832 | tf_op jit(solution)/shard_map/ppermute | solution.py:480
  25.2 3.9 %collective-permute-start.20 = (f32[2,8,2048]{2,1,0:T(8,128)S(1)}, f32[2,8,2048]{2,1,0:T(8,128)S(1)}, u32[]{:S(2)}, u32[]{:S(2)}) collective-permute-start(f32[2,8,2048]{2,1,0:T(8,128)S(1)} %shard_map.181.refs_10_), channel_id=1, source_target_pairs={{0,16},{1,17},{2,18},{3,19},{4,12},{5,13},{6,14},{7,15},{8,24},{9,... | collective-permute-start | bytes 393224 | tf_op jit(solution)/shard_map/ppermute | solution.py:480
  27.4 13.6 %copy-start.3 = (bf16[2,256,256]{2,1,0:T(8,128)(2,1)S(1)}, bf16[2,256,256]{2,1,0:T(8,128)(2,1)}, u32[]{:S(2)}) copy-start(bf16[2,256,256]{2,1,0:T(8,128)(2,1)} %constant.40.clone.refs_8_) | copy-start | bytes 786436
  27.4 13.6 %copy-start.4 = (bf16[2,256,256]{2,1,0:T(8,128)(2,1)S(1)}, bf16[2,256,256]{2,1,0:T(8,128)(2,1)}, u32[]{:S(2)}) copy-start(bf16[2,256,256]{2,1,0:T(8,128)(2,1)} %constant.39.clone.refs_7_) | copy-start | bytes 786436
  27.5 13.6 %copy-start.5 = (f32[512,128]{1,0:T(8,128)S(1)}, f32[512,128]{1,0:T(8,128)}, u32[]{:S(2)}) copy-start(f32[512,128]{1,0:T(8,128)} %constant.34.clone.refs_11_) | copy-start | bytes 786436
  27.5 13.6 %copy-start.8 = (bf16[256,256]{1,0:T(8,128)(2,1)S(1)}, bf16[256,256]{1,0:T(8,128)(2,1)}, u32[]{:S(2)}) copy-start(bf16[256,256]{1,0:T(8,128)(2,1)} %constant.44.clone.refs_10_) | copy-start | bytes 393220
  27.5 13.6 %copy-start.9 = (bf16[256,256]{1,0:T(8,128)(2,1)S(1)}, bf16[256,256]{1,0:T(8,128)(2,1)}, u32[]{:S(2)}) copy-start(bf16[256,256]{1,0:T(8,128)(2,1)} %constant.43.clone.refs_9_) | copy-start | bytes 393220
  27.5 13.6 %copy-start.10 = (f32[3,64,128]{2,1,0:T(8,128)S(1)}, f32[3,64,128]{2,1,0:T(8,128)}, u32[]{:S(2)}) copy-start(f32[3,64,128]{2,1,0:T(8,128)} %constant.36.clone.refs_14_) | copy-start | bytes 294916
  27.5 13.6 %copy-start.14 = (f32[2,8,128]{2,1,0:T(8,128)S(1)}, f32[2,8,128]{2,1,0:T(8,128)}, u32[]{:S(2)}) copy-start(f32[2,8,128]{2,1,0:T(8,128)} %constant.35.clone.refs_12_) | copy-start | bytes 24580
  29.1 5.8 %collective-permute-start.21 = (f32[2,8,2048]{2,1,0:T(8,128)S(1)}, f32[2,8,2048]{2,1,0:T(8,128)S(1)}, u32[]{:S(2)}, u32[]{:S(2)}) collective-permute-start(f32[2,8,2048]{2,1,0:T(8,128)S(1)} %shard_map.185.refs_4_), channel_id=1, source_target_pairs={{0,4},{1,5},{2,6},{3,7},{4,0},{5,1},{6,2},{7,3},{8,12},{9,13},{10,... | collective-permute-start | bytes 393224 | tf_op jit(solution)/shard_map/ppermute | solution.py:480
  32.3 5.9 %collective-permute-start.13 = (f32[64,256]{1,0:T(8,128)S(1)}, f32[64,256]{1,0:T(8,128)S(1)}, u32[]{:S(2)}, u32[]{:S(2)}) collective-permute-start(f32[64,256]{1,0:T(8,128)S(1)} %get-tuple-element.126), channel_id=1, source_target_pairs={{0,1},{1,0},{2,3},{3,2},{4,5},{5,4},{6,7},{7,6},{8,9},{9,8},{10,11... | collective-permute-start | bytes 196616 | tf_op jit(solution)/shard_map/ppermute | solution.py:484
  33.6 5.9 %collective-permute-start.14 = (f32[64,256]{1,0:T(8,128)S(1)}, f32[64,256]{1,0:T(8,128)S(1)}, u32[]{:S(2)}, u32[]{:S(2)}) collective-permute-start(f32[64,256]{1,0:T(8,128)S(1)} %get-tuple-element.127), channel_id=1, source_target_pairs={{0,2},{1,3},{2,0},{3,1},{4,6},{5,7},{6,4},{7,5},{8,10},{9,11},{10,... | collective-permute-start | bytes 196616 | tf_op jit(solution)/shard_map/ppermute | solution.py:484
  33.7 7.3 %collective-permute-start.15 = (f32[64,256]{1,0:T(8,128)S(1)}, f32[64,256]{1,0:T(8,128)S(1)}, u32[]{:S(2)}, u32[]{:S(2)}) collective-permute-start(f32[64,256]{1,0:T(8,128)S(1)} %get-tuple-element.128), channel_id=1, source_target_pairs={{0,3},{1,2},{2,1},{3,0},{4,7},{5,6},{6,5},{7,4},{8,11},{9,10},{10,... | collective-permute-start | bytes 196616 | tf_op jit(solution)/shard_map/ppermute | solution.py:484
  36.0 8.3 %collective-permute-start.22 = (f32[64,256]{1,0:T(8,128)S(1)}, f32[64,256]{1,0:T(8,128)S(1)}, u32[]{:S(2)}, u32[]{:S(2)}) collective-permute-start(f32[64,256]{1,0:T(8,128)S(1)} %get-tuple-element.132), channel_id=1, source_target_pairs={{0,1},{1,0},{2,3},{3,2},{4,5},{5,4},{6,7},{7,6},{8,9},{9,8},{10,11... | collective-permute-start | bytes 196616 | tf_op jit(solution)/shard_map/ppermute | solution.py:484
  38.2 6.1 %collective-permute-start.23 = (f32[64,256]{1,0:T(8,128)S(1)}, f32[64,256]{1,0:T(8,128)S(1)}, u32[]{:S(2)}, u32[]{:S(2)}) collective-permute-start(f32[64,256]{1,0:T(8,128)S(1)} %get-tuple-element.133), channel_id=1, source_target_pairs={{0,2},{1,3},{2,0},{3,1},{4,6},{5,7},{6,4},{7,5},{8,10},{9,11},{10,... | collective-permute-start | bytes 196616 | tf_op jit(solution)/shard_map/ppermute | solution.py:484
  38.3 8.1 %collective-permute-start.24 = (f32[64,256]{1,0:T(8,128)S(1)}, f32[64,256]{1,0:T(8,128)S(1)}, u32[]{:S(2)}, u32[]{:S(2)}) collective-permute-start(f32[64,256]{1,0:T(8,128)S(1)} %get-tuple-element.134), channel_id=1, source_target_pairs={{0,3},{1,2},{2,1},{3,0},{4,7},{5,6},{6,5},{7,4},{8,11},{9,10},{10,... | collective-permute-start | bytes 196616 | tf_op jit(solution)/shard_map/ppermute | solution.py:484
  42.8 6.8 %collective-permute-start.17 = (f32[8,4096]{1,0:T(8,128)S(1)}, f32[8,4096]{1,0:T(8,128)S(1)}, u32[]{:S(2)}, u32[]{:S(2)}) collective-permute-start(f32[8,4096]{1,0:T(8,128)S(1)} %shard_map.183.refs_18_), channel_id=1, source_target_pairs={{0,16},{1,17},{2,18},{3,19},{4,12},{5,13},{6,14},{7,15},{8,24},{9,... | collective-permute-start | bytes 393224 | tf_op jit(solution)/shard_map/ppermute | solution.py:480
  44.1 5.5 %collective-permute-start.16 = (f32[8,4096]{1,0:T(8,128)S(1)}, f32[8,4096]{1,0:T(8,128)S(1)}, u32[]{:S(2)}, u32[]{:S(2)}) collective-permute-start(f32[8,4096]{1,0:T(8,128)S(1)} %shard_map.183.refs_18_), channel_id=1, source_target_pairs={{0,8},{1,9},{2,10},{3,11},{4,20},{5,21},{6,22},{7,23},{8,0},{9,1},... | collective-permute-start | bytes 393224 | tf_op jit(solution)/shard_map/ppermute | solution.py:480
  48.1 6.1 %collective-permute-start.26 = (f32[8,4096]{1,0:T(8,128)S(1)}, f32[8,4096]{1,0:T(8,128)S(1)}, u32[]{:S(2)}, u32[]{:S(2)}) collective-permute-start(f32[8,4096]{1,0:T(8,128)S(1)} %shard_map.187), channel_id=1, source_target_pairs={{0,16},{1,17},{2,18},{3,19},{4,12},{5,13},{6,14},{7,15},{8,24},{9,... | collective-permute-start | bytes 393224 | tf_op jit(solution)/shard_map/ppermute | solution.py:480
  49.4 4.8 %collective-permute-start.25 = (f32[8,4096]{1,0:T(8,128)S(1)}, f32[8,4096]{1,0:T(8,128)S(1)}, u32[]{:S(2)}, u32[]{:S(2)}) collective-permute-start(f32[8,4096]{1,0:T(8,128)S(1)} %shard_map.187), channel_id=1, source_target_pairs={{0,8},{1,9},{2,10},{3,11},{4,20},{5,21},{6,22},{7,23},{8,0},{9,1},... | collective-permute-start | bytes 393224 | tf_op jit(solution)/shard_map/ppermute | solution.py:480
  49.6 10.1 %collective-permute-start.19 = (f32[2,8,4096]{2,1,0:T(8,128)S(1)}, f32[2,8,4096]{2,1,0:T(8,128)S(1)}, u32[]{:S(2)}, u32[]{:S(2)}) collective-permute-start(f32[2,8,4096]{2,1,0:T(8,128)S(1)} %shard_map.184), channel_id=1, source_target_pairs={{0,4},{1,5},{2,6},{3,7},{4,0},{5,1},{6,2},{7,3},{8,12},{9,13},{10,... | collective-permute-start | bytes 786440 | tf_op jit(solution)/shard_map/ppermute | solution.py:480
  54.2 5.5 %collective-permute-start.28 = (f32[2,8,4096]{2,1,0:T(8,128)S(1)}, f32[2,8,4096]{2,1,0:T(8,128)S(1)}, u32[]{:S(2)}, u32[]{:S(2)}) collective-permute-start(f32[2,8,4096]{2,1,0:T(8,128)S(1)} %shard_map.188), channel_id=1, source_target_pairs={{0,4},{1,5},{2,6},{3,7},{4,0},{5,1},{6,2},{7,3},{8,12},{9,13},{10,... | collective-permute-start | bytes 786440 | tf_op jit(solution)/shard_map/ppermute | solution.py:480
  58.1 1.3 %collective-permute-start.18 = (f32[8,4096]{1,0:T(8,128)S(1)}, f32[8,4096]{1,0:T(8,128)S(1)}, u32[]{:S(2)}, u32[]{:S(2)}) collective-permute-start(f32[8,4096]{1,0:T(8,128)S(1)} %shard_map.183.refs_18_), channel_id=1, source_target_pairs={{0,4},{1,5},{2,6},{3,7},{4,0},{5,1},{6,2},{7,3},{8,12},{9,13},{10,... | collective-permute-start | bytes 393224 | tf_op jit(solution)/shard_map/ppermute | solution.py:480
  58.2 1.5 %collective-permute-start.27 = (f32[8,4096]{1,0:T(8,128)S(1)}, f32[8,4096]{1,0:T(8,128)S(1)}, u32[]{:S(2)}, u32[]{:S(2)}) collective-permute-start(f32[8,4096]{1,0:T(8,128)S(1)} %shard_map.187), channel_id=1, source_target_pairs={{0,4},{1,5},{2,6},{3,7},{4,0},{5,1},{6,2},{7,3},{8,12},{9,13},{10,... | collective-permute-start | bytes 393224 | tf_op jit(solution)/shard_map/ppermute | solution.py:480

commit v5 on v4

--- a/solution.py
+++ b/solution.py
@@ -612,8 +612,10 @@
         )(flags, *inputs, *last))
         last = (terms[-1],)
 
-    near_1 = [swap(term, 2, 4) for term in terms]
-    near_2 = [swap(term, 4, 2) for term in terms]
+    near_1, near_2 = [], []
+    for term in terms:
+        near_1.append(swap(term, 2, 4))
+        near_2.append(swap(term, 4, 2))
     own_parts = [[term, x, y] for term, x, y in zip(terms, near_1, near_2)]
     sib_parts = []
     for term, x, y in own_parts:

time: 60.6 us -> 60.6 us (level)
  no operation moved by 1% of the time
where the time goes in v5:
time: 60.6 us; the launch traced here: 60.4 us
  starting transfers between devices  35.3 us (58%)
  Pallas kernels  13.5 us (22%)
  waiting for transfers between devices  10.4 us (17%)
  between operations  1 us (2%)
    ppermute x19, starting transfers between devices, swap(): return lax.ppermute(x, axes, moves)  29.1 us
    ppermute x19, waiting for transfers between devices, swap(): return lax.ppermute(x, axes, moves)  6.88 us
    ppermute x6, starting transfers between devices, cross(): return lax.ppermute(x, axes, moves)  6.16 us
    ppermute x6, waiting for transfers between devices, cross(): return lax.ppermute(x, axes, moves)  3.51 us
    pallas_call x2, Pallas kernels, tile_device(): pl.pallas_call(functools.partial(backward_kernel, u, (CHUNKS, CHUNKS, len...  3.49 us
    pallas_call x1, Pallas kernels, tile_device(): pl.pallas_call(functools.partial(ready_kernel, per_device, n_grid), out_s...  2.71 us
    pallas_call x2, Pallas kernels, tile_device(): pl.pallas_call(functools.partial(forward_kernel, u, counts + (n_grid - 1,...  2 us
    pallas_call x1, Pallas kernels, tile_device(): pl.pallas_call(fetch_kernel, out_shape=[part] * (2 * CHUNKS), in_specs=[H...  1.74 us
  transfers between devices with their start and end apart: 25, of which 9 were waited for; matrix products, arithmetic and copies ran while one was open for 0% of the time, Pallas kernels for 18%

profile of v5, /device:TPU:17, one launch (start us, length us, event | category | flops | bytes accessed | tf_op | source)
XLA Modules:
  0.0 60.4 jit_solution(12790154795340653139)
XLA Ops:
  0.0 1.7 %fetch.1 = (f32[16,8,1024]{2,1,0:T(8,128)S(1)}, f32[16,8,1024]{2,1,0:T(8,128)S(1)}, f32[16,8,1024]{2,1,0:T(8,128)S(1)}, f32[16,8,1024]{2,1,0:T(8,128)S(1)}) custom-call(f32[16,8,4096]{2,1,0:T(8,128)} %source.1), custom_call_target="tpu_custom_call" | custom-call | tf_op jit(solution)/shard_map/fetch/pallas_call | solution.py:490
  1.8 0.7 %collective-permute-start.4 = (f32[16,8,1024]{2,1,0:T(8,128)S(1)}, f32[16,8,1024]{2,1,0:T(8,128)S(1)}, u32[]{:S(2)}, u32[]{:S(2)}) collective-permute-start(f32[16,8,1024]{2,1,0:T(8,128)S(1)} %get-tuple-element.113), channel_id=1, source_target_pairs={{0,4},{1,5},{2,6},{3,7},{4,0},{5,1},{6,2},{7,3},{8,12},{9,13},{10,... | collective-permute-start | bytes 1572872 | tf_op jit(solution)/shard_map/ppermute | solution.py:480
  2.5 0.1 collective-permute-start.6
  2.6 0.1 copy.24.tiles
  2.7 1.0 %setup.1 = (bf16[256,256]{1,0:T(8,128)(2,1)S(1)}, bf16[256,256]{1,0:T(8,128)(2,1)S(1)}) custom-call(s32[4,2]{1,0:T(4,128)S(1)} %copy.24.tiles, s32[1024]{0:T(1024)S(1)} %copy-done.15, f32[128,128]{1,0:T(8,128)S(1)} %copy-done.11, f32[16,8,1024]{2,1,0:T(8,128)S(1)} %get-tuple-element.109.after), custom_call_target="tpu_custom_call" | custom-call | tf_op jit(solution)/shard_map/setup/pallas_call | solution.py:506
  3.7 0.3 collective-permute-done.4.rest_1_
  4.0 0.5 shard_map.174
  4.5 1.3 %collective-permute-start.5 = (f32[12,8,1024]{2,1,0:T(8,128)S(1)}, f32[12,8,1024]{2,1,0:T(8,128)S(1)}, u32[]{:S(2)}, u32[]{:S(2)}) collective-permute-start(f32[12,8,1024]{2,1,0:T(8,128)S(1)} %get-tuple-element.115.rest_2_), channel_id=1, source_target_pairs={{0,8},{1,9},{2,10},{3,11},{4,20},{5,21},{6,22},{7,23},{8,0},{9,1},... | collective-permute-start | bytes 1179656 | tf_op jit(solution)/shard_map/ppermute | solution.py:480
  5.8 0.5 shard_map.175
  6.4 0.0 copy-start.13
  6.4 0.3 collective-permute-start.8
  6.7 0.7 %shard_map.176 = (f32[4,8,2048]{2,1,0:T(8,128)S(1)}, f32[4,8,2048]{2,1,0:T(8,128)S(1)}) custom-call(bf16[256,256]{1,0:T(8,128)(2,1)S(1)} %get-tuple-element.110.high, bf16[256,256]{1,0:T(8,128)(2,1)S(1)} %get-tuple-element.111.low, f32[16,8,1024]{2,1,0:T(8,128)S(1)} %get-tuple-element.112.rest_0_, f32[16,8,1024]{2,1,0:T(8,128)S(1)} %collective-permute-done.4.rest_1_, ...), custom_call_target="tpu_custom_call" | custom-call | tf_op jit(solution)/shard_map/pallas_call | solution.py:513
  7.4 4.2 %collective-permute-done.5.got = f32[12,8,1024]{2,1,0:T(8,128)S(1)} collective-permute-done((f32[12,8,1024]{2,1,0:T(8,128)S(1)}, f32[12,8,1024]{2,1,0:T(8,128)S(1)}, u32[]{:S(2)}, u32[]{:S(2)}) %collective-permute-start.5) | collective-permute-done | bytes 393248 | tf_op jit(solution)/shard_map/ppermute | solution.py:480
  11.5 1.3 %collective-permute-start.7 = (f32[6,8,1024]{2,1,0:T(8,128)S(1)}, f32[6,8,1024]{2,1,0:T(8,128)S(1)}, u32[]{:S(2)}, u32[]{:S(2)}) collective-permute-start(f32[6,8,1024]{2,1,0:T(8,128)S(1)} %shard_map.177.rest_0_), channel_id=1, source_target_pairs={{0,16},{1,17},{2,18},{3,19},{4,12},{5,13},{6,14},{7,15},{8,24},{9,... | collective-permute-start | bytes 589832 | tf_op jit(solution)/shard_map/ppermute | solution.py:480
  12.8 2.7 %ready.1 = (f32[16,8,4096]{2,1,0:T(8,128)}, f32[6,64,128]{2,1,0:T(8,128)S(1)}, f32[8]{0:T(128)S(1)}, s32[40]{0:T(128)S(1)}, s32[1]{0:T(128)}) custom-call(s32[4,2]{1,0:T(4,128)S(1)} %copy.24.tiles, s32[1024]{0:T(1024)S(1)} %copy-done.15, s32[128,128]{1,0:T(8,128)S(1)} %copy-done.12, f32[64,128]{1,0:T(8,128)S(1)} %copy-done.13, ...), custom_call_target="tpu_custom_call" | custom-call | tf_op jit(solution)/shard_map/ready/pallas_call | solution.py:548
  15.5 0.2 collective-permute-done.8.got
  15.8 0.0 copy-start
  15.8 1.3 %collective-permute-start.9 = (f32[6,8,1024]{2,1,0:T(8,128)S(1)}, f32[6,8,1024]{2,1,0:T(8,128)S(1)}, u32[]{:S(2)}, u32[]{:S(2)}) collective-permute-start(f32[6,8,1024]{2,1,0:T(8,128)S(1)} %shard_map.178.rest_0_), channel_id=1, source_target_pairs={{0,16},{1,17},{2,18},{3,19},{4,12},{5,13},{6,14},{7,15},{8,24},{9,... | collective-permute-start | bytes 589832 | tf_op jit(solution)/shard_map/ppermute | solution.py:480
  17.1 1.2 %collective-permute-start.12 = (f32[4,8,2048]{2,1,0:T(8,128)S(1)}, f32[4,8,2048]{2,1,0:T(8,128)S(1)}, u32[]{:S(2)}, u32[]{:S(2)}) collective-permute-start(f32[4,8,2048]{2,1,0:T(8,128)S(1)} %get-tuple-element.118.rest_0_), channel_id=1, source_target_pairs={{0,8},{1,9},{2,10},{3,11},{4,20},{5,21},{6,22},{7,23},{8,0},{9,1},... | collective-permute-start | bytes 786440 | tf_op jit(solution)/shard_map/ppermute | solution.py:480
  18.3 0.2 collective-permute-done.7.passed
  18.6 3.8 %collective-permute-start.10 = (f32[6,8,1024]{2,1,0:T(8,128)S(1)}, f32[6,8,1024]{2,1,0:T(8,128)S(1)}, u32[]{:S(2)}, u32[]{:S(2)}) collective-permute-start(f32[6,8,1024]{2,1,0:T(8,128)S(1)} %shard_map.179.rest_0_.refs_0_), channel_id=1, source_target_pairs={{0,4},{1,5},{2,6},{3,7},{4,0},{5,1},{6,2},{7,3},{8,12},{9,13},{10,... | collective-permute-start | bytes 589832 | tf_op jit(solution)/shard_map/ppermute | solution.py:480
  22.5 2.8 %collective-permute-start.11 = (f32[6,8,1024]{2,1,0:T(8,128)S(1)}, f32[6,8,1024]{2,1,0:T(8,128)S(1)}, u32[]{:S(2)}, u32[]{:S(2)}) collective-permute-start(f32[6,8,1024]{2,1,0:T(8,128)S(1)} %shard_map.180.rest_0_.refs_1_), channel_id=1, source_target_pairs={{0,4},{1,5},{2,6},{3,7},{4,0},{5,1},{6,2},{7,3},{8,12},{9,13},{10,... | collective-permute-start | bytes 589832 | tf_op jit(solution)/shard_map/ppermute | solution.py:480
  25.2 1.1 %collective-permute-start.20 = (f32[2,8,2048]{2,1,0:T(8,128)S(1)}, f32[2,8,2048]{2,1,0:T(8,128)S(1)}, u32[]{:S(2)}, u32[]{:S(2)}) collective-permute-start(f32[2,8,2048]{2,1,0:T(8,128)S(1)} %shard_map.181.refs_10_), channel_id=1, source_target_pairs={{0,16},{1,17},{2,18},{3,19},{4,12},{5,13},{6,14},{7,15},{8,24},{9,... | collective-permute-start | bytes 393224 | tf_op jit(solution)/shard_map/ppermute | solution.py:480
  26.4 1.0 %shard_map.182 = (f32[64,256]{1,0:T(8,128)S(1)}, f32[64,256]{1,0:T(8,128)S(1)}, f32[64,256]{1,0:T(8,128)S(1)}, f32[512,256]{1,0:T(8,128)S(1)}, f32[64,256]{1,0:T(8,128)S(1)}, /*index=5*/f32[64,256]{1,0:T(8,128)S(1)}) custom-call(f32[6,8,1024]{2,1,0:T(8,128)S(1)} %shard_map.179.rest_0_.refs_0_, f32[6,8,1024]{2,1,0:T(8,128)S(1)} %shard_map.180.rest_0_.refs_1_, ...), custom_call_target="tpu_custom_call" | custom-call | tf_op jit(solution)/shard_map/pallas_call | solution.py:587
  27.5 1.6 %collective-permute-done.20.passed = f32[2,8,2048]{2,1,0:T(8,128)S(1)} collective-permute-done((f32[2,8,2048]{2,1,0:T(8,128)S(1)}, f32[2,8,2048]{2,1,0:T(8,128)S(1)}, u32[]{:S(2)}, u32[]{:S(2)}) %collective-permute-start.20) | collective-permute-done | bytes 131104 | tf_op jit(solution)/shard_map/ppermute | solution.py:480
  29.1 3.2 %collective-permute-start.21 = (f32[2,8,2048]{2,1,0:T(8,128)S(1)}, f32[2,8,2048]{2,1,0:T(8,128)S(1)}, u32[]{:S(2)}, u32[]{:S(2)}) collective-permute-start(f32[2,8,2048]{2,1,0:T(8,128)S(1)} %shard_map.185.refs_4_), channel_id=1, source_target_pairs={{0,4},{1,5},{2,6},{3,7},{4,0},{5,1},{6,2},{7,3},{8,12},{9,13},{10,... | collective-permute-start | bytes 393224 | tf_op jit(solution)/shard_map/ppermute | solution.py:480
  32.3 1.3 %collective-permute-start.13 = (f32[64,256]{1,0:T(8,128)S(1)}, f32[64,256]{1,0:T(8,128)S(1)}, u32[]{:S(2)}, u32[]{:S(2)}) collective-permute-start(f32[64,256]{1,0:T(8,128)S(1)} %get-tuple-element.126), channel_id=1, source_target_pairs={{0,1},{1,0},{2,3},{3,2},{4,5},{5,4},{6,7},{7,6},{8,9},{9,8},{10,11... | collective-permute-start | bytes 196616 | tf_op jit(solution)/shard_map/ppermute | solution.py:484
  33.6 0.1 collective-permute-start.14
  33.7 1.3 %collective-permute-start.15 = (f32[64,256]{1,0:T(8,128)S(1)}, f32[64,256]{1,0:T(8,128)S(1)}, u32[]{:S(2)}, u32[]{:S(2)}) collective-permute-start(f32[64,256]{1,0:T(8,128)S(1)} %get-tuple-element.128), channel_id=1, source_target_pairs={{0,3},{1,2},{2,1},{3,0},{4,7},{5,6},{6,5},{7,4},{8,11},{9,10},{10,... | collective-permute-start | bytes 196616 | tf_op jit(solution)/shard_map/ppermute | solution.py:484
  35.0 1.0 %shard_map.186 = (f32[64,256]{1,0:T(8,128)S(1)}, f32[64,256]{1,0:T(8,128)S(1)}, f32[64,256]{1,0:T(8,128)S(1)}, f32[512,256]{1,0:T(8,128)S(1)}, f32[64,256]{1,0:T(8,128)S(1)}, /*index=5*/f32[64,256]{1,0:T(8,128)S(1)}) custom-call(f32[6,8,1024]{2,1,0:T(8,128)S(1)} %shard_map.179.rest_0_.refs_0_, f32[6,8,1024]{2,1,0:T(8,128)S(1)} %shard_map.180.rest_0_.refs_1_, ...), custom_call_target="tpu_custom_call" | custom-call | tf_op jit(solution)/shard_map/pallas_call | solution.py:587
  36.0 2.3 %collective-permute-start.22 = (f32[64,256]{1,0:T(8,128)S(1)}, f32[64,256]{1,0:T(8,128)S(1)}, u32[]{:S(2)}, u32[]{:S(2)}) collective-permute-start(f32[64,256]{1,0:T(8,128)S(1)} %get-tuple-element.132), channel_id=1, source_target_pairs={{0,1},{1,0},{2,3},{3,2},{4,5},{5,4},{6,7},{7,6},{8,9},{9,8},{10,11... | collective-permute-start | bytes 196616 | tf_op jit(solution)/shard_map/ppermute | solution.py:484
  38.3 1.3 %collective-permute-start.24 = (f32[64,256]{1,0:T(8,128)S(1)}, f32[64,256]{1,0:T(8,128)S(1)}, u32[]{:S(2)}, u32[]{:S(2)}) collective-permute-start(f32[64,256]{1,0:T(8,128)S(1)} %get-tuple-element.134), channel_id=1, source_target_pairs={{0,3},{1,2},{2,1},{3,0},{4,7},{5,6},{6,5},{7,4},{8,11},{9,10},{10,... | collective-permute-start | bytes 196616 | tf_op jit(solution)/shard_map/ppermute | solution.py:484
  39.5 1.5 %collective-permute-done.15.refs_6_ = f32[64,256]{1,0:T(8,128)S(1)} collective-permute-done((f32[64,256]{1,0:T(8,128)S(1)}, f32[64,256]{1,0:T(8,128)S(1)}, u32[]{:S(2)}, u32[]{:S(2)}) %collective-permute-start.15) | collective-permute-done | bytes 65568 | tf_op jit(solution)/shard_map/ppermute | solution.py:484
  41.1 1.8 %shard_map.183.refs_18_ = f32[8,4096]{1,0:T(8,128)S(1)} custom-call(f32[8]{0:T(128)S(1)} %get-tuple-element.121.flags, f32[6,8,1024]{2,1,0:T(8,128)S(1)} %shard_map.179.rest_0_.refs_0_, f32[6,8,1024]{2,1,0:T(8,128)S(1)} %shard_map.180.rest_0_.refs_1_, f32[6,8,1024]{2,1,0:T(8,128)S(1)} %collective-permute-done.10.refs_2_, ...), custom_call_target="tpu_custom_call" | custom-call | tf_op jit(solution)/shard_map/pallas_call | solution.py:605
  42.8 1.3 %collective-permute-start.17 = (f32[8,4096]{1,0:T(8,128)S(1)}, f32[8,4096]{1,0:T(8,128)S(1)}, u32[]{:S(2)}, u32[]{:S(2)}) collective-permute-start(f32[8,4096]{1,0:T(8,128)S(1)} %shard_map.183.refs_18_), channel_id=1, source_target_pairs={{0,16},{1,17},{2,18},{3,19},{4,12},{5,13},{6,14},{7,15},{8,24},{9,... | collective-permute-start | bytes 393224 | tf_op jit(solution)/shard_map/ppermute | solution.py:480
  44.1 0.2 collective-permute-start.16
  44.3 2.0 %collective-permute-done.24.refs_6_ = f32[64,256]{1,0:T(8,128)S(1)} collective-permute-done((f32[64,256]{1,0:T(8,128)S(1)}, f32[64,256]{1,0:T(8,128)S(1)}, u32[]{:S(2)}, u32[]{:S(2)}) %collective-permute-start.24) | collective-permute-done | bytes 65568 | tf_op jit(solution)/shard_map/ppermute | solution.py:484
  46.3 1.7 %shard_map.187 = f32[8,4096]{1,0:T(8,128)S(1)} custom-call(f32[8]{0:T(128)S(1)} %get-tuple-element.121.flags, f32[6,8,1024]{2,1,0:T(8,128)S(1)} %shard_map.179.rest_0_.refs_0_, f32[6,8,1024]{2,1,0:T(8,128)S(1)} %shard_map.180.rest_0_.refs_1_, f32[6,8,1024]{2,1,0:T(8,128)S(1)} %collective-permute-done.10.refs_2_, ...), custom_call_target="tpu_custom_call" | custom-call | tf_op jit(solution)/shard_map/pallas_call | solution.py:605
  48.1 1.3 %collective-permute-start.26 = (f32[8,4096]{1,0:T(8,128)S(1)}, f32[8,4096]{1,0:T(8,128)S(1)}, u32[]{:S(2)}, u32[]{:S(2)}) collective-permute-start(f32[8,4096]{1,0:T(8,128)S(1)} %shard_map.187), channel_id=1, source_target_pairs={{0,16},{1,17},{2,18},{3,19},{4,12},{5,13},{6,14},{7,15},{8,24},{9,... | collective-permute-start | bytes 393224 | tf_op jit(solution)/shard_map/ppermute | solution.py:480
  49.4 0.2 collective-permute-start.25
  49.6 4.5 %collective-permute-start.19 = (f32[2,8,4096]{2,1,0:T(8,128)S(1)}, f32[2,8,4096]{2,1,0:T(8,128)S(1)}, u32[]{:S(2)}, u32[]{:S(2)}) collective-permute-start(f32[2,8,4096]{2,1,0:T(8,128)S(1)} %shard_map.184), channel_id=1, source_target_pairs={{0,4},{1,5},{2,6},{3,7},{4,0},{5,1},{6,2},{7,3},{8,12},{9,13},{10,... | collective-permute-start | bytes 786440 | tf_op jit(solution)/shard_map/ppermute | solution.py:480
  54.2 4.0 %collective-permute-start.28 = (f32[2,8,4096]{2,1,0:T(8,128)S(1)}, f32[2,8,4096]{2,1,0:T(8,128)S(1)}, u32[]{:S(2)}, u32[]{:S(2)}) collective-permute-start(f32[2,8,4096]{2,1,0:T(8,128)S(1)} %shard_map.188), channel_id=1, source_target_pairs={{0,4},{1,5},{2,6},{3,7},{4,0},{5,1},{6,2},{7,3},{8,12},{9,13},{10,... | collective-permute-start | bytes 786440 | tf_op jit(solution)/shard_map/ppermute | solution.py:480
  58.1 0.1 collective-permute-start.18
  58.2 0.4 collective-permute-start.27
  59.3 0.2 collective-permute-done.18
  59.5 0.2 collective-permute-done.27
  59.7 0.7 %conditional.1 = (f32[16,8,4096]{2,1,0:T(8,128)}) conditional(s32[]{:T(128)} %bitcast, (s32[40]{0:T(128)S(1)}, f32[8,4096]{1,0:T(8,128)S(1)}, f32[8,4096]{1,0:T(8,128)S(1)}, f32[8,4096]{1,0:T(8,128)S(1)}, f32[8,4096]{1,0:T(8,128)S(1)}, /*index=5*/f32[2,8,4096]{2,1,0:T(8,128)S(1)}, f32[8,4096]{1,0:T(8,128)S(1)}, f32[8,4096]{1,0:T(8,128)S(1)}, ...), branch_computations={%region_0.0_spmd, %region_1.0_spmd} | conditional | bytes 2097320 | solution.py:649
  59.7 0.7 %place.2 = f32[16,8,4096]{2,1,0:T(8,128)} custom-call(s32[40]{0:T(128)S(1)} %get-tuple-element.56.match, f32[8,4096]{1,0:T(8,128)S(1)} %get-tuple-element.57.refs_0_, f32[8,4096]{1,0:T(8,128)S(1)} %get-tuple-element.58.refs_1_, f32[8,4096]{1,0:T(8,128)S(1)} %get-tuple-element.59.refs_2_, ...), custom_call_target="tpu_custom_call", output_to_operand_aliasing={{}: (11, {})} | custom-call | tf_op jit(solution)/shard_map/cond/branch_0_fun/place/pallas_call | solution.py:631
  (57 shorter events, 0.3 us)
Async XLA Ops:
  0.0 2.7 %copy-start.15 = (s32[1024]{0:T(1024)S(1)}, s32[1024]{0:T(1024)}, u32[]{:S(2)}) copy-start(s32[1024]{0:T(1024)} %constant.31.clone.host) | copy-start | bytes 12292
  0.0 2.6 %copy-start.16 = (s32[4,2]{0,1:T(2,128)S(1)}, s32[4,2]{0,1:T(2,128)}, u32[]{:S(2)}) copy-start(s32[4,2]{0,1:T(2,128)} %param.22) | copy-start | bytes 100
  0.0 2.7 %copy-start.11 = (f32[128,128]{1,0:T(8,128)S(1)}, f32[128,128]{1,0:T(8,128)}, u32[]{:S(2)}) copy-start(f32[128,128]{1,0:T(8,128)} %rotation.1) | copy-start | bytes 196612
  1.8 2.3 %collective-permute-start.4 = (f32[16,8,1024]{2,1,0:T(8,128)S(1)}, f32[16,8,1024]{2,1,0:T(8,128)S(1)}, u32[]{:S(2)}, u32[]{:S(2)}) collective-permute-start(f32[16,8,1024]{2,1,0:T(8,128)S(1)} %get-tuple-element.113), channel_id=1, source_target_pairs={{0,4},{1,5},{2,6},{3,7},{4,0},{5,1},{6,2},{7,3},{8,12},{9,13},{10,... | collective-permute-start | bytes 1572872 | tf_op jit(solution)/shard_map/ppermute | solution.py:480
  2.5 3.3 %collective-permute-start.6 = (f32[16,8,1024]{2,1,0:T(8,128)S(1)}, f32[16,8,1024]{2,1,0:T(8,128)S(1)}, u32[]{:S(2)}, u32[]{:S(2)}) collective-permute-start(f32[16,8,1024]{2,1,0:T(8,128)S(1)} %get-tuple-element.109.after), channel_id=1, source_target_pairs={{0,4},{1,5},{2,6},{3,7},{4,0},{5,1},{6,2},{7,3},{8,12},{9,13},{10,... | collective-permute-start | bytes 1572872 | tf_op jit(solution)/shard_map/ppermute | solution.py:480
  4.5 7.0 %collective-permute-start.5 = (f32[12,8,1024]{2,1,0:T(8,128)S(1)}, f32[12,8,1024]{2,1,0:T(8,128)S(1)}, u32[]{:S(2)}, u32[]{:S(2)}) collective-permute-start(f32[12,8,1024]{2,1,0:T(8,128)S(1)} %get-tuple-element.115.rest_2_), channel_id=1, source_target_pairs={{0,8},{1,9},{2,10},{3,11},{4,20},{5,21},{6,22},{7,23},{8,0},{9,1},... | collective-permute-start | bytes 1179656 | tf_op jit(solution)/shard_map/ppermute | solution.py:480
  6.3 6.5 %copy-start.12 = (s32[128,128]{1,0:T(8,128)S(1)}, s32[128,128]{1,0:T(8,128)}, u32[]{:S(2)}) copy-start(s32[128,128]{1,0:T(8,128)} %mask.1) | copy-start | bytes 196612
  6.4 6.5 %copy-start.13 = (f32[64,128]{1,0:T(8,128)S(1)}, f32[64,128]{1,0:T(8,128)}, u32[]{:S(2)}) copy-start(f32[64,128]{1,0:T(8,128)} %constant.32.clone.log_r) | copy-start | bytes 98308
  6.4 9.4 %collective-permute-start.8 = (f32[12,8,1024]{2,1,0:T(8,128)S(1)}, f32[12,8,1024]{2,1,0:T(8,128)S(1)}, u32[]{:S(2)}, u32[]{:S(2)}) collective-permute-start(f32[12,8,1024]{2,1,0:T(8,128)S(1)} %get-tuple-element.117.rest_4_), channel_id=1, source_target_pairs={{0,8},{1,9},{2,10},{3,11},{4,20},{5,21},{6,22},{7,23},{8,0},{9,1},... | collective-permute-start | bytes 1179656 | tf_op jit(solution)/shard_map/ppermute | solution.py:480
  11.5 7.0 %collective-permute-start.7 = (f32[6,8,1024]{2,1,0:T(8,128)S(1)}, f32[6,8,1024]{2,1,0:T(8,128)S(1)}, u32[]{:S(2)}, u32[]{:S(2)}) collective-permute-start(f32[6,8,1024]{2,1,0:T(8,128)S(1)} %shard_map.177.rest_0_), channel_id=1, source_target_pairs={{0,16},{1,17},{2,18},{3,19},{4,12},{5,13},{6,14},{7,15},{8,24},{9,... | collective-permute-start | bytes 589832 | tf_op jit(solution)/shard_map/ppermute | solution.py:480
  15.8 10.6 %copy-start = (bf16[2,256,256]{2,1,0:T(8,128)(2,1)S(1)}, bf16[2,256,256]{2,1,0:T(8,128)(2,1)}, u32[]{:S(2)}) copy-start(bf16[2,256,256]{2,1,0:T(8,128)(2,1)} %constant.38.clone.refs_5_.refs_7_) | copy-start | bytes 786436
  15.8 10.6 %copy-start.1 = (bf16[2,256,256]{2,1,0:T(8,128)(2,1)S(1)}, bf16[2,256,256]{2,1,0:T(8,128)(2,1)}, u32[]{:S(2)}) copy-start(bf16[2,256,256]{2,1,0:T(8,128)(2,1)} %constant.37.clone.refs_4_.refs_6_) | copy-start | bytes 786436
  15.8 10.6 %copy-start.2 = (f32[512,128]{1,0:T(8,128)S(1)}, f32[512,128]{1,0:T(8,128)}, u32[]{:S(2)}) copy-start(f32[512,128]{1,0:T(8,128)} %constant.33.clone.refs_8_.refs_10_) | copy-start | bytes 786436
  15.8 10.6 %copy-start.6 = (bf16[256,256]{1,0:T(8,128)(2,1)S(1)}, bf16[256,256]{1,0:T(8,128)(2,1)}, u32[]{:S(2)}) copy-start(bf16[256,256]{1,0:T(8,128)(2,1)} %constant.42.clone.refs_7_.refs_9_) | copy-start | bytes 393220
  15.8 10.6 %copy-start.7 = (bf16[256,256]{1,0:T(8,128)(2,1)S(1)}, bf16[256,256]{1,0:T(8,128)(2,1)}, u32[]{:S(2)}) copy-start(bf16[256,256]{1,0:T(8,128)(2,1)} %constant.41.clone.refs_6_.refs_8_) | copy-start | bytes 393220
  15.8 6.6 %collective-permute-start.9 = (f32[6,8,1024]{2,1,0:T(8,128)S(1)}, f32[6,8,1024]{2,1,0:T(8,128)S(1)}, u32[]{:S(2)}, u32[]{:S(2)}) collective-permute-start(f32[6,8,1024]{2,1,0:T(8,128)S(1)} %shard_map.178.rest_0_), channel_id=1, source_target_pairs={{0,16},{1,17},{2,18},{3,19},{4,12},{5,13},{6,14},{7,15},{8,24},{9,... | collective-permute-start | bytes 589832 | tf_op jit(solution)/shard_map/ppermute | solution.py:480
  17.1 8.1 %collective-permute-start.12 = (f32[4,8,2048]{2,1,0:T(8,128)S(1)}, f32[4,8,2048]{2,1,0:T(8,128)S(1)}, u32[]{:S(2)}, u32[]{:S(2)}) collective-permute-start(f32[4,8,2048]{2,1,0:T(8,128)S(1)} %get-tuple-element.118.rest_0_), channel_id=1, source_target_pairs={{0,8},{1,9},{2,10},{3,11},{4,20},{5,21},{6,22},{7,23},{8,0},{9,1},... | collective-permute-start | bytes 786440 | tf_op jit(solution)/shard_map/ppermute | solution.py:480
  18.6 7.8 %collective-permute-start.10 = (f32[6,8,1024]{2,1,0:T(8,128)S(1)}, f32[6,8,1024]{2,1,0:T(8,128)S(1)}, u32[]{:S(2)}, u32[]{:S(2)}) collective-permute-start(f32[6,8,1024]{2,1,0:T(8,128)S(1)} %shard_map.179.rest_0_.refs_0_), channel_id=1, source_target_pairs={{0,4},{1,5},{2,6},{3,7},{4,0},{5,1},{6,2},{7,3},{8,12},{9,13},{10,... | collective-permute-start | bytes 589832 | tf_op jit(solution)/shard_map/ppermute | solution.py:480
  22.5 3.9 %collective-permute-start.11 = (f32[6,8,1024]{2,1,0:T(8,128)S(1)}, f32[6,8,1024]{2,1,0:T(8,128)S(1)}, u32[]{:S(2)}, u32[]{:S(2)}) collective-permute-start(f32[6,8,1024]{2,1,0:T(8,128)S(1)} %shard_map.180.rest_0_.refs_1_), channel_id=1, source_target_pairs={{0,4},{1,5},{2,6},{3,7},{4,0},{5,1},{6,2},{7,3},{8,12},{9,13},{10,... | collective-permute-start | bytes 589832 | tf_op jit(solution)/shard_map/ppermute | solution.py:480
  25.2 3.9 %collective-permute-start.20 = (f32[2,8,2048]{2,1,0:T(8,128)S(1)}, f32[2,8,2048]{2,1,0:T(8,128)S(1)}, u32[]{:S(2)}, u32[]{:S(2)}) collective-permute-start(f32[2,8,2048]{2,1,0:T(8,128)S(1)} %shard_map.181.refs_10_), channel_id=1, source_target_pairs={{0,16},{1,17},{2,18},{3,19},{4,12},{5,13},{6,14},{7,15},{8,24},{9,... | collective-permute-start | bytes 393224 | tf_op jit(solution)/shard_map/ppermute | solution.py:480
  27.4 13.6 %copy-start.3 = (bf16[2,256,256]{2,1,0:T(8,128)(2,1)S(1)}, bf16[2,256,256]{2,1,0:T(8,128)(2,1)}, u32[]{:S(2)}) copy-start(bf16[2,256,256]{2,1,0:T(8,128)(2,1)} %constant.40.clone.refs_8_) | copy-start | bytes 786436
  27.4 13.6 %copy-start.4 = (bf16[2,256,256]{2,1,0:T(8,128)(2,1)S(1)}, bf16[2,256,256]{2,1,0:T(8,128)(2,1)}, u32[]{:S(2)}) copy-start(bf16[2,256,256]{2,1,0:T(8,128)(2,1)} %constant.39.clone.refs_7_) | copy-start | bytes 786436
  27.5 13.6 %copy-start.5 = (f32[512,128]{1,0:T(8,128)S(1)}, f32[512,128]{1,0:T(8,128)}, u32[]{:S(2)}) copy-start(f32[512,128]{1,0:T(8,128)} %constant.34.clone.refs_11_) | copy-start | bytes 786436
  27.5 13.6 %copy-start.8 = (bf16[256,256]{1,0:T(8,128)(2,1)S(1)}, bf16[256,256]{1,0:T(8,128)(2,1)}, u32[]{:S(2)}) copy-start(bf16[256,256]{1,0:T(8,128)(2,1)} %constant.44.clone.refs_10_) | copy-start | bytes 393220
  27.5 13.6 %copy-start.9 = (bf16[256,256]{1,0:T(8,128)(2,1)S(1)}, bf16[256,256]{1,0:T(8,128)(2,1)}, u32[]{:S(2)}) copy-start(bf16[256,256]{1,0:T(8,128)(2,1)} %constant.43.clone.refs_9_) | copy-start | bytes 393220
  27.5 13.6 %copy-start.10 = (f32[3,64,128]{2,1,0:T(8,128)S(1)}, f32[3,64,128]{2,1,0:T(8,128)}, u32[]{:S(2)}) copy-start(f32[3,64,128]{2,1,0:T(8,128)} %constant.36.clone.refs_14_) | copy-start | bytes 294916
  27.5 13.6 %copy-start.14 = (f32[2,8,128]{2,1,0:T(8,128)S(1)}, f32[2,8,128]{2,1,0:T(8,128)}, u32[]{:S(2)}) copy-start(f32[2,8,128]{2,1,0:T(8,128)} %constant.35.clone.refs_12_) | copy-start | bytes 24580
  29.1 5.8 %collective-permute-start.21 = (f32[2,8,2048]{2,1,0:T(8,128)S(1)}, f32[2,8,2048]{2,1,0:T(8,128)S(1)}, u32[]{:S(2)}, u32[]{:S(2)}) collective-permute-start(f32[2,8,2048]{2,1,0:T(8,128)S(1)} %shard_map.185.refs_4_), channel_id=1, source_target_pairs={{0,4},{1,5},{2,6},{3,7},{4,0},{5,1},{6,2},{7,3},{8,12},{9,13},{10,... | collective-permute-start | bytes 393224 | tf_op jit(solution)/shard_map/ppermute | solution.py:480
  32.3 5.9 %collective-permute-start.13 = (f32[64,256]{1,0:T(8,128)S(1)}, f32[64,256]{1,0:T(8,128)S(1)}, u32[]{:S(2)}, u32[]{:S(2)}) collective-permute-start(f32[64,256]{1,0:T(8,128)S(1)} %get-tuple-element.126), channel_id=1, source_target_pairs={{0,1},{1,0},{2,3},{3,2},{4,5},{5,4},{6,7},{7,6},{8,9},{9,8},{10,11... | collective-permute-start | bytes 196616 | tf_op jit(solution)/shard_map/ppermute | solution.py:484
  33.6 5.9 %collective-permute-start.14 = (f32[64,256]{1,0:T(8,128)S(1)}, f32[64,256]{1,0:T(8,128)S(1)}, u32[]{:S(2)}, u32[]{:S(2)}) collective-permute-start(f32[64,256]{1,0:T(8,128)S(1)} %get-tuple-element.127), channel_id=1, source_target_pairs={{0,2},{1,3},{2,0},{3,1},{4,6},{5,7},{6,4},{7,5},{8,10},{9,11},{10,... | collective-permute-start | bytes 196616 | tf_op jit(solution)/shard_map/ppermute | solution.py:484
  33.7 7.3 %collective-permute-start.15 = (f32[64,256]{1,0:T(8,128)S(1)}, f32[64,256]{1,0:T(8,128)S(1)}, u32[]{:S(2)}, u32[]{:S(2)}) collective-permute-start(f32[64,256]{1,0:T(8,128)S(1)} %get-tuple-element.128), channel_id=1, source_target_pairs={{0,3},{1,2},{2,1},{3,0},{4,7},{5,6},{6,5},{7,4},{8,11},{9,10},{10,... | collective-permute-start | bytes 196616 | tf_op jit(solution)/shard_map/ppermute | solution.py:484
  36.0 8.3 %collective-permute-start.22 = (f32[64,256]{1,0:T(8,128)S(1)}, f32[64,256]{1,0:T(8,128)S(1)}, u32[]{:S(2)}, u32[]{:S(2)}) collective-permute-start(f32[64,256]{1,0:T(8,128)S(1)} %get-tuple-element.132), channel_id=1, source_target_pairs={{0,1},{1,0},{2,3},{3,2},{4,5},{5,4},{6,7},{7,6},{8,9},{9,8},{10,11... | collective-permute-start | bytes 196616 | tf_op jit(solution)/shard_map/ppermute | solution.py:484
  38.2 6.1 %collective-permute-start.23 = (f32[64,256]{1,0:T(8,128)S(1)}, f32[64,256]{1,0:T(8,128)S(1)}, u32[]{:S(2)}, u32[]{:S(2)}) collective-permute-start(f32[64,256]{1,0:T(8,128)S(1)} %get-tuple-element.133), channel_id=1, source_target_pairs={{0,2},{1,3},{2,0},{3,1},{4,6},{5,7},{6,4},{7,5},{8,10},{9,11},{10,... | collective-permute-start | bytes 196616 | tf_op jit(solution)/shard_map/ppermute | solution.py:484
  38.3 8.1 %collective-permute-start.24 = (f32[64,256]{1,0:T(8,128)S(1)}, f32[64,256]{1,0:T(8,128)S(1)}, u32[]{:S(2)}, u32[]{:S(2)}) collective-permute-start(f32[64,256]{1,0:T(8,128)S(1)} %get-tuple-element.134), channel_id=1, source_target_pairs={{0,3},{1,2},{2,1},{3,0},{4,7},{5,6},{6,5},{7,4},{8,11},{9,10},{10,... | collective-permute-start | bytes 196616 | tf_op jit(solution)/shard_map/ppermute | solution.py:484
  42.8 6.8 %collective-permute-start.17 = (f32[8,4096]{1,0:T(8,128)S(1)}, f32[8,4096]{1,0:T(8,128)S(1)}, u32[]{:S(2)}, u32[]{:S(2)}) collective-permute-start(f32[8,4096]{1,0:T(8,128)S(1)} %shard_map.183.refs_18_), channel_id=1, source_target_pairs={{0,16},{1,17},{2,18},{3,19},{4,12},{5,13},{6,14},{7,15},{8,24},{9,... | collective-permute-start | bytes 393224 | tf_op jit(solution)/shard_map/ppermute | solution.py:480
  44.1 5.5 %collective-permute-start.16 = (f32[8,4096]{1,0:T(8,128)S(1)}, f32[8,4096]{1,0:T(8,128)S(1)}, u32[]{:S(2)}, u32[]{:S(2)}) collective-permute-start(f32[8,4096]{1,0:T(8,128)S(1)} %shard_map.183.refs_18_), channel_id=1, source_target_pairs={{0,8},{1,9},{2,10},{3,11},{4,20},{5,21},{6,22},{7,23},{8,0},{9,1},... | collective-permute-start | bytes 393224 | tf_op jit(solution)/shard_map/ppermute | solution.py:480
  48.1 6.1 %collective-permute-start.26 = (f32[8,4096]{1,0:T(8,128)S(1)}, f32[8,4096]{1,0:T(8,128)S(1)}, u32[]{:S(2)}, u32[]{:S(2)}) collective-permute-start(f32[8,4096]{1,0:T(8,128)S(1)} %shard_map.187), channel_id=1, source_target_pairs={{0,16},{1,17},{2,18},{3,19},{4,12},{5,13},{6,14},{7,15},{8,24},{9,... | collective-permute-start | bytes 393224 | tf_op jit(solution)/shard_map/ppermute | solution.py:480
  49.4 4.8 %collective-permute-start.25 = (f32[8,4096]{1,0:T(8,128)S(1)}, f32[8,4096]{1,0:T(8,128)S(1)}, u32[]{:S(2)}, u32[]{:S(2)}) collective-permute-start(f32[8,4096]{1,0:T(8,128)S(1)} %shard_map.187), channel_id=1, source_target_pairs={{0,8},{1,9},{2,10},{3,11},{4,20},{5,21},{6,22},{7,23},{8,0},{9,1},... | collective-permute-start | bytes 393224 | tf_op jit(solution)/shard_map/ppermute | solution.py:480
  49.6 10.1 %collective-permute-start.19 = (f32[2,8,4096]{2,1,0:T(8,128)S(1)}, f32[2,8,4096]{2,1,0:T(8,128)S(1)}, u32[]{:S(2)}, u32[]{:S(2)}) collective-permute-start(f32[2,8,4096]{2,1,0:T(8,128)S(1)} %shard_map.184), channel_id=1, source_target_pairs={{0,4},{1,5},{2,6},{3,7},{4,0},{5,1},{6,2},{7,3},{8,12},{9,13},{10,... | collective-permute-start | bytes 786440 | tf_op jit(solution)/shard_map/ppermute | solution.py:480
  54.2 5.5 %collective-permute-start.28 = (f32[2,8,4096]{2,1,0:T(8,128)S(1)}, f32[2,8,4096]{2,1,0:T(8,128)S(1)}, u32[]{:S(2)}, u32[]{:S(2)}) collective-permute-start(f32[2,8,4096]{2,1,0:T(8,128)S(1)} %shard_map.188), channel_id=1, source_target_pairs={{0,4},{1,5},{2,6},{3,7},{4,0},{5,1},{6,2},{7,3},{8,12},{9,13},{10,... | collective-permute-start | bytes 786440 | tf_op jit(solution)/shard_map/ppermute | solution.py:480
  58.1 1.3 %collective-permute-start.18 = (f32[8,4096]{1,0:T(8,128)S(1)}, f32[8,4096]{1,0:T(8,128)S(1)}, u32[]{:S(2)}, u32[]{:S(2)}) collective-permute-start(f32[8,4096]{1,0:T(8,128)S(1)} %shard_map.183.refs_18_), channel_id=1, source_target_pairs={{0,4},{1,5},{2,6},{3,7},{4,0},{5,1},{6,2},{7,3},{8,12},{9,13},{10,... | collective-permute-start | bytes 393224 | tf_op jit(solution)/shard_map/ppermute | solution.py:480
  58.2 1.5 %collective-permute-start.27 = (f32[8,4096]{1,0:T(8,128)S(1)}, f32[8,4096]{1,0:T(8,128)S(1)}, u32[]{:S(2)}, u32[]{:S(2)}) collective-permute-start(f32[8,4096]{1,0:T(8,128)S(1)} %shard_map.187), channel_id=1, source_target_pairs={{0,4},{1,5},{2,6},{3,7},{4,0},{5,1},{6,2},{7,3},{8,12},{9,13},{10,... | collective-permute-start | bytes 393224 | tf_op jit(solution)/shard_map/ppermute | solution.py:480

commit v6 on v4

--- a/solution.py
+++ b/solution.py
@@ -223,7 +223,8 @@
     for u in range(pair):
         line = jnp.sum(jnp.where(row == a + at.core * pair + u, live, 0.0), axis=0, keepdims=True)
         for w in range(BLK):
-            flags[u * BLK + w] = jnp.sum(jnp.where(column == b + w, line, 0.0))
+            flag = jnp.sum(jnp.where(column == b + w, line, 0.0), axis=1, keepdims=True)
+            flags[u * BLK + w:u * BLK + w + 1, :] = jnp.broadcast_to(flag, (1, LANES))
     blocks = per_device // BLK
     parts = [0, at.bit_1, at.bit_2, 3, 0, at.bit_2, at.bit_1, 3]
     for n, flip in enumerate(parts):
@@ -406,6 +407,7 @@
         even, odd = work[:half, lanes], work[half:, lanes]
         rows = jnp.concatenate([even + odd, turned(even - odd)], axis=1)
         pot[:, q * 2 * LANES:(q + 1) * 2 * LANES] = dot3(split(rows), z)
+    live = [jnp.broadcast_to(flags[u * BLK + w:u * BLK + w + 1, :], (SUB, LANES)) for w in range(BLK)]
     for side, group in ((0, own), (1, other)):
         half = (core if side == 0 else 1 - core) * (len(own) * tiles)
         for n, ref in enumerate(group):
@@ -415,7 +417,7 @@
                 rows = pl.ds(pl.multiple_of(at * SUB, SUB), SUB)
                 total = None
                 for w in range(BLK):
-                    term = flags[u * BLK + w] * (pot[rows, w * LANES:(w + 1) * LANES] * ref[1 + w, :, lanes])
+                    term = live[w] * (pot[rows, w * LANES:(w + 1) * LANES] * ref[1 + w, :, lanes])
                     total = term if total is None else total + term
                 out[:, pl.ds(pl.multiple_of(at * LANES, LANES), LANES)] = -total
 
@@ -548,9 +550,9 @@
     empty, powers, flags, match, alone = pl.pallas_call(
         functools.partial(ready_kernel, per_device, n_grid),
         out_shape=(pltpu.HBM(shape, f32), jax.ShapeDtypeStruct((6, NY, LANES), f32),
-                   jax.ShapeDtypeStruct((pair * BLK,), f32), jax.ShapeDtypeStruct((blocks * 10,), jnp.int32),
+                   jax.ShapeDtypeStruct((pair * BLK, LANES), f32), jax.ShapeDtypeStruct((blocks * 10,), jnp.int32),
                    jax.ShapeDtypeStruct((1,), jnp.int32)),
-        in_specs=[SM, SM, VM, VM, ANY], out_specs=(HBM, VM, SM, SM, SM),
+        in_specs=[SM, SM, VM, VM, ANY], out_specs=(HBM, VM, VM, SM, SM),
         scratch_shapes=[pltpu.VMEM((pair, planes, width), f32), DMA((per_device // pair,))], name="ready",
         compiler_params=grant(4),
     )(tile_list, host, pair_mask, jnp.asarray(np.log(r), f32), step)
@@ -605,7 +607,7 @@
         terms.append(pl.pallas_call(
             functools.partial(backward_kernel, u, (CHUNKS, CHUNKS, len(received))),
             out_shape=jax.ShapeDtypeStruct((planes, width), f32),
-            in_specs=[SM] + [VM] * len(inputs) + [ANY] * len(last),
+            in_specs=[VM] * (1 + len(inputs)) + [ANY] * len(last),
             out_specs=VM,
             scratch_shapes=[pltpu.VMEM(cube, f32), wide],
             compiler_params=grant(16),

time: 60.6 us -> 59.5 us (0.982)
  the two profiles are of different devices: /device:TPU:17 before, /device:TPU:0 now
where the time goes in v6:
time: 59.5 us; the launch traced here: 58.5 us
  starting transfers between devices  23.9 us (40%)
  waiting for transfers between devices  20.9 us (35%)
  Pallas kernels  12.4 us (21%)
  between operations  1.03 us (2%)
    ppermute x19, waiting for transfers between devices, swap(): return lax.ppermute(x, axes, moves)  18.3 us
    ppermute x19, starting transfers between devices, swap(): return lax.ppermute(x, axes, moves)  15 us
    ppermute x6, starting transfers between devices, cross(): return lax.ppermute(x, axes, moves)  8.9 us
    pallas_call x1, Pallas kernels, tile_device(): pl.pallas_call(functools.partial(ready_kernel, per_device, n_grid), out_s...  2.69 us
    ppermute x6, waiting for transfers between devices, cross(): return lax.ppermute(x, axes, moves)  2.59 us
    pallas_call x2, Pallas kernels, tile_device(): pl.pallas_call(functools.partial(backward_kernel, u, (CHUNKS, CHUNKS, len...  2.39 us
    pallas_call x2, Pallas kernels, tile_device(): pl.pallas_call(functools.partial(forward_kernel, u, counts + (n_grid - 1,...  1.99 us
    pallas_call x1, Pallas kernels, tile_device(): pl.pallas_call(fetch_kernel, out_shape=[part] * (2 * CHUNKS), in_specs=[H...  1.73 us
  transfers between devices with their start and end apart: 25, of which 13 were waited for; matrix products, arithmetic and copies ran while one was open for 0% of the time, Pallas kernels for 17%

profile of v6, /device:TPU:0, one launch (start us, length us, event | category | flops | bytes accessed | tf_op | source)
XLA Modules:
  0.0 58.5 jit_solution(18162699890875042938)
XLA Ops:
  0.0 1.7 %fetch.1 = (f32[16,8,1024]{2,1,0:T(8,128)S(1)}, f32[16,8,1024]{2,1,0:T(8,128)S(1)}, f32[16,8,1024]{2,1,0:T(8,128)S(1)}, f32[16,8,1024]{2,1,0:T(8,128)S(1)}) custom-call(f32[16,8,4096]{2,1,0:T(8,128)} %source.1), custom_call_target="tpu_custom_call" | custom-call | tf_op jit(solution)/shard_map/fetch/pallas_call | solution.py:492
  1.7 0.6 collective-permute-start.4
  2.3 0.1 collective-permute-start.6
  2.4 0.1 copy.24.tiles
  2.5 1.0 %setup.1 = (bf16[256,256]{1,0:T(8,128)(2,1)S(1)}, bf16[256,256]{1,0:T(8,128)(2,1)S(1)}) custom-call(s32[4,2]{1,0:T(4,128)S(1)} %copy.24.tiles, s32[1024]{0:T(1024)S(1)} %copy-done.15, f32[128,128]{1,0:T(8,128)S(1)} %copy-done.11, f32[16,8,1024]{2,1,0:T(8,128)S(1)} %get-tuple-element.109.after), custom_call_target="tpu_custom_call" | custom-call | tf_op jit(solution)/shard_map/setup/pallas_call | solution.py:508
  3.5 0.3 collective-permute-done.4.rest_1_
  3.8 0.5 shard_map.174
  4.3 2.9 %collective-permute-start.5 = (f32[12,8,1024]{2,1,0:T(8,128)S(1)}, f32[12,8,1024]{2,1,0:T(8,128)S(1)}, u32[]{:S(2)}, u32[]{:S(2)}) collective-permute-start(f32[12,8,1024]{2,1,0:T(8,128)S(1)} %get-tuple-element.115.rest_2_), channel_id=1, source_target_pairs={{0,8},{1,9},{2,10},{3,11},{4,20},{5,21},{6,22},{7,23},{8,0},{9,1},... | collective-permute-start | bytes 1179656 | tf_op jit(solution)/shard_map/ppermute | solution.py:482
  7.3 0.5 shard_map.175
  7.8 0.2 collective-permute-start.8
  8.0 0.7 %shard_map.176 = (f32[4,8,2048]{2,1,0:T(8,128)S(1)}, f32[4,8,2048]{2,1,0:T(8,128)S(1)}) custom-call(bf16[256,256]{1,0:T(8,128)(2,1)S(1)} %get-tuple-element.110.high, bf16[256,256]{1,0:T(8,128)(2,1)S(1)} %get-tuple-element.111.low, f32[16,8,1024]{2,1,0:T(8,128)S(1)} %get-tuple-element.112.rest_0_, f32[16,8,1024]{2,1,0:T(8,128)S(1)} %collective-permute-done.4.rest_1_, ...), custom_call_target="tpu_custom_call" | custom-call | tf_op jit(solution)/shard_map/pallas_call | solution.py:515
  8.7 4.3 %collective-permute-done.5.got = f32[12,8,1024]{2,1,0:T(8,128)S(1)} collective-permute-done((f32[12,8,1024]{2,1,0:T(8,128)S(1)}, f32[12,8,1024]{2,1,0:T(8,128)S(1)}, u32[]{:S(2)}, u32[]{:S(2)}) %collective-permute-start.5) | collective-permute-done | bytes 393248 | tf_op jit(solution)/shard_map/ppermute | solution.py:482
  13.1 2.1 %collective-permute-start.7 = (f32[6,8,1024]{2,1,0:T(8,128)S(1)}, f32[6,8,1024]{2,1,0:T(8,128)S(1)}, u32[]{:S(2)}, u32[]{:S(2)}) collective-permute-start(f32[6,8,1024]{2,1,0:T(8,128)S(1)} %shard_map.177.rest_0_), channel_id=1, source_target_pairs={{0,16},{1,17},{2,18},{3,19},{4,12},{5,13},{6,14},{7,15},{8,24},{9,... | collective-permute-start | bytes 589832 | tf_op jit(solution)/shard_map/ppermute | solution.py:482
  15.2 2.7 %ready.1 = (f32[16,8,4096]{2,1,0:T(8,128)}, f32[6,64,128]{2,1,0:T(8,128)S(1)}, f32[8,128]{1,0:T(8,128)S(1)}, s32[40]{0:T(128)S(1)}, s32[1]{0:T(128)}) custom-call(s32[4,2]{1,0:T(4,128)S(1)} %copy.24.tiles, s32[1024]{0:T(1024)S(1)} %copy-done.15, s32[128,128]{1,0:T(8,128)S(1)} %copy-done.12, f32[64,128]{1,0:T(8,128)S(1)} %copy-done.14, ...), custom_call_target="tpu_custom_call" | custom-call | tf_op jit(solution)/shard_map/ready/pallas_call | solution.py:550
  17.9 1.3 %collective-permute-done.8.got = f32[12,8,1024]{2,1,0:T(8,128)S(1)} collective-permute-done((f32[12,8,1024]{2,1,0:T(8,128)S(1)}, f32[12,8,1024]{2,1,0:T(8,128)S(1)}, u32[]{:S(2)}, u32[]{:S(2)}) %collective-permute-start.8) | collective-permute-done | bytes 393248 | tf_op jit(solution)/shard_map/ppermute | solution.py:482
  19.3 2.4 %collective-permute-start.9 = (f32[6,8,1024]{2,1,0:T(8,128)S(1)}, f32[6,8,1024]{2,1,0:T(8,128)S(1)}, u32[]{:S(2)}, u32[]{:S(2)}) collective-permute-start(f32[6,8,1024]{2,1,0:T(8,128)S(1)} %shard_map.178.rest_0_), channel_id=1, source_target_pairs={{0,16},{1,17},{2,18},{3,19},{4,12},{5,13},{6,14},{7,15},{8,24},{9,... | collective-permute-start | bytes 589832 | tf_op jit(solution)/shard_map/ppermute | solution.py:482
  21.6 1.5 %collective-permute-start.12 = (f32[4,8,2048]{2,1,0:T(8,128)S(1)}, f32[4,8,2048]{2,1,0:T(8,128)S(1)}, u32[]{:S(2)}, u32[]{:S(2)}) collective-permute-start(f32[4,8,2048]{2,1,0:T(8,128)S(1)} %get-tuple-element.118.rest_0_), channel_id=1, source_target_pairs={{0,8},{1,9},{2,10},{3,11},{4,20},{5,21},{6,22},{7,23},{8,0},{9,1},... | collective-permute-start | bytes 786440 | tf_op jit(solution)/shard_map/ppermute | solution.py:482
  23.2 0.1 collective-permute-start.10
  23.2 2.7 %collective-permute-done.9.passed = f32[6,8,1024]{2,1,0:T(8,128)S(1)} collective-permute-done((f32[6,8,1024]{2,1,0:T(8,128)S(1)}, f32[6,8,1024]{2,1,0:T(8,128)S(1)}, u32[]{:S(2)}, u32[]{:S(2)}) %collective-permute-start.9) | collective-permute-done | bytes 196640 | tf_op jit(solution)/shard_map/ppermute | solution.py:482
  26.0 0.1 collective-permute-start.11
  26.0 2.0 %collective-permute-done.12.got = f32[4,8,2048]{2,1,0:T(8,128)S(1)} collective-permute-done((f32[4,8,2048]{2,1,0:T(8,128)S(1)}, f32[4,8,2048]{2,1,0:T(8,128)S(1)}, u32[]{:S(2)}, u32[]{:S(2)}) %collective-permute-start.12) | collective-permute-done | bytes 262176 | tf_op jit(solution)/shard_map/ppermute | solution.py:482
  28.0 0.1 collective-permute-start.20
  28.2 1.0 %shard_map.182 = (f32[64,256]{1,0:T(8,128)S(1)}, f32[64,256]{1,0:T(8,128)S(1)}, f32[64,256]{1,0:T(8,128)S(1)}, f32[512,256]{1,0:T(8,128)S(1)}, f32[64,256]{1,0:T(8,128)S(1)}, /*index=5*/f32[64,256]{1,0:T(8,128)S(1)}) custom-call(f32[6,8,1024]{2,1,0:T(8,128)S(1)} %shard_map.179.rest_0_.refs_0_, f32[6,8,1024]{2,1,0:T(8,128)S(1)} %shard_map.180.rest_0_.refs_1_, ...), custom_call_target="tpu_custom_call" | custom-call | tf_op jit(solution)/shard_map/pallas_call | solution.py:589
  29.3 3.7 %collective-permute-done.20.passed = f32[2,8,2048]{2,1,0:T(8,128)S(1)} collective-permute-done((f32[2,8,2048]{2,1,0:T(8,128)S(1)}, f32[2,8,2048]{2,1,0:T(8,128)S(1)}, u32[]{:S(2)}, u32[]{:S(2)}) %collective-permute-start.20) | collective-permute-done | bytes 131104 | tf_op jit(solution)/shard_map/ppermute | solution.py:482
  33.1 1.6 %collective-permute-start.13 = (f32[64,256]{1,0:T(8,128)S(1)}, f32[64,256]{1,0:T(8,128)S(1)}, u32[]{:S(2)}, u32[]{:S(2)}) collective-permute-start(f32[64,256]{1,0:T(8,128)S(1)} %get-tuple-element.126), channel_id=1, source_target_pairs={{0,1},{1,0},{2,3},{3,2},{4,5},{5,4},{6,7},{7,6},{8,9},{9,8},{10,11... | collective-permute-start | bytes 196616 | tf_op jit(solution)/shard_map/ppermute | solution.py:486
  34.8 2.6 %collective-permute-start.14 = (f32[64,256]{1,0:T(8,128)S(1)}, f32[64,256]{1,0:T(8,128)S(1)}, u32[]{:S(2)}, u32[]{:S(2)}) collective-permute-start(f32[64,256]{1,0:T(8,128)S(1)} %get-tuple-element.127), channel_id=1, source_target_pairs={{0,2},{1,3},{2,0},{3,1},{4,6},{5,7},{6,4},{7,5},{8,10},{9,11},{10,... | collective-permute-start | bytes 196616 | tf_op jit(solution)/shard_map/ppermute | solution.py:486
  37.4 0.2 collective-permute-start.15
  37.6 1.0 %shard_map.186 = (f32[64,256]{1,0:T(8,128)S(1)}, f32[64,256]{1,0:T(8,128)S(1)}, f32[64,256]{1,0:T(8,128)S(1)}, f32[512,256]{1,0:T(8,128)S(1)}, f32[64,256]{1,0:T(8,128)S(1)}, /*index=5*/f32[64,256]{1,0:T(8,128)S(1)}) custom-call(f32[6,8,1024]{2,1,0:T(8,128)S(1)} %shard_map.179.rest_0_.refs_0_, f32[6,8,1024]{2,1,0:T(8,128)S(1)} %shard_map.180.rest_0_.refs_1_, ...), custom_call_target="tpu_custom_call" | custom-call | tf_op jit(solution)/shard_map/pallas_call | solution.py:589
  38.6 0.7 %collective-permute-start.22 = (f32[64,256]{1,0:T(8,128)S(1)}, f32[64,256]{1,0:T(8,128)S(1)}, u32[]{:S(2)}, u32[]{:S(2)}) collective-permute-start(f32[64,256]{1,0:T(8,128)S(1)} %get-tuple-element.132), channel_id=1, source_target_pairs={{0,1},{1,0},{2,3},{3,2},{4,5},{5,4},{6,7},{7,6},{8,9},{9,8},{10,11... | collective-permute-start | bytes 196616 | tf_op jit(solution)/shard_map/ppermute | solution.py:486
  39.3 3.5 %collective-permute-start.23 = (f32[64,256]{1,0:T(8,128)S(1)}, f32[64,256]{1,0:T(8,128)S(1)}, u32[]{:S(2)}, u32[]{:S(2)}) collective-permute-start(f32[64,256]{1,0:T(8,128)S(1)} %get-tuple-element.133), channel_id=1, source_target_pairs={{0,2},{1,3},{2,0},{3,1},{4,6},{5,7},{6,4},{7,5},{8,10},{9,11},{10,... | collective-permute-start | bytes 196616 | tf_op jit(solution)/shard_map/ppermute | solution.py:486
  42.8 0.2 collective-permute-start.24
  43.1 1.1 %collective-permute-done.15.refs_6_ = f32[64,256]{1,0:T(8,128)S(1)} collective-permute-done((f32[64,256]{1,0:T(8,128)S(1)}, f32[64,256]{1,0:T(8,128)S(1)}, u32[]{:S(2)}, u32[]{:S(2)}) %collective-permute-start.15) | collective-permute-done | bytes 65568 | tf_op jit(solution)/shard_map/ppermute | solution.py:486
  44.2 1.2 %shard_map.183.refs_18_ = f32[8,4096]{1,0:T(8,128)S(1)} custom-call(f32[8,128]{1,0:T(8,128)S(1)} %get-tuple-element.121.flags, f32[6,8,1024]{2,1,0:T(8,128)S(1)} %shard_map.179.rest_0_.refs_0_, f32[6,8,1024]{2,1,0:T(8,128)S(1)} %shard_map.180.rest_0_.refs_1_, f32[6,8,1024]{2,1,0:T(8,128)S(1)} %collective-permute-done.10.refs_2_, ...), custom_call_target="tpu_custom_call" | custom-call | tf_op jit(solution)/shard_map/pallas_call | solution.py:607
  45.4 0.6 collective-permute-start.17
  46.0 1.5 %collective-permute-start.16 = (f32[8,4096]{1,0:T(8,128)S(1)}, f32[8,4096]{1,0:T(8,128)S(1)}, u32[]{:S(2)}, u32[]{:S(2)}) collective-permute-start(f32[8,4096]{1,0:T(8,128)S(1)} %shard_map.183.refs_18_), channel_id=1, source_target_pairs={{0,8},{1,9},{2,10},{3,11},{4,20},{5,21},{6,22},{7,23},{8,0},{9,1},... | collective-permute-start | bytes 393224 | tf_op jit(solution)/shard_map/ppermute | solution.py:482
  47.5 0.6 %collective-permute-done.23.refs_5_ = f32[64,256]{1,0:T(8,128)S(1)} collective-permute-done((f32[64,256]{1,0:T(8,128)S(1)}, f32[64,256]{1,0:T(8,128)S(1)}, u32[]{:S(2)}, u32[]{:S(2)}) %collective-permute-start.23) | collective-permute-done | bytes 65568 | tf_op jit(solution)/shard_map/ppermute | solution.py:486
  48.1 0.9 %collective-permute-done.24.refs_6_ = f32[64,256]{1,0:T(8,128)S(1)} collective-permute-done((f32[64,256]{1,0:T(8,128)S(1)}, f32[64,256]{1,0:T(8,128)S(1)}, u32[]{:S(2)}, u32[]{:S(2)}) %collective-permute-start.24) | collective-permute-done | bytes 65568 | tf_op jit(solution)/shard_map/ppermute | solution.py:486
  49.0 1.2 %shard_map.187 = f32[8,4096]{1,0:T(8,128)S(1)} custom-call(f32[8,128]{1,0:T(8,128)S(1)} %get-tuple-element.121.flags, f32[6,8,1024]{2,1,0:T(8,128)S(1)} %shard_map.179.rest_0_.refs_0_, f32[6,8,1024]{2,1,0:T(8,128)S(1)} %shard_map.180.rest_0_.refs_1_, f32[6,8,1024]{2,1,0:T(8,128)S(1)} %collective-permute-done.10.refs_2_, ...), custom_call_target="tpu_custom_call" | custom-call | tf_op jit(solution)/shard_map/pallas_call | solution.py:607
  50.2 0.6 collective-permute-start.26
  50.8 1.5 %collective-permute-start.25 = (f32[8,4096]{1,0:T(8,128)S(1)}, f32[8,4096]{1,0:T(8,128)S(1)}, u32[]{:S(2)}, u32[]{:S(2)}) collective-permute-start(f32[8,4096]{1,0:T(8,128)S(1)} %shard_map.187), channel_id=1, source_target_pairs={{0,8},{1,9},{2,10},{3,11},{4,20},{5,21},{6,22},{7,23},{8,0},{9,1},... | collective-permute-start | bytes 393224 | tf_op jit(solution)/shard_map/ppermute | solution.py:482
  52.4 2.9 %collective-permute-done.26.y = f32[8,4096]{1,0:T(8,128)S(1)} collective-permute-done((f32[8,4096]{1,0:T(8,128)S(1)}, f32[8,4096]{1,0:T(8,128)S(1)}, u32[]{:S(2)}, u32[]{:S(2)}) %collective-permute-start.26) | collective-permute-done | bytes 131104 | tf_op jit(solution)/shard_map/ppermute | solution.py:482
  55.2 0.5 collective-permute-done.25.x
  55.8 0.5 collective-permute-start.18
  56.3 0.1 collective-permute-start.27
  57.1 0.5 collective-permute-done.18
  57.5 0.2 collective-permute-done.27
  57.7 0.7 %conditional.1 = (f32[16,8,4096]{2,1,0:T(8,128)}) conditional(s32[]{:T(128)} %bitcast, (s32[40]{0:T(128)S(1)}, f32[8,4096]{1,0:T(8,128)S(1)}, f32[8,4096]{1,0:T(8,128)S(1)}, f32[8,4096]{1,0:T(8,128)S(1)}, f32[8,4096]{1,0:T(8,128)S(1)}, /*index=5*/f32[2,8,4096]{2,1,0:T(8,128)S(1)}, f32[8,4096]{1,0:T(8,128)S(1)}, f32[8,4096]{1,0:T(8,128)S(1)}, ...), branch_computations={%region_0.0_spmd, %region_1.0_spmd} | conditional | bytes 2097320 | solution.py:649
  57.7 0.7 %place.2 = f32[16,8,4096]{2,1,0:T(8,128)} custom-call(s32[40]{0:T(128)S(1)} %get-tuple-element.56.match, f32[8,4096]{1,0:T(8,128)S(1)} %get-tuple-element.57.refs_0_, f32[8,4096]{1,0:T(8,128)S(1)} %get-tuple-element.58.refs_1_, f32[8,4096]{1,0:T(8,128)S(1)} %get-tuple-element.59.refs_2_, ...), custom_call_target="tpu_custom_call", output_to_operand_aliasing={{}: (11, {})} | custom-call | tf_op jit(solution)/shard_map/cond/branch_0_fun/place/pallas_call | solution.py:631
  (57 shorter events, 0.5 us)
Async XLA Ops:
  0.0 2.5 %copy-start.15 = (s32[1024]{0:T(1024)S(1)}, s32[1024]{0:T(1024)}, u32[]{:S(2)}) copy-start(s32[1024]{0:T(1024)} %constant.31.clone.host) | copy-start | bytes 12292
  0.0 2.4 %copy-start.16 = (s32[4,2]{0,1:T(2,128)S(1)}, s32[4,2]{0,1:T(2,128)}, u32[]{:S(2)}) copy-start(s32[4,2]{0,1:T(2,128)} %param.22) | copy-start | bytes 100
  0.0 2.5 %copy-start.11 = (f32[128,128]{1,0:T(8,128)S(1)}, f32[128,128]{1,0:T(8,128)}, u32[]{:S(2)}) copy-start(f32[128,128]{1,0:T(8,128)} %rotation.1) | copy-start | bytes 196612
  1.7 2.1 %collective-permute-start.4 = (f32[16,8,1024]{2,1,0:T(8,128)S(1)}, f32[16,8,1024]{2,1,0:T(8,128)S(1)}, u32[]{:S(2)}, u32[]{:S(2)}) collective-permute-start(f32[16,8,1024]{2,1,0:T(8,128)S(1)} %get-tuple-element.113), channel_id=1, source_target_pairs={{0,4},{1,5},{2,6},{3,7},{4,0},{5,1},{6,2},{7,3},{8,12},{9,13},{10,... | collective-permute-start | bytes 1572872 | tf_op jit(solution)/shard_map/ppermute | solution.py:482
  2.3 5.0 %collective-permute-start.6 = (f32[16,8,1024]{2,1,0:T(8,128)S(1)}, f32[16,8,1024]{2,1,0:T(8,128)S(1)}, u32[]{:S(2)}, u32[]{:S(2)}) collective-permute-start(f32[16,8,1024]{2,1,0:T(8,128)S(1)} %get-tuple-element.109.after), channel_id=1, source_target_pairs={{0,4},{1,5},{2,6},{3,7},{4,0},{5,1},{6,2},{7,3},{8,12},{9,13},{10,... | collective-permute-start | bytes 1572872 | tf_op jit(solution)/shard_map/ppermute | solution.py:482
  4.3 8.7 %collective-permute-start.5 = (f32[12,8,1024]{2,1,0:T(8,128)S(1)}, f32[12,8,1024]{2,1,0:T(8,128)S(1)}, u32[]{:S(2)}, u32[]{:S(2)}) collective-permute-start(f32[12,8,1024]{2,1,0:T(8,128)S(1)} %get-tuple-element.115.rest_2_), channel_id=1, source_target_pairs={{0,8},{1,9},{2,10},{3,11},{4,20},{5,21},{6,22},{7,23},{8,0},{9,1},... | collective-permute-start | bytes 1179656 | tf_op jit(solution)/shard_map/ppermute | solution.py:482
  7.8 7.4 %copy-start.12 = (s32[128,128]{1,0:T(8,128)S(1)}, s32[128,128]{1,0:T(8,128)}, u32[]{:S(2)}) copy-start(s32[128,128]{1,0:T(8,128)} %mask.1) | copy-start | bytes 196612
  7.8 7.4 %copy-start.14 = (f32[64,128]{1,0:T(8,128)S(1)}, f32[64,128]{1,0:T(8,128)}, u32[]{:S(2)}) copy-start(f32[64,128]{1,0:T(8,128)} %constant.32.clone.log_r) | copy-start | bytes 98308
  7.8 11.4 %collective-permute-start.8 = (f32[12,8,1024]{2,1,0:T(8,128)S(1)}, f32[12,8,1024]{2,1,0:T(8,128)S(1)}, u32[]{:S(2)}, u32[]{:S(2)}) collective-permute-start(f32[12,8,1024]{2,1,0:T(8,128)S(1)} %get-tuple-element.117.rest_4_), channel_id=1, source_target_pairs={{0,8},{1,9},{2,10},{3,11},{4,20},{5,21},{6,22},{7,23},{8,0},{9,1},... | collective-permute-start | bytes 1179656 | tf_op jit(solution)/shard_map/ppermute | solution.py:482
  13.1 10.1 %collective-permute-start.7 = (f32[6,8,1024]{2,1,0:T(8,128)S(1)}, f32[6,8,1024]{2,1,0:T(8,128)S(1)}, u32[]{:S(2)}, u32[]{:S(2)}) collective-permute-start(f32[6,8,1024]{2,1,0:T(8,128)S(1)} %shard_map.177.rest_0_), channel_id=1, source_target_pairs={{0,16},{1,17},{2,18},{3,19},{4,12},{5,13},{6,14},{7,15},{8,24},{9,... | collective-permute-start | bytes 589832 | tf_op jit(solution)/shard_map/ppermute | solution.py:482
  19.2 9.0 %copy-start.3 = (bf16[2,256,256]{2,1,0:T(8,128)(2,1)S(1)}, bf16[2,256,256]{2,1,0:T(8,128)(2,1)}, u32[]{:S(2)}) copy-start(bf16[2,256,256]{2,1,0:T(8,128)(2,1)} %constant.38.clone.refs_5_.refs_7_) | copy-start | bytes 786436
  19.2 9.0 %copy-start.4 = (bf16[2,256,256]{2,1,0:T(8,128)(2,1)S(1)}, bf16[2,256,256]{2,1,0:T(8,128)(2,1)}, u32[]{:S(2)}) copy-start(bf16[2,256,256]{2,1,0:T(8,128)(2,1)} %constant.37.clone.refs_4_.refs_6_) | copy-start | bytes 786436
  19.2 9.0 %copy-start.5 = (f32[512,128]{1,0:T(8,128)S(1)}, f32[512,128]{1,0:T(8,128)}, u32[]{:S(2)}) copy-start(f32[512,128]{1,0:T(8,128)} %constant.33.clone.refs_8_.refs_10_) | copy-start | bytes 786436
  19.2 9.0 %copy-start.8 = (bf16[256,256]{1,0:T(8,128)(2,1)S(1)}, bf16[256,256]{1,0:T(8,128)(2,1)}, u32[]{:S(2)}) copy-start(bf16[256,256]{1,0:T(8,128)(2,1)} %constant.42.clone.refs_7_.refs_9_) | copy-start | bytes 393220
  19.2 9.0 %copy-start.9 = (bf16[256,256]{1,0:T(8,128)(2,1)S(1)}, bf16[256,256]{1,0:T(8,128)(2,1)}, u32[]{:S(2)}) copy-start(bf16[256,256]{1,0:T(8,128)(2,1)} %constant.41.clone.refs_6_.refs_8_) | copy-start | bytes 393220
  19.3 6.7 %collective-permute-start.9 = (f32[6,8,1024]{2,1,0:T(8,128)S(1)}, f32[6,8,1024]{2,1,0:T(8,128)S(1)}, u32[]{:S(2)}, u32[]{:S(2)}) collective-permute-start(f32[6,8,1024]{2,1,0:T(8,128)S(1)} %shard_map.178.rest_0_), channel_id=1, source_target_pairs={{0,16},{1,17},{2,18},{3,19},{4,12},{5,13},{6,14},{7,15},{8,24},{9,... | collective-permute-start | bytes 589832 | tf_op jit(solution)/shard_map/ppermute | solution.py:482
  21.6 6.4 %collective-permute-start.12 = (f32[4,8,2048]{2,1,0:T(8,128)S(1)}, f32[4,8,2048]{2,1,0:T(8,128)S(1)}, u32[]{:S(2)}, u32[]{:S(2)}) collective-permute-start(f32[4,8,2048]{2,1,0:T(8,128)S(1)} %get-tuple-element.118.rest_0_), channel_id=1, source_target_pairs={{0,8},{1,9},{2,10},{3,11},{4,20},{5,21},{6,22},{7,23},{8,0},{9,1},... | collective-permute-start | bytes 786440 | tf_op jit(solution)/shard_map/ppermute | solution.py:482
  23.2 5.0 %collective-permute-start.10 = (f32[6,8,1024]{2,1,0:T(8,128)S(1)}, f32[6,8,1024]{2,1,0:T(8,128)S(1)}, u32[]{:S(2)}, u32[]{:S(2)}) collective-permute-start(f32[6,8,1024]{2,1,0:T(8,128)S(1)} %shard_map.179.rest_0_.refs_0_), channel_id=1, source_target_pairs={{0,4},{1,5},{2,6},{3,7},{4,0},{5,1},{6,2},{7,3},{8,12},{9,13},{10,... | collective-permute-start | bytes 589832 | tf_op jit(solution)/shard_map/ppermute | solution.py:482
  26.0 2.2 %collective-permute-start.11 = (f32[6,8,1024]{2,1,0:T(8,128)S(1)}, f32[6,8,1024]{2,1,0:T(8,128)S(1)}, u32[]{:S(2)}, u32[]{:S(2)}) collective-permute-start(f32[6,8,1024]{2,1,0:T(8,128)S(1)} %shard_map.180.rest_0_.refs_1_), channel_id=1, source_target_pairs={{0,4},{1,5},{2,6},{3,7},{4,0},{5,1},{6,2},{7,3},{8,12},{9,13},{10,... | collective-permute-start | bytes 589832 | tf_op jit(solution)/shard_map/ppermute | solution.py:482
  28.0 5.0 %collective-permute-start.20 = (f32[2,8,2048]{2,1,0:T(8,128)S(1)}, f32[2,8,2048]{2,1,0:T(8,128)S(1)}, u32[]{:S(2)}, u32[]{:S(2)}) collective-permute-start(f32[2,8,2048]{2,1,0:T(8,128)S(1)} %shard_map.181.refs_10_), channel_id=1, source_target_pairs={{0,16},{1,17},{2,18},{3,19},{4,12},{5,13},{6,14},{7,15},{8,24},{9,... | collective-permute-start | bytes 393224 | tf_op jit(solution)/shard_map/ppermute | solution.py:482
  29.2 14.9 %copy-start = (bf16[2,256,256]{2,1,0:T(8,128)(2,1)S(1)}, bf16[2,256,256]{2,1,0:T(8,128)(2,1)}, u32[]{:S(2)}) copy-start(bf16[2,256,256]{2,1,0:T(8,128)(2,1)} %constant.40.clone.refs_8_) | copy-start | bytes 786436
  29.2 14.9 %copy-start.1 = (bf16[2,256,256]{2,1,0:T(8,128)(2,1)S(1)}, bf16[2,256,256]{2,1,0:T(8,128)(2,1)}, u32[]{:S(2)}) copy-start(bf16[2,256,256]{2,1,0:T(8,128)(2,1)} %constant.39.clone.refs_7_) | copy-start | bytes 786436
  29.2 14.9 %copy-start.2 = (f32[512,128]{1,0:T(8,128)S(1)}, f32[512,128]{1,0:T(8,128)}, u32[]{:S(2)}) copy-start(f32[512,128]{1,0:T(8,128)} %constant.34.clone.refs_11_) | copy-start | bytes 786436
  29.2 14.9 %copy-start.6 = (bf16[256,256]{1,0:T(8,128)(2,1)S(1)}, bf16[256,256]{1,0:T(8,128)(2,1)}, u32[]{:S(2)}) copy-start(bf16[256,256]{1,0:T(8,128)(2,1)} %constant.44.clone.refs_10_) | copy-start | bytes 393220
  29.3 14.9 %copy-start.7 = (bf16[256,256]{1,0:T(8,128)(2,1)S(1)}, bf16[256,256]{1,0:T(8,128)(2,1)}, u32[]{:S(2)}) copy-start(bf16[256,256]{1,0:T(8,128)(2,1)} %constant.43.clone.refs_9_) | copy-start | bytes 393220
  29.3 14.9 %copy-start.10 = (f32[3,64,128]{2,1,0:T(8,128)S(1)}, f32[3,64,128]{2,1,0:T(8,128)}, u32[]{:S(2)}) copy-start(f32[3,64,128]{2,1,0:T(8,128)} %constant.36.clone.refs_14_) | copy-start | bytes 294916
  29.3 14.9 %copy-start.13 = (f32[2,8,128]{2,1,0:T(8,128)S(1)}, f32[2,8,128]{2,1,0:T(8,128)}, u32[]{:S(2)}) copy-start(f32[2,8,128]{2,1,0:T(8,128)} %constant.35.clone.refs_12_) | copy-start | bytes 24580
  33.1 4.5 %collective-permute-start.21 = (f32[2,8,2048]{2,1,0:T(8,128)S(1)}, f32[2,8,2048]{2,1,0:T(8,128)S(1)}, u32[]{:S(2)}, u32[]{:S(2)}) collective-permute-start(f32[2,8,2048]{2,1,0:T(8,128)S(1)} %shard_map.185.refs_4_), channel_id=1, source_target_pairs={{0,4},{1,5},{2,6},{3,7},{4,0},{5,1},{6,2},{7,3},{8,12},{9,13},{10,... | collective-permute-start | bytes 393224 | tf_op jit(solution)/shard_map/ppermute | solution.py:482
  33.1 9.7 %collective-permute-start.13 = (f32[64,256]{1,0:T(8,128)S(1)}, f32[64,256]{1,0:T(8,128)S(1)}, u32[]{:S(2)}, u32[]{:S(2)}) collective-permute-start(f32[64,256]{1,0:T(8,128)S(1)} %get-tuple-element.126), channel_id=1, source_target_pairs={{0,1},{1,0},{2,3},{3,2},{4,5},{5,4},{6,7},{7,6},{8,9},{9,8},{10,11... | collective-permute-start | bytes 196616 | tf_op jit(solution)/shard_map/ppermute | solution.py:486
  34.8 8.3 %collective-permute-start.14 = (f32[64,256]{1,0:T(8,128)S(1)}, f32[64,256]{1,0:T(8,128)S(1)}, u32[]{:S(2)}, u32[]{:S(2)}) collective-permute-start(f32[64,256]{1,0:T(8,128)S(1)} %get-tuple-element.127), channel_id=1, source_target_pairs={{0,2},{1,3},{2,0},{3,1},{4,6},{5,7},{6,4},{7,5},{8,10},{9,11},{10,... | collective-permute-start | bytes 196616 | tf_op jit(solution)/shard_map/ppermute | solution.py:486
  37.4 6.8 %collective-permute-start.15 = (f32[64,256]{1,0:T(8,128)S(1)}, f32[64,256]{1,0:T(8,128)S(1)}, u32[]{:S(2)}, u32[]{:S(2)}) collective-permute-start(f32[64,256]{1,0:T(8,128)S(1)} %get-tuple-element.128), channel_id=1, source_target_pairs={{0,3},{1,2},{2,1},{3,0},{4,7},{5,6},{6,5},{7,4},{8,11},{9,10},{10,... | collective-permute-start | bytes 196616 | tf_op jit(solution)/shard_map/ppermute | solution.py:486
  38.6 8.9 %collective-permute-start.22 = (f32[64,256]{1,0:T(8,128)S(1)}, f32[64,256]{1,0:T(8,128)S(1)}, u32[]{:S(2)}, u32[]{:S(2)}) collective-permute-start(f32[64,256]{1,0:T(8,128)S(1)} %get-tuple-element.132), channel_id=1, source_target_pairs={{0,1},{1,0},{2,3},{3,2},{4,5},{5,4},{6,7},{7,6},{8,9},{9,8},{10,11... | collective-permute-start | bytes 196616 | tf_op jit(solution)/shard_map/ppermute | solution.py:486
  39.3 8.7 %collective-permute-start.23 = (f32[64,256]{1,0:T(8,128)S(1)}, f32[64,256]{1,0:T(8,128)S(1)}, u32[]{:S(2)}, u32[]{:S(2)}) collective-permute-start(f32[64,256]{1,0:T(8,128)S(1)} %get-tuple-element.133), channel_id=1, source_target_pairs={{0,2},{1,3},{2,0},{3,1},{4,6},{5,7},{6,4},{7,5},{8,10},{9,11},{10,... | collective-permute-start | bytes 196616 | tf_op jit(solution)/shard_map/ppermute | solution.py:486
  42.8 6.2 %collective-permute-start.24 = (f32[64,256]{1,0:T(8,128)S(1)}, f32[64,256]{1,0:T(8,128)S(1)}, u32[]{:S(2)}, u32[]{:S(2)}) collective-permute-start(f32[64,256]{1,0:T(8,128)S(1)} %get-tuple-element.134), channel_id=1, source_target_pairs={{0,3},{1,2},{2,1},{3,0},{4,7},{5,6},{6,5},{7,4},{8,11},{9,10},{10,... | collective-permute-start | bytes 196616 | tf_op jit(solution)/shard_map/ppermute | solution.py:486
  45.4 6.9 %collective-permute-start.17 = (f32[8,4096]{1,0:T(8,128)S(1)}, f32[8,4096]{1,0:T(8,128)S(1)}, u32[]{:S(2)}, u32[]{:S(2)}) collective-permute-start(f32[8,4096]{1,0:T(8,128)S(1)} %shard_map.183.refs_18_), channel_id=1, source_target_pairs={{0,16},{1,17},{2,18},{3,19},{4,12},{5,13},{6,14},{7,15},{8,24},{9,... | collective-permute-start | bytes 393224 | tf_op jit(solution)/shard_map/ppermute | solution.py:482
  46.0 6.3 %collective-permute-start.16 = (f32[8,4096]{1,0:T(8,128)S(1)}, f32[8,4096]{1,0:T(8,128)S(1)}, u32[]{:S(2)}, u32[]{:S(2)}) collective-permute-start(f32[8,4096]{1,0:T(8,128)S(1)} %shard_map.183.refs_18_), channel_id=1, source_target_pairs={{0,8},{1,9},{2,10},{3,11},{4,20},{5,21},{6,22},{7,23},{8,0},{9,1},... | collective-permute-start | bytes 393224 | tf_op jit(solution)/shard_map/ppermute | solution.py:482
  50.2 5.0 %collective-permute-start.26 = (f32[8,4096]{1,0:T(8,128)S(1)}, f32[8,4096]{1,0:T(8,128)S(1)}, u32[]{:S(2)}, u32[]{:S(2)}) collective-permute-start(f32[8,4096]{1,0:T(8,128)S(1)} %shard_map.187), channel_id=1, source_target_pairs={{0,16},{1,17},{2,18},{3,19},{4,12},{5,13},{6,14},{7,15},{8,24},{9,... | collective-permute-start | bytes 393224 | tf_op jit(solution)/shard_map/ppermute | solution.py:482
  50.8 5.0 %collective-permute-start.25 = (f32[8,4096]{1,0:T(8,128)S(1)}, f32[8,4096]{1,0:T(8,128)S(1)}, u32[]{:S(2)}, u32[]{:S(2)}) collective-permute-start(f32[8,4096]{1,0:T(8,128)S(1)} %shard_map.187), channel_id=1, source_target_pairs={{0,8},{1,9},{2,10},{3,11},{4,20},{5,21},{6,22},{7,23},{8,0},{9,1},... | collective-permute-start | bytes 393224 | tf_op jit(solution)/shard_map/ppermute | solution.py:482
  52.3 5.4 %collective-permute-start.19 = (f32[2,8,4096]{2,1,0:T(8,128)S(1)}, f32[2,8,4096]{2,1,0:T(8,128)S(1)}, u32[]{:S(2)}, u32[]{:S(2)}) collective-permute-start(f32[2,8,4096]{2,1,0:T(8,128)S(1)} %shard_map.184), channel_id=1, source_target_pairs={{0,4},{1,5},{2,6},{3,7},{4,0},{5,1},{6,2},{7,3},{8,12},{9,13},{10,... | collective-permute-start | bytes 786440 | tf_op jit(solution)/shard_map/ppermute | solution.py:482
  55.8 2.0 %collective-permute-start.28 = (f32[2,8,4096]{2,1,0:T(8,128)S(1)}, f32[2,8,4096]{2,1,0:T(8,128)S(1)}, u32[]{:S(2)}, u32[]{:S(2)}) collective-permute-start(f32[2,8,4096]{2,1,0:T(8,128)S(1)} %shard_map.188), channel_id=1, source_target_pairs={{0,4},{1,5},{2,6},{3,7},{4,0},{5,1},{6,2},{7,3},{8,12},{9,13},{10,... | collective-permute-start | bytes 786440 | tf_op jit(solution)/shard_map/ppermute | solution.py:482
  55.8 1.7 %collective-permute-start.18 = (f32[8,4096]{1,0:T(8,128)S(1)}, f32[8,4096]{1,0:T(8,128)S(1)}, u32[]{:S(2)}, u32[]{:S(2)}) collective-permute-start(f32[8,4096]{1,0:T(8,128)S(1)} %shard_map.183.refs_18_), channel_id=1, source_target_pairs={{0,4},{1,5},{2,6},{3,7},{4,0},{5,1},{6,2},{7,3},{8,12},{9,13},{10,... | collective-permute-start | bytes 393224 | tf_op jit(solution)/shard_map/ppermute | solution.py:482
  56.3 1.4 %collective-permute-start.27 = (f32[8,4096]{1,0:T(8,128)S(1)}, f32[8,4096]{1,0:T(8,128)S(1)}, u32[]{:S(2)}, u32[]{:S(2)}) collective-permute-start(f32[8,4096]{1,0:T(8,128)S(1)} %shard_map.187), channel_id=1, source_target_pairs={{0,4},{1,5},{2,6},{3,7},{4,0},{5,1},{6,2},{7,3},{8,12},{9,13},{10,... | collective-permute-start | bytes 393224 | tf_op jit(solution)/shard_map/ppermute | solution.py:482

commit v7 on v6

--- a/solution.py
+++ b/solution.py
@@ -226,17 +226,17 @@
             flag = jnp.sum(jnp.where(column == b + w, line, 0.0), axis=1, keepdims=True)
             flags[u * BLK + w:u * BLK + w + 1, :] = jnp.broadcast_to(flag, (1, LANES))
     blocks = per_device // BLK
-    parts = [0, at.bit_1, at.bit_2, 3, 0, at.bit_2, at.bit_1, 3]
-    for n, flip in enumerate(parts):
-        home = tiles[at.tile(at.chip ^ flip), 0]
+    flips = ((0, at.bit_1, at.bit_2), (0, at.bit_2, at.bit_1))
+    near, far = 0, 0
+    for side in range(2):
+        homes = [tiles[at.tile(at.chip ^ flip), 0] for flip in flips[side] + (3,)]
         for block in range(blocks):
-            hit = home == at.o * blocks + block
-            if n % 4 == 3:
-                hit = hit & at.same
-            found = hit.astype(jnp.int32)
-            match[block * len(parts) + n] = found
-            total = blocks * len(parts) + 2 * block + n // 4
-            match[total] = found if n % 4 == 0 else match[total] + found
+            bits = [(home == at.o * blocks + block).astype(jnp.int32) for home in homes]
+            for n in range(3):
+                near = near + bits[n] * (1 << ((2 * block + side) * 3 + n))
+            far = far + bits[3] * (1 << (2 * block + side))
+    match[0:1, :] = jnp.full((1, LANES), near.astype(f32))
+    match[1:2, :] = jnp.full((1, LANES), far.astype(f32))
     for copy in copies:
         copy.wait()
 
@@ -422,7 +422,7 @@
                 out[:, pl.ds(pl.multiple_of(at * LANES, LANES), LANES)] = -total
 
 
-def place_kernel(stride, match, *refs):
+def place_kernel(match, *refs):
     parts, (out, rows, sem) = refs[:-4], refs[-3:]
     pair = BLK // 2
     blocks = out.shape[0] // BLK
@@ -431,12 +431,20 @@
     for part in parts:
         values += [part] if len(part.shape) == 2 else [part.at[n] for n in range(part.shape[0])]
     parts, count = values, len(values) // pair
+    near = jnp.max(match[0:1, :]).astype(jnp.int32)
+    far = jnp.max(match[1:2, :]).astype(jnp.int32) if count > 6 else None
 
     def hits(b, side):
-        return [(match[b * stride + side * stride // 2 + n], side * count // 2 + n) for n in range(count // 2)]
+        at = 2 * b + side
+        bits = [(near & (1 << (at * 3 + n))) for n in range(3)]
+        if far is not None:
+            bits.append(far & (1 << at))
+        return [(bit, side * count // 2 + n) for n, bit in enumerate(bits)]
 
     def found(b, side):
-        return match[blocks * stride + 2 * b + side] > 0
+        at = 2 * b + side
+        any_near = near & (7 << (at * 3))
+        return any_near != 0 if far is None else (any_near != 0) | ((far & (1 << at)) != 0)
 
     def move(b, side):
         which = core if side == 0 else 1 - core
@@ -451,7 +459,7 @@
                 rows[b, side] = jnp.zeros(rows.shape[2:], f32)
                 for hit, n in hits(b, side):
 
-                    @pl.when(hit > 0)
+                    @pl.when(hit != 0)
                     def _():
                         for u in range(pair):
                             rows[b, side, u] += parts[u * count + n][...]
@@ -550,9 +558,9 @@
     empty, powers, flags, match, alone = pl.pallas_call(
         functools.partial(ready_kernel, per_device, n_grid),
         out_shape=(pltpu.HBM(shape, f32), jax.ShapeDtypeStruct((6, NY, LANES), f32),
-                   jax.ShapeDtypeStruct((pair * BLK, LANES), f32), jax.ShapeDtypeStruct((blocks * 10,), jnp.int32),
+                   jax.ShapeDtypeStruct((pair * BLK, LANES), f32), jax.ShapeDtypeStruct((SUB, LANES), f32),
                    jax.ShapeDtypeStruct((1,), jnp.int32)),
-        in_specs=[SM, SM, VM, VM, ANY], out_specs=(HBM, VM, VM, SM, SM),
+        in_specs=[SM, SM, VM, VM, ANY], out_specs=(HBM, VM, VM, VM, SM),
         scratch_shapes=[pltpu.VMEM((pair, planes, width), f32), DMA((per_device // pair,))], name="ready",
         compiler_params=grant(4),
     )(tile_list, host, pair_mask, jnp.asarray(np.log(r), f32), step)
@@ -629,9 +637,9 @@
     def place(target, groups):
         parts = [part for group in groups for part in group]
         return pl.pallas_call(
-            functools.partial(place_kernel, 8),
+            place_kernel,
             out_shape=pltpu.HBM(shape, f32),
-            in_specs=[SM] + [VM] * len(parts) + [HBM],
+            in_specs=[VM] * (1 + len(parts)) + [HBM],
             out_specs=HBM,
             input_output_aliases={len(parts) + 1: 0},
             scratch_shapes=[pltpu.VMEM((blocks, 2, pair, planes, width), f32), DMA((blocks, 2))],

time: 59.5 us -> 59 us (level)
  Pallas kernels: 12.4 us -> 11.8 us
where the time goes in v7:
time: 59 us; the launch traced here: 58 us
  starting transfers between devices  23.9 us (41%)
  waiting for transfers between devices  21 us (36%)
  Pallas kernels  11.8 us (20%)
  between operations  1.03 us (2%)
    ppermute x19, waiting for transfers between devices, swap(): return lax.ppermute(x, axes, moves)  18.4 us
    ppermute x19, starting transfers between devices, swap(): return lax.ppermute(x, axes, moves)  15 us
    ppermute x6, starting transfers between devices, cross(): return lax.ppermute(x, axes, moves)  8.9 us
    pallas_call x1, Pallas kernels, tile_device(): pl.pallas_call(functools.partial(ready_kernel, per_device, n_grid), out_s...  2.6 us
    ppermute x6, waiting for transfers between devices, cross(): return lax.ppermute(x, axes, moves)  2.59 us
    pallas_call x2, Pallas kernels, tile_device(): pl.pallas_call(functools.partial(backward_kernel, u, (CHUNKS, CHUNKS, len...  2.39 us
    pallas_call x2, Pallas kernels, tile_device(): pl.pallas_call(functools.partial(forward_kernel, u, counts + (n_grid - 1,...  1.99 us
    pallas_call x1, Pallas kernels, tile_device(): pl.pallas_call(fetch_kernel, out_shape=[part] * (2 * CHUNKS), in_specs=[H...  1.73 us
  transfers between devices with their start and end apart: 25, of which 13 were waited for; matrix products, arithmetic and copies ran while one was open for 0% of the time, Pallas kernels for 17%

profile of v7, /device:TPU:0, one launch (start us, length us, event | category | flops | bytes accessed | tf_op | source)
XLA Modules:
  0.0 58.0 jit_solution(2717955250494782469)
XLA Ops:
  0.0 1.7 %fetch.1 = (f32[16,8,1024]{2,1,0:T(8,128)S(1)}, f32[16,8,1024]{2,1,0:T(8,128)S(1)}, f32[16,8,1024]{2,1,0:T(8,128)S(1)}, f32[16,8,1024]{2,1,0:T(8,128)S(1)}) custom-call(f32[16,8,4096]{2,1,0:T(8,128)} %source.1), custom_call_target="tpu_custom_call" | custom-call | tf_op jit(solution)/shard_map/fetch/pallas_call | solution.py:500
  1.7 0.6 collective-permute-start.4
  2.3 0.1 collective-permute-start.6
  2.4 0.1 copy.24.tiles
  2.5 1.0 %setup.1 = (bf16[256,256]{1,0:T(8,128)(2,1)S(1)}, bf16[256,256]{1,0:T(8,128)(2,1)S(1)}) custom-call(s32[4,2]{1,0:T(4,128)S(1)} %copy.24.tiles, s32[1024]{0:T(1024)S(1)} %copy-done.15, f32[128,128]{1,0:T(8,128)S(1)} %copy-done.11, f32[16,8,1024]{2,1,0:T(8,128)S(1)} %get-tuple-element.109.after), custom_call_target="tpu_custom_call" | custom-call | tf_op jit(solution)/shard_map/setup/pallas_call | solution.py:516
  3.5 0.3 collective-permute-done.4.rest_1_
  3.8 0.5 shard_map.174
  4.3 2.9 %collective-permute-start.5 = (f32[12,8,1024]{2,1,0:T(8,128)S(1)}, f32[12,8,1024]{2,1,0:T(8,128)S(1)}, u32[]{:S(2)}, u32[]{:S(2)}) collective-permute-start(f32[12,8,1024]{2,1,0:T(8,128)S(1)} %get-tuple-element.115.rest_2_), channel_id=1, source_target_pairs={{0,8},{1,9},{2,10},{3,11},{4,20},{5,21},{6,22},{7,23},{8,0},{9,1},... | collective-permute-start | bytes 1179656 | tf_op jit(solution)/shard_map/ppermute | solution.py:490
  7.3 0.5 shard_map.175
  7.8 0.2 collective-permute-start.8
  8.0 0.7 %shard_map.176 = (f32[4,8,2048]{2,1,0:T(8,128)S(1)}, f32[4,8,2048]{2,1,0:T(8,128)S(1)}) custom-call(bf16[256,256]{1,0:T(8,128)(2,1)S(1)} %get-tuple-element.110.high, bf16[256,256]{1,0:T(8,128)(2,1)S(1)} %get-tuple-element.111.low, f32[16,8,1024]{2,1,0:T(8,128)S(1)} %get-tuple-element.112.rest_0_, f32[16,8,1024]{2,1,0:T(8,128)S(1)} %collective-permute-done.4.rest_1_, ...), custom_call_target="tpu_custom_call" | custom-call | tf_op jit(solution)/shard_map/pallas_call | solution.py:523
  8.7 4.3 %collective-permute-done.5.got = f32[12,8,1024]{2,1,0:T(8,128)S(1)} collective-permute-done((f32[12,8,1024]{2,1,0:T(8,128)S(1)}, f32[12,8,1024]{2,1,0:T(8,128)S(1)}, u32[]{:S(2)}, u32[]{:S(2)}) %collective-permute-start.5) | collective-permute-done | bytes 393248 | tf_op jit(solution)/shard_map/ppermute | solution.py:490
  13.1 2.1 %collective-permute-start.7 = (f32[6,8,1024]{2,1,0:T(8,128)S(1)}, f32[6,8,1024]{2,1,0:T(8,128)S(1)}, u32[]{:S(2)}, u32[]{:S(2)}) collective-permute-start(f32[6,8,1024]{2,1,0:T(8,128)S(1)} %shard_map.177.rest_0_), channel_id=1, source_target_pairs={{0,16},{1,17},{2,18},{3,19},{4,12},{5,13},{6,14},{7,15},{8,24},{9,... | collective-permute-start | bytes 589832 | tf_op jit(solution)/shard_map/ppermute | solution.py:490
  15.2 2.6 %ready.1 = (f32[16,8,4096]{2,1,0:T(8,128)}, f32[6,64,128]{2,1,0:T(8,128)S(1)}, f32[8,128]{1,0:T(8,128)S(1)}, f32[8,128]{1,0:T(8,128)S(1)}, s32[1]{0:T(128)}) custom-call(s32[4,2]{1,0:T(4,128)S(1)} %copy.24.tiles, s32[1024]{0:T(1024)S(1)} %copy-done.15, s32[128,128]{1,0:T(8,128)S(1)} %copy-done.12, f32[64,128]{1,0:T(8,128)S(1)} %copy-done.14, ...), custom_call_target="tpu_custom_call" | custom-call | tf_op jit(solution)/shard_map/ready/pallas_call | solution.py:558
  17.8 1.4 %collective-permute-done.8.got = f32[12,8,1024]{2,1,0:T(8,128)S(1)} collective-permute-done((f32[12,8,1024]{2,1,0:T(8,128)S(1)}, f32[12,8,1024]{2,1,0:T(8,128)S(1)}, u32[]{:S(2)}, u32[]{:S(2)}) %collective-permute-start.8) | collective-permute-done | bytes 393248 | tf_op jit(solution)/shard_map/ppermute | solution.py:490
  19.3 2.4 %collective-permute-start.9 = (f32[6,8,1024]{2,1,0:T(8,128)S(1)}, f32[6,8,1024]{2,1,0:T(8,128)S(1)}, u32[]{:S(2)}, u32[]{:S(2)}) collective-permute-start(f32[6,8,1024]{2,1,0:T(8,128)S(1)} %shard_map.178.rest_0_), channel_id=1, source_target_pairs={{0,16},{1,17},{2,18},{3,19},{4,12},{5,13},{6,14},{7,15},{8,24},{9,... | collective-permute-start | bytes 589832 | tf_op jit(solution)/shard_map/ppermute | solution.py:490
  21.6 1.5 %collective-permute-start.12 = (f32[4,8,2048]{2,1,0:T(8,128)S(1)}, f32[4,8,2048]{2,1,0:T(8,128)S(1)}, u32[]{:S(2)}, u32[]{:S(2)}) collective-permute-start(f32[4,8,2048]{2,1,0:T(8,128)S(1)} %get-tuple-element.118.rest_0_), channel_id=1, source_target_pairs={{0,8},{1,9},{2,10},{3,11},{4,20},{5,21},{6,22},{7,23},{8,0},{9,1},... | collective-permute-start | bytes 786440 | tf_op jit(solution)/shard_map/ppermute | solution.py:490
  23.2 0.1 collective-permute-start.10
  23.2 2.7 %collective-permute-done.9.passed = f32[6,8,1024]{2,1,0:T(8,128)S(1)} collective-permute-done((f32[6,8,1024]{2,1,0:T(8,128)S(1)}, f32[6,8,1024]{2,1,0:T(8,128)S(1)}, u32[]{:S(2)}, u32[]{:S(2)}) %collective-permute-start.9) | collective-permute-done | bytes 196640 | tf_op jit(solution)/shard_map/ppermute | solution.py:490
  26.0 0.1 collective-permute-start.11
  26.0 2.0 %collective-permute-done.12.got = f32[4,8,2048]{2,1,0:T(8,128)S(1)} collective-permute-done((f32[4,8,2048]{2,1,0:T(8,128)S(1)}, f32[4,8,2048]{2,1,0:T(8,128)S(1)}, u32[]{:S(2)}, u32[]{:S(2)}) %collective-permute-start.12) | collective-permute-done | bytes 262176 | tf_op jit(solution)/shard_map/ppermute | solution.py:490
  28.0 0.1 collective-permute-start.20
  28.2 1.0 %shard_map.182 = (f32[64,256]{1,0:T(8,128)S(1)}, f32[64,256]{1,0:T(8,128)S(1)}, f32[64,256]{1,0:T(8,128)S(1)}, f32[512,256]{1,0:T(8,128)S(1)}, f32[64,256]{1,0:T(8,128)S(1)}, /*index=5*/f32[64,256]{1,0:T(8,128)S(1)}) custom-call(f32[6,8,1024]{2,1,0:T(8,128)S(1)} %shard_map.179.rest_0_.refs_0_, f32[6,8,1024]{2,1,0:T(8,128)S(1)} %shard_map.180.rest_0_.refs_1_, ...), custom_call_target="tpu_custom_call" | custom-call | tf_op jit(solution)/shard_map/pallas_call | solution.py:597
  29.3 3.7 %collective-permute-done.20.passed = f32[2,8,2048]{2,1,0:T(8,128)S(1)} collective-permute-done((f32[2,8,2048]{2,1,0:T(8,128)S(1)}, f32[2,8,2048]{2,1,0:T(8,128)S(1)}, u32[]{:S(2)}, u32[]{:S(2)}) %collective-permute-start.20) | collective-permute-done | bytes 131104 | tf_op jit(solution)/shard_map/ppermute | solution.py:490
  33.1 1.6 %collective-permute-start.13 = (f32[64,256]{1,0:T(8,128)S(1)}, f32[64,256]{1,0:T(8,128)S(1)}, u32[]{:S(2)}, u32[]{:S(2)}) collective-permute-start(f32[64,256]{1,0:T(8,128)S(1)} %get-tuple-element.126), channel_id=1, source_target_pairs={{0,1},{1,0},{2,3},{3,2},{4,5},{5,4},{6,7},{7,6},{8,9},{9,8},{10,11... | collective-permute-start | bytes 196616 | tf_op jit(solution)/shard_map/ppermute | solution.py:494
  34.8 2.6 %collective-permute-start.14 = (f32[64,256]{1,0:T(8,128)S(1)}, f32[64,256]{1,0:T(8,128)S(1)}, u32[]{:S(2)}, u32[]{:S(2)}) collective-permute-start(f32[64,256]{1,0:T(8,128)S(1)} %get-tuple-element.127), channel_id=1, source_target_pairs={{0,2},{1,3},{2,0},{3,1},{4,6},{5,7},{6,4},{7,5},{8,10},{9,11},{10,... | collective-permute-start | bytes 196616 | tf_op jit(solution)/shard_map/ppermute | solution.py:494
  37.4 0.2 collective-permute-start.15
  37.6 1.0 %shard_map.186 = (f32[64,256]{1,0:T(8,128)S(1)}, f32[64,256]{1,0:T(8,128)S(1)}, f32[64,256]{1,0:T(8,128)S(1)}, f32[512,256]{1,0:T(8,128)S(1)}, f32[64,256]{1,0:T(8,128)S(1)}, /*index=5*/f32[64,256]{1,0:T(8,128)S(1)}) custom-call(f32[6,8,1024]{2,1,0:T(8,128)S(1)} %shard_map.179.rest_0_.refs_0_, f32[6,8,1024]{2,1,0:T(8,128)S(1)} %shard_map.180.rest_0_.refs_1_, ...), custom_call_target="tpu_custom_call" | custom-call | tf_op jit(solution)/shard_map/pallas_call | solution.py:597
  38.6 0.7 %collective-permute-start.22 = (f32[64,256]{1,0:T(8,128)S(1)}, f32[64,256]{1,0:T(8,128)S(1)}, u32[]{:S(2)}, u32[]{:S(2)}) collective-permute-start(f32[64,256]{1,0:T(8,128)S(1)} %get-tuple-element.132), channel_id=1, source_target_pairs={{0,1},{1,0},{2,3},{3,2},{4,5},{5,4},{6,7},{7,6},{8,9},{9,8},{10,11... | collective-permute-start | bytes 196616 | tf_op jit(solution)/shard_map/ppermute | solution.py:494
  39.3 3.5 %collective-permute-start.23 = (f32[64,256]{1,0:T(8,128)S(1)}, f32[64,256]{1,0:T(8,128)S(1)}, u32[]{:S(2)}, u32[]{:S(2)}) collective-permute-start(f32[64,256]{1,0:T(8,128)S(1)} %get-tuple-element.133), channel_id=1, source_target_pairs={{0,2},{1,3},{2,0},{3,1},{4,6},{5,7},{6,4},{7,5},{8,10},{9,11},{10,... | collective-permute-start | bytes 196616 | tf_op jit(solution)/shard_map/ppermute | solution.py:494
  42.8 0.2 collective-permute-start.24
  43.1 1.1 %collective-permute-done.15.refs_6_ = f32[64,256]{1,0:T(8,128)S(1)} collective-permute-done((f32[64,256]{1,0:T(8,128)S(1)}, f32[64,256]{1,0:T(8,128)S(1)}, u32[]{:S(2)}, u32[]{:S(2)}) %collective-permute-start.15) | collective-permute-done | bytes 65568 | tf_op jit(solution)/shard_map/ppermute | solution.py:494
  44.2 1.2 %shard_map.183.refs_18_ = f32[8,4096]{1,0:T(8,128)S(1)} custom-call(f32[8,128]{1,0:T(8,128)S(1)} %get-tuple-element.121.flags, f32[6,8,1024]{2,1,0:T(8,128)S(1)} %shard_map.179.rest_0_.refs_0_, f32[6,8,1024]{2,1,0:T(8,128)S(1)} %shard_map.180.rest_0_.refs_1_, f32[6,8,1024]{2,1,0:T(8,128)S(1)} %collective-permute-done.10.refs_2_, ...), custom_call_target="tpu_custom_call" | custom-call | tf_op jit(solution)/shard_map/pallas_call | solution.py:615
  45.4 0.6 collective-permute-start.17
  46.0 1.5 %collective-permute-start.16 = (f32[8,4096]{1,0:T(8,128)S(1)}, f32[8,4096]{1,0:T(8,128)S(1)}, u32[]{:S(2)}, u32[]{:S(2)}) collective-permute-start(f32[8,4096]{1,0:T(8,128)S(1)} %shard_map.183.refs_18_), channel_id=1, source_target_pairs={{0,8},{1,9},{2,10},{3,11},{4,20},{5,21},{6,22},{7,23},{8,0},{9,1},... | collective-permute-start | bytes 393224 | tf_op jit(solution)/shard_map/ppermute | solution.py:490
  47.5 0.6 %collective-permute-done.23.refs_5_ = f32[64,256]{1,0:T(8,128)S(1)} collective-permute-done((f32[64,256]{1,0:T(8,128)S(1)}, f32[64,256]{1,0:T(8,128)S(1)}, u32[]{:S(2)}, u32[]{:S(2)}) %collective-permute-start.23) | collective-permute-done | bytes 65568 | tf_op jit(solution)/shard_map/ppermute | solution.py:494
  48.1 0.9 %collective-permute-done.24.refs_6_ = f32[64,256]{1,0:T(8,128)S(1)} collective-permute-done((f32[64,256]{1,0:T(8,128)S(1)}, f32[64,256]{1,0:T(8,128)S(1)}, u32[]{:S(2)}, u32[]{:S(2)}) %collective-permute-start.24) | collective-permute-done | bytes 65568 | tf_op jit(solution)/shard_map/ppermute | solution.py:494
  49.0 1.2 %shard_map.187 = f32[8,4096]{1,0:T(8,128)S(1)} custom-call(f32[8,128]{1,0:T(8,128)S(1)} %get-tuple-element.121.flags, f32[6,8,1024]{2,1,0:T(8,128)S(1)} %shard_map.179.rest_0_.refs_0_, f32[6,8,1024]{2,1,0:T(8,128)S(1)} %shard_map.180.rest_0_.refs_1_, f32[6,8,1024]{2,1,0:T(8,128)S(1)} %collective-permute-done.10.refs_2_, ...), custom_call_target="tpu_custom_call" | custom-call | tf_op jit(solution)/shard_map/pallas_call | solution.py:615
  50.2 0.6 collective-permute-start.26
  50.8 1.5 %collective-permute-start.25 = (f32[8,4096]{1,0:T(8,128)S(1)}, f32[8,4096]{1,0:T(8,128)S(1)}, u32[]{:S(2)}, u32[]{:S(2)}) collective-permute-start(f32[8,4096]{1,0:T(8,128)S(1)} %shard_map.187), channel_id=1, source_target_pairs={{0,8},{1,9},{2,10},{3,11},{4,20},{5,21},{6,22},{7,23},{8,0},{9,1},... | collective-permute-start | bytes 393224 | tf_op jit(solution)/shard_map/ppermute | solution.py:490
  52.4 2.9 %collective-permute-done.26.y = f32[8,4096]{1,0:T(8,128)S(1)} collective-permute-done((f32[8,4096]{1,0:T(8,128)S(1)}, f32[8,4096]{1,0:T(8,128)S(1)}, u32[]{:S(2)}, u32[]{:S(2)}) %collective-permute-start.26) | collective-permute-done | bytes 131104 | tf_op jit(solution)/shard_map/ppermute | solution.py:490
  55.2 0.5 collective-permute-done.25.x
  55.8 0.5 collective-permute-start.18
  56.3 0.1 collective-permute-start.27
  57.1 0.5 collective-permute-done.18
  57.5 0.2 collective-permute-done.27
  57.7 0.3 conditional.1
  57.7 0.2 place.2
  (57 shorter events, 0.5 us)
Async XLA Ops:
  0.0 2.5 %copy-start.15 = (s32[1024]{0:T(1024)S(1)}, s32[1024]{0:T(1024)}, u32[]{:S(2)}) copy-start(s32[1024]{0:T(1024)} %constant.31.clone.host) | copy-start | bytes 12292
  0.0 2.4 %copy-start.16 = (s32[4,2]{0,1:T(2,128)S(1)}, s32[4,2]{0,1:T(2,128)}, u32[]{:S(2)}) copy-start(s32[4,2]{0,1:T(2,128)} %param.22) | copy-start | bytes 100
  0.0 2.5 %copy-start.11 = (f32[128,128]{1,0:T(8,128)S(1)}, f32[128,128]{1,0:T(8,128)}, u32[]{:S(2)}) copy-start(f32[128,128]{1,0:T(8,128)} %rotation.1) | copy-start | bytes 196612
  1.7 2.1 %collective-permute-start.4 = (f32[16,8,1024]{2,1,0:T(8,128)S(1)}, f32[16,8,1024]{2,1,0:T(8,128)S(1)}, u32[]{:S(2)}, u32[]{:S(2)}) collective-permute-start(f32[16,8,1024]{2,1,0:T(8,128)S(1)} %get-tuple-element.113), channel_id=1, source_target_pairs={{0,4},{1,5},{2,6},{3,7},{4,0},{5,1},{6,2},{7,3},{8,12},{9,13},{10,... | collective-permute-start | bytes 1572872 | tf_op jit(solution)/shard_map/ppermute | solution.py:490
  2.3 5.0 %collective-permute-start.6 = (f32[16,8,1024]{2,1,0:T(8,128)S(1)}, f32[16,8,1024]{2,1,0:T(8,128)S(1)}, u32[]{:S(2)}, u32[]{:S(2)}) collective-permute-start(f32[16,8,1024]{2,1,0:T(8,128)S(1)} %get-tuple-element.109.after), channel_id=1, source_target_pairs={{0,4},{1,5},{2,6},{3,7},{4,0},{5,1},{6,2},{7,3},{8,12},{9,13},{10,... | collective-permute-start | bytes 1572872 | tf_op jit(solution)/shard_map/ppermute | solution.py:490
  4.3 8.7 %collective-permute-start.5 = (f32[12,8,1024]{2,1,0:T(8,128)S(1)}, f32[12,8,1024]{2,1,0:T(8,128)S(1)}, u32[]{:S(2)}, u32[]{:S(2)}) collective-permute-start(f32[12,8,1024]{2,1,0:T(8,128)S(1)} %get-tuple-element.115.rest_2_), channel_id=1, source_target_pairs={{0,8},{1,9},{2,10},{3,11},{4,20},{5,21},{6,22},{7,23},{8,0},{9,1},... | collective-permute-start | bytes 1179656 | tf_op jit(solution)/shard_map/ppermute | solution.py:490
  7.8 7.4 %copy-start.12 = (s32[128,128]{1,0:T(8,128)S(1)}, s32[128,128]{1,0:T(8,128)}, u32[]{:S(2)}) copy-start(s32[128,128]{1,0:T(8,128)} %mask.1) | copy-start | bytes 196612
  7.8 7.4 %copy-start.14 = (f32[64,128]{1,0:T(8,128)S(1)}, f32[64,128]{1,0:T(8,128)}, u32[]{:S(2)}) copy-start(f32[64,128]{1,0:T(8,128)} %constant.32.clone.log_r) | copy-start | bytes 98308
  7.8 11.4 %collective-permute-start.8 = (f32[12,8,1024]{2,1,0:T(8,128)S(1)}, f32[12,8,1024]{2,1,0:T(8,128)S(1)}, u32[]{:S(2)}, u32[]{:S(2)}) collective-permute-start(f32[12,8,1024]{2,1,0:T(8,128)S(1)} %get-tuple-element.117.rest_4_), channel_id=1, source_target_pairs={{0,8},{1,9},{2,10},{3,11},{4,20},{5,21},{6,22},{7,23},{8,0},{9,1},... | collective-permute-start | bytes 1179656 | tf_op jit(solution)/shard_map/ppermute | solution.py:490
  13.1 10.1 %collective-permute-start.7 = (f32[6,8,1024]{2,1,0:T(8,128)S(1)}, f32[6,8,1024]{2,1,0:T(8,128)S(1)}, u32[]{:S(2)}, u32[]{:S(2)}) collective-permute-start(f32[6,8,1024]{2,1,0:T(8,128)S(1)} %shard_map.177.rest_0_), channel_id=1, source_target_pairs={{0,16},{1,17},{2,18},{3,19},{4,12},{5,13},{6,14},{7,15},{8,24},{9,... | collective-permute-start | bytes 589832 | tf_op jit(solution)/shard_map/ppermute | solution.py:490
  19.2 9.0 %copy-start.3 = (bf16[2,256,256]{2,1,0:T(8,128)(2,1)S(1)}, bf16[2,256,256]{2,1,0:T(8,128)(2,1)}, u32[]{:S(2)}) copy-start(bf16[2,256,256]{2,1,0:T(8,128)(2,1)} %constant.38.clone.refs_5_.refs_7_) | copy-start | bytes 786436
  19.2 9.0 %copy-start.4 = (bf16[2,256,256]{2,1,0:T(8,128)(2,1)S(1)}, bf16[2,256,256]{2,1,0:T(8,128)(2,1)}, u32[]{:S(2)}) copy-start(bf16[2,256,256]{2,1,0:T(8,128)(2,1)} %constant.37.clone.refs_4_.refs_6_) | copy-start | bytes 786436
  19.2 9.0 %copy-start.5 = (f32[512,128]{1,0:T(8,128)S(1)}, f32[512,128]{1,0:T(8,128)}, u32[]{:S(2)}) copy-start(f32[512,128]{1,0:T(8,128)} %constant.33.clone.refs_8_.refs_10_) | copy-start | bytes 786436
  19.2 9.0 %copy-start.8 = (bf16[256,256]{1,0:T(8,128)(2,1)S(1)}, bf16[256,256]{1,0:T(8,128)(2,1)}, u32[]{:S(2)}) copy-start(bf16[256,256]{1,0:T(8,128)(2,1)} %constant.42.clone.refs_7_.refs_9_) | copy-start | bytes 393220
  19.2 9.0 %copy-start.9 = (bf16[256,256]{1,0:T(8,128)(2,1)S(1)}, bf16[256,256]{1,0:T(8,128)(2,1)}, u32[]{:S(2)}) copy-start(bf16[256,256]{1,0:T(8,128)(2,1)} %constant.41.clone.refs_6_.refs_8_) | copy-start | bytes 393220
  19.3 6.7 %collective-permute-start.9 = (f32[6,8,1024]{2,1,0:T(8,128)S(1)}, f32[6,8,1024]{2,1,0:T(8,128)S(1)}, u32[]{:S(2)}, u32[]{:S(2)}) collective-permute-start(f32[6,8,1024]{2,1,0:T(8,128)S(1)} %shard_map.178.rest_0_), channel_id=1, source_target_pairs={{0,16},{1,17},{2,18},{3,19},{4,12},{5,13},{6,14},{7,15},{8,24},{9,... | collective-permute-start | bytes 589832 | tf_op jit(solution)/shard_map/ppermute | solution.py:490
  21.6 6.4 %collective-permute-start.12 = (f32[4,8,2048]{2,1,0:T(8,128)S(1)}, f32[4,8,2048]{2,1,0:T(8,128)S(1)}, u32[]{:S(2)}, u32[]{:S(2)}) collective-permute-start(f32[4,8,2048]{2,1,0:T(8,128)S(1)} %get-tuple-element.118.rest_0_), channel_id=1, source_target_pairs={{0,8},{1,9},{2,10},{3,11},{4,20},{5,21},{6,22},{7,23},{8,0},{9,1},... | collective-permute-start | bytes 786440 | tf_op jit(solution)/shard_map/ppermute | solution.py:490
  23.2 5.0 %collective-permute-start.10 = (f32[6,8,1024]{2,1,0:T(8,128)S(1)}, f32[6,8,1024]{2,1,0:T(8,128)S(1)}, u32[]{:S(2)}, u32[]{:S(2)}) collective-permute-start(f32[6,8,1024]{2,1,0:T(8,128)S(1)} %shard_map.179.rest_0_.refs_0_), channel_id=1, source_target_pairs={{0,4},{1,5},{2,6},{3,7},{4,0},{5,1},{6,2},{7,3},{8,12},{9,13},{10,... | collective-permute-start | bytes 589832 | tf_op jit(solution)/shard_map/ppermute | solution.py:490
  26.0 2.2 %collective-permute-start.11 = (f32[6,8,1024]{2,1,0:T(8,128)S(1)}, f32[6,8,1024]{2,1,0:T(8,128)S(1)}, u32[]{:S(2)}, u32[]{:S(2)}) collective-permute-start(f32[6,8,1024]{2,1,0:T(8,128)S(1)} %shard_map.180.rest_0_.refs_1_), channel_id=1, source_target_pairs={{0,4},{1,5},{2,6},{3,7},{4,0},{5,1},{6,2},{7,3},{8,12},{9,13},{10,... | collective-permute-start | bytes 589832 | tf_op jit(solution)/shard_map/ppermute | solution.py:490
  28.0 5.0 %collective-permute-start.20 = (f32[2,8,2048]{2,1,0:T(8,128)S(1)}, f32[2,8,2048]{2,1,0:T(8,128)S(1)}, u32[]{:S(2)}, u32[]{:S(2)}) collective-permute-start(f32[2,8,2048]{2,1,0:T(8,128)S(1)} %shard_map.181.refs_10_), channel_id=1, source_target_pairs={{0,16},{1,17},{2,18},{3,19},{4,12},{5,13},{6,14},{7,15},{8,24},{9,... | collective-permute-start | bytes 393224 | tf_op jit(solution)/shard_map/ppermute | solution.py:490
  29.2 14.9 %copy-start = (bf16[2,256,256]{2,1,0:T(8,128)(2,1)S(1)}, bf16[2,256,256]{2,1,0:T(8,128)(2,1)}, u32[]{:S(2)}) copy-start(bf16[2,256,256]{2,1,0:T(8,128)(2,1)} %constant.40.clone.refs_8_) | copy-start | bytes 786436
  29.2 14.9 %copy-start.1 = (bf16[2,256,256]{2,1,0:T(8,128)(2,1)S(1)}, bf16[2,256,256]{2,1,0:T(8,128)(2,1)}, u32[]{:S(2)}) copy-start(bf16[2,256,256]{2,1,0:T(8,128)(2,1)} %constant.39.clone.refs_7_) | copy-start | bytes 786436
  29.2 14.9 %copy-start.2 = (f32[512,128]{1,0:T(8,128)S(1)}, f32[512,128]{1,0:T(8,128)}, u32[]{:S(2)}) copy-start(f32[512,128]{1,0:T(8,128)} %constant.34.clone.refs_11_) | copy-start | bytes 786436
  29.2 14.9 %copy-start.6 = (bf16[256,256]{1,0:T(8,128)(2,1)S(1)}, bf16[256,256]{1,0:T(8,128)(2,1)}, u32[]{:S(2)}) copy-start(bf16[256,256]{1,0:T(8,128)(2,1)} %constant.44.clone.refs_10_) | copy-start | bytes 393220
  29.3 14.9 %copy-start.7 = (bf16[256,256]{1,0:T(8,128)(2,1)S(1)}, bf16[256,256]{1,0:T(8,128)(2,1)}, u32[]{:S(2)}) copy-start(bf16[256,256]{1,0:T(8,128)(2,1)} %constant.43.clone.refs_9_) | copy-start | bytes 393220
  29.3 14.9 %copy-start.10 = (f32[3,64,128]{2,1,0:T(8,128)S(1)}, f32[3,64,128]{2,1,0:T(8,128)}, u32[]{:S(2)}) copy-start(f32[3,64,128]{2,1,0:T(8,128)} %constant.36.clone.refs_14_) | copy-start | bytes 294916
  29.3 14.9 %copy-start.13 = (f32[2,8,128]{2,1,0:T(8,128)S(1)}, f32[2,8,128]{2,1,0:T(8,128)}, u32[]{:S(2)}) copy-start(f32[2,8,128]{2,1,0:T(8,128)} %constant.35.clone.refs_12_) | copy-start | bytes 24580
  33.1 4.5 %collective-permute-start.21 = (f32[2,8,2048]{2,1,0:T(8,128)S(1)}, f32[2,8,2048]{2,1,0:T(8,128)S(1)}, u32[]{:S(2)}, u32[]{:S(2)}) collective-permute-start(f32[2,8,2048]{2,1,0:T(8,128)S(1)} %shard_map.185.refs_4_), channel_id=1, source_target_pairs={{0,4},{1,5},{2,6},{3,7},{4,0},{5,1},{6,2},{7,3},{8,12},{9,13},{10,... | collective-permute-start | bytes 393224 | tf_op jit(solution)/shard_map/ppermute | solution.py:490
  33.1 9.7 %collective-permute-start.13 = (f32[64,256]{1,0:T(8,128)S(1)}, f32[64,256]{1,0:T(8,128)S(1)}, u32[]{:S(2)}, u32[]{:S(2)}) collective-permute-start(f32[64,256]{1,0:T(8,128)S(1)} %get-tuple-element.126), channel_id=1, source_target_pairs={{0,1},{1,0},{2,3},{3,2},{4,5},{5,4},{6,7},{7,6},{8,9},{9,8},{10,11... | collective-permute-start | bytes 196616 | tf_op jit(solution)/shard_map/ppermute | solution.py:494
  34.8 8.3 %collective-permute-start.14 = (f32[64,256]{1,0:T(8,128)S(1)}, f32[64,256]{1,0:T(8,128)S(1)}, u32[]{:S(2)}, u32[]{:S(2)}) collective-permute-start(f32[64,256]{1,0:T(8,128)S(1)} %get-tuple-element.127), channel_id=1, source_target_pairs={{0,2},{1,3},{2,0},{3,1},{4,6},{5,7},{6,4},{7,5},{8,10},{9,11},{10,... | collective-permute-start | bytes 196616 | tf_op jit(solution)/shard_map/ppermute | solution.py:494
  37.4 6.8 %collective-permute-start.15 = (f32[64,256]{1,0:T(8,128)S(1)}, f32[64,256]{1,0:T(8,128)S(1)}, u32[]{:S(2)}, u32[]{:S(2)}) collective-permute-start(f32[64,256]{1,0:T(8,128)S(1)} %get-tuple-element.128), channel_id=1, source_target_pairs={{0,3},{1,2},{2,1},{3,0},{4,7},{5,6},{6,5},{7,4},{8,11},{9,10},{10,... | collective-permute-start | bytes 196616 | tf_op jit(solution)/shard_map/ppermute | solution.py:494
  38.6 8.9 %collective-permute-start.22 = (f32[64,256]{1,0:T(8,128)S(1)}, f32[64,256]{1,0:T(8,128)S(1)}, u32[]{:S(2)}, u32[]{:S(2)}) collective-permute-start(f32[64,256]{1,0:T(8,128)S(1)} %get-tuple-element.132), channel_id=1, source_target_pairs={{0,1},{1,0},{2,3},{3,2},{4,5},{5,4},{6,7},{7,6},{8,9},{9,8},{10,11... | collective-permute-start | bytes 196616 | tf_op jit(solution)/shard_map/ppermute | solution.py:494
  39.3 8.7 %collective-permute-start.23 = (f32[64,256]{1,0:T(8,128)S(1)}, f32[64,256]{1,0:T(8,128)S(1)}, u32[]{:S(2)}, u32[]{:S(2)}) collective-permute-start(f32[64,256]{1,0:T(8,128)S(1)} %get-tuple-element.133), channel_id=1, source_target_pairs={{0,2},{1,3},{2,0},{3,1},{4,6},{5,7},{6,4},{7,5},{8,10},{9,11},{10,... | collective-permute-start | bytes 196616 | tf_op jit(solution)/shard_map/ppermute | solution.py:494
  42.8 6.2 %collective-permute-start.24 = (f32[64,256]{1,0:T(8,128)S(1)}, f32[64,256]{1,0:T(8,128)S(1)}, u32[]{:S(2)}, u32[]{:S(2)}) collective-permute-start(f32[64,256]{1,0:T(8,128)S(1)} %get-tuple-element.134), channel_id=1, source_target_pairs={{0,3},{1,2},{2,1},{3,0},{4,7},{5,6},{6,5},{7,4},{8,11},{9,10},{10,... | collective-permute-start | bytes 196616 | tf_op jit(solution)/shard_map/ppermute | solution.py:494
  45.4 6.9 %collective-permute-start.17 = (f32[8,4096]{1,0:T(8,128)S(1)}, f32[8,4096]{1,0:T(8,128)S(1)}, u32[]{:S(2)}, u32[]{:S(2)}) collective-permute-start(f32[8,4096]{1,0:T(8,128)S(1)} %shard_map.183.refs_18_), channel_id=1, source_target_pairs={{0,16},{1,17},{2,18},{3,19},{4,12},{5,13},{6,14},{7,15},{8,24},{9,... | collective-permute-start | bytes 393224 | tf_op jit(solution)/shard_map/ppermute | solution.py:490
  46.0 6.3 %collective-permute-start.16 = (f32[8,4096]{1,0:T(8,128)S(1)}, f32[8,4096]{1,0:T(8,128)S(1)}, u32[]{:S(2)}, u32[]{:S(2)}) collective-permute-start(f32[8,4096]{1,0:T(8,128)S(1)} %shard_map.183.refs_18_), channel_id=1, source_target_pairs={{0,8},{1,9},{2,10},{3,11},{4,20},{5,21},{6,22},{7,23},{8,0},{9,1},... | collective-permute-start | bytes 393224 | tf_op jit(solution)/shard_map/ppermute | solution.py:490
  50.2 5.0 %collective-permute-start.26 = (f32[8,4096]{1,0:T(8,128)S(1)}, f32[8,4096]{1,0:T(8,128)S(1)}, u32[]{:S(2)}, u32[]{:S(2)}) collective-permute-start(f32[8,4096]{1,0:T(8,128)S(1)} %shard_map.187), channel_id=1, source_target_pairs={{0,16},{1,17},{2,18},{3,19},{4,12},{5,13},{6,14},{7,15},{8,24},{9,... | collective-permute-start | bytes 393224 | tf_op jit(solution)/shard_map/ppermute | solution.py:490
  50.8 5.0 %collective-permute-start.25 = (f32[8,4096]{1,0:T(8,128)S(1)}, f32[8,4096]{1,0:T(8,128)S(1)}, u32[]{:S(2)}, u32[]{:S(2)}) collective-permute-start(f32[8,4096]{1,0:T(8,128)S(1)} %shard_map.187), channel_id=1, source_target_pairs={{0,8},{1,9},{2,10},{3,11},{4,20},{5,21},{6,22},{7,23},{8,0},{9,1},... | collective-permute-start | bytes 393224 | tf_op jit(solution)/shard_map/ppermute | solution.py:490
  52.3 5.4 %collective-permute-start.19 = (f32[2,8,4096]{2,1,0:T(8,128)S(1)}, f32[2,8,4096]{2,1,0:T(8,128)S(1)}, u32[]{:S(2)}, u32[]{:S(2)}) collective-permute-start(f32[2,8,4096]{2,1,0:T(8,128)S(1)} %shard_map.184), channel_id=1, source_target_pairs={{0,4},{1,5},{2,6},{3,7},{4,0},{5,1},{6,2},{7,3},{8,12},{9,13},{10,... | collective-permute-start | bytes 786440 | tf_op jit(solution)/shard_map/ppermute | solution.py:490
  55.8 2.0 %collective-permute-start.28 = (f32[2,8,4096]{2,1,0:T(8,128)S(1)}, f32[2,8,4096]{2,1,0:T(8,128)S(1)}, u32[]{:S(2)}, u32[]{:S(2)}) collective-permute-start(f32[2,8,4096]{2,1,0:T(8,128)S(1)} %shard_map.188), channel_id=1, source_target_pairs={{0,4},{1,5},{2,6},{3,7},{4,0},{5,1},{6,2},{7,3},{8,12},{9,13},{10,... | collective-permute-start | bytes 786440 | tf_op jit(solution)/shard_map/ppermute | solution.py:490
  55.8 1.7 %collective-permute-start.18 = (f32[8,4096]{1,0:T(8,128)S(1)}, f32[8,4096]{1,0:T(8,128)S(1)}, u32[]{:S(2)}, u32[]{:S(2)}) collective-permute-start(f32[8,4096]{1,0:T(8,128)S(1)} %shard_map.183.refs_18_), channel_id=1, source_target_pairs={{0,4},{1,5},{2,6},{3,7},{4,0},{5,1},{6,2},{7,3},{8,12},{9,13},{10,... | collective-permute-start | bytes 393224 | tf_op jit(solution)/shard_map/ppermute | solution.py:490
  56.3 1.4 %collective-permute-start.27 = (f32[8,4096]{1,0:T(8,128)S(1)}, f32[8,4096]{1,0:T(8,128)S(1)}, u32[]{:S(2)}, u32[]{:S(2)}) collective-permute-start(f32[8,4096]{1,0:T(8,128)S(1)} %shard_map.187), channel_id=1, source_target_pairs={{0,4},{1,5},{2,6},{3,7},{4,0},{5,1},{6,2},{7,3},{8,12},{9,13},{10,... | collective-permute-start | bytes 393224 | tf_op jit(solution)/shard_map/ppermute | solution.py:490

commit v8 on v7

--- a/solution.py
+++ b/solution.py
@@ -119,11 +119,7 @@
 
 def fetch_kernel(source, *rest):
     outs, (whole, sem) = rest[:-2], rest[-2:]
-    step = whole.shape[0] // len(outs)
-    copies = [
-        pltpu.make_async_copy(source.at[pl.ds(n * step, step)], whole.at[pl.ds(n * step, step)], sem.at[n])
-        for n in range(len(outs))
-    ]
+    copies = [pltpu.make_async_copy(source.at[n], whole.at[n], sem.at[n]) for n in range(whole.shape[0])]
     for copy in copies:
         copy.start()
     for copy in copies:
@@ -499,7 +495,7 @@
     part = jax.ShapeDtypeStruct((per_device, planes, chunk), f32)
     fetched = pl.pallas_call(
         fetch_kernel, out_shape=[part] * (2 * CHUNKS), in_specs=[HBM], out_specs=[VM] * (2 * CHUNKS),
-        scratch_shapes=[pltpu.VMEM(shape, f32), DMA((2 * CHUNKS,))], name="fetch", compiler_params=grant(8),
+        scratch_shapes=[pltpu.VMEM(shape, f32), DMA((max(per_device, 2 * CHUNKS),))], name="fetch", compiler_params=grant(8),
     )(orbitals)
     theirs, mine = [], fetched[CHUNKS:]
     for taken in fetched[:CHUNKS]:

time: 59 us -> 59.2 us (level)
  no operation moved by 1% of the time
where the time goes in v8:
time: 59.2 us; the launch traced here: 58.2 us
  starting transfers between devices  23.9 us (40%)
  waiting for transfers between devices  21 us (35%)
  Pallas kernels  12 us (20%)
  between operations  1.03 us (2%)
    ppermute x19, waiting for transfers between devices, swap(): return lax.ppermute(x, axes, moves)  18.4 us
    ppermute x19, starting transfers between devices, swap(): return lax.ppermute(x, axes, moves)  15 us
    ppermute x6, starting transfers between devices, cross(): return lax.ppermute(x, axes, moves)  8.9 us
    ppermute x6, waiting for transfers between devices, cross(): return lax.ppermute(x, axes, moves)  2.61 us
    pallas_call x1, Pallas kernels, tile_device(): pl.pallas_call(functools.partial(ready_kernel, per_device, n_grid), out_s...  2.6 us
    pallas_call x2, Pallas kernels, tile_device(): pl.pallas_call(functools.partial(backward_kernel, u, (CHUNKS, CHUNKS, len...  2.39 us
    pallas_call x2, Pallas kernels, tile_device(): pl.pallas_call(functools.partial(forward_kernel, u, counts + (n_grid - 1,...  1.99 us
    pallas_call x1, Pallas kernels, tile_device(): pl.pallas_call(fetch_kernel, out_shape=[part] * (2 * CHUNKS), in_specs=[H...  1.91 us
  transfers between devices with their start and end apart: 25, of which 13 were waited for; matrix products, arithmetic and copies ran while one was open for 0% of the time, Pallas kernels for 17%

profile of v8, /device:TPU:0, one launch (start us, length us, event | category | flops | bytes accessed | tf_op | source)
XLA Modules:
  0.0 58.2 jit_solution(8771826746251840710)
XLA Ops:
  0.0 1.9 %fetch.1 = (f32[16,8,1024]{2,1,0:T(8,128)S(1)}, f32[16,8,1024]{2,1,0:T(8,128)S(1)}, f32[16,8,1024]{2,1,0:T(8,128)S(1)}, f32[16,8,1024]{2,1,0:T(8,128)S(1)}) custom-call(f32[16,8,4096]{2,1,0:T(8,128)} %source.1), custom_call_target="tpu_custom_call" | custom-call | tf_op jit(solution)/shard_map/fetch/pallas_call | solution.py:496
  1.9 0.6 collective-permute-start.4
  2.5 0.1 collective-permute-start.6
  2.6 0.1 copy.24.tiles
  2.7 1.0 %setup.1 = (bf16[256,256]{1,0:T(8,128)(2,1)S(1)}, bf16[256,256]{1,0:T(8,128)(2,1)S(1)}) custom-call(s32[4,2]{1,0:T(4,128)S(1)} %copy.24.tiles, s32[1024]{0:T(1024)S(1)} %copy-done.15, f32[128,128]{1,0:T(8,128)S(1)} %copy-done.11, f32[16,8,1024]{2,1,0:T(8,128)S(1)} %get-tuple-element.109.after), custom_call_target="tpu_custom_call" | custom-call | tf_op jit(solution)/shard_map/setup/pallas_call | solution.py:512
  3.7 0.3 collective-permute-done.4.rest_1_
  4.0 0.5 shard_map.174
  4.5 2.9 %collective-permute-start.5 = (f32[12,8,1024]{2,1,0:T(8,128)S(1)}, f32[12,8,1024]{2,1,0:T(8,128)S(1)}, u32[]{:S(2)}, u32[]{:S(2)}) collective-permute-start(f32[12,8,1024]{2,1,0:T(8,128)S(1)} %get-tuple-element.115.rest_2_), channel_id=1, source_target_pairs={{0,8},{1,9},{2,10},{3,11},{4,20},{5,21},{6,22},{7,23},{8,0},{9,1},... | collective-permute-start | bytes 1179656 | tf_op jit(solution)/shard_map/ppermute | solution.py:486
  7.4 0.5 shard_map.175
  8.0 0.2 collective-permute-start.8
  8.2 0.7 %shard_map.176 = (f32[4,8,2048]{2,1,0:T(8,128)S(1)}, f32[4,8,2048]{2,1,0:T(8,128)S(1)}) custom-call(bf16[256,256]{1,0:T(8,128)(2,1)S(1)} %get-tuple-element.110.high, bf16[256,256]{1,0:T(8,128)(2,1)S(1)} %get-tuple-element.111.low, f32[16,8,1024]{2,1,0:T(8,128)S(1)} %get-tuple-element.112.rest_0_, f32[16,8,1024]{2,1,0:T(8,128)S(1)} %collective-permute-done.4.rest_1_, ...), custom_call_target="tpu_custom_call" | custom-call | tf_op jit(solution)/shard_map/pallas_call | solution.py:519
  8.9 4.3 %collective-permute-done.5.got = f32[12,8,1024]{2,1,0:T(8,128)S(1)} collective-permute-done((f32[12,8,1024]{2,1,0:T(8,128)S(1)}, f32[12,8,1024]{2,1,0:T(8,128)S(1)}, u32[]{:S(2)}, u32[]{:S(2)}) %collective-permute-start.5) | collective-permute-done | bytes 393248 | tf_op jit(solution)/shard_map/ppermute | solution.py:486
  13.2 2.1 %collective-permute-start.7 = (f32[6,8,1024]{2,1,0:T(8,128)S(1)}, f32[6,8,1024]{2,1,0:T(8,128)S(1)}, u32[]{:S(2)}, u32[]{:S(2)}) collective-permute-start(f32[6,8,1024]{2,1,0:T(8,128)S(1)} %shard_map.177.rest_0_), channel_id=1, source_target_pairs={{0,16},{1,17},{2,18},{3,19},{4,12},{5,13},{6,14},{7,15},{8,24},{9,... | collective-permute-start | bytes 589832 | tf_op jit(solution)/shard_map/ppermute | solution.py:486
  15.3 2.6 %ready.1 = (f32[16,8,4096]{2,1,0:T(8,128)}, f32[6,64,128]{2,1,0:T(8,128)S(1)}, f32[8,128]{1,0:T(8,128)S(1)}, f32[8,128]{1,0:T(8,128)S(1)}, s32[1]{0:T(128)}) custom-call(s32[4,2]{1,0:T(4,128)S(1)} %copy.24.tiles, s32[1024]{0:T(1024)S(1)} %copy-done.15, s32[128,128]{1,0:T(8,128)S(1)} %copy-done.12, f32[64,128]{1,0:T(8,128)S(1)} %copy-done.14, ...), custom_call_target="tpu_custom_call" | custom-call | tf_op jit(solution)/shard_map/ready/pallas_call | solution.py:554
  18.0 1.4 %collective-permute-done.8.got = f32[12,8,1024]{2,1,0:T(8,128)S(1)} collective-permute-done((f32[12,8,1024]{2,1,0:T(8,128)S(1)}, f32[12,8,1024]{2,1,0:T(8,128)S(1)}, u32[]{:S(2)}, u32[]{:S(2)}) %collective-permute-start.8) | collective-permute-done | bytes 393248 | tf_op jit(solution)/shard_map/ppermute | solution.py:486
  19.4 2.4 %collective-permute-start.9 = (f32[6,8,1024]{2,1,0:T(8,128)S(1)}, f32[6,8,1024]{2,1,0:T(8,128)S(1)}, u32[]{:S(2)}, u32[]{:S(2)}) collective-permute-start(f32[6,8,1024]{2,1,0:T(8,128)S(1)} %shard_map.178.rest_0_), channel_id=1, source_target_pairs={{0,16},{1,17},{2,18},{3,19},{4,12},{5,13},{6,14},{7,15},{8,24},{9,... | collective-permute-start | bytes 589832 | tf_op jit(solution)/shard_map/ppermute | solution.py:486
  21.8 1.5 %collective-permute-start.12 = (f32[4,8,2048]{2,1,0:T(8,128)S(1)}, f32[4,8,2048]{2,1,0:T(8,128)S(1)}, u32[]{:S(2)}, u32[]{:S(2)}) collective-permute-start(f32[4,8,2048]{2,1,0:T(8,128)S(1)} %get-tuple-element.118.rest_0_), channel_id=1, source_target_pairs={{0,8},{1,9},{2,10},{3,11},{4,20},{5,21},{6,22},{7,23},{8,0},{9,1},... | collective-permute-start | bytes 786440 | tf_op jit(solution)/shard_map/ppermute | solution.py:486
  23.3 0.1 collective-permute-start.10
  23.4 2.7 %collective-permute-done.9.passed = f32[6,8,1024]{2,1,0:T(8,128)S(1)} collective-permute-done((f32[6,8,1024]{2,1,0:T(8,128)S(1)}, f32[6,8,1024]{2,1,0:T(8,128)S(1)}, u32[]{:S(2)}, u32[]{:S(2)}) %collective-permute-start.9) | collective-permute-done | bytes 196640 | tf_op jit(solution)/shard_map/ppermute | solution.py:486
  26.2 2.0 %collective-permute-done.12.got = f32[4,8,2048]{2,1,0:T(8,128)S(1)} collective-permute-done((f32[4,8,2048]{2,1,0:T(8,128)S(1)}, f32[4,8,2048]{2,1,0:T(8,128)S(1)}, u32[]{:S(2)}, u32[]{:S(2)}) %collective-permute-start.12) | collective-permute-done | bytes 262176 | tf_op jit(solution)/shard_map/ppermute | solution.py:486
  28.2 0.1 collective-permute-start.20
  28.4 1.0 %shard_map.182 = (f32[64,256]{1,0:T(8,128)S(1)}, f32[64,256]{1,0:T(8,128)S(1)}, f32[64,256]{1,0:T(8,128)S(1)}, f32[512,256]{1,0:T(8,128)S(1)}, f32[64,256]{1,0:T(8,128)S(1)}, /*index=5*/f32[64,256]{1,0:T(8,128)S(1)}) custom-call(f32[6,8,1024]{2,1,0:T(8,128)S(1)} %shard_map.179.rest_0_.refs_0_, f32[6,8,1024]{2,1,0:T(8,128)S(1)} %shard_map.180.rest_0_.refs_1_, ...), custom_call_target="tpu_custom_call" | custom-call | tf_op jit(solution)/shard_map/pallas_call | solution.py:593
  29.5 3.7 %collective-permute-done.20.passed = f32[2,8,2048]{2,1,0:T(8,128)S(1)} collective-permute-done((f32[2,8,2048]{2,1,0:T(8,128)S(1)}, f32[2,8,2048]{2,1,0:T(8,128)S(1)}, u32[]{:S(2)}, u32[]{:S(2)}) %collective-permute-start.20) | collective-permute-done | bytes 131104 | tf_op jit(solution)/shard_map/ppermute | solution.py:486
  33.2 0.1 collective-permute-start.21
  33.3 1.6 %collective-permute-start.13 = (f32[64,256]{1,0:T(8,128)S(1)}, f32[64,256]{1,0:T(8,128)S(1)}, u32[]{:S(2)}, u32[]{:S(2)}) collective-permute-start(f32[64,256]{1,0:T(8,128)S(1)} %get-tuple-element.126), channel_id=1, source_target_pairs={{0,1},{1,0},{2,3},{3,2},{4,5},{5,4},{6,7},{7,6},{8,9},{9,8},{10,11... | collective-permute-start | bytes 196616 | tf_op jit(solution)/shard_map/ppermute | solution.py:490
  35.0 2.6 %collective-permute-start.14 = (f32[64,256]{1,0:T(8,128)S(1)}, f32[64,256]{1,0:T(8,128)S(1)}, u32[]{:S(2)}, u32[]{:S(2)}) collective-permute-start(f32[64,256]{1,0:T(8,128)S(1)} %get-tuple-element.127), channel_id=1, source_target_pairs={{0,2},{1,3},{2,0},{3,1},{4,6},{5,7},{6,4},{7,5},{8,10},{9,11},{10,... | collective-permute-start | bytes 196616 | tf_op jit(solution)/shard_map/ppermute | solution.py:490
  37.6 0.2 collective-permute-start.15
  37.8 1.0 %shard_map.186 = (f32[64,256]{1,0:T(8,128)S(1)}, f32[64,256]{1,0:T(8,128)S(1)}, f32[64,256]{1,0:T(8,128)S(1)}, f32[512,256]{1,0:T(8,128)S(1)}, f32[64,256]{1,0:T(8,128)S(1)}, /*index=5*/f32[64,256]{1,0:T(8,128)S(1)}) custom-call(f32[6,8,1024]{2,1,0:T(8,128)S(1)} %shard_map.179.rest_0_.refs_0_, f32[6,8,1024]{2,1,0:T(8,128)S(1)} %shard_map.180.rest_0_.refs_1_, ...), custom_call_target="tpu_custom_call" | custom-call | tf_op jit(solution)/shard_map/pallas_call | solution.py:593
  38.8 0.7 %collective-permute-start.22 = (f32[64,256]{1,0:T(8,128)S(1)}, f32[64,256]{1,0:T(8,128)S(1)}, u32[]{:S(2)}, u32[]{:S(2)}) collective-permute-start(f32[64,256]{1,0:T(8,128)S(1)} %get-tuple-element.132), channel_id=1, source_target_pairs={{0,1},{1,0},{2,3},{3,2},{4,5},{5,4},{6,7},{7,6},{8,9},{9,8},{10,11... | collective-permute-start | bytes 196616 | tf_op jit(solution)/shard_map/ppermute | solution.py:490
  39.5 3.5 %collective-permute-start.23 = (f32[64,256]{1,0:T(8,128)S(1)}, f32[64,256]{1,0:T(8,128)S(1)}, u32[]{:S(2)}, u32[]{:S(2)}) collective-permute-start(f32[64,256]{1,0:T(8,128)S(1)} %get-tuple-element.133), channel_id=1, source_target_pairs={{0,2},{1,3},{2,0},{3,1},{4,6},{5,7},{6,4},{7,5},{8,10},{9,11},{10,... | collective-permute-start | bytes 196616 | tf_op jit(solution)/shard_map/ppermute | solution.py:490
  43.0 0.2 collective-permute-start.24
  43.2 1.1 %collective-permute-done.15.refs_6_ = f32[64,256]{1,0:T(8,128)S(1)} collective-permute-done((f32[64,256]{1,0:T(8,128)S(1)}, f32[64,256]{1,0:T(8,128)S(1)}, u32[]{:S(2)}, u32[]{:S(2)}) %collective-permute-start.15) | collective-permute-done | bytes 65568 | tf_op jit(solution)/shard_map/ppermute | solution.py:490
  44.4 1.2 %shard_map.183.refs_18_ = f32[8,4096]{1,0:T(8,128)S(1)} custom-call(f32[8,128]{1,0:T(8,128)S(1)} %get-tuple-element.121.flags, f32[6,8,1024]{2,1,0:T(8,128)S(1)} %shard_map.179.rest_0_.refs_0_, f32[6,8,1024]{2,1,0:T(8,128)S(1)} %shard_map.180.rest_0_.refs_1_, f32[6,8,1024]{2,1,0:T(8,128)S(1)} %collective-permute-done.10.refs_2_, ...), custom_call_target="tpu_custom_call" | custom-call | tf_op jit(solution)/shard_map/pallas_call | solution.py:611
  45.6 0.6 collective-permute-start.17
  46.2 1.5 %collective-permute-start.16 = (f32[8,4096]{1,0:T(8,128)S(1)}, f32[8,4096]{1,0:T(8,128)S(1)}, u32[]{:S(2)}, u32[]{:S(2)}) collective-permute-start(f32[8,4096]{1,0:T(8,128)S(1)} %shard_map.183.refs_18_), channel_id=1, source_target_pairs={{0,8},{1,9},{2,10},{3,11},{4,20},{5,21},{6,22},{7,23},{8,0},{9,1},... | collective-permute-start | bytes 393224 | tf_op jit(solution)/shard_map/ppermute | solution.py:486
  47.7 0.6 %collective-permute-done.23.refs_5_ = f32[64,256]{1,0:T(8,128)S(1)} collective-permute-done((f32[64,256]{1,0:T(8,128)S(1)}, f32[64,256]{1,0:T(8,128)S(1)}, u32[]{:S(2)}, u32[]{:S(2)}) %collective-permute-start.23) | collective-permute-done | bytes 65568 | tf_op jit(solution)/shard_map/ppermute | solution.py:490
  48.3 0.9 %collective-permute-done.24.refs_6_ = f32[64,256]{1,0:T(8,128)S(1)} collective-permute-done((f32[64,256]{1,0:T(8,128)S(1)}, f32[64,256]{1,0:T(8,128)S(1)}, u32[]{:S(2)}, u32[]{:S(2)}) %collective-permute-start.24) | collective-permute-done | bytes 65568 | tf_op jit(solution)/shard_map/ppermute | solution.py:490
  49.2 1.2 %shard_map.187 = f32[8,4096]{1,0:T(8,128)S(1)} custom-call(f32[8,128]{1,0:T(8,128)S(1)} %get-tuple-element.121.flags, f32[6,8,1024]{2,1,0:T(8,128)S(1)} %shard_map.179.rest_0_.refs_0_, f32[6,8,1024]{2,1,0:T(8,128)S(1)} %shard_map.180.rest_0_.refs_1_, f32[6,8,1024]{2,1,0:T(8,128)S(1)} %collective-permute-done.10.refs_2_, ...), custom_call_target="tpu_custom_call" | custom-call | tf_op jit(solution)/shard_map/pallas_call | solution.py:611
  50.4 0.6 collective-permute-start.26
  50.9 1.5 %collective-permute-start.25 = (f32[8,4096]{1,0:T(8,128)S(1)}, f32[8,4096]{1,0:T(8,128)S(1)}, u32[]{:S(2)}, u32[]{:S(2)}) collective-permute-start(f32[8,4096]{1,0:T(8,128)S(1)} %shard_map.187), channel_id=1, source_target_pairs={{0,8},{1,9},{2,10},{3,11},{4,20},{5,21},{6,22},{7,23},{8,0},{9,1},... | collective-permute-start | bytes 393224 | tf_op jit(solution)/shard_map/ppermute | solution.py:486
  52.6 2.9 %collective-permute-done.26.y = f32[8,4096]{1,0:T(8,128)S(1)} collective-permute-done((f32[8,4096]{1,0:T(8,128)S(1)}, f32[8,4096]{1,0:T(8,128)S(1)}, u32[]{:S(2)}, u32[]{:S(2)}) %collective-permute-start.26) | collective-permute-done | bytes 131104 | tf_op jit(solution)/shard_map/ppermute | solution.py:486
  55.4 0.5 collective-permute-done.25.x
  56.0 0.5 collective-permute-start.18
  56.5 0.1 collective-permute-start.27
  57.3 0.5 collective-permute-done.18
  57.7 0.2 collective-permute-done.27
  57.9 0.3 conditional.1
  57.9 0.2 place.2
  (57 shorter events, 0.5 us)
Async XLA Ops:
  0.0 2.7 %copy-start.15 = (s32[1024]{0:T(1024)S(1)}, s32[1024]{0:T(1024)}, u32[]{:S(2)}) copy-start(s32[1024]{0:T(1024)} %constant.31.clone.host) | copy-start | bytes 12292
  0.0 2.6 %copy-start.16 = (s32[4,2]{0,1:T(2,128)S(1)}, s32[4,2]{0,1:T(2,128)}, u32[]{:S(2)}) copy-start(s32[4,2]{0,1:T(2,128)} %param.22) | copy-start | bytes 100
  0.0 2.7 %copy-start.11 = (f32[128,128]{1,0:T(8,128)S(1)}, f32[128,128]{1,0:T(8,128)}, u32[]{:S(2)}) copy-start(f32[128,128]{1,0:T(8,128)} %rotation.1) | copy-start | bytes 196612
  1.9 2.1 %collective-permute-start.4 = (f32[16,8,1024]{2,1,0:T(8,128)S(1)}, f32[16,8,1024]{2,1,0:T(8,128)S(1)}, u32[]{:S(2)}, u32[]{:S(2)}) collective-permute-start(f32[16,8,1024]{2,1,0:T(8,128)S(1)} %get-tuple-element.113), channel_id=1, source_target_pairs={{0,4},{1,5},{2,6},{3,7},{4,0},{5,1},{6,2},{7,3},{8,12},{9,13},{10,... | collective-permute-start | bytes 1572872 | tf_op jit(solution)/shard_map/ppermute | solution.py:486
  2.5 5.0 %collective-permute-start.6 = (f32[16,8,1024]{2,1,0:T(8,128)S(1)}, f32[16,8,1024]{2,1,0:T(8,128)S(1)}, u32[]{:S(2)}, u32[]{:S(2)}) collective-permute-start(f32[16,8,1024]{2,1,0:T(8,128)S(1)} %get-tuple-element.109.after), channel_id=1, source_target_pairs={{0,4},{1,5},{2,6},{3,7},{4,0},{5,1},{6,2},{7,3},{8,12},{9,13},{10,... | collective-permute-start | bytes 1572872 | tf_op jit(solution)/shard_map/ppermute | solution.py:486
  4.5 8.7 %collective-permute-start.5 = (f32[12,8,1024]{2,1,0:T(8,128)S(1)}, f32[12,8,1024]{2,1,0:T(8,128)S(1)}, u32[]{:S(2)}, u32[]{:S(2)}) collective-permute-start(f32[12,8,1024]{2,1,0:T(8,128)S(1)} %get-tuple-element.115.rest_2_), channel_id=1, source_target_pairs={{0,8},{1,9},{2,10},{3,11},{4,20},{5,21},{6,22},{7,23},{8,0},{9,1},... | collective-permute-start | bytes 1179656 | tf_op jit(solution)/shard_map/ppermute | solution.py:486
  7.9 7.4 %copy-start.12 = (s32[128,128]{1,0:T(8,128)S(1)}, s32[128,128]{1,0:T(8,128)}, u32[]{:S(2)}) copy-start(s32[128,128]{1,0:T(8,128)} %mask.1) | copy-start | bytes 196612
  8.0 7.4 %copy-start.14 = (f32[64,128]{1,0:T(8,128)S(1)}, f32[64,128]{1,0:T(8,128)}, u32[]{:S(2)}) copy-start(f32[64,128]{1,0:T(8,128)} %constant.32.clone.log_r) | copy-start | bytes 98308
  8.0 11.4 %collective-permute-start.8 = (f32[12,8,1024]{2,1,0:T(8,128)S(1)}, f32[12,8,1024]{2,1,0:T(8,128)S(1)}, u32[]{:S(2)}, u32[]{:S(2)}) collective-permute-start(f32[12,8,1024]{2,1,0:T(8,128)S(1)} %get-tuple-element.117.rest_4_), channel_id=1, source_target_pairs={{0,8},{1,9},{2,10},{3,11},{4,20},{5,21},{6,22},{7,23},{8,0},{9,1},... | collective-permute-start | bytes 1179656 | tf_op jit(solution)/shard_map/ppermute | solution.py:486
  13.2 10.1 %collective-permute-start.7 = (f32[6,8,1024]{2,1,0:T(8,128)S(1)}, f32[6,8,1024]{2,1,0:T(8,128)S(1)}, u32[]{:S(2)}, u32[]{:S(2)}) collective-permute-start(f32[6,8,1024]{2,1,0:T(8,128)S(1)} %shard_map.177.rest_0_), channel_id=1, source_target_pairs={{0,16},{1,17},{2,18},{3,19},{4,12},{5,13},{6,14},{7,15},{8,24},{9,... | collective-permute-start | bytes 589832 | tf_op jit(solution)/shard_map/ppermute | solution.py:486
  19.4 9.0 %copy-start.3 = (bf16[2,256,256]{2,1,0:T(8,128)(2,1)S(1)}, bf16[2,256,256]{2,1,0:T(8,128)(2,1)}, u32[]{:S(2)}) copy-start(bf16[2,256,256]{2,1,0:T(8,128)(2,1)} %constant.38.clone.refs_5_.refs_7_) | copy-start | bytes 786436
  19.4 9.0 %copy-start.4 = (bf16[2,256,256]{2,1,0:T(8,128)(2,1)S(1)}, bf16[2,256,256]{2,1,0:T(8,128)(2,1)}, u32[]{:S(2)}) copy-start(bf16[2,256,256]{2,1,0:T(8,128)(2,1)} %constant.37.clone.refs_4_.refs_6_) | copy-start | bytes 786436
  19.4 9.0 %copy-start.5 = (f32[512,128]{1,0:T(8,128)S(1)}, f32[512,128]{1,0:T(8,128)}, u32[]{:S(2)}) copy-start(f32[512,128]{1,0:T(8,128)} %constant.33.clone.refs_8_.refs_10_) | copy-start | bytes 786436
  19.4 9.0 %copy-start.8 = (bf16[256,256]{1,0:T(8,128)(2,1)S(1)}, bf16[256,256]{1,0:T(8,128)(2,1)}, u32[]{:S(2)}) copy-start(bf16[256,256]{1,0:T(8,128)(2,1)} %constant.42.clone.refs_7_.refs_9_) | copy-start | bytes 393220
  19.4 9.0 %copy-start.9 = (bf16[256,256]{1,0:T(8,128)(2,1)S(1)}, bf16[256,256]{1,0:T(8,128)(2,1)}, u32[]{:S(2)}) copy-start(bf16[256,256]{1,0:T(8,128)(2,1)} %constant.41.clone.refs_6_.refs_8_) | copy-start | bytes 393220
  19.4 6.7 %collective-permute-start.9 = (f32[6,8,1024]{2,1,0:T(8,128)S(1)}, f32[6,8,1024]{2,1,0:T(8,128)S(1)}, u32[]{:S(2)}, u32[]{:S(2)}) collective-permute-start(f32[6,8,1024]{2,1,0:T(8,128)S(1)} %shard_map.178.rest_0_), channel_id=1, source_target_pairs={{0,16},{1,17},{2,18},{3,19},{4,12},{5,13},{6,14},{7,15},{8,24},{9,... | collective-permute-start | bytes 589832 | tf_op jit(solution)/shard_map/ppermute | solution.py:486
  21.8 6.4 %collective-permute-start.12 = (f32[4,8,2048]{2,1,0:T(8,128)S(1)}, f32[4,8,2048]{2,1,0:T(8,128)S(1)}, u32[]{:S(2)}, u32[]{:S(2)}) collective-permute-start(f32[4,8,2048]{2,1,0:T(8,128)S(1)} %get-tuple-element.118.rest_0_), channel_id=1, source_target_pairs={{0,8},{1,9},{2,10},{3,11},{4,20},{5,21},{6,22},{7,23},{8,0},{9,1},... | collective-permute-start | bytes 786440 | tf_op jit(solution)/shard_map/ppermute | solution.py:486
  23.3 5.0 %collective-permute-start.10 = (f32[6,8,1024]{2,1,0:T(8,128)S(1)}, f32[6,8,1024]{2,1,0:T(8,128)S(1)}, u32[]{:S(2)}, u32[]{:S(2)}) collective-permute-start(f32[6,8,1024]{2,1,0:T(8,128)S(1)} %shard_map.179.rest_0_.refs_0_), channel_id=1, source_target_pairs={{0,4},{1,5},{2,6},{3,7},{4,0},{5,1},{6,2},{7,3},{8,12},{9,13},{10,... | collective-permute-start | bytes 589832 | tf_op jit(solution)/shard_map/ppermute | solution.py:486
  26.1 2.2 %collective-permute-start.11 = (f32[6,8,1024]{2,1,0:T(8,128)S(1)}, f32[6,8,1024]{2,1,0:T(8,128)S(1)}, u32[]{:S(2)}, u32[]{:S(2)}) collective-permute-start(f32[6,8,1024]{2,1,0:T(8,128)S(1)} %shard_map.180.rest_0_.refs_1_), channel_id=1, source_target_pairs={{0,4},{1,5},{2,6},{3,7},{4,0},{5,1},{6,2},{7,3},{8,12},{9,13},{10,... | collective-permute-start | bytes 589832 | tf_op jit(solution)/shard_map/ppermute | solution.py:486
  28.2 5.0 %collective-permute-start.20 = (f32[2,8,2048]{2,1,0:T(8,128)S(1)}, f32[2,8,2048]{2,1,0:T(8,128)S(1)}, u32[]{:S(2)}, u32[]{:S(2)}) collective-permute-start(f32[2,8,2048]{2,1,0:T(8,128)S(1)} %shard_map.181.refs_10_), channel_id=1, source_target_pairs={{0,16},{1,17},{2,18},{3,19},{4,12},{5,13},{6,14},{7,15},{8,24},{9,... | collective-permute-start | bytes 393224 | tf_op jit(solution)/shard_map/ppermute | solution.py:486
  29.4 14.9 %copy-start = (bf16[2,256,256]{2,1,0:T(8,128)(2,1)S(1)}, bf16[2,256,256]{2,1,0:T(8,128)(2,1)}, u32[]{:S(2)}) copy-start(bf16[2,256,256]{2,1,0:T(8,128)(2,1)} %constant.40.clone.refs_8_) | copy-start | bytes 786436
  29.4 14.9 %copy-start.1 = (bf16[2,256,256]{2,1,0:T(8,128)(2,1)S(1)}, bf16[2,256,256]{2,1,0:T(8,128)(2,1)}, u32[]{:S(2)}) copy-start(bf16[2,256,256]{2,1,0:T(8,128)(2,1)} %constant.39.clone.refs_7_) | copy-start | bytes 786436
  29.4 14.9 %copy-start.2 = (f32[512,128]{1,0:T(8,128)S(1)}, f32[512,128]{1,0:T(8,128)}, u32[]{:S(2)}) copy-start(f32[512,128]{1,0:T(8,128)} %constant.34.clone.refs_11_) | copy-start | bytes 786436
  29.4 14.9 %copy-start.6 = (bf16[256,256]{1,0:T(8,128)(2,1)S(1)}, bf16[256,256]{1,0:T(8,128)(2,1)}, u32[]{:S(2)}) copy-start(bf16[256,256]{1,0:T(8,128)(2,1)} %constant.44.clone.refs_10_) | copy-start | bytes 393220
  29.4 14.9 %copy-start.7 = (bf16[256,256]{1,0:T(8,128)(2,1)S(1)}, bf16[256,256]{1,0:T(8,128)(2,1)}, u32[]{:S(2)}) copy-start(bf16[256,256]{1,0:T(8,128)(2,1)} %constant.43.clone.refs_9_) | copy-start | bytes 393220
  29.5 14.9 %copy-start.10 = (f32[3,64,128]{2,1,0:T(8,128)S(1)}, f32[3,64,128]{2,1,0:T(8,128)}, u32[]{:S(2)}) copy-start(f32[3,64,128]{2,1,0:T(8,128)} %constant.36.clone.refs_14_) | copy-start | bytes 294916
  29.5 14.9 %copy-start.13 = (f32[2,8,128]{2,1,0:T(8,128)S(1)}, f32[2,8,128]{2,1,0:T(8,128)}, u32[]{:S(2)}) copy-start(f32[2,8,128]{2,1,0:T(8,128)} %constant.35.clone.refs_12_) | copy-start | bytes 24580
  33.2 4.5 %collective-permute-start.21 = (f32[2,8,2048]{2,1,0:T(8,128)S(1)}, f32[2,8,2048]{2,1,0:T(8,128)S(1)}, u32[]{:S(2)}, u32[]{:S(2)}) collective-permute-start(f32[2,8,2048]{2,1,0:T(8,128)S(1)} %shard_map.185.refs_4_), channel_id=1, source_target_pairs={{0,4},{1,5},{2,6},{3,7},{4,0},{5,1},{6,2},{7,3},{8,12},{9,13},{10,... | collective-permute-start | bytes 393224 | tf_op jit(solution)/shard_map/ppermute | solution.py:486
  33.3 9.7 %collective-permute-start.13 = (f32[64,256]{1,0:T(8,128)S(1)}, f32[64,256]{1,0:T(8,128)S(1)}, u32[]{:S(2)}, u32[]{:S(2)}) collective-permute-start(f32[64,256]{1,0:T(8,128)S(1)} %get-tuple-element.126), channel_id=1, source_target_pairs={{0,1},{1,0},{2,3},{3,2},{4,5},{5,4},{6,7},{7,6},{8,9},{9,8},{10,11... | collective-permute-start | bytes 196616 | tf_op jit(solution)/shard_map/ppermute | solution.py:490
  35.0 8.3 %collective-permute-start.14 = (f32[64,256]{1,0:T(8,128)S(1)}, f32[64,256]{1,0:T(8,128)S(1)}, u32[]{:S(2)}, u32[]{:S(2)}) collective-permute-start(f32[64,256]{1,0:T(8,128)S(1)} %get-tuple-element.127), channel_id=1, source_target_pairs={{0,2},{1,3},{2,0},{3,1},{4,6},{5,7},{6,4},{7,5},{8,10},{9,11},{10,... | collective-permute-start | bytes 196616 | tf_op jit(solution)/shard_map/ppermute | solution.py:490
  37.6 6.8 %collective-permute-start.15 = (f32[64,256]{1,0:T(8,128)S(1)}, f32[64,256]{1,0:T(8,128)S(1)}, u32[]{:S(2)}, u32[]{:S(2)}) collective-permute-start(f32[64,256]{1,0:T(8,128)S(1)} %get-tuple-element.128), channel_id=1, source_target_pairs={{0,3},{1,2},{2,1},{3,0},{4,7},{5,6},{6,5},{7,4},{8,11},{9,10},{10,... | collective-permute-start | bytes 196616 | tf_op jit(solution)/shard_map/ppermute | solution.py:490
  38.8 8.9 %collective-permute-start.22 = (f32[64,256]{1,0:T(8,128)S(1)}, f32[64,256]{1,0:T(8,128)S(1)}, u32[]{:S(2)}, u32[]{:S(2)}) collective-permute-start(f32[64,256]{1,0:T(8,128)S(1)} %get-tuple-element.132), channel_id=1, source_target_pairs={{0,1},{1,0},{2,3},{3,2},{4,5},{5,4},{6,7},{7,6},{8,9},{9,8},{10,11... | collective-permute-start | bytes 196616 | tf_op jit(solution)/shard_map/ppermute | solution.py:490
  39.5 8.7 %collective-permute-start.23 = (f32[64,256]{1,0:T(8,128)S(1)}, f32[64,256]{1,0:T(8,128)S(1)}, u32[]{:S(2)}, u32[]{:S(2)}) collective-permute-start(f32[64,256]{1,0:T(8,128)S(1)} %get-tuple-element.133), channel_id=1, source_target_pairs={{0,2},{1,3},{2,0},{3,1},{4,6},{5,7},{6,4},{7,5},{8,10},{9,11},{10,... | collective-permute-start | bytes 196616 | tf_op jit(solution)/shard_map/ppermute | solution.py:490
  43.0 6.2 %collective-permute-start.24 = (f32[64,256]{1,0:T(8,128)S(1)}, f32[64,256]{1,0:T(8,128)S(1)}, u32[]{:S(2)}, u32[]{:S(2)}) collective-permute-start(f32[64,256]{1,0:T(8,128)S(1)} %get-tuple-element.134), channel_id=1, source_target_pairs={{0,3},{1,2},{2,1},{3,0},{4,7},{5,6},{6,5},{7,4},{8,11},{9,10},{10,... | collective-permute-start | bytes 196616 | tf_op jit(solution)/shard_map/ppermute | solution.py:490
  45.6 6.9 %collective-permute-start.17 = (f32[8,4096]{1,0:T(8,128)S(1)}, f32[8,4096]{1,0:T(8,128)S(1)}, u32[]{:S(2)}, u32[]{:S(2)}) collective-permute-start(f32[8,4096]{1,0:T(8,128)S(1)} %shard_map.183.refs_18_), channel_id=1, source_target_pairs={{0,16},{1,17},{2,18},{3,19},{4,12},{5,13},{6,14},{7,15},{8,24},{9,... | collective-permute-start | bytes 393224 | tf_op jit(solution)/shard_map/ppermute | solution.py:486
  46.2 6.3 %collective-permute-start.16 = (f32[8,4096]{1,0:T(8,128)S(1)}, f32[8,4096]{1,0:T(8,128)S(1)}, u32[]{:S(2)}, u32[]{:S(2)}) collective-permute-start(f32[8,4096]{1,0:T(8,128)S(1)} %shard_map.183.refs_18_), channel_id=1, source_target_pairs={{0,8},{1,9},{2,10},{3,11},{4,20},{5,21},{6,22},{7,23},{8,0},{9,1},... | collective-permute-start | bytes 393224 | tf_op jit(solution)/shard_map/ppermute | solution.py:486
  50.4 5.0 %collective-permute-start.26 = (f32[8,4096]{1,0:T(8,128)S(1)}, f32[8,4096]{1,0:T(8,128)S(1)}, u32[]{:S(2)}, u32[]{:S(2)}) collective-permute-start(f32[8,4096]{1,0:T(8,128)S(1)} %shard_map.187), channel_id=1, source_target_pairs={{0,16},{1,17},{2,18},{3,19},{4,12},{5,13},{6,14},{7,15},{8,24},{9,... | collective-permute-start | bytes 393224 | tf_op jit(solution)/shard_map/ppermute | solution.py:486
  50.9 5.0 %collective-permute-start.25 = (f32[8,4096]{1,0:T(8,128)S(1)}, f32[8,4096]{1,0:T(8,128)S(1)}, u32[]{:S(2)}, u32[]{:S(2)}) collective-permute-start(f32[8,4096]{1,0:T(8,128)S(1)} %shard_map.187), channel_id=1, source_target_pairs={{0,8},{1,9},{2,10},{3,11},{4,20},{5,21},{6,22},{7,23},{8,0},{9,1},... | collective-permute-start | bytes 393224 | tf_op jit(solution)/shard_map/ppermute | solution.py:486
  52.5 5.4 %collective-permute-start.19 = (f32[2,8,4096]{2,1,0:T(8,128)S(1)}, f32[2,8,4096]{2,1,0:T(8,128)S(1)}, u32[]{:S(2)}, u32[]{:S(2)}) collective-permute-start(f32[2,8,4096]{2,1,0:T(8,128)S(1)} %shard_map.184), channel_id=1, source_target_pairs={{0,4},{1,5},{2,6},{3,7},{4,0},{5,1},{6,2},{7,3},{8,12},{9,13},{10,... | collective-permute-start | bytes 786440 | tf_op jit(solution)/shard_map/ppermute | solution.py:486
  55.9 2.0 %collective-permute-start.28 = (f32[2,8,4096]{2,1,0:T(8,128)S(1)}, f32[2,8,4096]{2,1,0:T(8,128)S(1)}, u32[]{:S(2)}, u32[]{:S(2)}) collective-permute-start(f32[2,8,4096]{2,1,0:T(8,128)S(1)} %shard_map.188), channel_id=1, source_target_pairs={{0,4},{1,5},{2,6},{3,7},{4,0},{5,1},{6,2},{7,3},{8,12},{9,13},{10,... | collective-permute-start | bytes 786440 | tf_op jit(solution)/shard_map/ppermute | solution.py:486
  56.0 1.7 %collective-permute-start.18 = (f32[8,4096]{1,0:T(8,128)S(1)}, f32[8,4096]{1,0:T(8,128)S(1)}, u32[]{:S(2)}, u32[]{:S(2)}) collective-permute-start(f32[8,4096]{1,0:T(8,128)S(1)} %shard_map.183.refs_18_), channel_id=1, source_target_pairs={{0,4},{1,5},{2,6},{3,7},{4,0},{5,1},{6,2},{7,3},{8,12},{9,13},{10,... | collective-permute-start | bytes 393224 | tf_op jit(solution)/shard_map/ppermute | solution.py:486
  56.5 1.4 %collective-permute-start.27 = (f32[8,4096]{1,0:T(8,128)S(1)}, f32[8,4096]{1,0:T(8,128)S(1)}, u32[]{:S(2)}, u32[]{:S(2)}) collective-permute-start(f32[8,4096]{1,0:T(8,128)S(1)} %shard_map.187), channel_id=1, source_target_pairs={{0,4},{1,5},{2,6},{3,7},{4,0},{5,1},{6,2},{7,3},{8,12},{9,13},{10,... | collective-permute-start | bytes 393224 | tf_op jit(solution)/shard_map/ppermute | solution.py:486

commit v9 on v8

--- a/solution.py
+++ b/solution.py
@@ -117,24 +117,29 @@
     return o, lax.rem(o, 2), lax.div(o, 2)
 
 
+def fetch(source, whole, sem, side):
+    number, half = sem.shape[0], whole.shape[2]
+    step = whole.shape[0] // number
+    lanes = pl.ds(pl.multiple_of(side * half, LANES), half)
+    return [
+        pltpu.make_async_copy(source.at[pl.ds(n * step, step), :, lanes], whole.at[pl.ds(n * step, step)], sem.at[n])
+        for n in range(number)
+    ]
+
+
+def hand_out(whole, outs):
+    for n, out in enumerate(outs):
+        out[...] = whole[:, :, n * out.shape[2]:(n + 1) * out.shape[2]]
+
+
 def fetch_kernel(source, *rest):
     outs, (whole, sem) = rest[:-2], rest[-2:]
-    copies = [pltpu.make_async_copy(source.at[n], whole.at[n], sem.at[n]) for n in range(whole.shape[0])]
+    copies = fetch(source, whole, sem, 1 - my_core())
     for copy in copies:
         copy.start()
     for copy in copies:
         copy.wait()
-    core = my_core()
-    copies = []
-    for n, out in enumerate(outs):
-        side = 1 - core if n < CHUNKS else core
-        at = side * (whole.shape[2] // 2) + n % CHUNKS * out.shape[2]
-        lanes = pl.ds(pl.multiple_of(at, LANES), out.shape[2])
-        copies.append(pltpu.make_async_copy(whole.at[:, :, lanes], out, sem.at[n]))
-    for copy in copies:
-        copy.start()
-    for copy in copies:
-        copy.wait()
+    hand_out(whole, outs)
 
 
 class Place:
@@ -159,8 +164,12 @@
         return BLK * self.tiles[tile, 0], BLK * self.tiles[tile, 1]
 
 
-def setup_kernel(per_device, tiles, host, rotation, after, high, low):
+def setup_kernel(per_device, tiles, host, rotation, source, after, *rest):
+    outs, (high, low, whole, sem) = rest[:-4], rest[-4:]
     core = my_core()
+    copies = fetch(source, whole, sem, core)
+    for copy in copies:
+        copy.start()
     at = Place(per_device, tiles, host)
     pair = BLK // 2
     heads = [at.heads(chip) for chip in (at.chip ^ 3, at.chip ^ at.bit_1, at.chip ^ at.bit_2, at.chip)]
@@ -186,6 +195,9 @@
         picked = lax.dot_general(chosen, values, (((1,), (1,)), ((), ())), preferred_element_type=f32).astype(bf16)
         for e in range(2):
             out[:, e * LANES:(e + 1) * LANES] = jnp.where(keep, dot(picked, columns[e]), 0.0).astype(bf16)
+    for copy in copies:
+        copy.wait()
+    hand_out(whole, outs)
 
 
 def ready_kernel(per_device, n_grid, tiles, host, mask, log_r, *rest):
@@ -493,12 +505,13 @@
     orbitals = pltpu.with_memory_space_constraint(orbitals, pltpu.HBM)
 
     part = jax.ShapeDtypeStruct((per_device, planes, chunk), f32)
+    scratch = [pltpu.VMEM((per_device, planes, half), f32), DMA((4,))]
     fetched = pl.pallas_call(
-        fetch_kernel, out_shape=[part] * (2 * CHUNKS), in_specs=[HBM], out_specs=[VM] * (2 * CHUNKS),
-        scratch_shapes=[pltpu.VMEM(shape, f32), DMA((max(per_device, 2 * CHUNKS),))], name="fetch", compiler_params=grant(8),
+        fetch_kernel, out_shape=[part] * CHUNKS, in_specs=[HBM], out_specs=[VM] * CHUNKS,
+        scratch_shapes=scratch, name="fetch", compiler_params=grant(8),
     )(orbitals)
-    theirs, mine = [], fetched[CHUNKS:]
-    for taken in fetched[:CHUNKS]:
+    theirs = []
+    for taken in fetched:
         theirs.append(swap(taken, 1, 1))
 
     pair = BLK // 2
@@ -509,10 +522,11 @@
     c, r = line_np()
     c, r = line_np()
     host = jnp.asarray(host_np(chips).reshape(-1))
-    high, low = pl.pallas_call(
-        functools.partial(setup_kernel, per_device), out_shape=[wide_table] * 2,
-        in_specs=[SM, SM, VM, ANY], out_specs=[VM] * 2, name="setup", compiler_params=grant(8),
-    )(tile_list, host, rotation, taken)
+    *mine, high, low = pl.pallas_call(
+        functools.partial(setup_kernel, per_device), out_shape=[part] * CHUNKS + [wide_table] * 2,
+        in_specs=[SM, SM, VM, HBM, ANY], out_specs=[VM] * (CHUNKS + 2), scratch_shapes=scratch, name="setup",
+        compiler_params=grant(8),
+    )(tile_list, host, rotation, orbitals, taken)
 
     def rotate(first, count, fields, *after):
         part = jax.ShapeDtypeStruct((count, planes, chunk * (len(fields) // 2)), f32)

time: 59.2 us -> 59.4 us (level)
  transfers between devices with their start and end apart: 25 -> 25, of which waited for: 13 -> 12; matrix products, arithmetic and copies ran while one was open for 0% -> 0% of each run, Pallas kernels for 17% -> 19%
where the time goes in v9:
time: 59.4 us; the launch traced here: 58.3 us
  starting transfers between devices  23.8 us (40%)
  waiting for transfers between devices  20.9 us (35%)
  Pallas kernels  12.4 us (21%)
  between operations  1.04 us (2%)
    ppermute x19, waiting for transfers between devices, swap(): return lax.ppermute(x, axes, moves)  18.3 us
    ppermute x19, starting transfers between devices, swap(): return lax.ppermute(x, axes, moves)  14.9 us
    ppermute x6, starting transfers between devices, cross(): return lax.ppermute(x, axes, moves)  8.9 us
    ppermute x6, waiting for transfers between devices, cross(): return lax.ppermute(x, axes, moves)  2.61 us
    pallas_call x1, Pallas kernels, tile_device(): pl.pallas_call(functools.partial(ready_kernel, per_device, n_grid), out_s...  2.6 us
    pallas_call x2, Pallas kernels, tile_device(): pl.pallas_call(functools.partial(backward_kernel, u, (CHUNKS, CHUNKS, len...  2.39 us
    pallas_call x2, Pallas kernels, tile_device(): pl.pallas_call(functools.partial(forward_kernel, u, counts + (n_grid - 1,...  1.99 us
    pallas_call x1, Pallas kernels, tile_device(): pl.pallas_call(functools.partial(setup_kernel, per_device), out_shape=[pa...  1.97 us
  transfers between devices with their start and end apart: 25, of which 12 were waited for; matrix products, arithmetic and copies ran while one was open for 0% of the time, Pallas kernels for 19%

profile of v9, /device:TPU:0, one launch (start us, length us, event | category | flops | bytes accessed | tf_op | source)
XLA Modules:
  0.0 58.3 jit_solution(8340548306462463264)
XLA Ops:
  0.0 1.3 %fetch.1 = (f32[16,8,1024]{2,1,0:T(8,128)S(1)}, f32[16,8,1024]{2,1,0:T(8,128)S(1)}) custom-call(f32[16,8,4096]{2,1,0:T(8,128)} %source.3), custom_call_target="tpu_custom_call" | custom-call | tf_op jit(solution)/shard_map/fetch/pallas_call | solution.py:509
  1.3 0.6 collective-permute-start.4
  1.9 0.1 collective-permute-start.6
  2.0 0.1 copy.24.tiles
  2.1 2.0 %setup.1 = (f32[16,8,1024]{2,1,0:T(8,128)S(1)}, f32[16,8,1024]{2,1,0:T(8,128)S(1)}, bf16[256,256]{1,0:T(8,128)(2,1)S(1)}, bf16[256,256]{1,0:T(8,128)(2,1)S(1)}) custom-call(s32[4,2]{1,0:T(4,128)S(1)} %copy.24.tiles, s32[1024]{0:T(1024)S(1)} %copy-done.15, f32[128,128]{1,0:T(8,128)S(1)} %copy-done.11, f32[16,8,4096]{2,1,0:T(8,128)} %source.3, ...), custom_call_target="tpu_custom_call" | custom-call | tf_op jit(solution)/shard_map/setup/pallas_call | solution.py:525
  4.1 0.5 shard_map.174
  4.6 3.0 %collective-permute-start.5 = (f32[12,8,1024]{2,1,0:T(8,128)S(1)}, f32[12,8,1024]{2,1,0:T(8,128)S(1)}, u32[]{:S(2)}, u32[]{:S(2)}) collective-permute-start(f32[12,8,1024]{2,1,0:T(8,128)S(1)} %get-tuple-element.115.rest_2_), channel_id=1, source_target_pairs={{0,8},{1,9},{2,10},{3,11},{4,20},{5,21},{6,22},{7,23},{8,0},{9,1},... | collective-permute-start | bytes 1179656 | tf_op jit(solution)/shard_map/ppermute | solution.py:498
  7.6 0.5 shard_map.175
  8.1 0.1 collective-permute-start.8
  8.2 0.7 %shard_map.176 = (f32[4,8,2048]{2,1,0:T(8,128)S(1)}, f32[4,8,2048]{2,1,0:T(8,128)S(1)}) custom-call(bf16[256,256]{1,0:T(8,128)(2,1)S(1)} %get-tuple-element.110.high, bf16[256,256]{1,0:T(8,128)(2,1)S(1)} %get-tuple-element.111.low, f32[16,8,1024]{2,1,0:T(8,128)S(1)} %get-tuple-element.112.rest_0_, f32[16,8,1024]{2,1,0:T(8,128)S(1)} %collective-permute-done.4.rest_1_, ...), custom_call_target="tpu_custom_call" | custom-call | tf_op jit(solution)/shard_map/pallas_call | solution.py:533
  8.9 4.4 %collective-permute-done.5.got = f32[12,8,1024]{2,1,0:T(8,128)S(1)} collective-permute-done((f32[12,8,1024]{2,1,0:T(8,128)S(1)}, f32[12,8,1024]{2,1,0:T(8,128)S(1)}, u32[]{:S(2)}, u32[]{:S(2)}) %collective-permute-start.5) | collective-permute-done | bytes 393248 | tf_op jit(solution)/shard_map/ppermute | solution.py:498
  13.3 2.1 %collective-permute-start.7 = (f32[6,8,1024]{2,1,0:T(8,128)S(1)}, f32[6,8,1024]{2,1,0:T(8,128)S(1)}, u32[]{:S(2)}, u32[]{:S(2)}) collective-permute-start(f32[6,8,1024]{2,1,0:T(8,128)S(1)} %shard_map.177.rest_0_), channel_id=1, source_target_pairs={{0,16},{1,17},{2,18},{3,19},{4,12},{5,13},{6,14},{7,15},{8,24},{9,... | collective-permute-start | bytes 589832 | tf_op jit(solution)/shard_map/ppermute | solution.py:498
  15.5 2.6 %ready.1 = (f32[16,8,4096]{2,1,0:T(8,128)}, f32[6,64,128]{2,1,0:T(8,128)S(1)}, f32[8,128]{1,0:T(8,128)S(1)}, f32[8,128]{1,0:T(8,128)S(1)}, s32[1]{0:T(128)}) custom-call(s32[4,2]{1,0:T(4,128)S(1)} %copy.24.tiles, s32[1024]{0:T(1024)S(1)} %copy-done.15, s32[128,128]{1,0:T(8,128)S(1)} %copy-done.12, f32[64,128]{1,0:T(8,128)S(1)} %copy-done.14, ...), custom_call_target="tpu_custom_call" | custom-call | tf_op jit(solution)/shard_map/ready/pallas_call | solution.py:568
  18.1 1.4 %collective-permute-done.8.got = f32[12,8,1024]{2,1,0:T(8,128)S(1)} collective-permute-done((f32[12,8,1024]{2,1,0:T(8,128)S(1)}, f32[12,8,1024]{2,1,0:T(8,128)S(1)}, u32[]{:S(2)}, u32[]{:S(2)}) %collective-permute-start.8) | collective-permute-done | bytes 393248 | tf_op jit(solution)/shard_map/ppermute | solution.py:498
  19.6 2.4 %collective-permute-start.9 = (f32[6,8,1024]{2,1,0:T(8,128)S(1)}, f32[6,8,1024]{2,1,0:T(8,128)S(1)}, u32[]{:S(2)}, u32[]{:S(2)}) collective-permute-start(f32[6,8,1024]{2,1,0:T(8,128)S(1)} %shard_map.178.rest_0_), channel_id=1, source_target_pairs={{0,16},{1,17},{2,18},{3,19},{4,12},{5,13},{6,14},{7,15},{8,24},{9,... | collective-permute-start | bytes 589832 | tf_op jit(solution)/shard_map/ppermute | solution.py:498
  22.0 1.5 %collective-permute-start.12 = (f32[4,8,2048]{2,1,0:T(8,128)S(1)}, f32[4,8,2048]{2,1,0:T(8,128)S(1)}, u32[]{:S(2)}, u32[]{:S(2)}) collective-permute-start(f32[4,8,2048]{2,1,0:T(8,128)S(1)} %get-tuple-element.118.rest_0_), channel_id=1, source_target_pairs={{0,8},{1,9},{2,10},{3,11},{4,20},{5,21},{6,22},{7,23},{8,0},{9,1},... | collective-permute-start | bytes 786440 | tf_op jit(solution)/shard_map/ppermute | solution.py:498
  23.5 0.1 collective-permute-start.10
  23.6 2.6 %collective-permute-done.9.passed = f32[6,8,1024]{2,1,0:T(8,128)S(1)} collective-permute-done((f32[6,8,1024]{2,1,0:T(8,128)S(1)}, f32[6,8,1024]{2,1,0:T(8,128)S(1)}, u32[]{:S(2)}, u32[]{:S(2)}) %collective-permute-start.9) | collective-permute-done | bytes 196640 | tf_op jit(solution)/shard_map/ppermute | solution.py:498
  26.3 2.1 %collective-permute-done.12.got = f32[4,8,2048]{2,1,0:T(8,128)S(1)} collective-permute-done((f32[4,8,2048]{2,1,0:T(8,128)S(1)}, f32[4,8,2048]{2,1,0:T(8,128)S(1)}, u32[]{:S(2)}, u32[]{:S(2)}) %collective-permute-start.12) | collective-permute-done | bytes 262176 | tf_op jit(solution)/shard_map/ppermute | solution.py:498
  28.4 0.1 collective-permute-start.20
  28.6 1.0 %shard_map.182 = (f32[64,256]{1,0:T(8,128)S(1)}, f32[64,256]{1,0:T(8,128)S(1)}, f32[64,256]{1,0:T(8,128)S(1)}, f32[512,256]{1,0:T(8,128)S(1)}, f32[64,256]{1,0:T(8,128)S(1)}, /*index=5*/f32[64,256]{1,0:T(8,128)S(1)}) custom-call(f32[6,8,1024]{2,1,0:T(8,128)S(1)} %shard_map.179.rest_0_.refs_0_, f32[6,8,1024]{2,1,0:T(8,128)S(1)} %shard_map.180.rest_0_.refs_1_, ...), custom_call_target="tpu_custom_call" | custom-call | tf_op jit(solution)/shard_map/pallas_call | solution.py:607
  29.6 3.7 %collective-permute-done.20.passed = f32[2,8,2048]{2,1,0:T(8,128)S(1)} collective-permute-done((f32[2,8,2048]{2,1,0:T(8,128)S(1)}, f32[2,8,2048]{2,1,0:T(8,128)S(1)}, u32[]{:S(2)}, u32[]{:S(2)}) %collective-permute-start.20) | collective-permute-done | bytes 131104 | tf_op jit(solution)/shard_map/ppermute | solution.py:498
  33.4 0.1 collective-permute-start.21
  33.5 1.6 %collective-permute-start.13 = (f32[64,256]{1,0:T(8,128)S(1)}, f32[64,256]{1,0:T(8,128)S(1)}, u32[]{:S(2)}, u32[]{:S(2)}) collective-permute-start(f32[64,256]{1,0:T(8,128)S(1)} %get-tuple-element.126), channel_id=1, source_target_pairs={{0,1},{1,0},{2,3},{3,2},{4,5},{5,4},{6,7},{7,6},{8,9},{9,8},{10,11... | collective-permute-start | bytes 196616 | tf_op jit(solution)/shard_map/ppermute | solution.py:502
  35.1 2.6 %collective-permute-start.14 = (f32[64,256]{1,0:T(8,128)S(1)}, f32[64,256]{1,0:T(8,128)S(1)}, u32[]{:S(2)}, u32[]{:S(2)}) collective-permute-start(f32[64,256]{1,0:T(8,128)S(1)} %get-tuple-element.127), channel_id=1, source_target_pairs={{0,2},{1,3},{2,0},{3,1},{4,6},{5,7},{6,4},{7,5},{8,10},{9,11},{10,... | collective-permute-start | bytes 196616 | tf_op jit(solution)/shard_map/ppermute | solution.py:502
  37.7 0.2 collective-permute-start.15
  37.9 1.0 %shard_map.186 = (f32[64,256]{1,0:T(8,128)S(1)}, f32[64,256]{1,0:T(8,128)S(1)}, f32[64,256]{1,0:T(8,128)S(1)}, f32[512,256]{1,0:T(8,128)S(1)}, f32[64,256]{1,0:T(8,128)S(1)}, /*index=5*/f32[64,256]{1,0:T(8,128)S(1)}) custom-call(f32[6,8,1024]{2,1,0:T(8,128)S(1)} %shard_map.179.rest_0_.refs_0_, f32[6,8,1024]{2,1,0:T(8,128)S(1)} %shard_map.180.rest_0_.refs_1_, ...), custom_call_target="tpu_custom_call" | custom-call | tf_op jit(solution)/shard_map/pallas_call | solution.py:607
  39.0 0.7 %collective-permute-start.22 = (f32[64,256]{1,0:T(8,128)S(1)}, f32[64,256]{1,0:T(8,128)S(1)}, u32[]{:S(2)}, u32[]{:S(2)}) collective-permute-start(f32[64,256]{1,0:T(8,128)S(1)} %get-tuple-element.132), channel_id=1, source_target_pairs={{0,1},{1,0},{2,3},{3,2},{4,5},{5,4},{6,7},{7,6},{8,9},{9,8},{10,11... | collective-permute-start | bytes 196616 | tf_op jit(solution)/shard_map/ppermute | solution.py:502
  39.7 3.5 %collective-permute-start.23 = (f32[64,256]{1,0:T(8,128)S(1)}, f32[64,256]{1,0:T(8,128)S(1)}, u32[]{:S(2)}, u32[]{:S(2)}) collective-permute-start(f32[64,256]{1,0:T(8,128)S(1)} %get-tuple-element.133), channel_id=1, source_target_pairs={{0,2},{1,3},{2,0},{3,1},{4,6},{5,7},{6,4},{7,5},{8,10},{9,11},{10,... | collective-permute-start | bytes 196616 | tf_op jit(solution)/shard_map/ppermute | solution.py:502
  43.2 0.2 collective-permute-start.24
  43.4 1.1 %collective-permute-done.15.refs_6_ = f32[64,256]{1,0:T(8,128)S(1)} collective-permute-done((f32[64,256]{1,0:T(8,128)S(1)}, f32[64,256]{1,0:T(8,128)S(1)}, u32[]{:S(2)}, u32[]{:S(2)}) %collective-permute-start.15) | collective-permute-done | bytes 65568 | tf_op jit(solution)/shard_map/ppermute | solution.py:502
  44.5 1.2 %shard_map.183.refs_18_ = f32[8,4096]{1,0:T(8,128)S(1)} custom-call(f32[8,128]{1,0:T(8,128)S(1)} %get-tuple-element.121.flags, f32[6,8,1024]{2,1,0:T(8,128)S(1)} %shard_map.179.rest_0_.refs_0_, f32[6,8,1024]{2,1,0:T(8,128)S(1)} %shard_map.180.rest_0_.refs_1_, f32[6,8,1024]{2,1,0:T(8,128)S(1)} %collective-permute-done.10.refs_2_, ...), custom_call_target="tpu_custom_call" | custom-call | tf_op jit(solution)/shard_map/pallas_call | solution.py:625
  45.8 0.6 collective-permute-start.17
  46.3 1.5 %collective-permute-start.16 = (f32[8,4096]{1,0:T(8,128)S(1)}, f32[8,4096]{1,0:T(8,128)S(1)}, u32[]{:S(2)}, u32[]{:S(2)}) collective-permute-start(f32[8,4096]{1,0:T(8,128)S(1)} %shard_map.183.refs_18_), channel_id=1, source_target_pairs={{0,8},{1,9},{2,10},{3,11},{4,20},{5,21},{6,22},{7,23},{8,0},{9,1},... | collective-permute-start | bytes 393224 | tf_op jit(solution)/shard_map/ppermute | solution.py:498
  47.8 0.6 %collective-permute-done.23.refs_5_ = f32[64,256]{1,0:T(8,128)S(1)} collective-permute-done((f32[64,256]{1,0:T(8,128)S(1)}, f32[64,256]{1,0:T(8,128)S(1)}, u32[]{:S(2)}, u32[]{:S(2)}) %collective-permute-start.23) | collective-permute-done | bytes 65568 | tf_op jit(solution)/shard_map/ppermute | solution.py:502
  48.4 0.9 %collective-permute-done.24.refs_6_ = f32[64,256]{1,0:T(8,128)S(1)} collective-permute-done((f32[64,256]{1,0:T(8,128)S(1)}, f32[64,256]{1,0:T(8,128)S(1)}, u32[]{:S(2)}, u32[]{:S(2)}) %collective-permute-start.24) | collective-permute-done | bytes 65568 | tf_op jit(solution)/shard_map/ppermute | solution.py:502
  49.3 1.2 %shard_map.187 = f32[8,4096]{1,0:T(8,128)S(1)} custom-call(f32[8,128]{1,0:T(8,128)S(1)} %get-tuple-element.121.flags, f32[6,8,1024]{2,1,0:T(8,128)S(1)} %shard_map.179.rest_0_.refs_0_, f32[6,8,1024]{2,1,0:T(8,128)S(1)} %shard_map.180.rest_0_.refs_1_, f32[6,8,1024]{2,1,0:T(8,128)S(1)} %collective-permute-done.10.refs_2_, ...), custom_call_target="tpu_custom_call" | custom-call | tf_op jit(solution)/shard_map/pallas_call | solution.py:625
  50.5 0.6 collective-permute-start.26
  51.1 1.5 %collective-permute-start.25 = (f32[8,4096]{1,0:T(8,128)S(1)}, f32[8,4096]{1,0:T(8,128)S(1)}, u32[]{:S(2)}, u32[]{:S(2)}) collective-permute-start(f32[8,4096]{1,0:T(8,128)S(1)} %shard_map.187), channel_id=1, source_target_pairs={{0,8},{1,9},{2,10},{3,11},{4,20},{5,21},{6,22},{7,23},{8,0},{9,1},... | collective-permute-start | bytes 393224 | tf_op jit(solution)/shard_map/ppermute | solution.py:498
  52.7 2.9 %collective-permute-done.26.y = f32[8,4096]{1,0:T(8,128)S(1)} collective-permute-done((f32[8,4096]{1,0:T(8,128)S(1)}, f32[8,4096]{1,0:T(8,128)S(1)}, u32[]{:S(2)}, u32[]{:S(2)}) %collective-permute-start.26) | collective-permute-done | bytes 131104 | tf_op jit(solution)/shard_map/ppermute | solution.py:498
  55.6 0.5 collective-permute-done.25.x
  56.1 0.1 collective-permute-start.28
  56.2 0.5 collective-permute-start.18
  56.7 0.1 collective-permute-start.27
  57.4 0.5 collective-permute-done.18
  57.9 0.2 collective-permute-done.27
  58.1 0.3 conditional.1
  58.1 0.2 place.2
  (57 shorter events, 0.5 us)
Async XLA Ops:
  0.0 2.1 %copy-start.15 = (s32[1024]{0:T(1024)S(1)}, s32[1024]{0:T(1024)}, u32[]{:S(2)}) copy-start(s32[1024]{0:T(1024)} %constant.31.clone.host) | copy-start | bytes 12292
  0.0 2.0 %copy-start.16 = (s32[4,2]{0,1:T(2,128)S(1)}, s32[4,2]{0,1:T(2,128)}, u32[]{:S(2)}) copy-start(s32[4,2]{0,1:T(2,128)} %param.22) | copy-start | bytes 100
  0.0 2.1 %copy-start.11 = (f32[128,128]{1,0:T(8,128)S(1)}, f32[128,128]{1,0:T(8,128)}, u32[]{:S(2)}) copy-start(f32[128,128]{1,0:T(8,128)} %rotation.1) | copy-start | bytes 196612
  1.3 2.7 %collective-permute-start.4 = (f32[16,8,1024]{2,1,0:T(8,128)S(1)}, f32[16,8,1024]{2,1,0:T(8,128)S(1)}, u32[]{:S(2)}, u32[]{:S(2)}) collective-permute-start(f32[16,8,1024]{2,1,0:T(8,128)S(1)} %get-tuple-element.113), channel_id=1, source_target_pairs={{0,4},{1,5},{2,6},{3,7},{4,0},{5,1},{6,2},{7,3},{8,12},{9,13},{10,... | collective-permute-start | bytes 1572872 | tf_op jit(solution)/shard_map/ppermute | solution.py:498
  1.9 5.6 %collective-permute-start.6 = (f32[16,8,1024]{2,1,0:T(8,128)S(1)}, f32[16,8,1024]{2,1,0:T(8,128)S(1)}, u32[]{:S(2)}, u32[]{:S(2)}) collective-permute-start(f32[16,8,1024]{2,1,0:T(8,128)S(1)} %get-tuple-element.109.after), channel_id=1, source_target_pairs={{0,4},{1,5},{2,6},{3,7},{4,0},{5,1},{6,2},{7,3},{8,12},{9,13},{10,... | collective-permute-start | bytes 1572872 | tf_op jit(solution)/shard_map/ppermute | solution.py:498
  4.6 8.7 %collective-permute-start.5 = (f32[12,8,1024]{2,1,0:T(8,128)S(1)}, f32[12,8,1024]{2,1,0:T(8,128)S(1)}, u32[]{:S(2)}, u32[]{:S(2)}) collective-permute-start(f32[12,8,1024]{2,1,0:T(8,128)S(1)} %get-tuple-element.115.rest_2_), channel_id=1, source_target_pairs={{0,8},{1,9},{2,10},{3,11},{4,20},{5,21},{6,22},{7,23},{8,0},{9,1},... | collective-permute-start | bytes 1179656 | tf_op jit(solution)/shard_map/ppermute | solution.py:498
  8.1 7.4 %copy-start.12 = (s32[128,128]{1,0:T(8,128)S(1)}, s32[128,128]{1,0:T(8,128)}, u32[]{:S(2)}) copy-start(s32[128,128]{1,0:T(8,128)} %mask.1) | copy-start | bytes 196612
  8.1 7.4 %copy-start.14 = (f32[64,128]{1,0:T(8,128)S(1)}, f32[64,128]{1,0:T(8,128)}, u32[]{:S(2)}) copy-start(f32[64,128]{1,0:T(8,128)} %constant.32.clone.log_r) | copy-start | bytes 98308
  8.1 11.4 %collective-permute-start.8 = (f32[12,8,1024]{2,1,0:T(8,128)S(1)}, f32[12,8,1024]{2,1,0:T(8,128)S(1)}, u32[]{:S(2)}, u32[]{:S(2)}) collective-permute-start(f32[12,8,1024]{2,1,0:T(8,128)S(1)} %get-tuple-element.117.rest_4_), channel_id=1, source_target_pairs={{0,8},{1,9},{2,10},{3,11},{4,20},{5,21},{6,22},{7,23},{8,0},{9,1},... | collective-permute-start | bytes 1179656 | tf_op jit(solution)/shard_map/ppermute | solution.py:498
  13.3 10.1 %collective-permute-start.7 = (f32[6,8,1024]{2,1,0:T(8,128)S(1)}, f32[6,8,1024]{2,1,0:T(8,128)S(1)}, u32[]{:S(2)}, u32[]{:S(2)}) collective-permute-start(f32[6,8,1024]{2,1,0:T(8,128)S(1)} %shard_map.177.rest_0_), channel_id=1, source_target_pairs={{0,16},{1,17},{2,18},{3,19},{4,12},{5,13},{6,14},{7,15},{8,24},{9,... | collective-permute-start | bytes 589832 | tf_op jit(solution)/shard_map/ppermute | solution.py:498
  19.5 9.0 %copy-start.3 = (bf16[2,256,256]{2,1,0:T(8,128)(2,1)S(1)}, bf16[2,256,256]{2,1,0:T(8,128)(2,1)}, u32[]{:S(2)}) copy-start(bf16[2,256,256]{2,1,0:T(8,128)(2,1)} %constant.38.clone.refs_5_.refs_7_) | copy-start | bytes 786436
  19.5 9.0 %copy-start.4 = (bf16[2,256,256]{2,1,0:T(8,128)(2,1)S(1)}, bf16[2,256,256]{2,1,0:T(8,128)(2,1)}, u32[]{:S(2)}) copy-start(bf16[2,256,256]{2,1,0:T(8,128)(2,1)} %constant.37.clone.refs_4_.refs_6_) | copy-start | bytes 786436
  19.6 9.0 %copy-start.5 = (f32[512,128]{1,0:T(8,128)S(1)}, f32[512,128]{1,0:T(8,128)}, u32[]{:S(2)}) copy-start(f32[512,128]{1,0:T(8,128)} %constant.33.clone.refs_8_.refs_10_) | copy-start | bytes 786436
  19.6 9.0 %copy-start.8 = (bf16[256,256]{1,0:T(8,128)(2,1)S(1)}, bf16[256,256]{1,0:T(8,128)(2,1)}, u32[]{:S(2)}) copy-start(bf16[256,256]{1,0:T(8,128)(2,1)} %constant.42.clone.refs_7_.refs_9_) | copy-start | bytes 393220
  19.6 9.0 %copy-start.9 = (bf16[256,256]{1,0:T(8,128)(2,1)S(1)}, bf16[256,256]{1,0:T(8,128)(2,1)}, u32[]{:S(2)}) copy-start(bf16[256,256]{1,0:T(8,128)(2,1)} %constant.41.clone.refs_6_.refs_8_) | copy-start | bytes 393220
  19.6 6.5 %collective-permute-start.9 = (f32[6,8,1024]{2,1,0:T(8,128)S(1)}, f32[6,8,1024]{2,1,0:T(8,128)S(1)}, u32[]{:S(2)}, u32[]{:S(2)}) collective-permute-start(f32[6,8,1024]{2,1,0:T(8,128)S(1)} %shard_map.178.rest_0_), channel_id=1, source_target_pairs={{0,16},{1,17},{2,18},{3,19},{4,12},{5,13},{6,14},{7,15},{8,24},{9,... | collective-permute-start | bytes 589832 | tf_op jit(solution)/shard_map/ppermute | solution.py:498
  22.0 6.4 %collective-permute-start.12 = (f32[4,8,2048]{2,1,0:T(8,128)S(1)}, f32[4,8,2048]{2,1,0:T(8,128)S(1)}, u32[]{:S(2)}, u32[]{:S(2)}) collective-permute-start(f32[4,8,2048]{2,1,0:T(8,128)S(1)} %get-tuple-element.118.rest_0_), channel_id=1, source_target_pairs={{0,8},{1,9},{2,10},{3,11},{4,20},{5,21},{6,22},{7,23},{8,0},{9,1},... | collective-permute-start | bytes 786440 | tf_op jit(solution)/shard_map/ppermute | solution.py:498
  23.5 5.0 %collective-permute-start.10 = (f32[6,8,1024]{2,1,0:T(8,128)S(1)}, f32[6,8,1024]{2,1,0:T(8,128)S(1)}, u32[]{:S(2)}, u32[]{:S(2)}) collective-permute-start(f32[6,8,1024]{2,1,0:T(8,128)S(1)} %shard_map.179.rest_0_.refs_0_), channel_id=1, source_target_pairs={{0,4},{1,5},{2,6},{3,7},{4,0},{5,1},{6,2},{7,3},{8,12},{9,13},{10,... | collective-permute-start | bytes 589832 | tf_op jit(solution)/shard_map/ppermute | solution.py:498
  26.2 2.3 %collective-permute-start.11 = (f32[6,8,1024]{2,1,0:T(8,128)S(1)}, f32[6,8,1024]{2,1,0:T(8,128)S(1)}, u32[]{:S(2)}, u32[]{:S(2)}) collective-permute-start(f32[6,8,1024]{2,1,0:T(8,128)S(1)} %shard_map.180.rest_0_.refs_1_), channel_id=1, source_target_pairs={{0,4},{1,5},{2,6},{3,7},{4,0},{5,1},{6,2},{7,3},{8,12},{9,13},{10,... | collective-permute-start | bytes 589832 | tf_op jit(solution)/shard_map/ppermute | solution.py:498
  28.4 5.0 %collective-permute-start.20 = (f32[2,8,2048]{2,1,0:T(8,128)S(1)}, f32[2,8,2048]{2,1,0:T(8,128)S(1)}, u32[]{:S(2)}, u32[]{:S(2)}) collective-permute-start(f32[2,8,2048]{2,1,0:T(8,128)S(1)} %shard_map.181.refs_10_), channel_id=1, source_target_pairs={{0,16},{1,17},{2,18},{3,19},{4,12},{5,13},{6,14},{7,15},{8,24},{9,... | collective-permute-start | bytes 393224 | tf_op jit(solution)/shard_map/ppermute | solution.py:498
  29.6 14.9 %copy-start = (bf16[2,256,256]{2,1,0:T(8,128)(2,1)S(1)}, bf16[2,256,256]{2,1,0:T(8,128)(2,1)}, u32[]{:S(2)}) copy-start(bf16[2,256,256]{2,1,0:T(8,128)(2,1)} %constant.40.clone.refs_8_) | copy-start | bytes 786436
  29.6 14.9 %copy-start.1 = (bf16[2,256,256]{2,1,0:T(8,128)(2,1)S(1)}, bf16[2,256,256]{2,1,0:T(8,128)(2,1)}, u32[]{:S(2)}) copy-start(bf16[2,256,256]{2,1,0:T(8,128)(2,1)} %constant.39.clone.refs_7_) | copy-start | bytes 786436
  29.6 14.9 %copy-start.2 = (f32[512,128]{1,0:T(8,128)S(1)}, f32[512,128]{1,0:T(8,128)}, u32[]{:S(2)}) copy-start(f32[512,128]{1,0:T(8,128)} %constant.34.clone.refs_11_) | copy-start | bytes 786436
  29.6 14.9 %copy-start.6 = (bf16[256,256]{1,0:T(8,128)(2,1)S(1)}, bf16[256,256]{1,0:T(8,128)(2,1)}, u32[]{:S(2)}) copy-start(bf16[256,256]{1,0:T(8,128)(2,1)} %constant.44.clone.refs_10_) | copy-start | bytes 393220
  29.6 14.9 %copy-start.7 = (bf16[256,256]{1,0:T(8,128)(2,1)S(1)}, bf16[256,256]{1,0:T(8,128)(2,1)}, u32[]{:S(2)}) copy-start(bf16[256,256]{1,0:T(8,128)(2,1)} %constant.43.clone.refs_9_) | copy-start | bytes 393220
  29.6 14.9 %copy-start.10 = (f32[3,64,128]{2,1,0:T(8,128)S(1)}, f32[3,64,128]{2,1,0:T(8,128)}, u32[]{:S(2)}) copy-start(f32[3,64,128]{2,1,0:T(8,128)} %constant.36.clone.refs_14_) | copy-start | bytes 294916
  29.6 14.9 %copy-start.13 = (f32[2,8,128]{2,1,0:T(8,128)S(1)}, f32[2,8,128]{2,1,0:T(8,128)}, u32[]{:S(2)}) copy-start(f32[2,8,128]{2,1,0:T(8,128)} %constant.35.clone.refs_12_) | copy-start | bytes 24580
  33.4 4.5 %collective-permute-start.21 = (f32[2,8,2048]{2,1,0:T(8,128)S(1)}, f32[2,8,2048]{2,1,0:T(8,128)S(1)}, u32[]{:S(2)}, u32[]{:S(2)}) collective-permute-start(f32[2,8,2048]{2,1,0:T(8,128)S(1)} %shard_map.185.refs_4_), channel_id=1, source_target_pairs={{0,4},{1,5},{2,6},{3,7},{4,0},{5,1},{6,2},{7,3},{8,12},{9,13},{10,... | collective-permute-start | bytes 393224 | tf_op jit(solution)/shard_map/ppermute | solution.py:498
  33.5 9.7 %collective-permute-start.13 = (f32[64,256]{1,0:T(8,128)S(1)}, f32[64,256]{1,0:T(8,128)S(1)}, u32[]{:S(2)}, u32[]{:S(2)}) collective-permute-start(f32[64,256]{1,0:T(8,128)S(1)} %get-tuple-element.126), channel_id=1, source_target_pairs={{0,1},{1,0},{2,3},{3,2},{4,5},{5,4},{6,7},{7,6},{8,9},{9,8},{10,11... | collective-permute-start | bytes 196616 | tf_op jit(solution)/shard_map/ppermute | solution.py:502
  35.1 8.3 %collective-permute-start.14 = (f32[64,256]{1,0:T(8,128)S(1)}, f32[64,256]{1,0:T(8,128)S(1)}, u32[]{:S(2)}, u32[]{:S(2)}) collective-permute-start(f32[64,256]{1,0:T(8,128)S(1)} %get-tuple-element.127), channel_id=1, source_target_pairs={{0,2},{1,3},{2,0},{3,1},{4,6},{5,7},{6,4},{7,5},{8,10},{9,11},{10,... | collective-permute-start | bytes 196616 | tf_op jit(solution)/shard_map/ppermute | solution.py:502
  37.7 6.8 %collective-permute-start.15 = (f32[64,256]{1,0:T(8,128)S(1)}, f32[64,256]{1,0:T(8,128)S(1)}, u32[]{:S(2)}, u32[]{:S(2)}) collective-permute-start(f32[64,256]{1,0:T(8,128)S(1)} %get-tuple-element.128), channel_id=1, source_target_pairs={{0,3},{1,2},{2,1},{3,0},{4,7},{5,6},{6,5},{7,4},{8,11},{9,10},{10,... | collective-permute-start | bytes 196616 | tf_op jit(solution)/shard_map/ppermute | solution.py:502
  39.0 8.9 %collective-permute-start.22 = (f32[64,256]{1,0:T(8,128)S(1)}, f32[64,256]{1,0:T(8,128)S(1)}, u32[]{:S(2)}, u32[]{:S(2)}) collective-permute-start(f32[64,256]{1,0:T(8,128)S(1)} %get-tuple-element.132), channel_id=1, source_target_pairs={{0,1},{1,0},{2,3},{3,2},{4,5},{5,4},{6,7},{7,6},{8,9},{9,8},{10,11... | collective-permute-start | bytes 196616 | tf_op jit(solution)/shard_map/ppermute | solution.py:502
  39.7 8.7 %collective-permute-start.23 = (f32[64,256]{1,0:T(8,128)S(1)}, f32[64,256]{1,0:T(8,128)S(1)}, u32[]{:S(2)}, u32[]{:S(2)}) collective-permute-start(f32[64,256]{1,0:T(8,128)S(1)} %get-tuple-element.133), channel_id=1, source_target_pairs={{0,2},{1,3},{2,0},{3,1},{4,6},{5,7},{6,4},{7,5},{8,10},{9,11},{10,... | collective-permute-start | bytes 196616 | tf_op jit(solution)/shard_map/ppermute | solution.py:502
  43.2 6.2 %collective-permute-start.24 = (f32[64,256]{1,0:T(8,128)S(1)}, f32[64,256]{1,0:T(8,128)S(1)}, u32[]{:S(2)}, u32[]{:S(2)}) collective-permute-start(f32[64,256]{1,0:T(8,128)S(1)} %get-tuple-element.134), channel_id=1, source_target_pairs={{0,3},{1,2},{2,1},{3,0},{4,7},{5,6},{6,5},{7,4},{8,11},{9,10},{10,... | collective-permute-start | bytes 196616 | tf_op jit(solution)/shard_map/ppermute | solution.py:502
  45.8 6.9 %collective-permute-start.17 = (f32[8,4096]{1,0:T(8,128)S(1)}, f32[8,4096]{1,0:T(8,128)S(1)}, u32[]{:S(2)}, u32[]{:S(2)}) collective-permute-start(f32[8,4096]{1,0:T(8,128)S(1)} %shard_map.183.refs_18_), channel_id=1, source_target_pairs={{0,16},{1,17},{2,18},{3,19},{4,12},{5,13},{6,14},{7,15},{8,24},{9,... | collective-permute-start | bytes 393224 | tf_op jit(solution)/shard_map/ppermute | solution.py:498
  46.3 6.3 %collective-permute-start.16 = (f32[8,4096]{1,0:T(8,128)S(1)}, f32[8,4096]{1,0:T(8,128)S(1)}, u32[]{:S(2)}, u32[]{:S(2)}) collective-permute-start(f32[8,4096]{1,0:T(8,128)S(1)} %shard_map.183.refs_18_), channel_id=1, source_target_pairs={{0,8},{1,9},{2,10},{3,11},{4,20},{5,21},{6,22},{7,23},{8,0},{9,1},... | collective-permute-start | bytes 393224 | tf_op jit(solution)/shard_map/ppermute | solution.py:498
  50.5 5.0 %collective-permute-start.26 = (f32[8,4096]{1,0:T(8,128)S(1)}, f32[8,4096]{1,0:T(8,128)S(1)}, u32[]{:S(2)}, u32[]{:S(2)}) collective-permute-start(f32[8,4096]{1,0:T(8,128)S(1)} %shard_map.187), channel_id=1, source_target_pairs={{0,16},{1,17},{2,18},{3,19},{4,12},{5,13},{6,14},{7,15},{8,24},{9,... | collective-permute-start | bytes 393224 | tf_op jit(solution)/shard_map/ppermute | solution.py:498
  51.1 5.0 %collective-permute-start.25 = (f32[8,4096]{1,0:T(8,128)S(1)}, f32[8,4096]{1,0:T(8,128)S(1)}, u32[]{:S(2)}, u32[]{:S(2)}) collective-permute-start(f32[8,4096]{1,0:T(8,128)S(1)} %shard_map.187), channel_id=1, source_target_pairs={{0,8},{1,9},{2,10},{3,11},{4,20},{5,21},{6,22},{7,23},{8,0},{9,1},... | collective-permute-start | bytes 393224 | tf_op jit(solution)/shard_map/ppermute | solution.py:498
  52.6 5.5 %collective-permute-start.19 = (f32[2,8,4096]{2,1,0:T(8,128)S(1)}, f32[2,8,4096]{2,1,0:T(8,128)S(1)}, u32[]{:S(2)}, u32[]{:S(2)}) collective-permute-start(f32[2,8,4096]{2,1,0:T(8,128)S(1)} %shard_map.184), channel_id=1, source_target_pairs={{0,4},{1,5},{2,6},{3,7},{4,0},{5,1},{6,2},{7,3},{8,12},{9,13},{10,... | collective-permute-start | bytes 786440 | tf_op jit(solution)/shard_map/ppermute | solution.py:498
  56.1 2.0 %collective-permute-start.28 = (f32[2,8,4096]{2,1,0:T(8,128)S(1)}, f32[2,8,4096]{2,1,0:T(8,128)S(1)}, u32[]{:S(2)}, u32[]{:S(2)}) collective-permute-start(f32[2,8,4096]{2,1,0:T(8,128)S(1)} %shard_map.188), channel_id=1, source_target_pairs={{0,4},{1,5},{2,6},{3,7},{4,0},{5,1},{6,2},{7,3},{8,12},{9,13},{10,... | collective-permute-start | bytes 786440 | tf_op jit(solution)/shard_map/ppermute | solution.py:498
  56.2 1.7 %collective-permute-start.18 = (f32[8,4096]{1,0:T(8,128)S(1)}, f32[8,4096]{1,0:T(8,128)S(1)}, u32[]{:S(2)}, u32[]{:S(2)}) collective-permute-start(f32[8,4096]{1,0:T(8,128)S(1)} %shard_map.183.refs_18_), channel_id=1, source_target_pairs={{0,4},{1,5},{2,6},{3,7},{4,0},{5,1},{6,2},{7,3},{8,12},{9,13},{10,... | collective-permute-start | bytes 393224 | tf_op jit(solution)/shard_map/ppermute | solution.py:498
  56.7 1.4 %collective-permute-start.27 = (f32[8,4096]{1,0:T(8,128)S(1)}, f32[8,4096]{1,0:T(8,128)S(1)}, u32[]{:S(2)}, u32[]{:S(2)}) collective-permute-start(f32[8,4096]{1,0:T(8,128)S(1)} %shard_map.187), channel_id=1, source_target_pairs={{0,4},{1,5},{2,6},{3,7},{4,0},{5,1},{6,2},{7,3},{8,12},{9,13},{10,... | collective-permute-start | bytes 393224 | tf_op jit(solution)/shard_map/ppermute | solution.py:498
